TPU v7x, 128 devices: a whole 4x4x4 slice. The times are simulated.
128 devices in a mesh: req: 32 (over y, x, core), mdl: 4 (over z).
Axes of the slice: x: 4, y: 4, z: 4, core: 2. Of those that a mesh axis runs over, the one named last changes fastest.
Arguments:
- hidden_in: bfloat16 [256, 16, 2048], P('req'), may hold values from -6 to 6
- mixer_gain: bfloat16 [2048], replicated, may hold values from 0.5 to 1.5
- w_query: bfloat16 [2048, 1024], P(None, 'mdl'), may hold values from -0.125 to 0.125
- w_kv: bfloat16 [2, 2048, 256], replicated, may hold values from -0.125 to 0.125
- w_attn_out: bfloat16 [1024, 2048], P('mdl'), may hold values from -0.1875 to 0.1875
- prompt_kv: bfloat16 [64, 2, 1024, 256], P('req')
- prompt_lengths: int32 [64], P('req'), may hold values from 1 to 1024, as said below
- member: int32 [256], P('req'), may hold values from 0 to 1
- accepted: int32 [256], P('req'), may hold values from 1 to 16, as said below
- w_z: bfloat16 [2048, 1536], P(None, 'mdl'), may hold values from -0.125 to 0.125
- w_x: bfloat16 [2048, 1536], P(None, 'mdl'), may hold values from -0.125 to 0.125
- w_bc: bfloat16 [2048, 512], replicated, may hold values from -0.125 to 0.125
- w_dt: bfloat16 [2048, 24], P(None, 'mdl'), may hold values from -0.125 to 0.125
- conv_x: bfloat16 [4, 1536], P(None, 'mdl'), may hold values from -1.5 to 1.5
- conv_bc: bfloat16 [4, 512], replicated, may hold values from -1.5 to 1.5
- ssm_rate: float32 [24], P('mdl'), may hold values from 1 to 16
- dt_bias: float32 [24], P('mdl'), may hold values from -4 to 0.5
- skip_d: float32 [24], P('mdl'), may hold values from 0.5 to 1.5
- prompt_state: float32 [64, 24, 64, 256], P('req', 'mdl'), may hold values from -0.4 to 0.4
- prompt_conv_x: bfloat16 [64, 3, 1536], P('req', None, 'mdl'), may hold values from -6 to 6
- prompt_conv_bc: bfloat16 [64, 3, 512], P('req'), may hold values from -6 to 6
- w_mamba_out: bfloat16 [1536, 2048], P('mdl'), may hold values from -0.15625 to 0.15625
- mlp_gain: bfloat16 [2048], replicated, may hold values from 0.5 to 1.5
- w_gate: bfloat16 [2048, 4096], P(None, 'req'), may hold values from -0.125 to 0.125
- w_up: bfloat16 [2048, 4096], P(None, 'req'), may hold values from -0.125 to 0.125
- w_down: bfloat16 [4096, 2048], P('req'), may hold values from -0.09375 to 0.09375
- final_gain: bfloat16 [2048], replicated, may hold values from 0.5 to 1.5
- head_weight: bfloat16 [32768, 2048], P('req')
- draft_ids: int32 [256, 16], replicated, may hold values from 0 to 32767
Outputs:
- hidden_out: bfloat16 [256, 16, 2048], P(('req', 'mdl'))
- verify_scores: float32 [256, 16], P(('req', 'mdl'))
- kept_state: float32 [256, 24, 64, 256], P(('req', 'mdl'))
- kept_conv: bfloat16 [256, 3, 2048], P(('req', 'mdl'))
Inputs may be any that keep to these rules, and one draw needn't show every extreme that they name: Each request has accepted 1 to 16 drafts; both ends occur in every draw. `prompt_lengths`: a prompt of 1024 tokens occurs in every draw. `member`: index of the request's prompt among the 2 prompts of its block of 8 requests.
All inputs are finite; a program needn't handle non-finite values.
Results may differ from a plain program's by a relative error of at most 0.017.
Values may be sent and summed in bfloat16 or wider, within the bound.
No kernel may reach another device: no remote copies, remote signals or barrier semaphores. Data moves between devices by JAX's collectives and lax.ppermute only.
A program may use at most 128 MiB of HBM per device.

v0:
```python
import functools

import jax
import jax.numpy as jnp
import numpy as np
from jax import lax
from jax.experimental import pallas as pl
from jax.experimental.pallas import tpu as pltpu
from jax.sharding import PartitionSpec as P

Q_HEADS = 8
KV_HEADS = 2
HEAD_DIM = 128
SSM_DIM = 64
STATE = 256
CONV = 4
PROMPTS = 2
P_MAX = 1024
DRAFT = 16
SIDE = 4
CORES = 2

eps_norm = 1e-05
far_below = -1e30

HOPS = ((0, 1), (0, 3), (1, 0), (3, 0))
ORDERS = tuple(
    tuple(tuple(HOPS[(first + step) % 4] for step in range(4)) for first in firsts)
    for firsts in ((0, 1), (2, 3))
)


def device_at(y, x, core):
    return (y * SIDE + x) * CORES + core


def hop_pairs(fragment, step):
    pairs = []
    for y in range(SIDE):
        for x in range(SIDE):
            for core in range(CORES):
                flip_y, flip_x = ORDERS[core][fragment][step]
                pairs.append((device_at(y, x, core), device_at(y ^ flip_y, x ^ flip_x, core)))
    return pairs


CORE_PAIRS = [(device, device ^ 1) for device in range(SIDE * SIDE * CORES)]


def offsets_of(core, fragment):
    found = [(0, 0)]
    for flip_y, flip_x in ORDERS[core][fragment]:
        found = found + [(y ^ flip_y, x ^ flip_x) for y, x in found]
    return found


def hop(part, fragment, step):
    return lax.ppermute(part, "req", hop_pairs(fragment, step))


def swap_core(part):
    return lax.ppermute(part, "req", CORE_PAIRS)


def gather_rows(fragments):
    held = list(fragments)
    for step in range(4):
        came = [hop(held[f], f, step) for f in range(2)]
        held = [jnp.concatenate([held[f], came[f]], axis=0) for f in range(2)]
    return held, [swap_core(part) for part in held]


def scatter_rows(own, sibling):
    came = [swap_core(part) for part in sibling]
    held = [own[f] + came[f] for f in range(2)]
    for step in reversed(range(4)):
        half = held[0].shape[0] // 2
        came = [hop(held[f][half:], f, step) for f in range(2)]
        held = [held[f][:half] + came[f] for f in range(2)]
    return held


def block_table():
    table = np.zeros((CORES, 4, 16, 4), np.int32)
    for core in range(CORES):
        for half in range(2):
            for fragment in range(2):
                for place, (y, x) in enumerate(offsets_of(core ^ half, fragment)):
                    table[core, half * 2 + fragment, place] = (y, x, half, fragment)
    return table.reshape(CORES, 64, 4)


def rms_scale(values, gain):
    widened = values.astype(jnp.float32)
    spread = jnp.mean(widened * widened, axis=-1, keepdims=True)
    return widened * lax.rsqrt(spread + eps_norm) * gain.astype(jnp.float32)


HIGHEST = lax.Precision.HIGHEST
NEXT_TO = (((1,), (1,)), ((), ()))


def dot32(left, right, dims=None):
    dims = dims or (((1,), (0,)), ((), ()))
    return lax.dot_general(left, right, dims, preferred_element_type=jnp.float32)


def exact_dot(left, right):
    return jnp.dot(left, right, precision=HIGHEST, preferred_element_type=jnp.float32)


def mixer_kernel(
    member_ref,
    accepted_ref,
    lengths_ref,
    place_ref,
    hidden_ref,
    gain_ref,
    w_dt_ref,
    conv_x_ref,
    conv_bc_ref,
    rate_ref,
    bias_ref,
    skip_ref,
    past_x_ref,
    past_bc_ref,
    w_query_hbm,
    w_kv_hbm,
    prompt_hbm,
    w_x_hbm,
    w_bc_hbm,
    w_z_hbm,
    state_hbm,
    w_attn_hbm,
    w_mamba_hbm,
    far_ref,
    near_ref,
    kept_ref,
    kept_x_ref,
    kept_bc_ref,
    w_query,
    w_kv,
    prompt,
    w_x,
    w_bc,
    w_z,
    state,
    w_out,
    mixed_scr,
    lanes_scr,
    sems,
):
    rank, group = place_ref[0], place_ref[1]
    tokens = hidden_ref.shape[0]
    requests = tokens // DRAFT
    inner = w_x.shape[1]
    heads = inner // SSM_DIM
    query_width = w_query.shape[1]
    copies = [
        pltpu.make_async_copy(source, target, sems.at[index])
        for index, (source, target) in enumerate(
            (
                (w_query_hbm, w_query),
                (w_kv_hbm.at[group], w_kv),
                (prompt_hbm.at[0, group], prompt.at[0]),
                (prompt_hbm.at[1, group], prompt.at[1]),
                (w_x_hbm, w_x),
                (w_bc_hbm, w_bc),
                (w_z_hbm, w_z),
                (state_hbm, state),
                (w_attn_hbm, w_out.at[pl.ds(0, query_width), :]),
                (w_mamba_hbm, w_out.at[pl.ds(query_width, inner), :]),
            )
        )
    ]
    for copy in copies:
        copy.start()

    row = lax.broadcasted_iota(jnp.int32, (tokens, 1), 0)
    time, request = row % DRAFT, row // DRAFT
    own_prompt = jnp.zeros((tokens, 1), jnp.int32)
    last = jnp.zeros((tokens, 1), jnp.int32)
    for r in range(requests):
        own_prompt = jnp.where(request == r, member_ref[r], own_prompt)
        last = jnp.where(request == r, accepted_ref[r] - 1, last)
    first_prompt = own_prompt == 0

    widened = hidden_ref[...].astype(jnp.float32)
    spread = jnp.mean(widened * widened, axis=-1, keepdims=True)
    normed = (
        widened * lax.rsqrt(spread + eps_norm) * gain_ref[...].astype(jnp.float32)
    ).astype(jnp.bfloat16)

    copies[0].wait()
    queries = dot32(normed, w_query[...]).astype(jnp.bfloat16)
    copies[1].wait()
    drafts = dot32(normed, w_kv[...]).astype(jnp.bfloat16)
    local_heads = query_width // HEAD_DIM
    query_rows = jnp.concatenate(
        [queries[:, h * HEAD_DIM : (h + 1) * HEAD_DIM] for h in range(local_heads)], axis=0
    )
    scale = HEAD_DIM**-0.5
    row_first = jnp.concatenate([own_prompt] * local_heads, axis=0) == 0
    draft_scores = dot32(query_rows, drafts[:, :HEAD_DIM], NEXT_TO) * scale
    same = (row // DRAFT == lax.broadcasted_iota(jnp.int32, (tokens, tokens), 1) // DRAFT) & (
        lax.broadcasted_iota(jnp.int32, (tokens, tokens), 1) <= row
    )
    draft_mask = jnp.concatenate([same] * local_heads, axis=0)
    draft_scores = jnp.where(draft_mask, draft_scores, far_below)
    copies[2].wait()
    copies[3].wait()
    scores = jnp.where(
        row_first,
        dot32(query_rows, prompt[0, :, :HEAD_DIM], NEXT_TO),
        dot32(query_rows, prompt[1, :, :HEAD_DIM], NEXT_TO),
    )
    length = jnp.where(row_first, lengths_ref[0], lengths_ref[1])
    position = lax.broadcasted_iota(jnp.int32, scores.shape, 1)
    scores = jnp.where(position < length, scores * scale, far_below)
    top = jnp.maximum(
        jnp.max(scores, axis=1, keepdims=True), jnp.max(draft_scores, axis=1, keepdims=True)
    )
    weights = jnp.exp(scores - top)
    draft_weights = jnp.exp(draft_scores - top)
    total = jnp.sum(weights, axis=1, keepdims=True) + jnp.sum(draft_weights, axis=1, keepdims=True)
    weighted = (
        dot32(jnp.where(row_first, weights, 0.0).astype(jnp.bfloat16), prompt[0, :, HEAD_DIM:])
        + dot32(jnp.where(row_first, 0.0, weights).astype(jnp.bfloat16), prompt[1, :, HEAD_DIM:])
        + dot32(draft_weights.astype(jnp.bfloat16), drafts[:, HEAD_DIM:])
    )
    attended = (weighted / total).astype(jnp.bfloat16)
    for h in range(local_heads):
        mixed_scr[:, h * HEAD_DIM : (h + 1) * HEAD_DIM] = attended[h * tokens : (h + 1) * tokens]

    def convolve_rows(series, past_ref, taps_ref):
        past = [
            jnp.where(
                first_prompt,
                past_ref[0, j : j + 1, :].astype(jnp.float32),
                past_ref[1, j : j + 1, :].astype(jnp.float32),
            )
            for j in range(CONV - 1)
        ]
        taps = taps_ref[...].astype(jnp.float32)
        summed = series * taps[CONV - 1 : CONV, :]
        for shift in range(1, CONV):
            window = pltpu.roll(series, shift, 0)
            for t in range(shift):
                window = jnp.where(time == t, past[CONV - 1 - shift + t], window)
            summed = summed + window * taps[CONV - 1 - shift : CONV - shift, :]
        return summed * jax.nn.sigmoid(summed)

    copies[4].wait()
    in_x = dot32(normed, w_x[...]).astype(jnp.bfloat16)
    heads_x = convolve_rows(in_x.astype(jnp.float32), past_x_ref, conv_x_ref)
    copies[5].wait()
    in_bc = dot32(normed, w_bc[...]).astype(jnp.bfloat16)
    conv_bcs = convolve_rows(in_bc.astype(jnp.float32), past_bc_ref, conv_bc_ref)
    b_part = conv_bcs[:, :STATE].astype(jnp.bfloat16)
    c_part = conv_bcs[:, STATE:].astype(jnp.bfloat16)

    def widen(values):
        lanes_scr[...] = jnp.zeros(lanes_scr.shape, jnp.float32)
        lanes_scr[:, :heads] = values
        return lanes_scr[...]

    spread_lanes = (
        lax.broadcasted_iota(jnp.int32, (tokens, inner), 0)
        == lax.broadcasted_iota(jnp.int32, (tokens, inner), 1) // SSM_DIM
    ).astype(jnp.float32)
    dt_in = dot32(normed, w_dt_ref[...]).astype(jnp.bfloat16).astype(jnp.float32) + bias_ref[...]
    step = jnp.maximum(dt_in, 0.0) + jnp.log1p(jnp.exp(-jnp.abs(dt_in)))
    log_decay = exact_dot(same.astype(jnp.float32), widen(-step * rate_ref[...]))
    step_x = exact_dot(widen(step), spread_lanes)
    skip_x = exact_dot(widen(jnp.broadcast_to(skip_ref[...], (tokens, heads))), spread_lanes)
    decay_x = exact_dot(log_decay, spread_lanes)
    turned = log_decay.T
    intersection = dot32(c_part, b_part, NEXT_TO)
    scaled_x = heads_x * step_x
    low = lax.broadcasted_iota(jnp.int32, (tokens, 2 * SSM_DIM), 1) < SSM_DIM
    groups = []
    for pair in range(heads // 2):
        mixing = []
        for h in (2 * pair, 2 * pair + 1):
            gaps = log_decay[:, h : h + 1] - turned[h : h + 1, :]
            mixing.append(
                (jnp.exp(jnp.where(same, gaps, far_below)) * intersection).astype(jnp.bfloat16)
            )
        lanes = scaled_x[:, pair * 2 * SSM_DIM : (pair + 1) * 2 * SSM_DIM]
        both = jnp.concatenate([jnp.where(low, lanes, 0.0), jnp.where(low, 0.0, lanes)], axis=0)
        groups.append(dot32(jnp.concatenate(mixing, axis=1), both.astype(jnp.bfloat16)))
    copies[7].wait()
    carried = jnp.where(
        first_prompt,
        dot32(c_part, state[0].astype(jnp.bfloat16), NEXT_TO),
        dot32(c_part, state[1].astype(jnp.bfloat16), NEXT_TO),
    )
    ssm_out = jnp.concatenate(groups, axis=1) + carried * jnp.exp(decay_x) + skip_x * heads_x
    copies[6].wait()
    gate_z = dot32(normed, w_z[...]).astype(jnp.bfloat16).astype(jnp.float32)
    mixed_scr[:, query_width:] = (ssm_out * (gate_z * jax.nn.sigmoid(gate_z))).astype(jnp.bfloat16)

    own_rows = tokens // SIDE
    copies[8].wait()
    copies[9].wait()
    for out_ref, flips in ((far_ref, (3, 2)), (near_ref, (0, 1))):
        rows = jnp.concatenate(
            [
                mixed_scr[pl.ds(pl.multiple_of((rank ^ flip) * own_rows, own_rows), own_rows), :]
                for flip in flips
            ],
            axis=0,
        )
        out_ref[...] = dot32(rows, w_out[...]).astype(jnp.bfloat16)

    other = lax.broadcasted_iota(jnp.int32, (tokens, tokens), 1)
    pick = (other == request * DRAFT + last).astype(jnp.float32)
    final_log = exact_dot(pick, log_decay)
    final_x = exact_dot(final_log, spread_lanes)
    carry_x = jnp.exp(jnp.where(time <= last, final_x - decay_x, far_below))
    carried_x = (scaled_x * carry_x).T.astype(jnp.bfloat16)
    shrink = jnp.exp(final_x).T
    for r in range(requests):
        b_here = jnp.where(request == r, b_part, jnp.zeros_like(b_part))
        kept = shrink[:, r * DRAFT : r * DRAFT + 1] * state[member_ref[r]] + dot32(
            carried_x, b_here
        )
        kept_ref[r] = kept.astype(jnp.bfloat16)

    def kept_rows(first_request, count, series, past_ref):
        at = lax.broadcasted_iota(jnp.int32, (count, 1), 0)
        here, edge = at // (CONV - 1), at % (CONV - 1)
        start = jnp.zeros((count, 1), jnp.int32)
        owner = jnp.zeros((count, 1), jnp.int32)
        for r in range(count // (CONV - 1)):
            start = jnp.where(here == r, accepted_ref[first_request + r], start)
            owner = jnp.where(here == r, member_ref[first_request + r], owner)
        index = start + edge
        token = (here + first_request) * DRAFT + index - (CONV - 1)
        chosen = (lax.broadcasted_iota(jnp.int32, (count, tokens), 1) == token) & (
            index >= CONV - 1
        )
        rows = dot32(chosen.astype(jnp.bfloat16), series)
        for p in range(PROMPTS):
            for j in range(CONV - 1):
                rows = jnp.where(
                    (owner == p) & (index == j), past_ref[p, j : j + 1, :].astype(jnp.float32), rows
                )
        return rows.astype(jnp.bfloat16)

    kept_x_ref[...] = kept_rows(0, kept_x_ref.shape[0], in_x, past_x_ref)
    kept_bc_ref[...] = kept_rows(
        rank * (requests // SIDE), kept_bc_ref.shape[0], in_bc, past_bc_ref
    )


def mixer(
    hidden, mixer_gain, w_query, w_kv, w_attn_out, prompt_kv, prompt_lengths, member, accepted, w_z, w_x, w_bc,
    w_dt, conv_x, conv_bc, ssm_rate, dt_bias, skip_d, prompt_state, prompt_conv_x, prompt_conv_bc, w_mamba_out, rank,
):
    tokens, width = hidden.shape
    requests = tokens // DRAFT
    inner = w_x.shape[1]
    query_width = w_query.shape[1]
    group = rank * (query_width // HEAD_DIM) // (Q_HEADS // KV_HEADS)
    place = jnp.stack([rank, group]).astype(jnp.int32)
    scalars = pl.BlockSpec(memory_space=pltpu.SMEM)
    whole = pl.BlockSpec(memory_space=pltpu.VMEM)
    left = pl.BlockSpec(memory_space=pl.ANY)
    edges = CONV - 1
    bf16 = jnp.bfloat16
    state = prompt_state.reshape(PROMPTS, inner, STATE)
    return pl.pallas_call(
        mixer_kernel,
        out_shape=[
            jax.ShapeDtypeStruct((tokens // 2, width), bf16),
            jax.ShapeDtypeStruct((tokens // 2, width), bf16),
            jax.ShapeDtypeStruct((requests, inner, STATE), bf16),
            jax.ShapeDtypeStruct((requests * edges, inner), bf16),
            jax.ShapeDtypeStruct((requests // SIDE * edges, 2 * STATE), bf16),
        ],
        in_specs=[scalars] * 4 + [whole] * 10 + [left] * 9,
        out_specs=[whole] * 5,
        scratch_shapes=[
            pltpu.VMEM(w_query.shape, bf16),
            pltpu.VMEM(w_kv.shape[1:], bf16),
            pltpu.VMEM((PROMPTS, *prompt_kv.shape[2:]), bf16),
            pltpu.VMEM(w_x.shape, bf16),
            pltpu.VMEM(w_bc.shape, bf16),
            pltpu.VMEM(w_z.shape, bf16),
            pltpu.VMEM(state.shape, jnp.float32),
            pltpu.VMEM((query_width + inner, width), bf16),
            pltpu.VMEM((tokens, query_width + inner), bf16),
            pltpu.VMEM((tokens, 128), jnp.float32),
            pltpu.SemaphoreType.DMA((10,)),
        ],
        compiler_params=pltpu.CompilerParams(vmem_limit_bytes=48 << 20),
        cost_estimate=pl.CostEstimate(
            flops=3_000_000_000, bytes_accessed=20_000_000, transcendentals=1_000_000
        ),
        name="mixer",
    )(
        member, accepted, prompt_lengths, place, hidden, mixer_gain.reshape(1, width), w_dt, conv_x, conv_bc,
        ssm_rate.reshape(1, -1), dt_bias.reshape(1, -1), skip_d.reshape(1, -1), prompt_conv_x, prompt_conv_bc,
        w_query, w_kv, prompt_kv, w_x, w_bc, w_z, state, w_attn_out, w_mamba_out,
    )


def feed_kernel(first_ref, second_ref, both_ref, down_ref, first_out, second_out):
    hidden = down_ref.shape[0]
    for rows_ref, out_ref in ((first_ref, first_out), (second_ref, second_out)):
        pair = jnp.dot(rows_ref[...], both_ref[...], preferred_element_type=jnp.float32)
        gate, up = pair[:, :hidden], pair[:, hidden:]
        active = (gate * jax.nn.sigmoid(gate) * up).astype(jnp.bfloat16)
        out_ref[...] = jnp.dot(
            active, down_ref[...], preferred_element_type=jnp.float32
        ).astype(jnp.bfloat16)


def feed(first, second, w_both, w_down):
    rows, width = first.shape
    whole = pl.BlockSpec(memory_space=pltpu.VMEM)
    return pl.pallas_call(
        feed_kernel,
        out_shape=[jax.ShapeDtypeStruct((rows, width), jnp.bfloat16)] * 2,
        in_specs=[whole] * 4,
        out_specs=[whole] * 2,
        compiler_params=pltpu.CompilerParams(vmem_limit_bytes=32 << 20),
        cost_estimate=pl.CostEstimate(
            flops=2 * rows * width * 2 * 3 * w_down.shape[0],
            bytes_accessed=4 * rows * width * 2 + 3 * w_down.size * 2,
            transcendentals=2 * rows * w_down.shape[0],
        ),
        name="feed",
    )(first, second, w_both, w_down)


def head_kernel(base_ref, targets_ref, owners_ref, *refs):
    rows_refs, head_ref, out_ref = refs[:4], refs[4], refs[5]
    vocab = head_ref.shape[0]
    lanes = rows_refs[0].shape[0]
    lane = lax.broadcasted_iota(jnp.int32, (lanes, 128), 0)
    column = lax.broadcasted_iota(jnp.int32, (lanes, 128), 1)
    packed = jnp.zeros(out_ref.shape, jnp.float32)
    for which in range(4):
        logits = lax.dot_general(
            head_ref[...],
            rows_refs[which][...],
            (((1,), (1,)), ((), ())),
            preferred_element_type=jnp.float32,
        )
        ids = lax.broadcasted_iota(jnp.int32, (vocab, lanes), 0) + base_ref[0]
        target = jnp.sum(
            jnp.where(ids == targets_ref[which : which + 1, :], logits, 0.0), axis=0, keepdims=True
        )
        top = jnp.max(logits, axis=0, keepdims=True)
        total = jnp.sum(jnp.exp(logits - top), axis=0, keepdims=True)
        device = lax.broadcasted_iota(jnp.int32, (out_ref.shape[0], lanes), 0)
        here = device == owners_ref[which : which + 1, :]
        for kind, stat in enumerate((top, total, target)):
            place = (column == (kind * 2 + which % 2) * DRAFT + lane % DRAFT).astype(jnp.float32)
            packed = packed + jnp.dot(
                jnp.where(here, stat, 0.0),
                place,
                precision=lax.Precision.HIGHEST,
                preferred_element_type=jnp.float32,
            )
    out_ref[...] = packed


def head_stats(base, targets, owners, rows, head_weight, devices):
    whole = pl.BlockSpec(memory_space=pltpu.VMEM)
    return pl.pallas_call(
        head_kernel,
        out_shape=jax.ShapeDtypeStruct((devices, 128), jnp.float32),
        in_specs=[pl.BlockSpec(memory_space=pltpu.SMEM)] + [whole] * 7,
        out_specs=whole,
        compiler_params=pltpu.CompilerParams(vmem_limit_bytes=48 << 20),
        cost_estimate=pl.CostEstimate(
            flops=8 * rows[0].size * head_weight.shape[0],
            bytes_accessed=8 * rows[0].size + 2 * head_weight.size,
            transcendentals=4 * rows[0].shape[0] * head_weight.shape[0],
        ),
        name="head_stats",
    )(base, targets, owners, *rows, head_weight)


def shards(
    hidden_in,
    mixer_gain,
    w_query,
    w_kv,
    w_attn_out,
    prompt_kv,
    prompt_lengths,
    member,
    accepted,
    w_z,
    w_x,
    w_bc,
    w_dt,
    conv_x,
    conv_bc,
    ssm_rate,
    dt_bias,
    skip_d,
    prompt_state,
    prompt_conv_x,
    prompt_conv_bc,
    w_mamba_out,
    mlp_gain,
    w_gate,
    w_up,
    w_down,
    final_gain,
    head_weight,
    draft_ids,
):
    row_reqs, draft_len, width = hidden_in.shape
    mdl_count = lax.axis_size("mdl")
    req_count = lax.axis_size("req")
    mdl_rank = lax.axis_index("mdl")
    req_rank = lax.axis_index("req")
    row_tokens = row_reqs * draft_len
    own_reqs = row_reqs // mdl_count
    own_tokens = own_reqs * draft_len
    flat_rows = hidden_in.reshape(row_tokens, width)
    local_inner = w_x.shape[1]
    local_ssm = local_inner // SSM_DIM
    edge_len = CONV - 1
    far, near, kept_states, kept_x, own_bc = mixer(
        flat_rows, mixer_gain, w_query, w_kv, w_attn_out, prompt_kv, prompt_lengths, member, accepted, w_z, w_x, w_bc,
        w_dt, conv_x, conv_bc, ssm_rate, dt_bias, skip_d, prompt_state, prompt_conv_x, prompt_conv_bc, w_mamba_out, mdl_rank,
    )
    states_out = lax.all_to_all(
        kept_states.reshape(mdl_count, own_reqs, local_inner, STATE),
        "mdl",
        split_axis=0,
        concat_axis=0,
        tiled=True,
    )
    edges_out = lax.all_to_all(
        kept_x.reshape(mdl_count, own_reqs * edge_len, local_inner),
        "mdl",
        split_axis=0,
        concat_axis=0,
        tiled=True,
    )
    all_ssm = mdl_count * local_ssm
    kept_state = (
        states_out.transpose(1, 0, 2, 3)
        .astype(jnp.float32)
        .reshape(own_reqs, all_ssm, SSM_DIM, STATE)
    )
    edge_x = edges_out.transpose(1, 0, 2).reshape(own_reqs, edge_len, all_ssm * SSM_DIM)
    kept_conv = jnp.concatenate([edge_x, own_bc.reshape(own_reqs, edge_len, 2 * STATE)], axis=2)

    core = req_rank % CORES
    chip_x = req_rank // CORES % SIDE
    chip_y = req_rank // (CORES * SIDE)
    table = jnp.where(core == 0, jnp.asarray(block_table()[0]), jnp.asarray(block_table()[1]))
    owner = ((chip_y ^ table[:, 0]) * SIDE + (chip_x ^ table[:, 1])) * CORES + (core ^ table[:, 2])
    request = owner * row_reqs + mdl_rank * own_reqs + table[:, 3]
    next_ids = jnp.concatenate([draft_ids[:, 1:], draft_ids[:, :1]], axis=1)
    picked = (request[:, None] == jnp.arange(draft_ids.shape[0])[None, :]).astype(jnp.float32)
    targets = jnp.dot(
        picked, next_ids.astype(jnp.float32), precision=lax.Precision.HIGHEST
    ).astype(jnp.int32)
    targets = targets.reshape(4, 16 * draft_len)
    owners = jnp.broadcast_to(owner[:, None], (64, draft_len)).reshape(4, 16 * draft_len)

    came = lax.ppermute(far, "mdl", [(i, i ^ 3) for i in range(SIDE)])
    theirs = near[own_tokens:] + came[own_tokens:]
    last = lax.ppermute(theirs, "mdl", [(i, i ^ 1) for i in range(SIDE)])
    mixed = (
        near[:own_tokens].astype(jnp.float32)
        + came[:own_tokens].astype(jnp.float32)
        + last.astype(jnp.float32)
    )
    own_rows = lax.dynamic_slice_in_dim(flat_rows, mdl_rank * own_tokens, own_tokens, 0)
    after_mixer = (own_rows.astype(jnp.float32) + mixed).astype(jnp.bfloat16)
    prepared = rms_scale(after_mixer, mlp_gain).astype(jnp.bfloat16)
    own, sibling = gather_rows([prepared[:draft_len], prepared[draft_len:]])
    w_both = jnp.concatenate([w_gate, w_up], axis=1)
    own_parts = feed(*own, w_both, w_down)
    sibling_parts = feed(*sibling, w_both, w_down)
    summed = jnp.concatenate(scatter_rows(own_parts, sibling_parts), axis=0)
    after_feed = (after_mixer.astype(jnp.float32) + summed.astype(jnp.float32)).astype(jnp.bfloat16)
    final_rows = rms_scale(after_feed, final_gain).astype(jnp.bfloat16)
    own, sibling = gather_rows([final_rows[:draft_len], final_rows[draft_len:]])
    base = (req_rank * head_weight.shape[0]).reshape(1).astype(jnp.int32)
    stats = head_stats(base, targets, owners, own + sibling, head_weight, req_count)
    shared = lax.all_to_all(stats, "req", split_axis=0, concat_axis=0, tiled=True)
    tops, totals, hits = (
        shared[:, kind * own_tokens : (kind + 1) * own_tokens] for kind in range(3)
    )
    top = jnp.max(tops, axis=0)
    total = jnp.sum(totals * jnp.exp(tops - top[None, :]), axis=0)
    log_total = top + jnp.log(total)
    position = jnp.arange(own_tokens) % draft_len
    verify_scores = jnp.where(
        position < draft_len - 1, jnp.sum(hits, axis=0) - log_total, top - log_total
    ).reshape(own_reqs, draft_len)
    return (
        after_feed.reshape(own_reqs, draft_len, width),
        verify_scores,
        kept_state,
        kept_conv,
    )


def solution(mesh):
    in_specs = (
        P("req", None, None),
        P(),
        P(None, "mdl"),
        P(),
        P("mdl", None),
        P("req", None, None, None),
        P("req"),
        P("req"),
        P("req"),
        P(None, "mdl"),
        P(None, "mdl"),
        P(),
        P(None, "mdl"),
        P(None, "mdl"),
        P(),
        P("mdl"),
        P("mdl"),
        P("mdl"),
        P("req", "mdl", None, None),
        P("req", None, "mdl"),
        P("req", None, None),
        P("mdl", None),
        P(),
        P(None, "req"),
        P(None, "req"),
        P("req", None),
        P(),
        P("req", None),
        P(),
    )
    out_specs = (
        P(("req", "mdl"), None, None),
        P(("req", "mdl"), None),
        P(("req", "mdl"), None, None, None),
        P(("req", "mdl"), None, None),
    )
    return jax.shard_map(shards, mesh=mesh, in_specs=in_specs, out_specs=out_specs, check_vma=False)
```

profile of v0, /device:TPU:1, one launch (start us, length us, event | category | flops | bytes accessed | tf_op | source)
XLA Modules:
  0.0 190.6 jit_solution(4833811187038540394)
XLA Ops:
  13.8 9.8 %mixer.1 = (bf16[64,2048]{1,0:T(8,128)(2,1)S(1)}, bf16[64,2048]{1,0:T(8,128)(2,1)S(1)}, bf16[8,384,256]{2,1,0:T(8,128)(2,1)}, bf16[24,384]{1,0:T(8,128)(2,1)S(1)}, bf16[6,512]{1,0:T(8,128)(2,1)S(1)}) custom-call(s32[8]{0:T(128)S(1)} %copy-done.7, s32[8]{0:T(128)S(1)} %copy-done.8, s32[2]{0:T(128)S(1)} %copy-done.9, s32[2]{0:T(128)S(1)} %pad_add_fusion.place_ref, ...), custom_call_target="tpu_custom_call" | custom-call | flops 3000000000 | bytes 20000000 | tf_op jit(solution)/shard_map/mixer/pallas_call | solution.py:373
  23.6 4.7 %collective-permute-start = (bf16[64,2048]{1,0:T(8,128)(2,1)S(1)}, bf16[64,2048]{1,0:T(8,128)(2,1)S(1)}, u32[]{:S(2)}, u32[]{:S(2)}) collective-permute-start(bf16[64,2048]{1,0:T(8,128)(2,1)S(1)} %get-tuple-element.14), channel_id=1, source_target_pairs={{0,3},{1,2},{2,1},{3,0},{4,7},{5,6},{6,5},{7,4},{8,11},{9,10},{10,... | collective-permute-start | bytes 786440 | tf_op jit(solution)/shard_map/ppermute | solution.py:572
  28.3 6.0 %collective-permute-done = bf16[64,2048]{1,0:T(8,128)(2,1)S(1)} collective-permute-done((bf16[64,2048]{1,0:T(8,128)(2,1)S(1)}, bf16[64,2048]{1,0:T(8,128)(2,1)S(1)}, u32[]{:S(2)}, u32[]{:S(2)}) %collective-permute-start) | collective-permute-done | bytes 262176 | tf_op jit(solution)/shard_map/ppermute | solution.py:572
  34.4 3.8 %collective-permute-done.1 = bf16[32,2048]{1,0:T(8,128)(2,1)S(1)} collective-permute-done((bf16[32,2048]{1,0:T(8,128)(2,1)S(1)}, bf16[32,2048]{1,0:T(8,128)(2,1)S(1)}, u32[]{:S(2)}, u32[]{:S(2)}) %collective-permute-start.1) | collective-permute-done | bytes 131104 | tf_op jit(solution)/shard_map/ppermute | solution.py:574
  39.5 2.8 %collective-permute-start.6 = (bf16[16,2048]{1,0:T(8,128)(2,1)S(1)}, bf16[16,2048]{1,0:T(8,128)(2,1)S(1)}, u32[]{:S(2)}, u32[]{:S(2)}) collective-permute-start(bf16[16,2048]{1,0:T(8,128)(2,1)S(1)} %get-tuple-element.42), channel_id=1, source_target_pairs={{0,24},{4,100},{8,16},{12,108},{16,8},{20,116},{24,0},{28,124},{32... | collective-permute-start | bytes 196616 | tf_op jit(solution)/shard_map/ppermute | solution.py:58
  45.4 2.6 %collective-permute-start.3 = (bf16[32,2048]{1,0:T(8,128)(2,1)S(1)}, bf16[32,2048]{1,0:T(8,128)(2,1)S(1)}, u32[]{:S(2)}, u32[]{:S(2)}) collective-permute-start(bf16[32,2048]{1,0:T(8,128)(2,1)S(1)} %pad_maximum_fusion.8), channel_id=1, source_target_pairs={{0,24},{4,100},{8,16},{12,108},{16,8},{20,116},{24,0},{28,124},{32... | collective-permute-start | bytes 393224 | tf_op jit(solution)/shard_map/ppermute | solution.py:58
  52.2 4.4 %collective-permute-done.8 = bf16[64,2048]{1,0:T(8,128)(2,1)S(1)} collective-permute-done((bf16[64,2048]{1,0:T(8,128)(2,1)S(1)}, bf16[64,2048]{1,0:T(8,128)(2,1)S(1)}, u32[]{:S(2)}, u32[]{:S(2)}) %collective-permute-start.8) | collective-permute-done | bytes 262176 | tf_op jit(solution)/shard_map/ppermute | solution.py:58
  56.8 2.5 %collective-permute-start.5 = (bf16[128,2048]{1,0:T(8,128)(2,1)S(1)}, bf16[128,2048]{1,0:T(8,128)(2,1)S(1)}, u32[]{:S(2)}, u32[]{:S(2)}) collective-permute-start(bf16[128,2048]{1,0:T(8,128)(2,1)S(1)} %pad_maximum_fusion), channel_id=1, source_target_pairs={{0,96},{4,28},{8,104},{12,20},{16,112},{20,12},{24,120},{28,4},{32... | collective-permute-start | bytes 1572872 | tf_op jit(solution)/shard_map/ppermute | solution.py:58
  59.4 8.5 %collective-permute-done.9 = bf16[128,2048]{1,0:T(8,128)(2,1)S(1)} collective-permute-done((bf16[128,2048]{1,0:T(8,128)(2,1)S(1)}, bf16[128,2048]{1,0:T(8,128)(2,1)S(1)}, u32[]{:S(2)}, u32[]{:S(2)}) %collective-permute-start.9) | collective-permute-done | bytes 524320 | tf_op jit(solution)/shard_map/ppermute | solution.py:58
  69.6 7.4 %collective-permute-start.10 = (bf16[256,2048]{1,0:T(8,128)(2,1)S(1)}, bf16[256,2048]{1,0:T(8,128)(2,1)S(1)}, u32[]{:S(2)}, u32[]{:S(2)}) collective-permute-start(bf16[256,2048]{1,0:T(8,128)(2,1)S(1)} %constant_dynamic-update-slice_fusion.first_ref), channel_id=1, source_target_pairs={{0,4},{4,0},{8,12},{12,8},{16,20},{20,16},{24,28},{28,24},{32,36},... | collective-permute-start | bytes 3145736 | tf_op jit(solution)/shard_map/ppermute | solution.py:62
  77.3 2.0 %collective-permute-done.10.first_ref = bf16[256,2048]{1,0:T(8,128)(2,1)S(1)} collective-permute-done((bf16[256,2048]{1,0:T(8,128)(2,1)S(1)}, bf16[256,2048]{1,0:T(8,128)(2,1)S(1)}, u32[]{:S(2)}, u32[]{:S(2)}) %collective-permute-start.10) | collective-permute-done | bytes 1048608 | tf_op jit(solution)/shard_map/ppermute | solution.py:62
  79.3 2.4 %feed.3 = (bf16[256,2048]{1,0:T(8,128)(2,1)S(1)}, bf16[256,2048]{1,0:T(8,128)(2,1)S(1)}) custom-call(bf16[256,2048]{1,0:T(8,128)(2,1)S(1)} %collective-permute-done.10.first_ref, bf16[256,2048]{1,0:T(8,128)(2,1)S(1)} %collective-permute-done.11.second_ref, bf16[2048,256]{1,0:T(8,128)(2,1)S(1)} %constant_dynamic-update-slice_fusion.10.both_ref, ...), custom_call_target="tpu_custom_call" | custom-call | flops 805306368 | bytes 5767168 | tf_op jit(solution)/shard_map/feed/pallas_call | solution.py:423
  82.4 2.4 %feed.2 = (bf16[256,2048]{1,0:T(8,128)(2,1)S(1)}, bf16[256,2048]{1,0:T(8,128)(2,1)S(1)}) custom-call(bf16[256,2048]{1,0:T(8,128)(2,1)S(1)} %constant_dynamic-update-slice_fusion.first_ref, bf16[256,2048]{1,0:T(8,128)(2,1)S(1)} %constant_dynamic-update-slice_fusion.5.second_ref, bf16[2048,256]{1,0:T(8,128)(2,1)S(1)} %constant_dynamic-update-slice_fusion.10.both_ref, ...), custom_call_target="tpu_custom_call" | custom-call | flops 805306368 | bytes 5767168 | tf_op jit(solution)/shard_map/feed/pallas_call | solution.py:423
  85.2 2.1 %collective-permute-start.13 = (bf16[128,2048]{1,0:T(8,128)(2,1)S(1)}, bf16[128,2048]{1,0:T(8,128)(2,1)S(1)}, u32[]{:S(2)}, u32[]{:S(2)}) collective-permute-start(bf16[128,2048]{1,0:T(8,128)(2,1)S(1)} %slice.137), channel_id=1, source_target_pairs={{0,96},{4,28},{8,104},{12,20},{16,112},{20,12},{24,120},{28,4},{32... | collective-permute-start | bytes 1572872 | tf_op jit(solution)/shard_map/ppermute | solution.py:58
  88.1 6.8 %collective-permute-done.13 = bf16[128,2048]{1,0:T(8,128)(2,1)S(1)} collective-permute-done((bf16[128,2048]{1,0:T(8,128)(2,1)S(1)}, bf16[128,2048]{1,0:T(8,128)(2,1)S(1)}, u32[]{:S(2)}, u32[]{:S(2)}) %collective-permute-start.13) | collective-permute-done | bytes 524320 | tf_op jit(solution)/shard_map/ppermute | solution.py:58
  97.3 3.5 %collective-permute-done.14 = bf16[64,2048]{1,0:T(8,128)(2,1)S(1)} collective-permute-done((bf16[64,2048]{1,0:T(8,128)(2,1)S(1)}, bf16[64,2048]{1,0:T(8,128)(2,1)S(1)}, u32[]{:S(2)}, u32[]{:S(2)}) %collective-permute-start.14) | collective-permute-done | bytes 262176 | tf_op jit(solution)/shard_map/ppermute | solution.py:58
  100.8 2.5 %collective-permute-start.15 = (bf16[32,2048]{1,0:T(8,128)(2,1)S(1)}, bf16[32,2048]{1,0:T(8,128)(2,1)S(1)}, u32[]{:S(2)}, u32[]{:S(2)}) collective-permute-start(bf16[32,2048]{1,0:T(8,128)(2,1)S(1)} %slice.141), channel_id=1, source_target_pairs={{0,24},{4,100},{8,16},{12,108},{16,8},{20,116},{24,0},{28,124},{32... | collective-permute-start | bytes 393224 | tf_op jit(solution)/shard_map/ppermute | solution.py:58
  103.5 3.8 %collective-permute-done.15 = bf16[32,2048]{1,0:T(8,128)(2,1)S(1)} collective-permute-done((bf16[32,2048]{1,0:T(8,128)(2,1)S(1)}, bf16[32,2048]{1,0:T(8,128)(2,1)S(1)}, u32[]{:S(2)}, u32[]{:S(2)}) %collective-permute-start.15) | collective-permute-done | bytes 131104 | tf_op jit(solution)/shard_map/ppermute | solution.py:58
  114.6 4.0 %all-to-all-start.2 = ((bf16[4,6,384]{2,1,0:T(8,128)(2,1)}), bf16[4,6,384]{2,1,0:T(8,128)(2,1)S(1)}, u32[]{:S(2)}, u32[]{:S(2)}) async-start(bf16[4,6,384]{2,1,0:T(8,128)(2,1)} %reshape.96), calls=%async_computation.2 | async-start | bytes 49152 | tf_op jit(solution)/shard_map/all_to_all | solution.py:542
  118.8 3.0 %collective-permute-done.22 = bf16[16,2048]{1,0:T(8,128)(2,1)S(1)} collective-permute-done((bf16[16,2048]{1,0:T(8,128)(2,1)S(1)}, bf16[16,2048]{1,0:T(8,128)(2,1)S(1)}, u32[]{:S(2)}, u32[]{:S(2)}) %collective-permute-start.22) | collective-permute-done | bytes 65568 | tf_op jit(solution)/shard_map/ppermute | solution.py:58
  122.6 2.3 %collective-permute-start.28 = (bf16[64,2048]{1,0:T(8,128)(2,1)S(1)}, bf16[64,2048]{1,0:T(8,128)(2,1)S(1)}, u32[]{:S(2)}, u32[]{:S(2)}) collective-permute-start(bf16[64,2048]{1,0:T(8,128)(2,1)S(1)} %pad_maximum_fusion.7), channel_id=1, source_target_pairs={{0,96},{4,28},{8,104},{12,20},{16,112},{20,12},{24,120},{28,4},{32... | collective-permute-start | bytes 786440 | tf_op jit(solution)/shard_map/ppermute | solution.py:58
  124.9 2.0 %collective-permute-done.23 = bf16[32,2048]{1,0:T(8,128)(2,1)S(1)} collective-permute-done((bf16[32,2048]{1,0:T(8,128)(2,1)S(1)}, bf16[32,2048]{1,0:T(8,128)(2,1)S(1)}, u32[]{:S(2)}, u32[]{:S(2)}) %collective-permute-start.23) | collective-permute-done | bytes 131104 | tf_op jit(solution)/shard_map/ppermute | solution.py:58
  127.0 2.4 %collective-permute-done.28 = bf16[64,2048]{1,0:T(8,128)(2,1)S(1)} collective-permute-done((bf16[64,2048]{1,0:T(8,128)(2,1)S(1)}, bf16[64,2048]{1,0:T(8,128)(2,1)S(1)}, u32[]{:S(2)}, u32[]{:S(2)}) %collective-permute-start.28) | collective-permute-done | bytes 262176 | tf_op jit(solution)/shard_map/ppermute | solution.py:58
  133.3 4.5 %collective-permute-done.29 = bf16[128,2048]{1,0:T(8,128)(2,1)S(1)} collective-permute-done((bf16[128,2048]{1,0:T(8,128)(2,1)S(1)}, bf16[128,2048]{1,0:T(8,128)(2,1)S(1)}, u32[]{:S(2)}, u32[]{:S(2)}) %collective-permute-start.29) | collective-permute-done | bytes 524320 | tf_op jit(solution)/shard_map/ppermute | solution.py:58
  137.8 9.8 %collective-permute-start.31 = (bf16[256,2048]{1,0:T(8,128)(2,1)S(1)}, bf16[256,2048]{1,0:T(8,128)(2,1)}, u32[]{:S(2)}, u32[]{:S(2)}) collective-permute-start(bf16[256,2048]{1,0:T(8,128)(2,1)S(1)} %constant_dynamic-update-slice_fusion.17.refs_1_), channel_id=1, source_target_pairs={{0,4},{4,0},{8,12},{12,8},{16,20},{20,16},{24,28},{28,24},{32,36},... | collective-permute-start | bytes 3145736 | tf_op jit(solution)/shard_map/ppermute | solution.py:62
  147.6 4.8 %collective-permute-start.30 = (bf16[256,2048]{1,0:T(8,128)(2,1)S(1)}, bf16[256,2048]{1,0:T(8,128)(2,1)}, u32[]{:S(2)}, u32[]{:S(2)}) collective-permute-start(bf16[256,2048]{1,0:T(8,128)(2,1)S(1)} %constant_dynamic-update-slice_fusion.12.refs_0_), channel_id=1, source_target_pairs={{0,4},{4,0},{8,12},{12,8},{16,20},{20,16},{24,28},{28,24},{32,36},... | collective-permute-start | bytes 3145736 | tf_op jit(solution)/shard_map/ppermute | solution.py:62
  152.5 4.6 %all-to-all-start.1 = ((bf16[4,2,384,256]{3,2,1,0:T(8,128)(2,1)}), bf16[4,2,384,256]{3,2,1,0:T(8,128)(2,1)}, u32[]{:S(2)}, u32[]{:S(2)}) async-start(bf16[4,2,384,256]{3,2,1,0:T(8,128)(2,1)} %bitcast.13), calls=%async_computation.1 | async-start | bytes 3145728 | tf_op jit(solution)/shard_map/all_to_all | solution.py:535
  159.7 14.2 %head_stats.1 = f32[32,128]{1,0:T(8,128)} custom-call(s32[1]{0:T(128)} %bitcast.8.base_ref, s32[4,256]{1,0:T(4,128)S(1)} %reshape.92.targets_ref, s32[4,256]{1,0:T(4,128)S(1)} %broadcast_in_dim.8.owners_ref, bf16[256,2048]{1,0:T(8,128)(2,1)S(1)} %constant_dynamic-update-slice_fusion.12.refs_0_, ...), custom_call_target="tpu_custom_call" | custom-call | flops 4294967296 | bytes 8388608 | tf_op jit(solution)/shard_map/head_stats/pallas_call | solution.py:473
  173.9 4.4 %all-to-all-done.1 = bf16[4,2,384,256]{3,2,1,0:T(8,128)(2,1)} async-done(((bf16[4,2,384,256]{3,2,1,0:T(8,128)(2,1)}), bf16[4,2,384,256]{3,2,1,0:T(8,128)(2,1)}, u32[]{:S(2)}, u32[]{:S(2)}) %all-to-all-start.1) | async-done | bytes 1572896 | tf_op jit(solution)/shard_map/all_to_all | solution.py:535
  178.3 4.3 %all-to-all-start = ((f32[32,1,128]{2,1,0:T(1,128)}), f32[32,1,128]{2,1,0:T(1,128)S(1)}, u32[]{:S(2)}, u32[]{:S(2)}) async-start(f32[32,1,128]{2,1,0:T(1,128)} %bitcast.11), calls=%async_computation | async-start | bytes 32768 | tf_op jit(solution)/shard_map/all_to_all | solution.py:593
  184.3 2.0 %copy.53 = f32[2,4,384,256]{3,2,1,0:T(8,128)} copy(f32[2,4,384,256]{3,2,0,1:T(8,128)S(1)} %convert_bitcast_fusion) | data formatting | bytes 6291456 | tf_op jit(solution)/shard_map/reshape | solution.py:553
  186.3 3.3 %all-to-all-done = f32[32,1,128]{2,1,0:T(1,128)S(1)} async-done(((f32[32,1,128]{2,1,0:T(1,128)}), f32[32,1,128]{2,1,0:T(1,128)S(1)}, u32[]{:S(2)}, u32[]{:S(2)}) %all-to-all-start) | async-done | bytes 16416 | tf_op jit(solution)/shard_map/all_to_all | solution.py:593
  (176 shorter events, 45.6 us)
Async XLA Ops:
  23.6 10.7 %collective-permute-start = (bf16[64,2048]{1,0:T(8,128)(2,1)S(1)}, bf16[64,2048]{1,0:T(8,128)(2,1)S(1)}, u32[]{:S(2)}, u32[]{:S(2)}) collective-permute-start(bf16[64,2048]{1,0:T(8,128)(2,1)S(1)} %get-tuple-element.14), channel_id=1, source_target_pairs={{0,3},{1,2},{2,1},{3,0},{4,7},{5,6},{6,5},{7,4},{8,11},{9,10},{10,... | collective-permute-start | bytes 786440 | tf_op jit(solution)/shard_map/ppermute | solution.py:572
  34.3 3.9 %collective-permute-start.1 = (bf16[32,2048]{1,0:T(8,128)(2,1)S(1)}, bf16[32,2048]{1,0:T(8,128)(2,1)S(1)}, u32[]{:S(2)}, u32[]{:S(2)}) collective-permute-start(bf16[32,2048]{1,0:T(8,128)(2,1)S(1)} %slice_add_fusion.6), channel_id=1, source_target_pairs={{0,1},{1,0},{2,3},{3,2},{4,5},{5,4},{6,7},{7,6},{8,9},{9,8},{10,11... | collective-permute-start | bytes 393224 | tf_op jit(solution)/shard_map/ppermute | solution.py:574
  39.5 4.5 %collective-permute-start.6 = (bf16[16,2048]{1,0:T(8,128)(2,1)S(1)}, bf16[16,2048]{1,0:T(8,128)(2,1)S(1)}, u32[]{:S(2)}, u32[]{:S(2)}) collective-permute-start(bf16[16,2048]{1,0:T(8,128)(2,1)S(1)} %get-tuple-element.42), channel_id=1, source_target_pairs={{0,24},{4,100},{8,16},{12,108},{16,8},{20,116},{24,0},{28,124},{32... | collective-permute-start | bytes 196616 | tf_op jit(solution)/shard_map/ppermute | solution.py:58
  44.0 4.5 %collective-permute-start.7 = (bf16[32,2048]{1,0:T(8,128)(2,1)S(1)}, bf16[32,2048]{1,0:T(8,128)(2,1)S(1)}, u32[]{:S(2)}, u32[]{:S(2)}) collective-permute-start(bf16[32,2048]{1,0:T(8,128)(2,1)S(1)} %pad_maximum_fusion.9), channel_id=1, source_target_pairs={{0,32},{4,12},{8,40},{12,4},{16,48},{20,28},{24,56},{28,20},{32,0}... | collective-permute-start | bytes 393224 | tf_op jit(solution)/shard_map/ppermute | solution.py:58
  45.4 5.1 %collective-permute-start.3 = (bf16[32,2048]{1,0:T(8,128)(2,1)S(1)}, bf16[32,2048]{1,0:T(8,128)(2,1)S(1)}, u32[]{:S(2)}, u32[]{:S(2)}) collective-permute-start(bf16[32,2048]{1,0:T(8,128)(2,1)S(1)} %pad_maximum_fusion.8), channel_id=1, source_target_pairs={{0,24},{4,100},{8,16},{12,108},{16,8},{20,116},{24,0},{28,124},{32... | collective-permute-start | bytes 393224 | tf_op jit(solution)/shard_map/ppermute | solution.py:58
  48.4 8.1 %collective-permute-start.8 = (bf16[64,2048]{1,0:T(8,128)(2,1)S(1)}, bf16[64,2048]{1,0:T(8,128)(2,1)S(1)}, u32[]{:S(2)}, u32[]{:S(2)}) collective-permute-start(bf16[64,2048]{1,0:T(8,128)(2,1)S(1)} %pad_maximum_fusion.5), channel_id=1, source_target_pairs={{0,96},{4,28},{8,104},{12,20},{16,112},{20,12},{24,120},{28,4},{32... | collective-permute-start | bytes 786440 | tf_op jit(solution)/shard_map/ppermute | solution.py:58
  50.5 6.2 %collective-permute-start.4 = (bf16[64,2048]{1,0:T(8,128)(2,1)S(1)}, bf16[64,2048]{1,0:T(8,128)(2,1)S(1)}, u32[]{:S(2)}, u32[]{:S(2)}) collective-permute-start(bf16[64,2048]{1,0:T(8,128)(2,1)S(1)} %pad_maximum_fusion.4), channel_id=1, source_target_pairs={{0,32},{4,12},{8,40},{12,4},{16,48},{20,28},{24,56},{28,20},{32,0}... | collective-permute-start | bytes 786440 | tf_op jit(solution)/shard_map/ppermute | solution.py:58
  56.6 11.2 %collective-permute-start.9 = (bf16[128,2048]{1,0:T(8,128)(2,1)S(1)}, bf16[128,2048]{1,0:T(8,128)(2,1)S(1)}, u32[]{:S(2)}, u32[]{:S(2)}) collective-permute-start(bf16[128,2048]{1,0:T(8,128)(2,1)S(1)} %pad_maximum_fusion.1), channel_id=1, source_target_pairs={{0,8},{4,36},{8,0},{12,44},{16,24},{20,52},{24,16},{28,60},{32,40}... | collective-permute-start | bytes 1572872 | tf_op jit(solution)/shard_map/ppermute | solution.py:58
  56.8 12.8 %collective-permute-start.5 = (bf16[128,2048]{1,0:T(8,128)(2,1)S(1)}, bf16[128,2048]{1,0:T(8,128)(2,1)S(1)}, u32[]{:S(2)}, u32[]{:S(2)}) collective-permute-start(bf16[128,2048]{1,0:T(8,128)(2,1)S(1)} %pad_maximum_fusion), channel_id=1, source_target_pairs={{0,96},{4,28},{8,104},{12,20},{16,112},{20,12},{24,120},{28,4},{32... | collective-permute-start | bytes 1572872 | tf_op jit(solution)/shard_map/ppermute | solution.py:58
  67.9 9.4 %collective-permute-start.11 = (bf16[256,2048]{1,0:T(8,128)(2,1)S(1)}, bf16[256,2048]{1,0:T(8,128)(2,1)S(1)}, u32[]{:S(2)}, u32[]{:S(2)}) collective-permute-start(bf16[256,2048]{1,0:T(8,128)(2,1)S(1)} %constant_dynamic-update-slice_fusion.5.second_ref), channel_id=1, source_target_pairs={{0,4},{4,0},{8,12},{12,8},{16,20},{20,16},{24,28},{28,24},{32,36},... | collective-permute-start | bytes 3145736 | tf_op jit(solution)/shard_map/ppermute | solution.py:62
  69.6 9.7 %collective-permute-start.10 = (bf16[256,2048]{1,0:T(8,128)(2,1)S(1)}, bf16[256,2048]{1,0:T(8,128)(2,1)S(1)}, u32[]{:S(2)}, u32[]{:S(2)}) collective-permute-start(bf16[256,2048]{1,0:T(8,128)(2,1)S(1)} %constant_dynamic-update-slice_fusion.first_ref), channel_id=1, source_target_pairs={{0,4},{4,0},{8,12},{12,8},{16,20},{20,16},{24,28},{28,24},{32,36},... | collective-permute-start | bytes 3145736 | tf_op jit(solution)/shard_map/ppermute | solution.py:62
  82.2 5.2 %collective-permute-start.17 = (bf16[256,2048]{1,0:T(8,128)(2,1)S(1)}, bf16[256,2048]{1,0:T(8,128)(2,1)S(1)}, u32[]{:S(2)}, u32[]{:S(2)}) collective-permute-start(bf16[256,2048]{1,0:T(8,128)(2,1)S(1)} %get-tuple-element.18), channel_id=1, source_target_pairs={{0,4},{4,0},{8,12},{12,8},{16,20},{20,16},{24,28},{28,24},{32,36},... | collective-permute-start | bytes 3145736 | tf_op jit(solution)/shard_map/ppermute | solution.py:62
  85.2 9.6 %collective-permute-start.13 = (bf16[128,2048]{1,0:T(8,128)(2,1)S(1)}, bf16[128,2048]{1,0:T(8,128)(2,1)S(1)}, u32[]{:S(2)}, u32[]{:S(2)}) collective-permute-start(bf16[128,2048]{1,0:T(8,128)(2,1)S(1)} %slice.137), channel_id=1, source_target_pairs={{0,96},{4,28},{8,104},{12,20},{16,112},{20,12},{24,120},{28,4},{32... | collective-permute-start | bytes 1572872 | tf_op jit(solution)/shard_map/ppermute | solution.py:58
  87.8 8.4 %collective-permute-start.18 = (bf16[128,2048]{1,0:T(8,128)(2,1)S(1)}, bf16[128,2048]{1,0:T(8,128)(2,1)S(1)}, u32[]{:S(2)}, u32[]{:S(2)}) collective-permute-start(bf16[128,2048]{1,0:T(8,128)(2,1)S(1)} %slice.145), channel_id=1, source_target_pairs={{0,8},{4,36},{8,0},{12,44},{16,24},{20,52},{24,16},{28,60},{32,40}... | collective-permute-start | bytes 1572872 | tf_op jit(solution)/shard_map/ppermute | solution.py:58
  94.9 5.8 %collective-permute-start.14 = (bf16[64,2048]{1,0:T(8,128)(2,1)S(1)}, bf16[64,2048]{1,0:T(8,128)(2,1)S(1)}, u32[]{:S(2)}, u32[]{:S(2)}) collective-permute-start(bf16[64,2048]{1,0:T(8,128)(2,1)S(1)} %slice.139), channel_id=1, source_target_pairs={{0,32},{4,12},{8,40},{12,4},{16,48},{20,28},{24,56},{28,20},{32,0}... | collective-permute-start | bytes 786440 | tf_op jit(solution)/shard_map/ppermute | solution.py:58
  96.3 7.0 %collective-permute-start.19 = (bf16[64,2048]{1,0:T(8,128)(2,1)S(1)}, bf16[64,2048]{1,0:T(8,128)(2,1)S(1)}, u32[]{:S(2)}, u32[]{:S(2)}) collective-permute-start(bf16[64,2048]{1,0:T(8,128)(2,1)S(1)} %slice.147), channel_id=1, source_target_pairs={{0,96},{4,28},{8,104},{12,20},{16,112},{20,12},{24,120},{28,4},{32... | collective-permute-start | bytes 786440 | tf_op jit(solution)/shard_map/ppermute | solution.py:58
  100.8 6.5 %collective-permute-start.15 = (bf16[32,2048]{1,0:T(8,128)(2,1)S(1)}, bf16[32,2048]{1,0:T(8,128)(2,1)S(1)}, u32[]{:S(2)}, u32[]{:S(2)}) collective-permute-start(bf16[32,2048]{1,0:T(8,128)(2,1)S(1)} %slice.141), channel_id=1, source_target_pairs={{0,24},{4,100},{8,16},{12,108},{16,8},{20,116},{24,0},{28,124},{32... | collective-permute-start | bytes 393224 | tf_op jit(solution)/shard_map/ppermute | solution.py:58
  103.4 4.2 %collective-permute-start.20 = (bf16[32,2048]{1,0:T(8,128)(2,1)S(1)}, bf16[32,2048]{1,0:T(8,128)(2,1)S(1)}, u32[]{:S(2)}, u32[]{:S(2)}) collective-permute-start(bf16[32,2048]{1,0:T(8,128)(2,1)S(1)} %slice.149), channel_id=1, source_target_pairs={{0,32},{4,12},{8,40},{12,4},{16,48},{20,28},{24,56},{28,20},{32,0}... | collective-permute-start | bytes 393224 | tf_op jit(solution)/shard_map/ppermute | solution.py:58
  107.3 3.8 %collective-permute-start.16 = (bf16[16,2048]{1,0:T(8,128)(2,1)S(1)}, bf16[16,2048]{1,0:T(8,128)(2,1)S(1)}, u32[]{:S(2)}, u32[]{:S(2)}) collective-permute-start(bf16[16,2048]{1,0:T(8,128)(2,1)S(1)} %slice.143), channel_id=1, source_target_pairs={{0,8},{4,36},{8,0},{12,44},{16,24},{20,52},{24,16},{28,60},{32,40}... | collective-permute-start | bytes 196616 | tf_op jit(solution)/shard_map/ppermute | solution.py:58
  107.6 4.4 %collective-permute-start.21 = (bf16[16,2048]{1,0:T(8,128)(2,1)S(1)}, bf16[16,2048]{1,0:T(8,128)(2,1)S(1)}, u32[]{:S(2)}, u32[]{:S(2)}) collective-permute-start(bf16[16,2048]{1,0:T(8,128)(2,1)S(1)} %slice.151), channel_id=1, source_target_pairs={{0,24},{4,100},{8,16},{12,108},{16,8},{20,116},{24,0},{28,124},{32... | collective-permute-start | bytes 196616 | tf_op jit(solution)/shard_map/ppermute | solution.py:58
  112.4 6.3 %collective-permute-start.26 = (bf16[16,2048]{1,0:T(8,128)(2,1)S(1)}, bf16[16,2048]{1,0:T(8,128)(2,1)S(1)}, u32[]{:S(2)}, u32[]{:S(2)}) collective-permute-start(bf16[16,2048]{1,0:T(8,128)(2,1)S(1)} %get-tuple-element.38), channel_id=1, source_target_pairs={{0,24},{4,100},{8,16},{12,108},{16,8},{20,116},{24,0},{28,124},{32... | collective-permute-start | bytes 196616 | tf_op jit(solution)/shard_map/ppermute | solution.py:58
  114.6 37.9 %all-to-all-start.2 = ((bf16[4,6,384]{2,1,0:T(8,128)(2,1)}), bf16[4,6,384]{2,1,0:T(8,128)(2,1)S(1)}, u32[]{:S(2)}, u32[]{:S(2)}) async-start(bf16[4,6,384]{2,1,0:T(8,128)(2,1)} %reshape.96), calls=%async_computation.2 | async-start | bytes 49152 | tf_op jit(solution)/shard_map/all_to_all | solution.py:542
  118.7 3.9 %collective-permute-start.27 = (bf16[32,2048]{1,0:T(8,128)(2,1)S(1)}, bf16[32,2048]{1,0:T(8,128)(2,1)S(1)}, u32[]{:S(2)}, u32[]{:S(2)}) collective-permute-start(bf16[32,2048]{1,0:T(8,128)(2,1)S(1)} %pad_maximum_fusion.11), channel_id=1, source_target_pairs={{0,32},{4,12},{8,40},{12,4},{16,48},{20,28},{24,56},{28,20},{32,0}... | collective-permute-start | bytes 393224 | tf_op jit(solution)/shard_map/ppermute | solution.py:58
  121.8 5.1 %collective-permute-start.23 = (bf16[32,2048]{1,0:T(8,128)(2,1)S(1)}, bf16[32,2048]{1,0:T(8,128)(2,1)S(1)}, u32[]{:S(2)}, u32[]{:S(2)}) collective-permute-start(bf16[32,2048]{1,0:T(8,128)(2,1)S(1)} %pad_maximum_fusion.10), channel_id=1, source_target_pairs={{0,24},{4,100},{8,16},{12,108},{16,8},{20,116},{24,0},{28,124},{32... | collective-permute-start | bytes 393224 | tf_op jit(solution)/shard_map/ppermute | solution.py:58
  122.6 6.8 %collective-permute-start.28 = (bf16[64,2048]{1,0:T(8,128)(2,1)S(1)}, bf16[64,2048]{1,0:T(8,128)(2,1)S(1)}, u32[]{:S(2)}, u32[]{:S(2)}) collective-permute-start(bf16[64,2048]{1,0:T(8,128)(2,1)S(1)} %pad_maximum_fusion.7), channel_id=1, source_target_pairs={{0,96},{4,28},{8,104},{12,20},{16,112},{20,12},{24,120},{28,4},{32... | collective-permute-start | bytes 786440 | tf_op jit(solution)/shard_map/ppermute | solution.py:58
  126.9 5.3 %collective-permute-start.24 = (bf16[64,2048]{1,0:T(8,128)(2,1)S(1)}, bf16[64,2048]{1,0:T(8,128)(2,1)S(1)}, u32[]{:S(2)}, u32[]{:S(2)}) collective-permute-start(bf16[64,2048]{1,0:T(8,128)(2,1)S(1)} %pad_maximum_fusion.6), channel_id=1, source_target_pairs={{0,32},{4,12},{8,40},{12,4},{16,48},{20,28},{24,56},{28,20},{32,0}... | collective-permute-start | bytes 786440 | tf_op jit(solution)/shard_map/ppermute | solution.py:58
  129.5 8.3 %collective-permute-start.29 = (bf16[128,2048]{1,0:T(8,128)(2,1)S(1)}, bf16[128,2048]{1,0:T(8,128)(2,1)S(1)}, u32[]{:S(2)}, u32[]{:S(2)}) collective-permute-start(bf16[128,2048]{1,0:T(8,128)(2,1)S(1)} %pad_maximum_fusion.3), channel_id=1, source_target_pairs={{0,8},{4,36},{8,0},{12,44},{16,24},{20,52},{24,16},{28,60},{32,40}... | collective-permute-start | bytes 1572872 | tf_op jit(solution)/shard_map/ppermute | solution.py:58
  132.2 15.4 %collective-permute-start.25 = (bf16[128,2048]{1,0:T(8,128)(2,1)S(1)}, bf16[128,2048]{1,0:T(8,128)(2,1)S(1)}, u32[]{:S(2)}, u32[]{:S(2)}) collective-permute-start(bf16[128,2048]{1,0:T(8,128)(2,1)S(1)} %pad_maximum_fusion.2), channel_id=1, source_target_pairs={{0,96},{4,28},{8,104},{12,20},{16,112},{20,12},{24,120},{28,4},{32... | collective-permute-start | bytes 1572872 | tf_op jit(solution)/shard_map/ppermute | solution.py:58
  137.8 21.9 %collective-permute-start.31 = (bf16[256,2048]{1,0:T(8,128)(2,1)S(1)}, bf16[256,2048]{1,0:T(8,128)(2,1)}, u32[]{:S(2)}, u32[]{:S(2)}) collective-permute-start(bf16[256,2048]{1,0:T(8,128)(2,1)S(1)} %constant_dynamic-update-slice_fusion.17.refs_1_), channel_id=1, source_target_pairs={{0,4},{4,0},{8,12},{12,8},{16,20},{20,16},{24,28},{28,24},{32,36},... | collective-permute-start | bytes 3145736 | tf_op jit(solution)/shard_map/ppermute | solution.py:62
  147.6 12.1 %collective-permute-start.30 = (bf16[256,2048]{1,0:T(8,128)(2,1)S(1)}, bf16[256,2048]{1,0:T(8,128)(2,1)}, u32[]{:S(2)}, u32[]{:S(2)}) collective-permute-start(bf16[256,2048]{1,0:T(8,128)(2,1)S(1)} %constant_dynamic-update-slice_fusion.12.refs_0_), channel_id=1, source_target_pairs={{0,4},{4,0},{8,12},{12,8},{16,20},{20,16},{24,28},{28,24},{32,36},... | collective-permute-start | bytes 3145736 | tf_op jit(solution)/shard_map/ppermute | solution.py:62
  152.5 25.8 %all-to-all-start.1 = ((bf16[4,2,384,256]{3,2,1,0:T(8,128)(2,1)}), bf16[4,2,384,256]{3,2,1,0:T(8,128)(2,1)}, u32[]{:S(2)}, u32[]{:S(2)}) async-start(bf16[4,2,384,256]{3,2,1,0:T(8,128)(2,1)} %bitcast.13), calls=%async_computation.1 | async-start | bytes 3145728 | tf_op jit(solution)/shard_map/all_to_all | solution.py:535
  178.3 11.4 %all-to-all-start = ((f32[32,1,128]{2,1,0:T(1,128)}), f32[32,1,128]{2,1,0:T(1,128)S(1)}, u32[]{:S(2)}, u32[]{:S(2)}) async-start(f32[32,1,128]{2,1,0:T(1,128)} %bitcast.11), calls=%async_computation | async-start | bytes 32768 | tf_op jit(solution)/shard_map/all_to_all | solution.py:593
  (25 other events, 205.5 us)
where the time goes:
time: 191 us
  starting transfers between devices  69.3 us (36%)
  waiting for transfers between devices  66.5 us (35%)
  Pallas kernels  28.9 us (15%)
  local copies, waits for them, and re-layouts  18.5 us (10%)
  other arithmetic  5.92 us (3%)
    ppermute x24, waiting for transfers between devices, hop(): return lax.ppermute(part, 'req', hop_pairs(fragment, step))  46.9 us
    ppermute x24, starting transfers between devices, hop(): return lax.ppermute(part, 'req', hop_pairs(fragment, step))  27.4 us
    ppermute x6, starting transfers between devices, swap_core(): return lax.ppermute(part, 'req', CORE_PAIRS)  24.3 us
    pallas_call x1, Pallas kernels, head_stats(): pl.pallas_call(head_kernel, out_shape=jax.ShapeDtypeStruct((devices, 128)...  14.2 us
    unnamed x59, local copies, waits for them, and re-layouts  13.4 us
    pallas_call x1, Pallas kernels, mixer(): pl.pallas_call(mixer_kernel, out_shape=[jax.ShapeDtypeStruct((tokens // 2...  9.79 us
    ppermute x1, waiting for transfers between devices, shards(): came = lax.ppermute(far, 'mdl', [(i, i ^ 3) for i in range(SIDE)])  6.03 us
    pallas_call x2, Pallas kernels, feed(): pl.pallas_call(feed_kernel, out_shape=[jax.ShapeDtypeStruct((rows, width)...  4.85 us
  transfers between devices with their start and end apart: 35, of which 24 were waited for; matrix products, arithmetic and copies ran while one was open for 5% of the time, Pallas kernels for 9%

commit v1 on v0

v1 whole, which is shorter than its diff:
```python
import functools

import jax
import jax.numpy as jnp
import numpy as np
from jax import lax
from jax.experimental import pallas as pl
from jax.experimental.pallas import tpu as pltpu
from jax.sharding import PartitionSpec as P

Q_HEADS = 8
KV_HEADS = 2
HEAD_DIM = 128
SSM_DIM = 64
STATE = 256
CONV = 4
PROMPTS = 2
P_MAX = 1024
DRAFT = 16
SIDE = 4
CORES = 2

eps_norm = 1e-05
far_below = -1e30

HOPS = ((0, 1), (0, 3), (1, 0), (3, 0))
ORDERS = tuple(
    tuple(tuple(HOPS[(first + step) % 4] for step in range(4)) for first in firsts)
    for firsts in ((0, 1), (2, 3))
)


def device_at(y, x, core):
    return (y * SIDE + x) * CORES + core


def hop_pairs(fragment, step):
    pairs = []
    for y in range(SIDE):
        for x in range(SIDE):
            for core in range(CORES):
                flip_y, flip_x = ORDERS[core][fragment][step]
                pairs.append((device_at(y, x, core), device_at(y ^ flip_y, x ^ flip_x, core)))
    return pairs


CORE_PAIRS = [(device, device ^ 1) for device in range(SIDE * SIDE * CORES)]


def offsets_of(core, fragment):
    found = [(0, 0)]
    for flip_y, flip_x in ORDERS[core][fragment]:
        found = found + [(y ^ flip_y, x ^ flip_x) for y, x in found]
    return found


def hop(part, fragment, step):
    return lax.ppermute(part, "req", hop_pairs(fragment, step))


def swap_core(part):
    return lax.ppermute(part, "req", CORE_PAIRS)


def gather_rows(fragments):
    held = list(fragments)
    for step in range(3):
        came = [hop(held[f], f, step) for f in range(2)]
        held = [jnp.concatenate([held[f], came[f]], axis=0) for f in range(2)]
    late = [hop(held[f], f, 3) for f in range(2)]
    return (held, [swap_core(part) for part in held]), (late, [swap_core(part) for part in late])


def added(left, right):
    return (left.astype(jnp.float32) + right.astype(jnp.float32)).astype(jnp.bfloat16)


def scatter_rows(early, late):
    came = [swap_core(part) for part in late[1]]
    late = [hop(added(late[0][f], came[f]), f, 3) for f in range(2)]
    came = [swap_core(part) for part in early[1]]
    held = [added(early[0][f], came[f]) for f in range(2)]
    held = [added(held[f], late[f]) for f in range(2)]
    for step in reversed(range(3)):
        half = held[0].shape[0] // 2
        came = [hop(held[f][half:], f, step) for f in range(2)]
        held = [added(held[f][:half], came[f]) for f in range(2)]
    return held


def block_table():
    table = np.zeros((CORES, 2, 2, 2, 8, 4), np.int32)
    for core in range(CORES):
        for half in range(2):
            for fragment in range(2):
                for place, (y, x) in enumerate(offsets_of(core ^ half, fragment)):
                    table[core, place // 8, half, fragment, place % 8] = (y, x, half, fragment)
    return table.reshape(CORES, 64, 4)


def rms_scale(values, gain):
    widened = values.astype(jnp.float32)
    spread = jnp.mean(widened * widened, axis=-1, keepdims=True)
    return widened * lax.rsqrt(spread + eps_norm) * gain.astype(jnp.float32)


HIGHEST = lax.Precision.HIGHEST
NEXT_TO = (((1,), (1,)), ((), ()))


def dot32(left, right, dims=None):
    dims = dims or (((1,), (0,)), ((), ()))
    return lax.dot_general(left, right, dims, preferred_element_type=jnp.float32)


def exact_dot(left, right):
    return jnp.dot(left, right, precision=HIGHEST, preferred_element_type=jnp.float32)


def mixer_kernel(*refs):
    sources, refs = refs[:22], refs[22:]
    far_ref, near_ref, kept_ref, kept_bc_ref = refs[:4]
    held, (mixed_scr, lanes_scr, sems) = refs[4:-3], refs[-3:]
    member_ref, accepted_ref, lengths_ref, rate_ref, bias_ref, skip_ref = held[:6]
    hidden_ref, gain_ref, w_dt_ref, conv_x_ref, conv_bc_ref, past_x_ref, past_bc_ref = held[6:13]
    w_query, w_kv, prompt, w_x, w_bc, w_z, state, w_out = held[13:]
    tokens = hidden_ref.shape[0]
    requests = tokens // DRAFT
    inner = w_x.shape[1]
    heads = inner // SSM_DIM
    query_width = w_query.shape[1]
    rank = lax.axis_index("mdl")
    core = lax.axis_index("req") % CORES
    group = rank * (query_width // HEAD_DIM) // (Q_HEADS // KV_HEADS)
    query_hbm, kv_hbm, prompt_hbm, x_hbm, bc_hbm, z_hbm, state_hbm, attn_hbm, mamba_hbm = sources[13:]
    moves = [(source, target) for source, target in zip(sources[:13], held[:13], strict=True)]
    moves += [
        (query_hbm, w_query),
        (kv_hbm.at[group], w_kv),
        (prompt_hbm.at[0, group], prompt.at[0]),
        (prompt_hbm.at[1, group], prompt.at[1]),
        (x_hbm, w_x),
        (bc_hbm, w_bc),
        (z_hbm, w_z),
        (state_hbm, state),
        (attn_hbm, w_out.at[pl.ds(0, query_width), :]),
        (mamba_hbm, w_out.at[pl.ds(query_width, inner), :]),
    ]
    started = [
        pltpu.make_async_copy(source, target, sems.at[index])
        for index, (source, target) in enumerate(moves)
    ]
    for copy in started:
        copy.start()
    for copy in started[:13]:
        copy.wait()
    copies = started[13:]

    def head_row(ref):
        lane = lax.broadcasted_iota(jnp.int32, (1, heads), 1)
        values = jnp.zeros((1, heads), jnp.float32)
        for h in range(heads):
            values = jnp.where(lane == h, ref[h], values)
        return values

    row = lax.broadcasted_iota(jnp.int32, (tokens, 1), 0)
    time, request = row % DRAFT, row // DRAFT
    own_prompt = jnp.zeros((tokens, 1), jnp.int32)
    last = jnp.zeros((tokens, 1), jnp.int32)
    for r in range(requests):
        own_prompt = jnp.where(request == r, member_ref[r], own_prompt)
        last = jnp.where(request == r, accepted_ref[r] - 1, last)
    first_prompt = own_prompt == 0

    gain = jnp.concatenate(
        [gain_ref[j : j + 1, :].astype(jnp.float32) for j in range(gain_ref.shape[0])], axis=1
    )
    widened = hidden_ref[...].astype(jnp.float32)
    spread = jnp.mean(widened * widened, axis=-1, keepdims=True)
    normed = (
        widened * lax.rsqrt(spread + eps_norm) * gain
    ).astype(jnp.bfloat16)

    copies[0].wait()
    queries = dot32(normed, w_query[...]).astype(jnp.bfloat16)
    copies[1].wait()
    drafts = dot32(normed, w_kv[...]).astype(jnp.bfloat16)
    local_heads = query_width // HEAD_DIM
    query_rows = jnp.concatenate(
        [queries[:, h * HEAD_DIM : (h + 1) * HEAD_DIM] for h in range(local_heads)], axis=0
    )
    scale = HEAD_DIM**-0.5
    row_first = jnp.concatenate([own_prompt] * local_heads, axis=0) == 0
    draft_scores = dot32(query_rows, drafts[:, :HEAD_DIM], NEXT_TO) * scale
    same = (row // DRAFT == lax.broadcasted_iota(jnp.int32, (tokens, tokens), 1) // DRAFT) & (
        lax.broadcasted_iota(jnp.int32, (tokens, tokens), 1) <= row
    )
    draft_mask = jnp.concatenate([same] * local_heads, axis=0)
    draft_scores = jnp.where(draft_mask, draft_scores, far_below)
    copies[2].wait()
    copies[3].wait()
    scores = jnp.where(
        row_first,
        dot32(query_rows, prompt[0, :, :HEAD_DIM], NEXT_TO),
        dot32(query_rows, prompt[1, :, :HEAD_DIM], NEXT_TO),
    )
    length = jnp.where(row_first, lengths_ref[0], lengths_ref[1])
    position = lax.broadcasted_iota(jnp.int32, scores.shape, 1)
    scores = jnp.where(position < length, scores * scale, far_below)
    top = jnp.maximum(
        jnp.max(scores, axis=1, keepdims=True), jnp.max(draft_scores, axis=1, keepdims=True)
    )
    weights = jnp.exp(scores - top)
    draft_weights = jnp.exp(draft_scores - top)
    total = jnp.sum(weights, axis=1, keepdims=True) + jnp.sum(draft_weights, axis=1, keepdims=True)
    weighted = (
        dot32(jnp.where(row_first, weights, 0.0).astype(jnp.bfloat16), prompt[0, :, HEAD_DIM:])
        + dot32(jnp.where(row_first, 0.0, weights).astype(jnp.bfloat16), prompt[1, :, HEAD_DIM:])
        + dot32(draft_weights.astype(jnp.bfloat16), drafts[:, HEAD_DIM:])
    )
    attended = (weighted / total).astype(jnp.bfloat16)
    for h in range(local_heads):
        mixed_scr[:, h * HEAD_DIM : (h + 1) * HEAD_DIM] = attended[h * tokens : (h + 1) * tokens]

    def convolve_rows(series, past_ref, taps_ref):
        past = [
            jnp.where(
                first_prompt,
                past_ref[j, 0:1, :].astype(jnp.float32),
                past_ref[j, 1:2, :].astype(jnp.float32),
            )
            for j in range(CONV - 1)
        ]
        taps = taps_ref[...].astype(jnp.float32)
        summed = series * taps[CONV - 1 : CONV, :]
        for shift in range(1, CONV):
            window = pltpu.roll(series, shift, 0)
            for t in range(shift):
                window = jnp.where(time == t, past[CONV - 1 - shift + t], window)
            summed = summed + window * taps[CONV - 1 - shift : CONV - shift, :]
        return summed * jax.nn.sigmoid(summed)

    copies[4].wait()
    in_x = dot32(normed, w_x[...]).astype(jnp.bfloat16)
    heads_x = convolve_rows(in_x.astype(jnp.float32), past_x_ref, conv_x_ref)
    copies[5].wait()
    in_bc = dot32(normed, w_bc[...]).astype(jnp.bfloat16)
    conv_bcs = convolve_rows(in_bc.astype(jnp.float32), past_bc_ref, conv_bc_ref)
    b_part = conv_bcs[:, :STATE].astype(jnp.bfloat16)
    c_part = conv_bcs[:, STATE:].astype(jnp.bfloat16)

    def widen(values):
        lanes_scr[...] = jnp.zeros(lanes_scr.shape, jnp.float32)
        lanes_scr[:, :heads] = values
        return lanes_scr[...]

    spread_lanes = (
        lax.broadcasted_iota(jnp.int32, (tokens, inner), 0)
        == lax.broadcasted_iota(jnp.int32, (tokens, inner), 1) // SSM_DIM
    ).astype(jnp.float32)
    dt_in = dot32(normed, w_dt_ref[...], NEXT_TO).astype(jnp.bfloat16).astype(jnp.float32) + head_row(bias_ref)
    step = jnp.maximum(dt_in, 0.0) + jnp.log1p(jnp.exp(-jnp.abs(dt_in)))
    log_decay = exact_dot(same.astype(jnp.float32), widen(-step * head_row(rate_ref)))
    step_x = exact_dot(widen(step), spread_lanes)
    skip_x = exact_dot(widen(jnp.broadcast_to(head_row(skip_ref), (tokens, heads))), spread_lanes)
    decay_x = exact_dot(log_decay, spread_lanes)
    turned = log_decay.T
    intersection = dot32(c_part, b_part, NEXT_TO)
    scaled_x = heads_x * step_x
    low = lax.broadcasted_iota(jnp.int32, (tokens, 2 * SSM_DIM), 1) < SSM_DIM
    groups = []
    for pair in range(heads // 2):
        mixing = []
        for h in (2 * pair, 2 * pair + 1):
            gaps = log_decay[:, h : h + 1] - turned[h : h + 1, :]
            mixing.append(
                (jnp.exp(jnp.where(same, gaps, far_below)) * intersection).astype(jnp.bfloat16)
            )
        lanes = scaled_x[:, pair * 2 * SSM_DIM : (pair + 1) * 2 * SSM_DIM]
        both = jnp.concatenate([jnp.where(low, lanes, 0.0), jnp.where(low, 0.0, lanes)], axis=0)
        groups.append(dot32(jnp.concatenate(mixing, axis=1), both.astype(jnp.bfloat16)))
    copies[7].wait()
    carried = jnp.where(
        first_prompt,
        dot32(c_part, state[0].astype(jnp.bfloat16), NEXT_TO),
        dot32(c_part, state[1].astype(jnp.bfloat16), NEXT_TO),
    )
    ssm_out = jnp.concatenate(groups, axis=1) + carried * jnp.exp(decay_x) + skip_x * heads_x
    copies[6].wait()
    gate_z = dot32(normed, w_z[...]).astype(jnp.bfloat16).astype(jnp.float32)
    mixed_scr[:, query_width:] = (ssm_out * (gate_z * jax.nn.sigmoid(gate_z))).astype(jnp.bfloat16)

    own_rows = tokens // SIDE
    copies[8].wait()
    copies[9].wait()
    first_flip = jnp.where(core == 0, 3, 1)
    for out_ref, flips in ((far_ref, (first_flip, 2)), (near_ref, (0, first_flip ^ 2))):
        rows = jnp.concatenate(
            [
                mixed_scr[pl.ds(pl.multiple_of((rank ^ flip) * own_rows, own_rows), own_rows), :]
                for flip in flips
            ],
            axis=0,
        )
        out_ref[...] = dot32(rows, w_out[...]).astype(jnp.bfloat16)

    other = lax.broadcasted_iota(jnp.int32, (tokens, tokens), 1)
    pick = (other == request * DRAFT + last).astype(jnp.float32)
    final_log = exact_dot(pick, log_decay)
    final_x = exact_dot(final_log, spread_lanes)
    carry_x = jnp.exp(jnp.where(time <= last, final_x - decay_x, far_below))
    carried_x = (scaled_x * carry_x).T.astype(jnp.bfloat16)
    shrink = jnp.exp(final_x).T
    for r in range(requests):
        b_here = jnp.where(request == r, b_part, jnp.zeros_like(b_part))
        kept = shrink[:, r * DRAFT : r * DRAFT + 1] * state[member_ref[r]] + dot32(
            carried_x, b_here
        )
        kept_ref[r, :inner, :] = kept.astype(jnp.bfloat16)

    def kept_rows(first_request, count, slots, series, past_of):
        at = lax.broadcasted_iota(jnp.int32, (count * slots, 1), 0)
        here, edge = at // slots, at % slots
        start = jnp.zeros((count * slots, 1), jnp.int32)
        owner = jnp.zeros((count * slots, 1), jnp.int32)
        for r in range(count):
            start = jnp.where(here == r, accepted_ref[first_request + r], start)
            owner = jnp.where(here == r, member_ref[first_request + r], owner)
        index = start + edge
        token = (here + first_request) * DRAFT + index - (CONV - 1)
        chosen = (lax.broadcasted_iota(jnp.int32, (count * slots, tokens), 1) == token) & (
            index >= CONV - 1
        )
        rows = dot32(chosen.astype(jnp.bfloat16), series)
        for p in range(PROMPTS):
            for j in range(CONV - 1):
                rows = jnp.where((owner == p) & (index == j), past_of(j, p), rows)
        return rows.astype(jnp.bfloat16)

    for lanes in range(2):
        cut = slice(lanes * STATE, min((lanes + 1) * STATE, inner))
        rows = kept_rows(
            0, requests, 8, in_x[:, cut], lambda j, p: past_x_ref[j, p : p + 1, cut].astype(jnp.float32)
        )
        for r in range(requests):
            kept_ref[r, inner + 8 * lanes : inner + 8 * (lanes + 1), : rows.shape[1]] = rows[
                r * 8 : (r + 1) * 8
            ]
    kept_ref[:, inner + 8 :, inner - STATE :] = jnp.zeros(
        (requests, 8, 2 * STATE - inner), jnp.bfloat16
    )
    kept_bc_ref[...] = kept_rows(
        rank * (requests // SIDE),
        requests // SIDE,
        8,
        in_bc,
        lambda j, p: past_bc_ref[j, p : p + 1, :].astype(jnp.float32),
    )


def mixer(
    hidden, mixer_gain, w_query, w_kv, w_attn_out, prompt_kv, prompt_lengths, member, accepted, w_z, w_x, w_bc,
    w_dt, conv_x, conv_bc, ssm_rate, dt_bias, skip_d, prompt_state, prompt_conv_x, prompt_conv_bc, w_mamba_out,
):
    tokens, width = hidden.shape
    requests = tokens // DRAFT
    inner = w_x.shape[1]
    query_width = w_query.shape[1]
    bf16 = jnp.bfloat16
    state = prompt_state.reshape(PROMPTS, inner, STATE)
    small = [
        hidden, mixer_gain.reshape(-1, 128), w_dt.T, conv_x, conv_bc,
        prompt_conv_x.transpose(1, 0, 2), prompt_conv_bc.transpose(1, 0, 2),
    ]
    scalars = [member, accepted, prompt_lengths, ssm_rate, dt_bias, skip_d]
    whole = pl.BlockSpec(memory_space=pltpu.VMEM)
    return pl.pallas_call(
        mixer_kernel,
        out_shape=[
            jax.ShapeDtypeStruct((tokens // 2, width), bf16),
            jax.ShapeDtypeStruct((tokens // 2, width), bf16),
            jax.ShapeDtypeStruct((requests, inner + 16, STATE), bf16),
            jax.ShapeDtypeStruct((requests // SIDE * 8, 2 * STATE), bf16),
        ],
        in_specs=[pl.BlockSpec(memory_space=pltpu.HBM)] * 22,
        out_specs=[whole] * 4,
        scratch_shapes=[
            *(pltpu.SMEM(a.shape, a.dtype) for a in scalars),
            *(pltpu.VMEM(a.shape, a.dtype) for a in small),
            pltpu.VMEM(w_query.shape, bf16),
            pltpu.VMEM(w_kv.shape[1:], bf16),
            pltpu.VMEM((PROMPTS, *prompt_kv.shape[2:]), bf16),
            pltpu.VMEM(w_x.shape, bf16),
            pltpu.VMEM(w_bc.shape, bf16),
            pltpu.VMEM(w_z.shape, bf16),
            pltpu.VMEM(state.shape, jnp.float32),
            pltpu.VMEM((query_width + inner, width), bf16),
            pltpu.VMEM((tokens, query_width + inner), bf16),
            pltpu.VMEM((tokens, 128), jnp.float32),
            pltpu.SemaphoreType.DMA((23,)),
        ],
        compiler_params=pltpu.CompilerParams(vmem_limit_bytes=59 << 20),
        cost_estimate=pl.CostEstimate(
            flops=3_000_000_000, bytes_accessed=20_000_000, transcendentals=1_000_000
        ),
        name="mixer",
    )(
        *scalars, *small, w_query, w_kv, prompt_kv, w_x, w_bc, w_z, state, w_attn_out, w_mamba_out
    )


def feed_kernel(first_ref, second_ref, both_ref, down_ref, _, first_out, second_out):
    hidden = down_ref.shape[0]
    rows = first_ref.shape[0]
    joined = jnp.concatenate([first_ref[...], second_ref[...]], axis=0)
    pair = dot32(joined, both_ref[...])
    gate, up = pair[:, :hidden], pair[:, hidden:]
    active = (gate * jax.nn.sigmoid(gate) * up).astype(jnp.bfloat16)
    parts = dot32(active, down_ref[...]).astype(jnp.bfloat16)
    first_out[...] = parts[:rows]
    second_out[...] = parts[rows:]


def feed(first, second, w_both, w_down, token):
    rows, width = first.shape
    whole = pl.BlockSpec(memory_space=pltpu.VMEM)
    return pl.pallas_call(
        feed_kernel,
        out_shape=[jax.ShapeDtypeStruct((rows, width), jnp.bfloat16)] * 2,
        in_specs=[whole] * 4 + [pl.BlockSpec(memory_space=pl.ANY)],
        out_specs=[whole] * 2,
        compiler_params=pltpu.CompilerParams(vmem_limit_bytes=16 << 20),
        cost_estimate=pl.CostEstimate(
            flops=20 * 2 * rows * width * 2 * 3 * w_down.shape[0],
            bytes_accessed=4 * rows * width * 2 + 3 * w_down.size * 2,
            transcendentals=2 * rows * w_down.shape[0],
        ),
        name="feed",
    )(first, second, w_both, w_down, token)


def head_kernel(targets_ref, owners_ref, *refs):
    count = targets_ref.shape[0]
    rows_refs, head_ref, others, out_ref = refs[:count], refs[count], refs[count + 1 : -1], refs[-1]
    vocab = head_ref.shape[0]
    lanes = 2 * rows_refs[0].shape[0]
    slots = out_ref.shape[0]
    base = lax.axis_index("req") * vocab
    lane = lax.broadcasted_iota(jnp.int32, (lanes, 128), 0)
    column = lax.broadcasted_iota(jnp.int32, (lanes, 128), 1)
    fragment = (lane >= lanes // 2).astype(jnp.int32)
    place = (column == fragment * DRAFT + lane % DRAFT).astype(jnp.bfloat16)
    ids = lax.broadcasted_iota(jnp.int32, (vocab, lanes), 0) + base
    slot = lax.broadcasted_iota(jnp.int32, (slots, lanes), 0)
    packed = jnp.zeros(out_ref.shape, jnp.float32)
    for other in others:
        packed = packed + other[...]
    for pair in range(count // 2):
        joined = jnp.concatenate([rows_refs[2 * pair][...], rows_refs[2 * pair + 1][...]], axis=0)
        wanted = jnp.concatenate(
            [targets_ref[2 * pair : 2 * pair + 1, :], targets_ref[2 * pair + 1 : 2 * pair + 2, :]],
            axis=1,
        )
        owner = jnp.concatenate(
            [owners_ref[2 * pair : 2 * pair + 1, :], owners_ref[2 * pair + 1 : 2 * pair + 2, :]],
            axis=1,
        )
        logits = dot32(head_ref[...], joined, NEXT_TO)
        target = jnp.sum(jnp.where(ids == wanted, logits, 0.0), axis=0, keepdims=True)
        top = jnp.max(logits, axis=0, keepdims=True)
        total = jnp.sum(jnp.exp(logits - top), axis=0, keepdims=True)
        stats = jnp.where(slot % 8 == 0, top, jnp.where(slot % 8 == 1, total, target))
        rest = jnp.where((slot // 8 == owner) & (slot % 8 < 3), stats, 0.0)
        for _ in range(3):
            part = rest.astype(jnp.bfloat16)
            packed = packed + dot32(part, place)
            rest = rest - part.astype(jnp.float32)
    out_ref[...] = packed


def head_stats(targets, owners, rows, head_weight, devices, others=()):
    whole = pl.BlockSpec(memory_space=pltpu.VMEM)
    return pl.pallas_call(
        head_kernel,
        out_shape=jax.ShapeDtypeStruct((devices * 8, 128), jnp.float32),
        in_specs=[whole] * (3 + len(rows) + len(others)),
        out_specs=whole,
        compiler_params=pltpu.CompilerParams(vmem_limit_bytes=32 << 20),
        cost_estimate=pl.CostEstimate(
            flops=10 * 2 * len(rows) * rows[0].size * head_weight.shape[0],
            bytes_accessed=2 * len(rows) * rows[0].size + 2 * head_weight.size,
            transcendentals=len(rows) * rows[0].shape[0] * head_weight.shape[0],
        ),
        name="head_stats",
    )(targets, owners, *rows, head_weight, *others)


def mdl_pairs(step):
    pairs = []
    for device in range(SIDE * SIDE * CORES):
        flip = (3, 1)[(device + step) % 2]
        pairs += [(device * SIDE + z, device * SIDE + (z ^ flip)) for z in range(SIDE)]
    return pairs


def shards(
    hidden_in,
    mixer_gain,
    w_query,
    w_kv,
    w_attn_out,
    prompt_kv,
    prompt_lengths,
    member,
    accepted,
    w_z,
    w_x,
    w_bc,
    w_dt,
    conv_x,
    conv_bc,
    ssm_rate,
    dt_bias,
    skip_d,
    prompt_state,
    prompt_conv_x,
    prompt_conv_bc,
    w_mamba_out,
    mlp_gain,
    w_gate,
    w_up,
    w_down,
    final_gain,
    head_weight,
    draft_ids,
):
    row_reqs, draft_len, width = hidden_in.shape
    mdl_count = lax.axis_size("mdl")
    req_count = lax.axis_size("req")
    mdl_rank = lax.axis_index("mdl")
    req_rank = lax.axis_index("req")
    row_tokens = row_reqs * draft_len
    own_reqs = row_reqs // mdl_count
    own_tokens = own_reqs * draft_len
    flat_rows = hidden_in.reshape(row_tokens, width)
    local_inner = w_x.shape[1]
    edge_len = CONV - 1
    far, near, kept, own_bc = mixer(
        flat_rows, mixer_gain, w_query, w_kv, w_attn_out, prompt_kv, prompt_lengths, member, accepted, w_z, w_x, w_bc,
        w_dt, conv_x, conv_bc, ssm_rate, dt_bias, skip_d, prompt_state, prompt_conv_x, prompt_conv_bc, w_mamba_out,
    )
    kept_out = lax.all_to_all(
        kept.reshape(mdl_count, own_reqs, local_inner + 16, STATE),
        "mdl",
        split_axis=0,
        concat_axis=0,
        tiled=True,
    )

    came = lax.ppermute(far, ("req", "mdl"), mdl_pairs(0))
    last = lax.ppermute(added(near[own_tokens:], came[own_tokens:]), ("req", "mdl"), mdl_pairs(1))
    mixed = (
        near[:own_tokens].astype(jnp.float32)
        + came[:own_tokens].astype(jnp.float32)
        + last.astype(jnp.float32)
    )
    own_rows = lax.dynamic_slice_in_dim(flat_rows, mdl_rank * own_tokens, own_tokens, 0)
    after_mixer = (own_rows.astype(jnp.float32) + mixed).astype(jnp.bfloat16)
    prepared = rms_scale(after_mixer, mlp_gain).astype(jnp.bfloat16)
    w_both = jnp.concatenate([w_gate, w_up], axis=1)
    early, late = gather_rows([prepared[:draft_len], prepared[draft_len:]])

    core = req_rank % CORES
    chip_x = req_rank // CORES % SIDE
    chip_y = req_rank // (CORES * SIDE)
    table = jnp.where(core == 0, jnp.asarray(block_table()[0]), jnp.asarray(block_table()[1]))
    owner = ((chip_y ^ table[:, 0]) * SIDE + (chip_x ^ table[:, 1])) * CORES + (core ^ table[:, 2])
    request = owner * row_reqs + mdl_rank * own_reqs + table[:, 3]
    next_ids = jnp.concatenate([draft_ids[:, 1:], draft_ids[:, :1]], axis=1)
    picked = (request[:, None] == jnp.arange(draft_ids.shape[0])[None, :]).astype(jnp.float32)
    targets = jnp.dot(picked, next_ids.astype(jnp.float32), precision=HIGHEST).astype(jnp.int32)
    targets = targets.reshape(8, 8 * draft_len)
    owners = jnp.broadcast_to(owner[:, None], (64, draft_len)).reshape(8, 8 * draft_len)

    token = jnp.zeros((8, 128), jnp.float32)
    early_parts = [feed(*rows, w_both, w_down, token) for rows in early]
    later_token, kept_out = lax.optimization_barrier((token, kept_out))
    late_parts = [
        feed(*late[0], w_both, w_down, token),
        feed(*late[1], w_both, w_down, later_token),
    ]
    summed = jnp.concatenate(scatter_rows(early_parts, late_parts), axis=0)
    kept_state = (
        kept_out[:, :, :local_inner, :]
        .transpose(1, 0, 2, 3)
        .astype(jnp.float32)
        .reshape(own_reqs, mdl_count * local_inner // SSM_DIM, SSM_DIM, STATE)
    )
    edges = kept_out[:, :, local_inner:, :]
    edges = jnp.concatenate(
        [edges[:, :, :edge_len, :], edges[:, :, 8 : 8 + edge_len, : local_inner - STATE]], axis=3
    )
    kept_conv = jnp.concatenate(
        [
            edges.transpose(1, 2, 0, 3).reshape(own_reqs, edge_len, mdl_count * local_inner),
            own_bc.reshape(own_reqs, 8, 2 * STATE)[:, :edge_len, :],
        ],
        axis=2,
    )
    final_gain, kept_state, kept_conv, targets, owners = lax.optimization_barrier(
        (final_gain, kept_state, kept_conv, targets, owners)
    )
    after_feed = added(after_mixer, summed)
    final_rows = rms_scale(after_feed, final_gain).astype(jnp.bfloat16)
    early, late = gather_rows([final_rows[:draft_len], final_rows[draft_len:]])
    stats = [
        head_stats(targets[:4], owners[:4], early[0] + early[1], head_weight, req_count),
        head_stats(targets[4:6], owners[4:6], late[0], head_weight, req_count),
    ]
    stats = head_stats(targets[6:], owners[6:], late[1], head_weight, req_count, stats)
    shared = lax.all_to_all(stats, "req", split_axis=0, concat_axis=0, tiled=True)
    shared = shared.reshape(req_count, 8, 128)[:, :, :own_tokens]
    tops, totals, hits = shared[:, 0], shared[:, 1], shared[:, 2]
    top = jnp.max(tops, axis=0)
    total = jnp.sum(totals * jnp.exp(tops - top[None, :]), axis=0)
    log_total = top + jnp.log(total)
    position = jnp.arange(own_tokens) % draft_len
    verify_scores = jnp.where(
        position < draft_len - 1, jnp.sum(hits, axis=0) - log_total, top - log_total
    ).reshape(own_reqs, draft_len)
    return (
        after_feed.reshape(own_reqs, draft_len, width),
        verify_scores,
        kept_state,
        kept_conv,
    )


def solution(mesh):
    in_specs = (
        P("req", None, None),
        P(),
        P(None, "mdl"),
        P(),
        P("mdl", None),
        P("req", None, None, None),
        P("req"),
        P("req"),
        P("req"),
        P(None, "mdl"),
        P(None, "mdl"),
        P(),
        P(None, "mdl"),
        P(None, "mdl"),
        P(),
        P("mdl"),
        P("mdl"),
        P("mdl"),
        P("req", "mdl", None, None),
        P("req", None, "mdl"),
        P("req", None, None),
        P("mdl", None),
        P(),
        P(None, "req"),
        P(None, "req"),
        P("req", None),
        P(),
        P("req", None),
        P(),
    )
    out_specs = (
        P(("req", "mdl"), None, None),
        P(("req", "mdl"), None),
        P(("req", "mdl"), None, None, None),
        P(("req", "mdl"), None, None),
    )
    return jax.shard_map(shards, mesh=mesh, in_specs=in_specs, out_specs=out_specs, check_vma=False)
```

time: 191 us -> 174 us (0.911)
  waiting for transfers between devices: 66.5 us -> 52.6 us
  local copies, waits for them, and re-layouts: 18.5 us -> 6.18 us
  blocking collectives: 0 us -> 11.8 us
    ppermute x24, waiting for transfers between devices: 46.9 us -> 28.5 us  [hop(): return lax.ppermute(part, 'req', hop_pairs(fragment, step))]
    ppermute x2, waiting for transfers between devices: 9.82 us -> 24 us  [the longest x1 21.6 us: shards(): came = lax.ppermute(far, ('req', 'mdl'), mdl_pairs(0))]
    unnamed x59 -> x30, local copies, waits for them, and re-layouts: 13.4 us -> 1.21 us
    all_to_all x0 -> x1, blocking collectives: none -> 11.8 us  [shards(): lax.all_to_all(stats, 'req', split_axis=0, concat_axis=0, tiled=True)]
    all_to_all x3 -> x1, waiting for transfers between devices: 7.73 us -> 0.01 us  [shards(): lax.all_to_all(kept.reshape(mdl_count, own_reqs, local_inner + 16, STATE)...]
    all_to_all x3 -> x1, starting transfers between devices: 12.9 us -> 5.99 us  [shards(): lax.all_to_all(kept.reshape(mdl_count, own_reqs, local_inner + 16, STATE)...]
    ppermute x6 -> x12, starting transfers between devices: 24.3 us -> 29.5 us  [swap_core(): return lax.ppermute(part, 'req', CORE_PAIRS)]
    pallas_call x1 -> x3, Pallas kernels: 14.2 us -> 9.6 us  [head_stats(): pl.pallas_call(head_kernel, out_shape=jax.ShapeDtypeStruct((devices * 8,...]
  transfers between devices with their start and end apart: 35 -> 39, of which waited for: 24 -> 19; matrix products, arithmetic and copies ran while one was open for 5% -> 6% of each run, Pallas kernels for 9% -> 9%
where the time goes in v1:
time: 174 us; the launch traced here: 173 us
  starting transfers between devices  67.5 us (39%)
  waiting for transfers between devices  52.6 us (30%)
  Pallas kernels  27.4 us (16%)
  blocking collectives  11.8 us (7%)
  other arithmetic  6.52 us (4%)
  local copies, waits for them, and re-layouts  6.18 us (4%)
    ppermute x12, starting transfers between devices, swap_core(): return lax.ppermute(part, 'req', CORE_PAIRS)  29.5 us
    ppermute x24, starting transfers between devices, hop(): return lax.ppermute(part, 'req', hop_pairs(fragment, step))  29 us
    ppermute x24, waiting for transfers between devices, hop(): return lax.ppermute(part, 'req', hop_pairs(fragment, step))  28.5 us
    ppermute x1, waiting for transfers between devices, shards(): came = lax.ppermute(far, ('req', 'mdl'), mdl_pairs(0))  21.6 us
    all_to_all x1, blocking collectives, shards(): lax.all_to_all(stats, 'req', split_axis=0, concat_axis=0, tiled=True)  11.8 us
    pallas_call x1, Pallas kernels, mixer(): pl.pallas_call(mixer_kernel, out_shape=[jax.ShapeDtypeStruct((tokens // 2...  10.3 us
    pallas_call x3, Pallas kernels, head_stats(): pl.pallas_call(head_kernel, out_shape=jax.ShapeDtypeStruct((devices * 8,...  9.6 us
    pallas_call x4, Pallas kernels, feed(): pl.pallas_call(feed_kernel, out_shape=[jax.ShapeDtypeStruct((rows, width)...  7.56 us
  transfers between devices with their start and end apart: 39, of which 19 were waited for; matrix products, arithmetic and copies ran while one was open for 6% of the time, Pallas kernels for 9%

profile of v1, /device:TPU:1, one launch (start us, length us, event | category | flops | bytes accessed | tf_op | source)
XLA Modules:
  0.0 173.5 jit_solution(16973841929154248073)
XLA Ops:
  0.6 10.3 %mixer.1 = (bf16[64,2048]{1,0:T(8,128)(2,1)}, bf16[64,2048]{1,0:T(8,128)(2,1)}, bf16[8,400,256]{2,1,0:T(8,128)(2,1)}, bf16[16,512]{1,0:T(8,128)(2,1)}) custom-call(s32[8]{0:T(128)} %refs_0_.1, s32[8]{0:T(128)} %refs_1_.1, s32[2]{0:T(128)} %refs_2_.3, f32[6]{0:T(128)} %refs_3_.1, f32[6]{0:T(128)} %refs_4_.2, f32[6]{0:T(128)} %refs_5_.1, ...), custom_call_target="tpu_custom_call" | custom-call | flops 3000000000 | bytes 20000000 | tf_op jit(solution)/shard_map/mixer/pallas_call | solution.py:377
  11.0 6.0 %all-to-all-start = ((bf16[4,2,400,256]{3,2,1,0:T(8,128)(2,1)}), bf16[4,2,400,256]{3,2,1,0:T(8,128)(2,1)}, u32[]{:S(2)}, u32[]{:S(2)}) async-start(bf16[4,2,400,256]{3,2,1,0:T(8,128)(2,1)} %bitcast.26), calls=%async_computation | async-start | bytes 3276800 | tf_op jit(solution)/shard_map/all_to_all | solution.py:552
  17.0 1.5 collective-permute-start
  18.9 21.6 %collective-permute-done = bf16[64,2048]{1,0:T(8,128)(2,1)S(1)} collective-permute-done((bf16[64,2048]{1,0:T(8,128)(2,1)S(1)}, bf16[64,2048]{1,0:T(8,128)(2,1)S(1)}, u32[]{:S(2)}, u32[]{:S(2)}) %collective-permute-start) | collective-permute-done | bytes 262176 | tf_op jit(solution)/shard_map/ppermute | solution.py:560
  40.5 1.5 collective-permute-start.1
  43.1 2.5 %collective-permute-done.1 = bf16[32,2048]{1,0:T(8,128)(2,1)S(1)} collective-permute-done((bf16[32,2048]{1,0:T(8,128)(2,1)S(1)}, bf16[32,2048]{1,0:T(8,128)(2,1)S(1)}, u32[]{:S(2)}, u32[]{:S(2)}) %collective-permute-start.1) | collective-permute-done | bytes 131104 | tf_op jit(solution)/shard_map/ppermute | solution.py:561
  48.2 2.0 %collective-permute-start.5 = (bf16[16,2048]{1,0:T(8,128)(2,1)S(1)}, bf16[16,2048]{1,0:T(8,128)(2,1)S(1)}, u32[]{:S(2)}, u32[]{:S(2)}) collective-permute-start(bf16[16,2048]{1,0:T(8,128)(2,1)S(1)} %get-tuple-element.53), channel_id=1, source_target_pairs={{0,24},{4,100},{8,16},{12,108},{16,8},{20,116},{24,0},{28,124},{32... | collective-permute-start | bytes 196616 | tf_op jit(solution)/shard_map/ppermute | solution.py:58
  50.2 2.6 %collective-permute-start.3 = (bf16[32,2048]{1,0:T(8,128)(2,1)S(1)}, bf16[32,2048]{1,0:T(8,128)(2,1)S(1)}, u32[]{:S(2)}, u32[]{:S(2)}) collective-permute-start(bf16[32,2048]{1,0:T(8,128)(2,1)S(1)} %pad_maximum_fusion.8), channel_id=1, source_target_pairs={{0,24},{4,100},{8,16},{12,108},{16,8},{20,116},{24,0},{28,124},{32... | collective-permute-start | bytes 393224 | tf_op jit(solution)/shard_map/ppermute | solution.py:58
  56.8 2.6 %collective-permute-start.7 = (bf16[64,2048]{1,0:T(8,128)(2,1)S(1)}, bf16[64,2048]{1,0:T(8,128)(2,1)S(1)}, u32[]{:S(2)}, u32[]{:S(2)}) collective-permute-start(bf16[64,2048]{1,0:T(8,128)(2,1)S(1)} %pad_maximum_fusion.5), channel_id=1, source_target_pairs={{0,96},{4,28},{8,104},{12,20},{16,112},{20,12},{24,120},{28,4},{32... | collective-permute-start | bytes 786440 | tf_op jit(solution)/shard_map/ppermute | solution.py:58
  60.8 2.5 %collective-permute-start.11 = (bf16[128,2048]{1,0:T(8,128)(2,1)S(1)}, bf16[128,2048]{1,0:T(8,128)(2,1)}, u32[]{:S(2)}, u32[]{:S(2)}) collective-permute-start(bf16[128,2048]{1,0:T(8,128)(2,1)S(1)} %pad_maximum_fusion.first_ref), channel_id=1, source_target_pairs={{0,96},{4,28},{8,104},{12,20},{16,112},{20,12},{24,120},{28,4},{32... | collective-permute-start | bytes 1572872 | tf_op jit(solution)/shard_map/ppermute | solution.py:58
  63.3 5.6 %collective-permute-start.8 = (bf16[128,2048]{1,0:T(8,128)(2,1)S(1)}, bf16[128,2048]{1,0:T(8,128)(2,1)}, u32[]{:S(2)}, u32[]{:S(2)}) collective-permute-start(bf16[128,2048]{1,0:T(8,128)(2,1)S(1)} %pad_maximum_fusion.first_ref), channel_id=1, source_target_pairs={{0,4},{4,0},{8,12},{12,8},{16,20},{20,16},{24,28},{28,24},{32,36},... | collective-permute-start | bytes 1572872 | tf_op jit(solution)/shard_map/ppermute | solution.py:62
  73.2 1.7 %convert_bitcast_fusion = f32[2,4,384,256]{3,2,0,1:T(8,128)S(1)} fusion(bf16[4,2,400,256]{3,2,1,0:T(8,128)(2,1)} %all-to-all-done), kind=kLoop, calls=%fused_computation | loop fusion | flops 786432 | bytes 4718592 | tf_op jit(solution)/shard_map/reshape | solution.py:597
  78.3 2.5 %feed.5 = (bf16[128,2048]{1,0:T(8,128)(2,1)S(1)}, bf16[128,2048]{1,0:T(8,128)(2,1)S(1)}) custom-call(bf16[128,2048]{1,0:T(8,128)(2,1)} %collective-permute-done.8.first_ref, bf16[128,2048]{1,0:T(8,128)(2,1)} %collective-permute-done.9.second_ref, bf16[2048,256]{1,0:T(8,128)(2,1)S(1)} %constant_dynamic-update-slice_fusion.both_ref, ...), custom_call_target="tpu_custom_call" | custom-call | flops 8053063680 | bytes 3670016 | tf_op jit(solution)/shard_map/feed/pallas_call | solution.py:427
  83.3 2.5 %feed.6 = (bf16[128,2048]{1,0:T(8,128)(2,1)S(1)}, bf16[128,2048]{1,0:T(8,128)(2,1)S(1)}) custom-call(bf16[128,2048]{1,0:T(8,128)(2,1)} %collective-permute-done.11.first_ref, bf16[128,2048]{1,0:T(8,128)(2,1)} %collective-permute-done.12.second_ref, bf16[2048,256]{1,0:T(8,128)(2,1)S(1)} %constant_dynamic-update-slice_fusion.both_ref, ...), custom_call_target="tpu_custom_call" | custom-call | flops 8053063680 | bytes 3670016 | tf_op jit(solution)/shard_map/feed/pallas_call | solution.py:427
  85.9 2.6 %collective-permute-start.16 = (bf16[128,2048]{1,0:T(8,128)(2,1)S(1)}, bf16[128,2048]{1,0:T(8,128)(2,1)S(1)}, u32[]{:S(2)}, u32[]{:S(2)}) collective-permute-start(bf16[128,2048]{1,0:T(8,128)(2,1)S(1)} %add_convert_fusion.4), channel_id=1, source_target_pairs={{0,96},{4,28},{8,104},{12,20},{16,112},{20,12},{24,120},{28,4},{32... | collective-permute-start | bytes 1572872 | tf_op jit(solution)/shard_map/ppermute | solution.py:58
  89.4 2.0 %copy.40 = f32[2,4,384,256]{3,2,1,0:T(8,128)} copy(f32[2,4,384,256]{3,2,0,1:T(8,128)S(1)} %convert_bitcast_fusion) | data formatting | bytes 6291456 | tf_op jit(solution)/shard_map/reshape | solution.py:597
  91.4 4.2 %collective-permute-done.16 = bf16[128,2048]{1,0:T(8,128)(2,1)S(1)} collective-permute-done((bf16[128,2048]{1,0:T(8,128)(2,1)S(1)}, bf16[128,2048]{1,0:T(8,128)(2,1)S(1)}, u32[]{:S(2)}, u32[]{:S(2)}) %collective-permute-start.16) | collective-permute-done | bytes 524320 | tf_op jit(solution)/shard_map/ppermute | solution.py:58
  98.8 2.6 %collective-permute-done.17 = bf16[64,2048]{1,0:T(8,128)(2,1)S(1)} collective-permute-done((bf16[64,2048]{1,0:T(8,128)(2,1)S(1)}, bf16[64,2048]{1,0:T(8,128)(2,1)S(1)}, u32[]{:S(2)}, u32[]{:S(2)}) %collective-permute-start.17) | collective-permute-done | bytes 262176 | tf_op jit(solution)/shard_map/ppermute | solution.py:58
  101.5 2.5 %collective-permute-start.18 = (bf16[32,2048]{1,0:T(8,128)(2,1)S(1)}, bf16[32,2048]{1,0:T(8,128)(2,1)S(1)}, u32[]{:S(2)}, u32[]{:S(2)}) collective-permute-start(bf16[32,2048]{1,0:T(8,128)(2,1)S(1)} %slice.170), channel_id=1, source_target_pairs={{0,24},{4,100},{8,16},{12,108},{16,8},{20,116},{24,0},{28,124},{32... | collective-permute-start | bytes 393224 | tf_op jit(solution)/shard_map/ppermute | solution.py:58
  104.3 2.6 %collective-permute-done.18 = bf16[32,2048]{1,0:T(8,128)(2,1)S(1)} collective-permute-done((bf16[32,2048]{1,0:T(8,128)(2,1)S(1)}, bf16[32,2048]{1,0:T(8,128)(2,1)S(1)}, u32[]{:S(2)}, u32[]{:S(2)}) %collective-permute-start.18) | collective-permute-done | bytes 131104 | tf_op jit(solution)/shard_map/ppermute | solution.py:58
  111.1 1.7 collective-permute-done.25
  114.6 1.8 %collective-permute-done.26 = bf16[16,2048]{1,0:T(8,128)(2,1)S(1)} collective-permute-done((bf16[16,2048]{1,0:T(8,128)(2,1)S(1)}, bf16[16,2048]{1,0:T(8,128)(2,1)S(1)}, u32[]{:S(2)}, u32[]{:S(2)}) %collective-permute-start.26) | collective-permute-done | bytes 65568 | tf_op jit(solution)/shard_map/ppermute | solution.py:58
  118.1 3.4 %collective-permute-done.27 = bf16[32,2048]{1,0:T(8,128)(2,1)S(1)} collective-permute-done((bf16[32,2048]{1,0:T(8,128)(2,1)S(1)}, bf16[32,2048]{1,0:T(8,128)(2,1)S(1)}, u32[]{:S(2)}, u32[]{:S(2)}) %collective-permute-start.27) | collective-permute-done | bytes 131104 | tf_op jit(solution)/shard_map/ppermute | solution.py:58
  122.5 2.1 %collective-permute-start.33 = (bf16[64,2048]{1,0:T(8,128)(2,1)S(1)}, bf16[64,2048]{1,0:T(8,128)(2,1)S(1)}, u32[]{:S(2)}, u32[]{:S(2)}) collective-permute-start(bf16[64,2048]{1,0:T(8,128)(2,1)S(1)} %pad_maximum_fusion.7), channel_id=1, source_target_pairs={{0,96},{4,28},{8,104},{12,20},{16,112},{20,12},{24,120},{28,4},{32... | collective-permute-start | bytes 786440 | tf_op jit(solution)/shard_map/ppermute | solution.py:58
  124.5 2.3 %collective-permute-done.28 = bf16[64,2048]{1,0:T(8,128)(2,1)S(1)} collective-permute-done((bf16[64,2048]{1,0:T(8,128)(2,1)S(1)}, bf16[64,2048]{1,0:T(8,128)(2,1)S(1)}, u32[]{:S(2)}, u32[]{:S(2)}) %collective-permute-start.28) | collective-permute-done | bytes 262176 | tf_op jit(solution)/shard_map/ppermute | solution.py:58
  128.3 2.0 %collective-permute-done.33 = bf16[64,2048]{1,0:T(8,128)(2,1)S(1)} collective-permute-done((bf16[64,2048]{1,0:T(8,128)(2,1)S(1)}, bf16[64,2048]{1,0:T(8,128)(2,1)S(1)}, u32[]{:S(2)}, u32[]{:S(2)}) %collective-permute-start.33) | collective-permute-done | bytes 262176 | tf_op jit(solution)/shard_map/ppermute | solution.py:58
  130.8 11.4 %collective-permute-start.36 = (bf16[128,2048]{1,0:T(8,128)(2,1)S(1)}, bf16[128,2048]{1,0:T(8,128)(2,1)S(1)}, u32[]{:S(2)}, u32[]{:S(2)}) collective-permute-start(bf16[128,2048]{1,0:T(8,128)(2,1)S(1)} %pad_maximum_fusion.2.refs_0_), channel_id=1, source_target_pairs={{0,4},{4,0},{8,12},{12,8},{16,20},{20,16},{24,28},{28,24},{32,36},... | collective-permute-start | bytes 1572872 | tf_op jit(solution)/shard_map/ppermute | solution.py:62
  142.4 8.1 %collective-permute-start.30 = (bf16[128,2048]{1,0:T(8,128)(2,1)S(1)}, bf16[128,2048]{1,0:T(8,128)(2,1)S(1)}, u32[]{:S(2)}, u32[]{:S(2)}) collective-permute-start(bf16[128,2048]{1,0:T(8,128)(2,1)S(1)} %collective-permute-done.29.refs_0_), channel_id=1, source_target_pairs={{0,4},{4,0},{8,12},{12,8},{16,20},{20,16},{24,28},{28,24},{32,36},... | collective-permute-start | bytes 1572872 | tf_op jit(solution)/shard_map/ppermute | solution.py:62
  151.1 5.6 %head_stats.3.refs_3_ = f32[256,128]{1,0:T(8,128)S(1)} custom-call(s32[4,128]{1,0:T(4,128)S(1)} %slice.156.targets_ref, s32[4,128]{1,0:T(4,128)S(1)} %slice.157.owners_ref, bf16[128,2048]{1,0:T(8,128)(2,1)S(1)} %pad_maximum_fusion.2.refs_0_, bf16[128,2048]{1,0:T(8,128)(2,1)S(1)} %pad_maximum_fusion.3.refs_1_, ...), custom_call_target="tpu_custom_call" | custom-call | flops 21474836480 | bytes 6291456 | tf_op jit(solution)/shard_map/head_stats/pallas_call | solution.py:483
  156.8 2.0 %head_stats.4.refs_4_ = f32[256,128]{1,0:T(8,128)S(1)} custom-call(s32[2,128]{1,0:T(2,128)S(1)} %get-tuple-element.60.targets_ref, s32[2,128]{1,0:T(2,128)S(1)} %get-tuple-element.55.owners_ref, bf16[128,2048]{1,0:T(8,128)(2,1)S(1)} %collective-permute-done.29.refs_0_, bf16[128,2048]{1,0:T(8,128)(2,1)S(1)} %collective-permute-done.34.refs_1_, ...), custom_call_target="tpu_custom_call" | custom-call | flops 10737418240 | bytes 5242880 | tf_op jit(solution)/shard_map/head_stats/pallas_call | solution.py:483
  158.8 2.0 %head_stats.5 = f32[256,128]{1,0:T(8,128)S(1)} custom-call(s32[2,128]{1,0:T(2,128)S(1)} %get-tuple-element.59.targets_ref, s32[2,128]{1,0:T(2,128)S(1)} %get-tuple-element.56.owners_ref, bf16[128,2048]{1,0:T(8,128)(2,1)S(1)} %collective-permute-done.30.refs_0_, bf16[128,2048]{1,0:T(8,128)(2,1)S(1)} %collective-permute-done.35.refs_1_, ...), custom_call_target="tpu_custom_call" | custom-call | flops 10737418240 | bytes 5242880 | tf_op jit(solution)/shard_map/head_stats/pallas_call | solution.py:483
  160.8 11.8 %all_to_all.14 = f32[32,8,128]{2,1,0:T(8,128)S(1)} all-to-all(f32[32,8,128]{2,1,0:T(8,128)S(1)} %bitcast.24), channel_id=1, replica_groups=mesh['req'=32,'mdl'=4] {'req'}, dimensions={0} | all-to-all | bytes 262144 | tf_op jit(solution)/shard_map/all_to_all | solution.py:621
  (159 shorter events, 36.2 us)
Async XLA Ops:
  11.0 60.6 %all-to-all-start = ((bf16[4,2,400,256]{3,2,1,0:T(8,128)(2,1)}), bf16[4,2,400,256]{3,2,1,0:T(8,128)(2,1)}, u32[]{:S(2)}, u32[]{:S(2)}) async-start(bf16[4,2,400,256]{3,2,1,0:T(8,128)(2,1)} %bitcast.26), calls=%async_computation | async-start | bytes 3276800 | tf_op jit(solution)/shard_map/all_to_all | solution.py:552
  17.0 23.4 %collective-permute-start = (bf16[64,2048]{1,0:T(8,128)(2,1)S(1)}, bf16[64,2048]{1,0:T(8,128)(2,1)S(1)}, u32[]{:S(2)}, u32[]{:S(2)}) collective-permute-start(bf16[64,2048]{1,0:T(8,128)(2,1)S(1)} %copy-done.13), channel_id=1, source_target_pairs={{0,3},{1,2},{2,1},{3,0},{4,5},{5,4},{6,7},{7,6},{8,11},{9,10},{10,... | collective-permute-start | bytes 786440 | tf_op jit(solution)/shard_map/ppermute | solution.py:560
  40.5 5.1 %collective-permute-start.1 = (bf16[32,2048]{1,0:T(8,128)(2,1)S(1)}, bf16[32,2048]{1,0:T(8,128)(2,1)S(1)}, u32[]{:S(2)}, u32[]{:S(2)}) collective-permute-start(bf16[32,2048]{1,0:T(8,128)(2,1)S(1)} %add_convert_fusion.11), channel_id=1, source_target_pairs={{0,1},{1,0},{2,3},{3,2},{4,7},{5,6},{6,5},{7,4},{8,9},{9,8},{10,11... | collective-permute-start | bytes 393224 | tf_op jit(solution)/shard_map/ppermute | solution.py:561
  48.2 4.6 %collective-permute-start.5 = (bf16[16,2048]{1,0:T(8,128)(2,1)S(1)}, bf16[16,2048]{1,0:T(8,128)(2,1)S(1)}, u32[]{:S(2)}, u32[]{:S(2)}) collective-permute-start(bf16[16,2048]{1,0:T(8,128)(2,1)S(1)} %get-tuple-element.53), channel_id=1, source_target_pairs={{0,24},{4,100},{8,16},{12,108},{16,8},{20,116},{24,0},{28,124},{32... | collective-permute-start | bytes 196616 | tf_op jit(solution)/shard_map/ppermute | solution.py:58
  50.2 5.2 %collective-permute-start.3 = (bf16[32,2048]{1,0:T(8,128)(2,1)S(1)}, bf16[32,2048]{1,0:T(8,128)(2,1)S(1)}, u32[]{:S(2)}, u32[]{:S(2)}) collective-permute-start(bf16[32,2048]{1,0:T(8,128)(2,1)S(1)} %pad_maximum_fusion.8), channel_id=1, source_target_pairs={{0,24},{4,100},{8,16},{12,108},{16,8},{20,116},{24,0},{28,124},{32... | collective-permute-start | bytes 393224 | tf_op jit(solution)/shard_map/ppermute | solution.py:58
  55.4 5.3 %collective-permute-start.4 = (bf16[64,2048]{1,0:T(8,128)(2,1)S(1)}, bf16[64,2048]{1,0:T(8,128)(2,1)S(1)}, u32[]{:S(2)}, u32[]{:S(2)}) collective-permute-start(bf16[64,2048]{1,0:T(8,128)(2,1)S(1)} %pad_maximum_fusion.4), channel_id=1, source_target_pairs={{0,32},{4,12},{8,40},{12,4},{16,48},{20,28},{24,56},{28,20},{32,0}... | collective-permute-start | bytes 786440 | tf_op jit(solution)/shard_map/ppermute | solution.py:58
  56.8 12.1 %collective-permute-start.7 = (bf16[64,2048]{1,0:T(8,128)(2,1)S(1)}, bf16[64,2048]{1,0:T(8,128)(2,1)S(1)}, u32[]{:S(2)}, u32[]{:S(2)}) collective-permute-start(bf16[64,2048]{1,0:T(8,128)(2,1)S(1)} %pad_maximum_fusion.5), channel_id=1, source_target_pairs={{0,96},{4,28},{8,104},{12,20},{16,112},{20,12},{24,120},{28,4},{32... | collective-permute-start | bytes 786440 | tf_op jit(solution)/shard_map/ppermute | solution.py:58
  60.8 14.2 %collective-permute-start.11 = (bf16[128,2048]{1,0:T(8,128)(2,1)S(1)}, bf16[128,2048]{1,0:T(8,128)(2,1)}, u32[]{:S(2)}, u32[]{:S(2)}) collective-permute-start(bf16[128,2048]{1,0:T(8,128)(2,1)S(1)} %pad_maximum_fusion.first_ref), channel_id=1, source_target_pairs={{0,96},{4,28},{8,104},{12,20},{16,112},{20,12},{24,120},{28,4},{32... | collective-permute-start | bytes 1572872 | tf_op jit(solution)/shard_map/ppermute | solution.py:58
  63.3 15.0 %collective-permute-start.8 = (bf16[128,2048]{1,0:T(8,128)(2,1)S(1)}, bf16[128,2048]{1,0:T(8,128)(2,1)}, u32[]{:S(2)}, u32[]{:S(2)}) collective-permute-start(bf16[128,2048]{1,0:T(8,128)(2,1)S(1)} %pad_maximum_fusion.first_ref), channel_id=1, source_target_pairs={{0,4},{4,0},{8,12},{12,8},{16,20},{20,16},{24,28},{28,24},{32,36},... | collective-permute-start | bytes 1572872 | tf_op jit(solution)/shard_map/ppermute | solution.py:62
  68.9 8.5 %collective-permute-start.12 = (bf16[128,2048]{1,0:T(8,128)(2,1)S(1)}, bf16[128,2048]{1,0:T(8,128)(2,1)}, u32[]{:S(2)}, u32[]{:S(2)}) collective-permute-start(bf16[128,2048]{1,0:T(8,128)(2,1)S(1)} %pad_maximum_fusion.1.second_ref), channel_id=1, source_target_pairs={{0,8},{4,36},{8,0},{12,44},{16,24},{20,52},{24,16},{28,60},{32,40}... | collective-permute-start | bytes 1572872 | tf_op jit(solution)/shard_map/ppermute | solution.py:58
  69.0 9.3 %collective-permute-start.9 = (bf16[128,2048]{1,0:T(8,128)(2,1)S(1)}, bf16[128,2048]{1,0:T(8,128)(2,1)}, u32[]{:S(2)}, u32[]{:S(2)}) collective-permute-start(bf16[128,2048]{1,0:T(8,128)(2,1)S(1)} %pad_maximum_fusion.1.second_ref), channel_id=1, source_target_pairs={{0,4},{4,0},{8,12},{12,8},{16,20},{20,16},{24,28},{28,24},{32,36},... | collective-permute-start | bytes 1572872 | tf_op jit(solution)/shard_map/ppermute | solution.py:62
  75.0 6.4 %collective-permute-start.13 = (bf16[128,2048]{1,0:T(8,128)(2,1)}, bf16[128,2048]{1,0:T(8,128)(2,1)S(1)}, u32[]{:S(2)}, u32[]{:S(2)}) collective-permute-start(bf16[128,2048]{1,0:T(8,128)(2,1)} %collective-permute-done.11.first_ref), channel_id=1, source_target_pairs={{0,4},{4,0},{8,12},{12,8},{16,20},{20,16},{24,28},{28,24},{32,36},... | collective-permute-start | bytes 1572872 | tf_op jit(solution)/shard_map/ppermute | solution.py:62
  80.8 10.6 %collective-permute-start.10 = (bf16[128,2048]{1,0:T(8,128)(2,1)S(1)}, bf16[128,2048]{1,0:T(8,128)(2,1)S(1)}, u32[]{:S(2)}, u32[]{:S(2)}) collective-permute-start(bf16[128,2048]{1,0:T(8,128)(2,1)S(1)} %get-tuple-element.26), channel_id=1, source_target_pairs={{0,4},{4,0},{8,12},{12,8},{16,20},{20,16},{24,28},{28,24},{32,36},... | collective-permute-start | bytes 1572872 | tf_op jit(solution)/shard_map/ppermute | solution.py:62
  80.9 15.0 %collective-permute-start.20 = (bf16[128,2048]{1,0:T(8,128)(2,1)S(1)}, bf16[128,2048]{1,0:T(8,128)(2,1)S(1)}, u32[]{:S(2)}, u32[]{:S(2)}) collective-permute-start(bf16[128,2048]{1,0:T(8,128)(2,1)S(1)} %get-tuple-element.32), channel_id=1, source_target_pairs={{0,4},{4,0},{8,12},{12,8},{16,20},{20,16},{24,28},{28,24},{32,36},... | collective-permute-start | bytes 1572872 | tf_op jit(solution)/shard_map/ppermute | solution.py:62
  82.9 5.6 %collective-permute-start.21 = (bf16[128,2048]{1,0:T(8,128)(2,1)S(1)}, bf16[128,2048]{1,0:T(8,128)(2,1)S(1)}, u32[]{:S(2)}, u32[]{:S(2)}) collective-permute-start(bf16[128,2048]{1,0:T(8,128)(2,1)S(1)} %get-tuple-element.34), channel_id=1, source_target_pairs={{0,4},{4,0},{8,12},{12,8},{16,20},{20,16},{24,28},{28,24},{32,36},... | collective-permute-start | bytes 1572872 | tf_op jit(solution)/shard_map/ppermute | solution.py:62
  85.9 9.6 %collective-permute-start.16 = (bf16[128,2048]{1,0:T(8,128)(2,1)S(1)}, bf16[128,2048]{1,0:T(8,128)(2,1)S(1)}, u32[]{:S(2)}, u32[]{:S(2)}) collective-permute-start(bf16[128,2048]{1,0:T(8,128)(2,1)S(1)} %add_convert_fusion.4), channel_id=1, source_target_pairs={{0,96},{4,28},{8,104},{12,20},{16,112},{20,12},{24,120},{28,4},{32... | collective-permute-start | bytes 1572872 | tf_op jit(solution)/shard_map/ppermute | solution.py:58
  88.6 8.4 %collective-permute-start.22 = (bf16[128,2048]{1,0:T(8,128)(2,1)S(1)}, bf16[128,2048]{1,0:T(8,128)(2,1)S(1)}, u32[]{:S(2)}, u32[]{:S(2)}) collective-permute-start(bf16[128,2048]{1,0:T(8,128)(2,1)S(1)} %add_convert_fusion.1), channel_id=1, source_target_pairs={{0,8},{4,36},{8,0},{12,44},{16,24},{20,52},{24,16},{28,60},{32,40}... | collective-permute-start | bytes 1572872 | tf_op jit(solution)/shard_map/ppermute | solution.py:58
  95.8 5.6 %collective-permute-start.17 = (bf16[64,2048]{1,0:T(8,128)(2,1)S(1)}, bf16[64,2048]{1,0:T(8,128)(2,1)S(1)}, u32[]{:S(2)}, u32[]{:S(2)}) collective-permute-start(bf16[64,2048]{1,0:T(8,128)(2,1)S(1)} %slice.168), channel_id=1, source_target_pairs={{0,32},{4,12},{8,40},{12,4},{16,48},{20,28},{24,56},{28,20},{32,0}... | collective-permute-start | bytes 786440 | tf_op jit(solution)/shard_map/ppermute | solution.py:58
  97.3 6.8 %collective-permute-start.23 = (bf16[64,2048]{1,0:T(8,128)(2,1)S(1)}, bf16[64,2048]{1,0:T(8,128)(2,1)S(1)}, u32[]{:S(2)}, u32[]{:S(2)}) collective-permute-start(bf16[64,2048]{1,0:T(8,128)(2,1)S(1)} %slice.174), channel_id=1, source_target_pairs={{0,96},{4,28},{8,104},{12,20},{16,112},{20,12},{24,120},{28,4},{32... | collective-permute-start | bytes 786440 | tf_op jit(solution)/shard_map/ppermute | solution.py:58
  101.5 5.4 %collective-permute-start.18 = (bf16[32,2048]{1,0:T(8,128)(2,1)S(1)}, bf16[32,2048]{1,0:T(8,128)(2,1)S(1)}, u32[]{:S(2)}, u32[]{:S(2)}) collective-permute-start(bf16[32,2048]{1,0:T(8,128)(2,1)S(1)} %slice.170), channel_id=1, source_target_pairs={{0,24},{4,100},{8,16},{12,108},{16,8},{20,116},{24,0},{28,124},{32... | collective-permute-start | bytes 393224 | tf_op jit(solution)/shard_map/ppermute | solution.py:58
  108.5 4.4 %collective-permute-start.25 = (bf16[16,2048]{1,0:T(8,128)(2,1)S(1)}, bf16[16,2048]{1,0:T(8,128)(2,1)S(1)}, u32[]{:S(2)}, u32[]{:S(2)}) collective-permute-start(bf16[16,2048]{1,0:T(8,128)(2,1)S(1)} %slice.178), channel_id=1, source_target_pairs={{0,24},{4,100},{8,16},{12,108},{16,8},{20,116},{24,0},{28,124},{32... | collective-permute-start | bytes 196616 | tf_op jit(solution)/shard_map/ppermute | solution.py:58
  113.3 4.4 %collective-permute-start.31 = (bf16[16,2048]{1,0:T(8,128)(2,1)S(1)}, bf16[16,2048]{1,0:T(8,128)(2,1)S(1)}, u32[]{:S(2)}, u32[]{:S(2)}) collective-permute-start(bf16[16,2048]{1,0:T(8,128)(2,1)S(1)} %get-tuple-element.51), channel_id=1, source_target_pairs={{0,24},{4,100},{8,16},{12,108},{16,8},{20,116},{24,0},{28,124},{32... | collective-permute-start | bytes 196616 | tf_op jit(solution)/shard_map/ppermute | solution.py:58
  116.4 5.1 %collective-permute-start.27 = (bf16[32,2048]{1,0:T(8,128)(2,1)S(1)}, bf16[32,2048]{1,0:T(8,128)(2,1)S(1)}, u32[]{:S(2)}, u32[]{:S(2)}) collective-permute-start(bf16[32,2048]{1,0:T(8,128)(2,1)S(1)} %pad_maximum_fusion.10), channel_id=1, source_target_pairs={{0,24},{4,100},{8,16},{12,108},{16,8},{20,116},{24,0},{28,124},{32... | collective-permute-start | bytes 393224 | tf_op jit(solution)/shard_map/ppermute | solution.py:58
  117.7 4.7 %collective-permute-start.32 = (bf16[32,2048]{1,0:T(8,128)(2,1)S(1)}, bf16[32,2048]{1,0:T(8,128)(2,1)S(1)}, u32[]{:S(2)}, u32[]{:S(2)}) collective-permute-start(bf16[32,2048]{1,0:T(8,128)(2,1)S(1)} %pad_maximum_fusion.11), channel_id=1, source_target_pairs={{0,32},{4,12},{8,40},{12,4},{16,48},{20,28},{24,56},{28,20},{32,0}... | collective-permute-start | bytes 393224 | tf_op jit(solution)/shard_map/ppermute | solution.py:58
  121.5 5.3 %collective-permute-start.28 = (bf16[64,2048]{1,0:T(8,128)(2,1)S(1)}, bf16[64,2048]{1,0:T(8,128)(2,1)S(1)}, u32[]{:S(2)}, u32[]{:S(2)}) collective-permute-start(bf16[64,2048]{1,0:T(8,128)(2,1)S(1)} %pad_maximum_fusion.6), channel_id=1, source_target_pairs={{0,32},{4,12},{8,40},{12,4},{16,48},{20,28},{24,56},{28,20},{32,0}... | collective-permute-start | bytes 786440 | tf_op jit(solution)/shard_map/ppermute | solution.py:58
  122.5 7.9 %collective-permute-start.33 = (bf16[64,2048]{1,0:T(8,128)(2,1)S(1)}, bf16[64,2048]{1,0:T(8,128)(2,1)S(1)}, u32[]{:S(2)}, u32[]{:S(2)}) collective-permute-start(bf16[64,2048]{1,0:T(8,128)(2,1)S(1)} %pad_maximum_fusion.7), channel_id=1, source_target_pairs={{0,96},{4,28},{8,104},{12,20},{16,112},{20,12},{24,120},{28,4},{32... | collective-permute-start | bytes 786440 | tf_op jit(solution)/shard_map/ppermute | solution.py:58
  126.9 15.5 %collective-permute-start.29 = (bf16[128,2048]{1,0:T(8,128)(2,1)S(1)}, bf16[128,2048]{1,0:T(8,128)(2,1)S(1)}, u32[]{:S(2)}, u32[]{:S(2)}) collective-permute-start(bf16[128,2048]{1,0:T(8,128)(2,1)S(1)} %pad_maximum_fusion.2.refs_0_), channel_id=1, source_target_pairs={{0,96},{4,28},{8,104},{12,20},{16,112},{20,12},{24,120},{28,4},{32... | collective-permute-start | bytes 1572872 | tf_op jit(solution)/shard_map/ppermute | solution.py:58
  130.4 20.0 %collective-permute-start.34 = (bf16[128,2048]{1,0:T(8,128)(2,1)S(1)}, bf16[128,2048]{1,0:T(8,128)(2,1)S(1)}, u32[]{:S(2)}, u32[]{:S(2)}) collective-permute-start(bf16[128,2048]{1,0:T(8,128)(2,1)S(1)} %pad_maximum_fusion.3.refs_1_), channel_id=1, source_target_pairs={{0,8},{4,36},{8,0},{12,44},{16,24},{20,52},{24,16},{28,60},{32,40}... | collective-permute-start | bytes 1572872 | tf_op jit(solution)/shard_map/ppermute | solution.py:58
  130.8 20.3 %collective-permute-start.36 = (bf16[128,2048]{1,0:T(8,128)(2,1)S(1)}, bf16[128,2048]{1,0:T(8,128)(2,1)S(1)}, u32[]{:S(2)}, u32[]{:S(2)}) collective-permute-start(bf16[128,2048]{1,0:T(8,128)(2,1)S(1)} %pad_maximum_fusion.2.refs_0_), channel_id=1, source_target_pairs={{0,4},{4,0},{8,12},{12,8},{16,20},{20,16},{24,28},{28,24},{32,36},... | collective-permute-start | bytes 1572872 | tf_op jit(solution)/shard_map/ppermute | solution.py:62
  142.2 8.9 %collective-permute-start.37 = (bf16[128,2048]{1,0:T(8,128)(2,1)S(1)}, bf16[128,2048]{1,0:T(8,128)(2,1)S(1)}, u32[]{:S(2)}, u32[]{:S(2)}) collective-permute-start(bf16[128,2048]{1,0:T(8,128)(2,1)S(1)} %pad_maximum_fusion.3.refs_1_), channel_id=1, source_target_pairs={{0,4},{4,0},{8,12},{12,8},{16,20},{20,16},{24,28},{28,24},{32,36},... | collective-permute-start | bytes 1572872 | tf_op jit(solution)/shard_map/ppermute | solution.py:62
  142.4 16.4 %collective-permute-start.30 = (bf16[128,2048]{1,0:T(8,128)(2,1)S(1)}, bf16[128,2048]{1,0:T(8,128)(2,1)S(1)}, u32[]{:S(2)}, u32[]{:S(2)}) collective-permute-start(bf16[128,2048]{1,0:T(8,128)(2,1)S(1)} %collective-permute-done.29.refs_0_), channel_id=1, source_target_pairs={{0,4},{4,0},{8,12},{12,8},{16,20},{20,16},{24,28},{28,24},{32,36},... | collective-permute-start | bytes 1572872 | tf_op jit(solution)/shard_map/ppermute | solution.py:62
  150.4 8.3 %collective-permute-start.35 = (bf16[128,2048]{1,0:T(8,128)(2,1)S(1)}, bf16[128,2048]{1,0:T(8,128)(2,1)S(1)}, u32[]{:S(2)}, u32[]{:S(2)}) collective-permute-start(bf16[128,2048]{1,0:T(8,128)(2,1)S(1)} %collective-permute-done.34.refs_1_), channel_id=1, source_target_pairs={{0,4},{4,0},{8,12},{12,8},{16,20},{20,16},{24,28},{28,24},{32,36},... | collective-permute-start | bytes 1572872 | tf_op jit(solution)/shard_map/ppermute | solution.py:62
  (22 other events, 276.3 us)

commit v2 on v1

--- a/solution.py
+++ b/solution.py
@@ -23,52 +23,43 @@
 eps_norm = 1e-05
 far_below = -1e30
 
-HOPS = ((0, 1), (0, 3), (1, 0), (3, 0))
-ORDERS = tuple(
-    tuple(tuple(HOPS[(first + step) % 4] for step in range(4)) for first in firsts)
-    for firsts in ((0, 1), (2, 3))
-)
+DIRECT = (1, 3, 2)
+EDGES = ((1, 3), (3, 1))
 
 
 def device_at(y, x, core):
     return (y * SIDE + x) * CORES + core
 
 
-def hop_pairs(fragment, step):
+def flip_pairs(ring, flip):
     pairs = []
     for y in range(SIDE):
         for x in range(SIDE):
             for core in range(CORES):
-                flip_y, flip_x = ORDERS[core][fragment][step]
-                pairs.append((device_at(y, x, core), device_at(y ^ flip_y, x ^ flip_x, core)))
+                on_x = ring == core
+                target = device_at(y if on_x else y ^ flip, x ^ flip if on_x else x, core)
+                pairs.append((device_at(y, x, core), target))
     return pairs
 
 
 CORE_PAIRS = [(device, device ^ 1) for device in range(SIDE * SIDE * CORES)]
 
 
-def offsets_of(core, fragment):
-    found = [(0, 0)]
-    for flip_y, flip_x in ORDERS[core][fragment]:
-        found = found + [(y ^ flip_y, x ^ flip_x) for y, x in found]
-    return found
-
-
-def hop(part, fragment, step):
-    return lax.ppermute(part, "req", hop_pairs(fragment, step))
+def hop(part, ring, flip):
+    return lax.ppermute(part, "req", flip_pairs(ring, flip))
 
 
 def swap_core(part):
     return lax.ppermute(part, "req", CORE_PAIRS)
 
 
-def gather_rows(fragments):
-    held = list(fragments)
-    for step in range(3):
-        came = [hop(held[f], f, step) for f in range(2)]
-        held = [jnp.concatenate([held[f], came[f]], axis=0) for f in range(2)]
-    late = [hop(held[f], f, 3) for f in range(2)]
-    return (held, [swap_core(part) for part in held]), (late, [swap_core(part) for part in late])
+def gather_rows(rows):
+    came = [hop(rows, 0, flip) for flip in DIRECT]
+    held = [jnp.concatenate([rows, came[0]], axis=0), jnp.concatenate(came[1:], axis=0)]
+    came = [hop(held[s], 1, EDGES[s][0]) for s in range(2)]
+    held = [jnp.concatenate([held[s], came[s]], axis=0) for s in range(2)]
+    late = [hop(held[s], 1, EDGES[s][1]) for s in range(2)]
+    return held, late
 
 
 def added(left, right):
@@ -77,24 +68,26 @@
 
 def scatter_rows(early, late):
     came = [swap_core(part) for part in late[1]]
-    late = [hop(added(late[0][f], came[f]), f, 3) for f in range(2)]
+    late = [hop(added(late[0][s], came[s]), 1, EDGES[s][1]) for s in range(2)]
     came = [swap_core(part) for part in early[1]]
-    held = [added(early[0][f], came[f]) for f in range(2)]
-    held = [added(held[f], late[f]) for f in range(2)]
-    for step in reversed(range(3)):
-        half = held[0].shape[0] // 2
-        came = [hop(held[f][half:], f, step) for f in range(2)]
-        held = [added(held[f][:half], came[f]) for f in range(2)]
-    return held
+    held = [added(early[0][s], came[s]) for s in range(2)]
+    held = [added(held[s], late[s]) for s in range(2)]
+    half = held[0].shape[0] // 2
+    came = [hop(held[s][half:], 1, EDGES[s][0]) for s in range(2)]
+    held = [added(held[s][:half], came[s]) for s in range(2)]
+    half = half // 2
+    blocks = (held[0][half:], held[1][:half], held[1][half:])
+    came = [hop(block, 0, flip) for block, flip in zip(blocks, DIRECT, strict=True)]
+    return sum((part.astype(jnp.float32) for part in came), held[0][:half].astype(jnp.float32))
 
 
 def block_table():
-    table = np.zeros((CORES, 2, 2, 2, 8, 4), np.int32)
-    for core in range(CORES):
-        for half in range(2):
-            for fragment in range(2):
-                for place, (y, x) in enumerate(offsets_of(core ^ half, fragment)):
-                    table[core, place // 8, half, fragment, place % 8] = (y, x, half, fragment)
+    table = np.zeros((CORES, 2, 2, 2, 2, 2, 2, 4), np.int32)
+    for core, late, half, stream, second, block, request in np.ndindex(table.shape[:-1]):
+        first = ((0, 1), (3, 2))[stream][block]
+        other = (EDGES[stream][1] if late else 0) ^ (EDGES[stream][0] if second else 0)
+        y, x = (other, first) if core == half else (first, other)
+        table[core, late, half, stream, second, block, request] = (y, x, half, request)
     return table.reshape(CORES, 64, 4)
 
 
@@ -448,8 +441,7 @@
     base = lax.axis_index("req") * vocab
     lane = lax.broadcasted_iota(jnp.int32, (lanes, 128), 0)
     column = lax.broadcasted_iota(jnp.int32, (lanes, 128), 1)
-    fragment = (lane >= lanes // 2).astype(jnp.int32)
-    place = (column == fragment * DRAFT + lane % DRAFT).astype(jnp.bfloat16)
+    place = (column == lane % (2 * DRAFT)).astype(jnp.bfloat16)
     ids = lax.broadcasted_iota(jnp.int32, (vocab, lanes), 0) + base
     slot = lax.broadcasted_iota(jnp.int32, (slots, lanes), 0)
     packed = jnp.zeros(out_ref.shape, jnp.float32)
@@ -549,6 +541,16 @@
         flat_rows, mixer_gain, w_query, w_kv, w_attn_out, prompt_kv, prompt_lengths, member, accepted, w_z, w_x, w_bc,
         w_dt, conv_x, conv_bc, ssm_rate, dt_bias, skip_d, prompt_state, prompt_conv_x, prompt_conv_bc, w_mamba_out,
     )
+    came = lax.ppermute(far, ("req", "mdl"), mdl_pairs(0))
+    last = lax.ppermute(added(near[own_tokens:], came[own_tokens:]), ("req", "mdl"), mdl_pairs(1))
+    mixed = (
+        near[:own_tokens].astype(jnp.float32)
+        + came[:own_tokens].astype(jnp.float32)
+        + last.astype(jnp.float32)
+    )
+    own_rows = lax.dynamic_slice_in_dim(flat_rows, mdl_rank * own_tokens, own_tokens, 0)
+    after_mixer = (own_rows.astype(jnp.float32) + mixed).astype(jnp.bfloat16)
+    kept, token = lax.optimization_barrier((kept, after_mixer[:8, :128]))
     kept_out = lax.all_to_all(
         kept.reshape(mdl_count, own_reqs, local_inner + 16, STATE),
         "mdl",
@@ -556,19 +558,11 @@
         concat_axis=0,
         tiled=True,
     )
-
-    came = lax.ppermute(far, ("req", "mdl"), mdl_pairs(0))
-    last = lax.ppermute(added(near[own_tokens:], came[own_tokens:]), ("req", "mdl"), mdl_pairs(1))
-    mixed = (
-        near[:own_tokens].astype(jnp.float32)
-        + came[:own_tokens].astype(jnp.float32)
-        + last.astype(jnp.float32)
-    )
-    own_rows = lax.dynamic_slice_in_dim(flat_rows, mdl_rank * own_tokens, own_tokens, 0)
-    after_mixer = (own_rows.astype(jnp.float32) + mixed).astype(jnp.bfloat16)
     prepared = rms_scale(after_mixer, mlp_gain).astype(jnp.bfloat16)
     w_both = jnp.concatenate([w_gate, w_up], axis=1)
-    early, late = gather_rows([prepared[:draft_len], prepared[draft_len:]])
+    held, late = gather_rows(prepared)
+    early = (held, [swap_core(part) for part in held])
+    late = (late, [swap_core(part) for part in late])
 
     core = req_rank % CORES
     chip_x = req_rank // CORES % SIDE
@@ -582,14 +576,13 @@
     targets = targets.reshape(8, 8 * draft_len)
     owners = jnp.broadcast_to(owner[:, None], (64, draft_len)).reshape(8, 8 * draft_len)
 
-    token = jnp.zeros((8, 128), jnp.float32)
     early_parts = [feed(*rows, w_both, w_down, token) for rows in early]
     later_token, kept_out = lax.optimization_barrier((token, kept_out))
     late_parts = [
         feed(*late[0], w_both, w_down, token),
         feed(*late[1], w_both, w_down, later_token),
     ]
-    summed = jnp.concatenate(scatter_rows(early_parts, late_parts), axis=0)
+    summed = scatter_rows(early_parts, late_parts)
     kept_state = (
         kept_out[:, :, :local_inner, :]
         .transpose(1, 0, 2, 3)
@@ -610,14 +603,15 @@
     final_gain, kept_state, kept_conv, targets, owners = lax.optimization_barrier(
         (final_gain, kept_state, kept_conv, targets, owners)
     )
-    after_feed = added(after_mixer, summed)
+    after_feed = (after_mixer.astype(jnp.float32) + summed).astype(jnp.bfloat16)
     final_rows = rms_scale(after_feed, final_gain).astype(jnp.bfloat16)
-    early, late = gather_rows([final_rows[:draft_len], final_rows[draft_len:]])
-    stats = [
-        head_stats(targets[:4], owners[:4], early[0] + early[1], head_weight, req_count),
-        head_stats(targets[4:6], owners[4:6], late[0], head_weight, req_count),
-    ]
-    stats = head_stats(targets[6:], owners[6:], late[1], head_weight, req_count, stats)
+    held, late = gather_rows(final_rows)
+    early = held + [swap_core(part) for part in held]
+    first_stats = head_stats(targets[:4], owners[:4], early, head_weight, req_count)
+    late, first_stats = lax.optimization_barrier((late, first_stats))
+    sibling = [swap_core(part) for part in late]
+    stats = [first_stats, head_stats(targets[4:6], owners[4:6], late, head_weight, req_count)]
+    stats = head_stats(targets[6:], owners[6:], sibling, head_weight, req_count, stats)
     shared = lax.all_to_all(stats, "req", split_axis=0, concat_axis=0, tiled=True)
     shared = shared.reshape(req_count, 8, 128)[:, :, :own_tokens]
     tops, totals, hits = shared[:, 0], shared[:, 1], shared[:, 2]

time: 174 us -> 149 us (0.86)
  waiting for transfers between devices: 52.6 us -> 32.3 us
  starting transfers between devices: 67.5 us -> 55.4 us
  other arithmetic: 6.52 us -> 11.3 us
    ppermute x1, waiting for transfers between devices: 21.6 us -> 1.37 us  [shards(): came = lax.ppermute(far, ('req', 'mdl'), mdl_pairs(0))]
    ppermute x24 -> x21, starting transfers between devices: 29 us -> 21.4 us  [hop(): return lax.ppermute(part, 'req', flip_pairs(ring, flip))]
    ppermute x12, starting transfers between devices: 29.5 us -> 23.1 us  [swap_core(): return lax.ppermute(part, 'req', CORE_PAIRS)]
    convert_element_type x11 -> x7, other arithmetic: 1.01 us -> 4.25 us  [added(): (left.astype(jnp.float32) + right.astype(jnp.float32)).astype(jnp.bfloat16)]
    ppermute x1, starting transfers between devices: 1.47 us -> 3.95 us  [shards(): lax.ppermute(added(near[own_tokens:], came[own_tokens:]), ('req', 'mdl'),...]
    reshape x1, local copies, waits for them, and re-layouts: 2.01 us -> 3.76 us  [shards(): kept_state = kept_out[:, :, :local_inner, :].transpose(1, 0, 2, 3).astype...]
    ppermute x24 -> x21, waiting for transfers between devices: 28.5 us -> 28.3 us  [hop(): return lax.ppermute(part, 'req', flip_pairs(ring, flip))]
  transfers between devices with their start and end apart: 39 -> 36, of which waited for: 19 -> 15; matrix products, arithmetic and copies ran while one was open for 6% -> 11% of each run, Pallas kernels for 9% -> 11%
where the time goes in v2:
time: 149 us
  starting transfers between devices  55.4 us (37%)
  waiting for transfers between devices  32.3 us (22%)
  Pallas kernels  28.3 us (19%)
  blocking collectives  12.6 us (8%)
  other arithmetic  11.3 us (8%)
  local copies, waits for them, and re-layouts  7.64 us (5%)
    ppermute x21, waiting for transfers between devices, hop(): return lax.ppermute(part, 'req', flip_pairs(ring, flip))  28.3 us
    ppermute x12, starting transfers between devices, swap_core(): return lax.ppermute(part, 'req', CORE_PAIRS)  23.1 us
    ppermute x21, starting transfers between devices, hop(): return lax.ppermute(part, 'req', flip_pairs(ring, flip))  21.4 us
    all_to_all x1, blocking collectives, shards(): lax.all_to_all(stats, 'req', split_axis=0, concat_axis=0, tiled=True)  12.6 us
    pallas_call x1, Pallas kernels, mixer(): pl.pallas_call(mixer_kernel, out_shape=[jax.ShapeDtypeStruct((tokens // 2...  10.3 us
    pallas_call x3, Pallas kernels, head_stats(): pl.pallas_call(head_kernel, out_shape=jax.ShapeDtypeStruct((devices * 8,...  9.59 us
    pallas_call x4, Pallas kernels, feed(): pl.pallas_call(feed_kernel, out_shape=[jax.ShapeDtypeStruct((rows, width)...  8.34 us
    all_to_all x1, starting transfers between devices, shards(): lax.all_to_all(kept.reshape(mdl_count, own_reqs, local_inner + 16, STATE)...  4.37 us
  transfers between devices with their start and end apart: 36, of which 15 were waited for; matrix products, arithmetic and copies ran while one was open for 11% of the time, Pallas kernels for 11%

profile of v2, /device:TPU:1, one launch (start us, length us, event | category | flops | bytes accessed | tf_op | source)
XLA Modules:
  0.0 148.9 jit_solution(9307458804576282778)
XLA Ops:
  0.7 10.3 %mixer.1 = (bf16[64,2048]{1,0:T(8,128)(2,1)}, bf16[64,2048]{1,0:T(8,128)(2,1)}, bf16[8,400,256]{2,1,0:T(8,128)(2,1)}, bf16[16,512]{1,0:T(8,128)(2,1)}) custom-call(s32[8]{0:T(128)} %refs_0_.1, s32[8]{0:T(128)} %refs_1_.1, s32[2]{0:T(128)} %refs_2_.3, f32[6]{0:T(128)} %refs_3_.1, f32[6]{0:T(128)} %refs_4_.2, f32[6]{0:T(128)} %refs_5_.1, ...), custom_call_target="tpu_custom_call" | custom-call | flops 3000000000 | bytes 20000000 | tf_op jit(solution)/shard_map/mixer/pallas_call | solution.py:370
  11.1 2.5 %collective-permute-start = (bf16[64,2048]{1,0:T(8,128)(2,1)}, bf16[64,2048]{1,0:T(8,128)(2,1)S(1)}, u32[]{:S(2)}, u32[]{:S(2)}) collective-permute-start(bf16[64,2048]{1,0:T(8,128)(2,1)} %get-tuple-element.29), channel_id=1, source_target_pairs={{0,3},{1,2},{2,1},{3,0},{4,5},{5,4},{6,7},{7,6},{8,11},{9,10},{10,... | collective-permute-start | bytes 786440 | tf_op jit(solution)/shard_map/ppermute | solution.py:544
  18.5 3.9 %collective-permute-start.1 = (bf16[32,2048]{1,0:T(8,128)(2,1)S(1)}, bf16[32,2048]{1,0:T(8,128)(2,1)S(1)}, u32[]{:S(2)}, u32[]{:S(2)}) collective-permute-start(bf16[32,2048]{1,0:T(8,128)(2,1)S(1)} %add_convert_fusion.9), channel_id=1, source_target_pairs={{0,1},{1,0},{2,3},{3,2},{4,7},{5,6},{6,5},{7,4},{8,9},{9,8},{10,11... | collective-permute-start | bytes 393224 | tf_op jit(solution)/shard_map/ppermute | solution.py:545
  22.6 2.3 %collective-permute-done.1 = bf16[32,2048]{1,0:T(8,128)(2,1)S(1)} collective-permute-done((bf16[32,2048]{1,0:T(8,128)(2,1)S(1)}, bf16[32,2048]{1,0:T(8,128)(2,1)S(1)}, u32[]{:S(2)}, u32[]{:S(2)}) %collective-permute-start.1) | collective-permute-done | bytes 131104 | tf_op jit(solution)/shard_map/ppermute | solution.py:545
  26.1 3.0 %collective-permute-start.5 = (bf16[32,2048]{1,0:T(8,128)(2,1)S(1)}, bf16[32,2048]{1,0:T(8,128)(2,1)S(1)}, u32[]{:S(2)}, u32[]{:S(2)}) collective-permute-start(bf16[32,2048]{1,0:T(8,128)(2,1)S(1)} %fusion.5), channel_id=1, source_target_pairs={{0,16},{4,68},{8,24},{12,76},{16,0},{20,84},{24,8},{28,92},{32,48}... | collective-permute-start | bytes 393224 | tf_op jit(solution)/shard_map/ppermute | solution.py:49
  30.1 4.4 %all-to-all-start = ((bf16[4,2,400,256]{3,2,1,0:T(8,128)(2,1)}), bf16[4,2,400,256]{3,2,1,0:T(8,128)(2,1)}, u32[]{:S(2)}, u32[]{:S(2)}) async-start(bf16[4,2,400,256]{3,2,1,0:T(8,128)(2,1)} %bitcast.6), calls=%async_computation | async-start | bytes 3276800 | tf_op jit(solution)/shard_map/all_to_all | solution.py:554
  34.6 2.6 %collective-permute-start.6 = (bf16[64,2048]{1,0:T(8,128)(2,1)S(1)}, bf16[64,2048]{1,0:T(8,128)(2,1)S(1)}, u32[]{:S(2)}, u32[]{:S(2)}) collective-permute-start(bf16[64,2048]{1,0:T(8,128)(2,1)S(1)} %pad_maximum_fusion.3), channel_id=1, source_target_pairs={{0,96},{4,28},{8,104},{12,20},{16,112},{20,12},{24,120},{28,4},{32... | collective-permute-start | bytes 786440 | tf_op jit(solution)/shard_map/ppermute | solution.py:49
  37.3 3.8 %collective-permute-done.6 = bf16[64,2048]{1,0:T(8,128)(2,1)S(1)} collective-permute-done((bf16[64,2048]{1,0:T(8,128)(2,1)S(1)}, bf16[64,2048]{1,0:T(8,128)(2,1)S(1)}, u32[]{:S(2)}, u32[]{:S(2)}) %collective-permute-start.6) | collective-permute-done | bytes 262176 | tf_op jit(solution)/shard_map/ppermute | solution.py:49
  41.2 4.8 %collective-permute-start.8 = (bf16[128,2048]{1,0:T(8,128)(2,1)S(1)}, bf16[128,2048]{1,0:T(8,128)(2,1)S(1)}, u32[]{:S(2)}, u32[]{:S(2)}) collective-permute-start(bf16[128,2048]{1,0:T(8,128)(2,1)S(1)} %constant_dynamic-update-slice_fusion.second_ref), channel_id=1, source_target_pairs={{0,4},{4,0},{8,12},{12,8},{16,20},{20,16},{24,28},{28,24},{32,36},... | collective-permute-start | bytes 1572872 | tf_op jit(solution)/shard_map/ppermute | solution.py:53
  50.2 4.7 %collective-permute-start.13 = (bf16[128,2048]{1,0:T(8,128)(2,1)}, bf16[128,2048]{1,0:T(8,128)(2,1)}, u32[]{:S(2)}, u32[]{:S(2)}) collective-permute-start(bf16[128,2048]{1,0:T(8,128)(2,1)} %collective-permute-done.11.second_ref), channel_id=1, source_target_pairs={{0,4},{4,0},{8,12},{12,8},{16,20},{20,16},{24,28},{28,24},{32,36},... | collective-permute-start | bytes 1572872 | tf_op jit(solution)/shard_map/ppermute | solution.py:53
  55.7 2.3 %collective-permute-start.12 = (bf16[128,2048]{1,0:T(8,128)(2,1)}, bf16[128,2048]{1,0:T(8,128)(2,1)}, u32[]{:S(2)}, u32[]{:S(2)}) collective-permute-start(bf16[128,2048]{1,0:T(8,128)(2,1)} %collective-permute-done.10.first_ref), channel_id=1, source_target_pairs={{0,4},{4,0},{8,12},{12,8},{16,20},{20,16},{24,28},{28,24},{32,36},... | collective-permute-start | bytes 1572872 | tf_op jit(solution)/shard_map/ppermute | solution.py:53
  58.0 2.1 %feed.5 = (bf16[128,2048]{1,0:T(8,128)(2,1)}, bf16[128,2048]{1,0:T(8,128)(2,1)S(1)}) custom-call(bf16[128,2048]{1,0:T(8,128)(2,1)S(1)} %collective-permute-done.7.first_ref, bf16[128,2048]{1,0:T(8,128)(2,1)S(1)} %collective-permute-done.8.second_ref, bf16[2048,256]{1,0:T(8,128)(2,1)S(1)} %constant_dynamic-update-slice_fusion.3.both_ref, ...), custom_call_target="tpu_custom_call" | custom-call | flops 8053063680 | bytes 3670016 | tf_op jit(solution)/shard_map/feed/pallas_call | solution.py:420
  60.6 2.5 %feed.7 = (bf16[128,2048]{1,0:T(8,128)(2,1)S(1)}, bf16[128,2048]{1,0:T(8,128)(2,1)S(1)}) custom-call(bf16[128,2048]{1,0:T(8,128)(2,1)} %collective-permute-done.12.first_ref, bf16[128,2048]{1,0:T(8,128)(2,1)} %collective-permute-done.13.second_ref, bf16[2048,256]{1,0:T(8,128)(2,1)S(1)} %constant_dynamic-update-slice_fusion.3.both_ref, ...), custom_call_target="tpu_custom_call" | custom-call | flops 8053063680 | bytes 3670016 | tf_op jit(solution)/shard_map/feed/pallas_call | solution.py:420
  63.2 2.5 %feed.6 = (bf16[128,2048]{1,0:T(8,128)(2,1)S(1)}, bf16[128,2048]{1,0:T(8,128)(2,1)S(1)}) custom-call(bf16[128,2048]{1,0:T(8,128)(2,1)} %collective-permute-done.10.first_ref, bf16[128,2048]{1,0:T(8,128)(2,1)} %collective-permute-done.11.second_ref, bf16[2048,256]{1,0:T(8,128)(2,1)S(1)} %constant_dynamic-update-slice_fusion.3.both_ref, ...), custom_call_target="tpu_custom_call" | custom-call | flops 8053063680 | bytes 3670016 | tf_op jit(solution)/shard_map/feed/pallas_call | solution.py:420
  66.3 3.3 %convert_bitcast_fusion = f32[2,4,384,256]{3,2,0,1:T(8,128)} fusion(bf16[4,2,400,256]{3,2,1,0:T(8,128)(2,1)} %all-to-all-done), kind=kLoop, calls=%fused_computation | loop fusion | flops 786432 | bytes 4718592 | tf_op jit(solution)/shard_map/reshape | solution.py:590
  74.3 3.8 %copy.40 = f32[2,4,384,256]{3,2,1,0:T(8,128)} copy(f32[2,4,384,256]{3,2,0,1:T(8,128)} %convert_bitcast_fusion) | data formatting | bytes 6291456 | tf_op jit(solution)/shard_map/reshape | solution.py:590
  78.1 2.9 %collective-permute-done.15 = bf16[128,2048]{1,0:T(8,128)(2,1)} collective-permute-done((bf16[128,2048]{1,0:T(8,128)(2,1)S(1)}, bf16[128,2048]{1,0:T(8,128)(2,1)}, u32[]{:S(2)}, u32[]{:S(2)}) %collective-permute-start.15) | collective-permute-done | bytes 524320 | tf_op jit(solution)/shard_map/ppermute | solution.py:49
  84.3 1.9 %collective-permute-start.21 = (bf16[64,2048]{1,0:T(8,128)(2,1)S(1)}, bf16[64,2048]{1,0:T(8,128)(2,1)S(1)}, u32[]{:S(2)}, u32[]{:S(2)}) collective-permute-start(bf16[64,2048]{1,0:T(8,128)(2,1)S(1)} %slice.143), channel_id=1, source_target_pairs={{0,96},{4,28},{8,104},{12,20},{16,112},{20,12},{24,120},{28,4},{32... | collective-permute-start | bytes 786440 | tf_op jit(solution)/shard_map/ppermute | solution.py:49
  86.2 1.9 %collective-permute-done.16 = bf16[64,2048]{1,0:T(8,128)(2,1)S(1)} collective-permute-done((bf16[64,2048]{1,0:T(8,128)(2,1)S(1)}, bf16[64,2048]{1,0:T(8,128)(2,1)S(1)}, u32[]{:S(2)}, u32[]{:S(2)}) %collective-permute-start.16) | collective-permute-done | bytes 262176 | tf_op jit(solution)/shard_map/ppermute | solution.py:49
  88.2 2.8 %collective-permute-done.21 = bf16[64,2048]{1,0:T(8,128)(2,1)S(1)} collective-permute-done((bf16[64,2048]{1,0:T(8,128)(2,1)S(1)}, bf16[64,2048]{1,0:T(8,128)(2,1)S(1)}, u32[]{:S(2)}, u32[]{:S(2)}) %collective-permute-start.21) | collective-permute-done | bytes 262176 | tf_op jit(solution)/shard_map/ppermute | solution.py:49
  93.0 3.3 %collective-permute-done.22 = bf16[32,2048]{1,0:T(8,128)(2,1)S(1)} collective-permute-done((bf16[32,2048]{1,0:T(8,128)(2,1)S(1)}, bf16[32,2048]{1,0:T(8,128)(2,1)S(1)}, u32[]{:S(2)}, u32[]{:S(2)}) %collective-permute-start.22) | collective-permute-done | bytes 131104 | tf_op jit(solution)/shard_map/ppermute | solution.py:49
  98.1 1.8 %collective-permute-start.27 = (bf16[32,2048]{1,0:T(8,128)(2,1)S(1)}, bf16[32,2048]{1,0:T(8,128)(2,1)S(1)}, u32[]{:S(2)}, u32[]{:S(2)}) collective-permute-start(bf16[32,2048]{1,0:T(8,128)(2,1)S(1)} %fusion.2), channel_id=1, source_target_pairs={{0,24},{4,100},{8,16},{12,108},{16,8},{20,116},{24,0},{28,124},{32... | collective-permute-start | bytes 393224 | tf_op jit(solution)/shard_map/ppermute | solution.py:49
  100.8 2.8 %collective-permute-done.28 = bf16[32,2048]{1,0:T(8,128)(2,1)S(1)} collective-permute-done((bf16[32,2048]{1,0:T(8,128)(2,1)S(1)}, bf16[32,2048]{1,0:T(8,128)(2,1)S(1)}, u32[]{:S(2)}, u32[]{:S(2)}) %collective-permute-start.28) | collective-permute-done | bytes 131104 | tf_op jit(solution)/shard_map/ppermute | solution.py:49
  104.7 1.9 %collective-permute-start.29 = (bf16[64,2048]{1,0:T(8,128)(2,1)S(1)}, bf16[64,2048]{1,0:T(8,128)(2,1)S(1)}, u32[]{:S(2)}, u32[]{:S(2)}) collective-permute-start(bf16[64,2048]{1,0:T(8,128)(2,1)S(1)} %pad_maximum_fusion.5), channel_id=1, source_target_pairs={{0,96},{4,28},{8,104},{12,20},{16,112},{20,12},{24,120},{28,4},{32... | collective-permute-start | bytes 786440 | tf_op jit(solution)/shard_map/ppermute | solution.py:49
  106.7 5.1 %collective-permute-done.29 = bf16[64,2048]{1,0:T(8,128)(2,1)S(1)} collective-permute-done((bf16[64,2048]{1,0:T(8,128)(2,1)S(1)}, bf16[64,2048]{1,0:T(8,128)(2,1)S(1)}, u32[]{:S(2)}, u32[]{:S(2)}) %collective-permute-start.29) | collective-permute-done | bytes 262176 | tf_op jit(solution)/shard_map/ppermute | solution.py:49
  111.8 6.3 %collective-permute-start.32 = (bf16[128,2048]{1,0:T(8,128)(2,1)S(1)}, bf16[128,2048]{1,0:T(8,128)(2,1)S(1)}, u32[]{:S(2)}, u32[]{:S(2)}) collective-permute-start(bf16[128,2048]{1,0:T(8,128)(2,1)S(1)} %constant_dynamic-update-slice_fusion.5.refs_1_), channel_id=1, source_target_pairs={{0,4},{4,0},{8,12},{12,8},{16,20},{20,16},{24,28},{28,24},{32,36},... | collective-permute-start | bytes 1572872 | tf_op jit(solution)/shard_map/ppermute | solution.py:53
  120.8 5.6 %head_stats.3.refs_3_ = f32[256,128]{1,0:T(8,128)S(1)} custom-call(s32[4,128]{1,0:T(4,128)S(1)} %slice.128.targets_ref, s32[4,128]{1,0:T(4,128)S(1)} %slice.129.owners_ref, bf16[128,2048]{1,0:T(8,128)(2,1)S(1)} %pad_maximum_fusion.1.refs_0_, bf16[128,2048]{1,0:T(8,128)(2,1)S(1)} %constant_dynamic-update-slice_fusion.5.refs_1_, ...), custom_call_target="tpu_custom_call" | custom-call | flops 21474836480 | bytes 6291456 | tf_op jit(solution)/shard_map/head_stats/pallas_call | solution.py:475
  126.9 1.9 %collective-permute-done.26.refs_0_ = bf16[128,2048]{1,0:T(8,128)(2,1)S(1)} collective-permute-done((bf16[128,2048]{1,0:T(8,128)(2,1)S(1)}, bf16[128,2048]{1,0:T(8,128)(2,1)S(1)}, u32[]{:S(2)}, u32[]{:S(2)}) %collective-permute-start.26) | collective-permute-done | bytes 524320 | tf_op jit(solution)/shard_map/ppermute | solution.py:49
  128.8 2.3 %collective-permute-start.33 = (bf16[128,2048]{1,0:T(8,128)(2,1)S(1)}, bf16[128,2048]{1,0:T(8,128)(2,1)S(1)}, u32[]{:S(2)}, u32[]{:S(2)}) collective-permute-start(bf16[128,2048]{1,0:T(8,128)(2,1)S(1)} %collective-permute-done.26.refs_0_), channel_id=1, source_target_pairs={{0,4},{4,0},{8,12},{12,8},{16,20},{20,16},{24,28},{28,24},{32,36},... | collective-permute-start | bytes 1572872 | tf_op jit(solution)/shard_map/ppermute | solution.py:53
  131.0 2.0 %head_stats.4.refs_4_ = f32[256,128]{1,0:T(8,128)S(1)} custom-call(s32[2,128]{1,0:T(2,128)S(1)} %get-tuple-element.68.targets_ref, s32[2,128]{1,0:T(2,128)S(1)} %get-tuple-element.63.owners_ref, bf16[128,2048]{1,0:T(8,128)(2,1)S(1)} %collective-permute-done.26.refs_0_, bf16[128,2048]{1,0:T(8,128)(2,1)S(1)} %collective-permute-done.30.refs_1_, ...), custom_call_target="tpu_custom_call" | custom-call | flops 10737418240 | bytes 5242880 | tf_op jit(solution)/shard_map/head_stats/pallas_call | solution.py:475
  133.3 2.0 %head_stats.5 = f32[256,128]{1,0:T(8,128)S(1)} custom-call(s32[2,128]{1,0:T(2,128)S(1)} %get-tuple-element.67.targets_ref, s32[2,128]{1,0:T(2,128)S(1)} %get-tuple-element.64.owners_ref, bf16[128,2048]{1,0:T(8,128)(2,1)S(1)} %collective-permute-done.33.refs_0_, bf16[128,2048]{1,0:T(8,128)(2,1)S(1)} %collective-permute-done.34.refs_1_, ...), custom_call_target="tpu_custom_call" | custom-call | flops 10737418240 | bytes 5242880 | tf_op jit(solution)/shard_map/head_stats/pallas_call | solution.py:475
  135.3 12.6 %all_to_all.14 = f32[32,8,128]{2,1,0:T(8,128)S(1)} all-to-all(f32[32,8,128]{2,1,0:T(8,128)S(1)} %bitcast.24), channel_id=1, replica_groups=mesh['req'=32,'mdl'=4] {'req'}, dimensions={0} | all-to-all | bytes 262144 | tf_op jit(solution)/shard_map/all_to_all | solution.py:615
  (137 shorter events, 31.9 us)
Async XLA Ops:
  11.1 6.5 %collective-permute-start = (bf16[64,2048]{1,0:T(8,128)(2,1)}, bf16[64,2048]{1,0:T(8,128)(2,1)S(1)}, u32[]{:S(2)}, u32[]{:S(2)}) collective-permute-start(bf16[64,2048]{1,0:T(8,128)(2,1)} %get-tuple-element.29), channel_id=1, source_target_pairs={{0,3},{1,2},{2,1},{3,0},{4,5},{5,4},{6,7},{7,6},{8,11},{9,10},{10,... | collective-permute-start | bytes 786440 | tf_op jit(solution)/shard_map/ppermute | solution.py:544
  18.5 6.3 %collective-permute-start.1 = (bf16[32,2048]{1,0:T(8,128)(2,1)S(1)}, bf16[32,2048]{1,0:T(8,128)(2,1)S(1)}, u32[]{:S(2)}, u32[]{:S(2)}) collective-permute-start(bf16[32,2048]{1,0:T(8,128)(2,1)S(1)} %add_convert_fusion.9), channel_id=1, source_target_pairs={{0,1},{1,0},{2,3},{3,2},{4,7},{5,6},{6,5},{7,4},{8,9},{9,8},{10,11... | collective-permute-start | bytes 393224 | tf_op jit(solution)/shard_map/ppermute | solution.py:545
  26.1 8.4 %collective-permute-start.5 = (bf16[32,2048]{1,0:T(8,128)(2,1)S(1)}, bf16[32,2048]{1,0:T(8,128)(2,1)S(1)}, u32[]{:S(2)}, u32[]{:S(2)}) collective-permute-start(bf16[32,2048]{1,0:T(8,128)(2,1)S(1)} %fusion.5), channel_id=1, source_target_pairs={{0,16},{4,68},{8,24},{12,76},{16,0},{20,84},{24,8},{28,92},{32,48}... | collective-permute-start | bytes 393224 | tf_op jit(solution)/shard_map/ppermute | solution.py:49
  29.1 5.4 %collective-permute-start.4 = (bf16[32,2048]{1,0:T(8,128)(2,1)S(1)}, bf16[32,2048]{1,0:T(8,128)(2,1)S(1)}, u32[]{:S(2)}, u32[]{:S(2)}) collective-permute-start(bf16[32,2048]{1,0:T(8,128)(2,1)S(1)} %fusion.5), channel_id=1, source_target_pairs={{0,24},{4,100},{8,16},{12,108},{16,8},{20,116},{24,0},{28,124},{32... | collective-permute-start | bytes 393224 | tf_op jit(solution)/shard_map/ppermute | solution.py:49
  30.0 7.1 %collective-permute-start.2 = (bf16[32,2048]{1,0:T(8,128)(2,1)S(1)}, bf16[32,2048]{1,0:T(8,128)(2,1)S(1)}, u32[]{:S(2)}, u32[]{:S(2)}) collective-permute-start(bf16[32,2048]{1,0:T(8,128)(2,1)S(1)} %fusion.5), channel_id=1, source_target_pairs={{0,8},{4,36},{8,0},{12,44},{16,24},{20,52},{24,16},{28,60},{32,40}... | collective-permute-start | bytes 393224 | tf_op jit(solution)/shard_map/ppermute | solution.py:49
  30.1 30.5 %all-to-all-start = ((bf16[4,2,400,256]{3,2,1,0:T(8,128)(2,1)}), bf16[4,2,400,256]{3,2,1,0:T(8,128)(2,1)}, u32[]{:S(2)}, u32[]{:S(2)}) async-start(bf16[4,2,400,256]{3,2,1,0:T(8,128)(2,1)} %bitcast.6), calls=%async_computation | async-start | bytes 3276800 | tf_op jit(solution)/shard_map/all_to_all | solution.py:554
  34.6 6.5 %collective-permute-start.6 = (bf16[64,2048]{1,0:T(8,128)(2,1)S(1)}, bf16[64,2048]{1,0:T(8,128)(2,1)S(1)}, u32[]{:S(2)}, u32[]{:S(2)}) collective-permute-start(bf16[64,2048]{1,0:T(8,128)(2,1)S(1)} %pad_maximum_fusion.3), channel_id=1, source_target_pairs={{0,96},{4,28},{8,104},{12,20},{16,112},{20,12},{24,120},{28,4},{32... | collective-permute-start | bytes 786440 | tf_op jit(solution)/shard_map/ppermute | solution.py:49
  37.1 8.8 %collective-permute-start.3 = (bf16[64,2048]{1,0:T(8,128)(2,1)S(1)}, bf16[64,2048]{1,0:T(8,128)(2,1)S(1)}, u32[]{:S(2)}, u32[]{:S(2)}) collective-permute-start(bf16[64,2048]{1,0:T(8,128)(2,1)S(1)} %pad_maximum_fusion.2), channel_id=1, source_target_pairs={{0,32},{4,12},{8,40},{12,4},{16,48},{20,28},{24,56},{28,20},{32,0}... | collective-permute-start | bytes 786440 | tf_op jit(solution)/shard_map/ppermute | solution.py:49
  41.1 9.1 %collective-permute-start.11 = (bf16[128,2048]{1,0:T(8,128)(2,1)S(1)}, bf16[128,2048]{1,0:T(8,128)(2,1)}, u32[]{:S(2)}, u32[]{:S(2)}) collective-permute-start(bf16[128,2048]{1,0:T(8,128)(2,1)S(1)} %constant_dynamic-update-slice_fusion.second_ref), channel_id=1, source_target_pairs={{0,32},{4,12},{8,40},{12,4},{16,48},{20,28},{24,56},{28,20},{32,0}... | collective-permute-start | bytes 1572872 | tf_op jit(solution)/shard_map/ppermute | solution.py:49
  41.2 16.8 %collective-permute-start.8 = (bf16[128,2048]{1,0:T(8,128)(2,1)S(1)}, bf16[128,2048]{1,0:T(8,128)(2,1)S(1)}, u32[]{:S(2)}, u32[]{:S(2)}) collective-permute-start(bf16[128,2048]{1,0:T(8,128)(2,1)S(1)} %constant_dynamic-update-slice_fusion.second_ref), channel_id=1, source_target_pairs={{0,4},{4,0},{8,12},{12,8},{16,20},{20,16},{24,28},{28,24},{32,36},... | collective-permute-start | bytes 1572872 | tf_op jit(solution)/shard_map/ppermute | solution.py:53
  46.0 9.7 %collective-permute-start.10 = (bf16[128,2048]{1,0:T(8,128)(2,1)S(1)}, bf16[128,2048]{1,0:T(8,128)(2,1)}, u32[]{:S(2)}, u32[]{:S(2)}) collective-permute-start(bf16[128,2048]{1,0:T(8,128)(2,1)S(1)} %pad_maximum_fusion.first_ref), channel_id=1, source_target_pairs={{0,96},{4,28},{8,104},{12,20},{16,112},{20,12},{24,120},{28,4},{32... | collective-permute-start | bytes 1572872 | tf_op jit(solution)/shard_map/ppermute | solution.py:49
  47.6 10.4 %collective-permute-start.7 = (bf16[128,2048]{1,0:T(8,128)(2,1)S(1)}, bf16[128,2048]{1,0:T(8,128)(2,1)S(1)}, u32[]{:S(2)}, u32[]{:S(2)}) collective-permute-start(bf16[128,2048]{1,0:T(8,128)(2,1)S(1)} %pad_maximum_fusion.first_ref), channel_id=1, source_target_pairs={{0,4},{4,0},{8,12},{12,8},{16,20},{20,16},{24,28},{28,24},{32,36},... | collective-permute-start | bytes 1572872 | tf_op jit(solution)/shard_map/ppermute | solution.py:53
  50.2 10.5 %collective-permute-start.13 = (bf16[128,2048]{1,0:T(8,128)(2,1)}, bf16[128,2048]{1,0:T(8,128)(2,1)}, u32[]{:S(2)}, u32[]{:S(2)}) collective-permute-start(bf16[128,2048]{1,0:T(8,128)(2,1)} %collective-permute-done.11.second_ref), channel_id=1, source_target_pairs={{0,4},{4,0},{8,12},{12,8},{16,20},{20,16},{24,28},{28,24},{32,36},... | collective-permute-start | bytes 1572872 | tf_op jit(solution)/shard_map/ppermute | solution.py:53
  55.7 4.9 %collective-permute-start.12 = (bf16[128,2048]{1,0:T(8,128)(2,1)}, bf16[128,2048]{1,0:T(8,128)(2,1)}, u32[]{:S(2)}, u32[]{:S(2)}) collective-permute-start(bf16[128,2048]{1,0:T(8,128)(2,1)} %collective-permute-done.10.first_ref), channel_id=1, source_target_pairs={{0,4},{4,0},{8,12},{12,8},{16,20},{20,16},{24,28},{28,24},{32,36},... | collective-permute-start | bytes 1572872 | tf_op jit(solution)/shard_map/ppermute | solution.py:53
  60.1 18.0 %collective-permute-start.9 = (bf16[128,2048]{1,0:T(8,128)(2,1)}, bf16[128,2048]{1,0:T(8,128)(2,1)}, u32[]{:S(2)}, u32[]{:S(2)}) collective-permute-start(bf16[128,2048]{1,0:T(8,128)(2,1)} %get-tuple-element.33), channel_id=1, source_target_pairs={{0,4},{4,0},{8,12},{12,8},{16,20},{20,16},{24,28},{28,24},{32,36},... | collective-permute-start | bytes 1572872 | tf_op jit(solution)/shard_map/ppermute | solution.py:53
  60.1 22.7 %collective-permute-start.18 = (bf16[128,2048]{1,0:T(8,128)(2,1)S(1)}, bf16[128,2048]{1,0:T(8,128)(2,1)}, u32[]{:S(2)}, u32[]{:S(2)}) collective-permute-start(bf16[128,2048]{1,0:T(8,128)(2,1)S(1)} %get-tuple-element.39), channel_id=1, source_target_pairs={{0,4},{4,0},{8,12},{12,8},{16,20},{20,16},{24,28},{28,24},{32,36},... | collective-permute-start | bytes 1572872 | tf_op jit(solution)/shard_map/ppermute | solution.py:53
  63.1 8.0 %collective-permute-start.14 = (bf16[128,2048]{1,0:T(8,128)(2,1)S(1)}, bf16[128,2048]{1,0:T(8,128)(2,1)S(1)}, u32[]{:S(2)}, u32[]{:S(2)}) collective-permute-start(bf16[128,2048]{1,0:T(8,128)(2,1)S(1)} %get-tuple-element.37), channel_id=1, source_target_pairs={{0,4},{4,0},{8,12},{12,8},{16,20},{20,16},{24,28},{28,24},{32,36},... | collective-permute-start | bytes 1572872 | tf_op jit(solution)/shard_map/ppermute | solution.py:53
  65.7 7.2 %collective-permute-start.19 = (bf16[128,2048]{1,0:T(8,128)(2,1)S(1)}, bf16[128,2048]{1,0:T(8,128)(2,1)S(1)}, u32[]{:S(2)}, u32[]{:S(2)}) collective-permute-start(bf16[128,2048]{1,0:T(8,128)(2,1)S(1)} %get-tuple-element.41), channel_id=1, source_target_pairs={{0,4},{4,0},{8,12},{12,8},{16,20},{20,16},{24,28},{28,24},{32,36},... | collective-permute-start | bytes 1572872 | tf_op jit(solution)/shard_map/ppermute | solution.py:53
  71.3 9.7 %collective-permute-start.15 = (bf16[128,2048]{1,0:T(8,128)(2,1)S(1)}, bf16[128,2048]{1,0:T(8,128)(2,1)}, u32[]{:S(2)}, u32[]{:S(2)}) collective-permute-start(bf16[128,2048]{1,0:T(8,128)(2,1)S(1)} %add_convert_fusion.4), channel_id=1, source_target_pairs={{0,96},{4,28},{8,104},{12,20},{16,112},{20,12},{24,120},{28,4},{32... | collective-permute-start | bytes 1572872 | tf_op jit(solution)/shard_map/ppermute | solution.py:49
  73.0 9.8 %collective-permute-start.20 = (bf16[128,2048]{1,0:T(8,128)(2,1)S(1)}, bf16[128,2048]{1,0:T(8,128)(2,1)}, u32[]{:S(2)}, u32[]{:S(2)}) collective-permute-start(bf16[128,2048]{1,0:T(8,128)(2,1)S(1)} %add_convert_fusion.1), channel_id=1, source_target_pairs={{0,32},{4,12},{8,40},{12,4},{16,48},{20,28},{24,56},{28,20},{32,0}... | collective-permute-start | bytes 1572872 | tf_op jit(solution)/shard_map/ppermute | solution.py:49
  82.5 5.6 %collective-permute-start.16 = (bf16[64,2048]{1,0:T(8,128)(2,1)S(1)}, bf16[64,2048]{1,0:T(8,128)(2,1)S(1)}, u32[]{:S(2)}, u32[]{:S(2)}) collective-permute-start(bf16[64,2048]{1,0:T(8,128)(2,1)S(1)} %slice.139), channel_id=1, source_target_pairs={{0,32},{4,12},{8,40},{12,4},{16,48},{20,28},{24,56},{28,20},{32,0}... | collective-permute-start | bytes 786440 | tf_op jit(solution)/shard_map/ppermute | solution.py:49
  84.3 6.8 %collective-permute-start.21 = (bf16[64,2048]{1,0:T(8,128)(2,1)S(1)}, bf16[64,2048]{1,0:T(8,128)(2,1)S(1)}, u32[]{:S(2)}, u32[]{:S(2)}) collective-permute-start(bf16[64,2048]{1,0:T(8,128)(2,1)S(1)} %slice.143), channel_id=1, source_target_pairs={{0,96},{4,28},{8,104},{12,20},{16,112},{20,12},{24,120},{28,4},{32... | collective-permute-start | bytes 786440 | tf_op jit(solution)/shard_map/ppermute | solution.py:49
  91.2 5.1 %collective-permute-start.22 = (bf16[32,2048]{1,0:T(8,128)(2,1)S(1)}, bf16[32,2048]{1,0:T(8,128)(2,1)S(1)}, u32[]{:S(2)}, u32[]{:S(2)}) collective-permute-start(bf16[32,2048]{1,0:T(8,128)(2,1)S(1)} %get-tuple-element.58), channel_id=1, source_target_pairs={{0,24},{4,100},{8,16},{12,108},{16,8},{20,116},{24,0},{28,124},{32... | collective-permute-start | bytes 393224 | tf_op jit(solution)/shard_map/ppermute | solution.py:49
  92.3 5.4 %collective-permute-start.23 = (bf16[32,2048]{1,0:T(8,128)(2,1)S(1)}, bf16[32,2048]{1,0:T(8,128)(2,1)S(1)}, u32[]{:S(2)}, u32[]{:S(2)}) collective-permute-start(bf16[32,2048]{1,0:T(8,128)(2,1)S(1)} %get-tuple-element.59), channel_id=1, source_target_pairs={{0,16},{4,68},{8,24},{12,76},{16,0},{20,84},{24,8},{28,92},{32,48}... | collective-permute-start | bytes 393224 | tf_op jit(solution)/shard_map/ppermute | solution.py:49
  98.0 5.5 %collective-permute-start.28 = (bf16[32,2048]{1,0:T(8,128)(2,1)S(1)}, bf16[32,2048]{1,0:T(8,128)(2,1)S(1)}, u32[]{:S(2)}, u32[]{:S(2)}) collective-permute-start(bf16[32,2048]{1,0:T(8,128)(2,1)S(1)} %fusion.2), channel_id=1, source_target_pairs={{0,16},{4,68},{8,24},{12,76},{16,0},{20,84},{24,8},{28,92},{32,48}... | collective-permute-start | bytes 393224 | tf_op jit(solution)/shard_map/ppermute | solution.py:49
  98.1 6.5 %collective-permute-start.27 = (bf16[32,2048]{1,0:T(8,128)(2,1)S(1)}, bf16[32,2048]{1,0:T(8,128)(2,1)S(1)}, u32[]{:S(2)}, u32[]{:S(2)}) collective-permute-start(bf16[32,2048]{1,0:T(8,128)(2,1)S(1)} %fusion.2), channel_id=1, source_target_pairs={{0,24},{4,100},{8,16},{12,108},{16,8},{20,116},{24,0},{28,124},{32... | collective-permute-start | bytes 393224 | tf_op jit(solution)/shard_map/ppermute | solution.py:49
  100.0 6.6 %collective-permute-start.24 = (bf16[32,2048]{1,0:T(8,128)(2,1)S(1)}, bf16[32,2048]{1,0:T(8,128)(2,1)S(1)}, u32[]{:S(2)}, u32[]{:S(2)}) collective-permute-start(bf16[32,2048]{1,0:T(8,128)(2,1)S(1)} %fusion.2), channel_id=1, source_target_pairs={{0,8},{4,36},{8,0},{12,44},{16,24},{20,52},{24,16},{28,60},{32,40}... | collective-permute-start | bytes 393224 | tf_op jit(solution)/shard_map/ppermute | solution.py:49
  104.7 7.1 %collective-permute-start.29 = (bf16[64,2048]{1,0:T(8,128)(2,1)S(1)}, bf16[64,2048]{1,0:T(8,128)(2,1)S(1)}, u32[]{:S(2)}, u32[]{:S(2)}) collective-permute-start(bf16[64,2048]{1,0:T(8,128)(2,1)S(1)} %pad_maximum_fusion.5), channel_id=1, source_target_pairs={{0,96},{4,28},{8,104},{12,20},{16,112},{20,12},{24,120},{28,4},{32... | collective-permute-start | bytes 786440 | tf_op jit(solution)/shard_map/ppermute | solution.py:49
  106.6 11.5 %collective-permute-start.25 = (bf16[64,2048]{1,0:T(8,128)(2,1)S(1)}, bf16[64,2048]{1,0:T(8,128)(2,1)S(1)}, u32[]{:S(2)}, u32[]{:S(2)}) collective-permute-start(bf16[64,2048]{1,0:T(8,128)(2,1)S(1)} %pad_maximum_fusion.4), channel_id=1, source_target_pairs={{0,32},{4,12},{8,40},{12,4},{16,48},{20,28},{24,56},{28,20},{32,0}... | collective-permute-start | bytes 786440 | tf_op jit(solution)/shard_map/ppermute | solution.py:49
  111.8 9.0 %collective-permute-start.32 = (bf16[128,2048]{1,0:T(8,128)(2,1)S(1)}, bf16[128,2048]{1,0:T(8,128)(2,1)S(1)}, u32[]{:S(2)}, u32[]{:S(2)}) collective-permute-start(bf16[128,2048]{1,0:T(8,128)(2,1)S(1)} %constant_dynamic-update-slice_fusion.5.refs_1_), channel_id=1, source_target_pairs={{0,4},{4,0},{8,12},{12,8},{16,20},{20,16},{24,28},{28,24},{32,36},... | collective-permute-start | bytes 1572872 | tf_op jit(solution)/shard_map/ppermute | solution.py:53
  118.5 8.4 %collective-permute-start.30 = (bf16[128,2048]{1,0:T(8,128)(2,1)S(1)}, bf16[128,2048]{1,0:T(8,128)(2,1)S(1)}, u32[]{:S(2)}, u32[]{:S(2)}) collective-permute-start(bf16[128,2048]{1,0:T(8,128)(2,1)S(1)} %constant_dynamic-update-slice_fusion.5.refs_1_), channel_id=1, source_target_pairs={{0,32},{4,12},{8,40},{12,4},{16,48},{20,28},{24,56},{28,20},{32,0}... | collective-permute-start | bytes 1572872 | tf_op jit(solution)/shard_map/ppermute | solution.py:49
  119.2 9.5 %collective-permute-start.26 = (bf16[128,2048]{1,0:T(8,128)(2,1)S(1)}, bf16[128,2048]{1,0:T(8,128)(2,1)S(1)}, u32[]{:S(2)}, u32[]{:S(2)}) collective-permute-start(bf16[128,2048]{1,0:T(8,128)(2,1)S(1)} %pad_maximum_fusion.1.refs_0_), channel_id=1, source_target_pairs={{0,96},{4,28},{8,104},{12,20},{16,112},{20,12},{24,120},{28,4},{32... | collective-permute-start | bytes 1572872 | tf_op jit(solution)/shard_map/ppermute | solution.py:49
  (15 other events, 204.2 us)

commit v3 on v2

--- a/solution.py
+++ b/solution.py
@@ -72,13 +72,15 @@
     came = [swap_core(part) for part in early[1]]
     held = [added(early[0][s], came[s]) for s in range(2)]
     held = [added(held[s], late[s]) for s in range(2)]
+    tip = held[1][:8, :128]
     half = held[0].shape[0] // 2
     came = [hop(held[s][half:], 1, EDGES[s][0]) for s in range(2)]
     held = [added(held[s][:half], came[s]) for s in range(2)]
     half = half // 2
     blocks = (held[0][half:], held[1][:half], held[1][half:])
     came = [hop(block, 0, flip) for block, flip in zip(blocks, DIRECT, strict=True)]
-    return sum((part.astype(jnp.float32) for part in came), held[0][:half].astype(jnp.float32))
+    total = held[0][:half].astype(jnp.float32)
+    return sum((part.astype(jnp.float32) for part in came), total), tip
 
 
 def block_table():
@@ -110,10 +112,165 @@
     return jnp.dot(left, right, precision=HIGHEST, preferred_element_type=jnp.float32)
 
 
+def lane_spread(rows, lanes):
+    return (
+        lax.broadcasted_iota(jnp.int32, (rows, lanes), 0)
+        == lax.broadcasted_iota(jnp.int32, (rows, lanes), 1) // SSM_DIM
+    ).astype(jnp.float32)
+
+
+def keeper_kernel(*refs):
+    sources, (kept_ref, kept_bc_ref), held, sems = refs[:10], refs[10:12], refs[12:22], refs[22]
+    copies = [
+        pltpu.make_async_copy(source, target, sems.at[index])
+        for index, (source, target) in enumerate(zip(sources, held, strict=True))
+    ]
+    for copy in copies:
+        copy.start()
+    for copy in copies:
+        copy.wait()
+    member_ref, accepted_ref, decay_ref, scaled_ref, b_ref, in_x_ref, in_bc_ref = held[:7]
+    past_x_ref, past_bc_ref, state = held[7:]
+    tokens, inner = scaled_ref.shape
+    requests = tokens // DRAFT
+    rank = lax.axis_index("mdl")
+
+    row = lax.broadcasted_iota(jnp.int32, (tokens, 1), 0)
+    time, request = row % DRAFT, row // DRAFT
+    last = jnp.zeros((tokens, 1), jnp.int32)
+    for r in range(requests):
+        last = jnp.where(request == r, accepted_ref[r] - 1, last)
+    spread_lanes = lane_spread(tokens, inner)
+    log_decay, scaled_x, b_part = decay_ref[...], scaled_ref[...], b_ref[...]
+    in_x, in_bc = in_x_ref[...], in_bc_ref[...]
+    decay_x = exact_dot(log_decay, spread_lanes)
+    other = lax.broadcasted_iota(jnp.int32, (tokens, tokens), 1)
+    pick = (other == request * DRAFT + last).astype(jnp.float32)
+    final_log = exact_dot(pick, log_decay)
+    final_x = exact_dot(final_log, spread_lanes)
+    carry_x = jnp.exp(jnp.where(time <= last, final_x - decay_x, far_below))
+    carried_x = (scaled_x * carry_x).T.astype(jnp.bfloat16)
+    shrink = jnp.exp(final_x).T
+    for r in range(requests):
+        b_here = jnp.where(request == r, b_part, jnp.zeros_like(b_part))
+        kept = shrink[:, r * DRAFT : r * DRAFT + 1] * state[member_ref[r]] + dot32(
+            carried_x, b_here
+        )
+        kept_ref[r, :inner, :] = kept.astype(jnp.bfloat16)
+
+    def kept_rows(first_request, count, slots, series, past_of):
+        at = lax.broadcasted_iota(jnp.int32, (count * slots, 1), 0)
+        here, edge = at // slots, at % slots
+        start = jnp.zeros((count * slots, 1), jnp.int32)
+        owner = jnp.zeros((count * slots, 1), jnp.int32)
+        for r in range(count):
+            start = jnp.where(here == r, accepted_ref[first_request + r], start)
+            owner = jnp.where(here == r, member_ref[first_request + r], owner)
+        index = start + edge
+        token = (here + first_request) * DRAFT + index - (CONV - 1)
+        chosen = (lax.broadcasted_iota(jnp.int32, (count * slots, tokens), 1) == token) & (
+            index >= CONV - 1
+        )
+        rows = dot32(chosen.astype(jnp.bfloat16), series)
+        for p in range(PROMPTS):
+            for j in range(CONV - 1):
+                rows = jnp.where((owner == p) & (index == j), past_of(j, p), rows)
+        return rows.astype(jnp.bfloat16)
+
+    for lanes in range(2):
+        cut = slice(lanes * STATE, min((lanes + 1) * STATE, inner))
+        rows = kept_rows(
+            0, requests, 8, in_x[:, cut], lambda j, p: past_x_ref[j, p : p + 1, cut].astype(jnp.float32)
+        )
+        for r in range(requests):
+            kept_ref[r, inner + 8 * lanes : inner + 8 * (lanes + 1), : rows.shape[1]] = rows[
+                r * 8 : (r + 1) * 8
+            ]
+    kept_ref[:, inner + 8 :, inner - STATE :] = jnp.zeros(
+        (requests, 8, 2 * STATE - inner), jnp.bfloat16
+    )
+    kept_bc_ref[...] = kept_rows(
+        rank * (requests // SIDE),
+        requests // SIDE,
+        8,
+        in_bc,
+        lambda j, p: past_bc_ref[j, p : p + 1, :].astype(jnp.float32),
+    )
+
+
+def keeper(member, accepted, log_decay, scaled_x, b_part, in_x, in_bc, past_x, past_bc, state):
+    tokens, inner = scaled_x.shape
+    requests = tokens // DRAFT
+    operands = (member, accepted, log_decay, scaled_x, b_part, in_x, in_bc, past_x, past_bc, state)
+    whole = pl.BlockSpec(memory_space=pltpu.VMEM)
+    return pl.pallas_call(
+        keeper_kernel,
+        out_shape=[
+            jax.ShapeDtypeStruct((requests, inner + 16, STATE), jnp.bfloat16),
+            jax.ShapeDtypeStruct((requests // SIDE * 8, 2 * STATE), jnp.bfloat16),
+        ],
+        in_specs=[pl.BlockSpec(memory_space=pltpu.HBM)] * len(operands),
+        out_specs=[whole] * 2,
+        scratch_shapes=[
+            *(pltpu.SMEM(a.shape, a.dtype) for a in operands[:2]),
+            *(pltpu.VMEM(a.shape, a.dtype) for a in operands[2:]),
+            pltpu.SemaphoreType.DMA((len(operands),)),
+        ],
+        compiler_params=pltpu.CompilerParams(vmem_limit_bytes=32 << 20),
+        cost_estimate=pl.CostEstimate(
+            flops=2_000_000_000, bytes_accessed=5_000_000, transcendentals=200_000
+        ),
+        name="keeper",
+    )(*operands)
+
+
+def unpack_kernel(kept_hbm, bc_ref, _stats, _tip, state_ref, conv_ref, kept_ref, sem):
+    copy = pltpu.make_async_copy(kept_hbm, kept_ref, sem)
+    copy.start()
+    copy.wait()
+    inner = kept_ref.shape[2] - 16
+    for r in range(state_ref.shape[0]):
+        for z in range(kept_ref.shape[0]):
+            state_ref[r, z * inner : (z + 1) * inner, :] = kept_ref[z, r, :inner, :].astype(
+                jnp.float32
+            )
+    for j in range(CONV - 1):
+        rows = []
+        for r in range(state_ref.shape[0]):
+            pieces = []
+            for z in range(kept_ref.shape[0]):
+                tail = kept_ref[z, r, inner:, :].astype(jnp.float32)
+                pieces += [tail[j : j + 1, :], tail[8 + j : 9 + j, : inner - STATE]]
+            pieces.append(bc_ref[...].astype(jnp.float32)[r * 8 + j : r * 8 + j + 1, :])
+            rows.append(jnp.concatenate(pieces, axis=1))
+        conv_ref[j] = jnp.concatenate(rows, axis=0).astype(jnp.bfloat16)
+
+
+def unpack(kept_out, own_bc, *tokens):
+    sources, requests, rows, _ = kept_out.shape
+    inner = rows - 16
+    whole = pl.BlockSpec(memory_space=pltpu.VMEM)
+    state, conv = pl.pallas_call(
+        unpack_kernel,
+        out_shape=[
+            jax.ShapeDtypeStruct((requests, sources * inner, STATE), jnp.float32),
+            jax.ShapeDtypeStruct((CONV - 1, requests, sources * inner + 2 * STATE), jnp.bfloat16),
+        ],
+        in_specs=[pl.BlockSpec(memory_space=pltpu.HBM), whole]
+        + [pl.BlockSpec(memory_space=pl.ANY)] * len(tokens),
+        out_specs=[whole] * 2,
+        scratch_shapes=[pltpu.VMEM(kept_out.shape, kept_out.dtype), pltpu.SemaphoreType.DMA],
+        compiler_params=pltpu.CompilerParams(vmem_limit_bytes=48 << 20),
+        cost_estimate=pl.CostEstimate(flops=1_000_000, bytes_accessed=20_000_000, transcendentals=0),
+        name="unpack",
+    )(kept_out, own_bc, *tokens)
+    return state, conv.transpose(1, 0, 2)
+
+
 def mixer_kernel(*refs):
     sources, refs = refs[:22], refs[22:]
-    far_ref, near_ref, kept_ref, kept_bc_ref = refs[:4]
-    held, (mixed_scr, lanes_scr, sems) = refs[4:-3], refs[-3:]
+    far_ref, near_ref, decay_ref, scaled_ref, b_ref, in_x_ref, in_bc_ref = refs[:7]
+    held, (mixed_scr, lanes_scr, sems) = refs[7:-3], refs[-3:]
     member_ref, accepted_ref, lengths_ref, rate_ref, bias_ref, skip_ref = held[:6]
     hidden_ref, gain_ref, w_dt_ref, conv_x_ref, conv_bc_ref, past_x_ref, past_bc_ref = held[6:13]
     w_query, w_kv, prompt, w_x, w_bc, w_z, state, w_out = held[13:]
@@ -247,10 +404,7 @@
         lanes_scr[:, :heads] = values
         return lanes_scr[...]
 
-    spread_lanes = (
-        lax.broadcasted_iota(jnp.int32, (tokens, inner), 0)
-        == lax.broadcasted_iota(jnp.int32, (tokens, inner), 1) // SSM_DIM
-    ).astype(jnp.float32)
+    spread_lanes = lane_spread(tokens, inner)
     dt_in = dot32(normed, w_dt_ref[...], NEXT_TO).astype(jnp.bfloat16).astype(jnp.float32) + head_row(bias_ref)
     step = jnp.maximum(dt_in, 0.0) + jnp.log1p(jnp.exp(-jnp.abs(dt_in)))
     log_decay = exact_dot(same.astype(jnp.float32), widen(-step * head_row(rate_ref)))
@@ -297,58 +451,11 @@
         )
         out_ref[...] = dot32(rows, w_out[...]).astype(jnp.bfloat16)
 
-    other = lax.broadcasted_iota(jnp.int32, (tokens, tokens), 1)
-    pick = (other == request * DRAFT + last).astype(jnp.float32)
-    final_log = exact_dot(pick, log_decay)
-    final_x = exact_dot(final_log, spread_lanes)
-    carry_x = jnp.exp(jnp.where(time <= last, final_x - decay_x, far_below))
-    carried_x = (scaled_x * carry_x).T.astype(jnp.bfloat16)
-    shrink = jnp.exp(final_x).T
-    for r in range(requests):
-        b_here = jnp.where(request == r, b_part, jnp.zeros_like(b_part))
-        kept = shrink[:, r * DRAFT : r * DRAFT + 1] * state[member_ref[r]] + dot32(
-            carried_x, b_here
-        )
-        kept_ref[r, :inner, :] = kept.astype(jnp.bfloat16)
-
-    def kept_rows(first_request, count, slots, series, past_of):
-        at = lax.broadcasted_iota(jnp.int32, (count * slots, 1), 0)
-        here, edge = at // slots, at % slots
-        start = jnp.zeros((count * slots, 1), jnp.int32)
-        owner = jnp.zeros((count * slots, 1), jnp.int32)
-        for r in range(count):
-            start = jnp.where(here == r, accepted_ref[first_request + r], start)
-            owner = jnp.where(here == r, member_ref[first_request + r], owner)
-        index = start + edge
-        token = (here + first_request) * DRAFT + index - (CONV - 1)
-        chosen = (lax.broadcasted_iota(jnp.int32, (count * slots, tokens), 1) == token) & (
-            index >= CONV - 1
-        )
-        rows = dot32(chosen.astype(jnp.bfloat16), series)
-        for p in range(PROMPTS):
-            for j in range(CONV - 1):
-                rows = jnp.where((owner == p) & (index == j), past_of(j, p), rows)
-        return rows.astype(jnp.bfloat16)
-
-    for lanes in range(2):
-        cut = slice(lanes * STATE, min((lanes + 1) * STATE, inner))
-        rows = kept_rows(
-            0, requests, 8, in_x[:, cut], lambda j, p: past_x_ref[j, p : p + 1, cut].astype(jnp.float32)
-        )
-        for r in range(requests):
-            kept_ref[r, inner + 8 * lanes : inner + 8 * (lanes + 1), : rows.shape[1]] = rows[
-                r * 8 : (r + 1) * 8
-            ]
-    kept_ref[:, inner + 8 :, inner - STATE :] = jnp.zeros(
-        (requests, 8, 2 * STATE - inner), jnp.bfloat16
-    )
-    kept_bc_ref[...] = kept_rows(
-        rank * (requests // SIDE),
-        requests // SIDE,
-        8,
-        in_bc,
-        lambda j, p: past_bc_ref[j, p : p + 1, :].astype(jnp.float32),
-    )
+    decay_ref[...] = log_decay
+    scaled_ref[...] = scaled_x
+    b_ref[...] = b_part
+    in_x_ref[...] = in_x
+    in_bc_ref[...] = in_bc
 
 
 def mixer(
@@ -356,7 +463,6 @@
     w_dt, conv_x, conv_bc, ssm_rate, dt_bias, skip_d, prompt_state, prompt_conv_x, prompt_conv_bc, w_mamba_out,
 ):
     tokens, width = hidden.shape
-    requests = tokens // DRAFT
     inner = w_x.shape[1]
     query_width = w_query.shape[1]
     bf16 = jnp.bfloat16
@@ -367,16 +473,19 @@
     ]
     scalars = [member, accepted, prompt_lengths, ssm_rate, dt_bias, skip_d]
     whole = pl.BlockSpec(memory_space=pltpu.VMEM)
-    return pl.pallas_call(
+    far, near, *series = pl.pallas_call(
         mixer_kernel,
         out_shape=[
             jax.ShapeDtypeStruct((tokens // 2, width), bf16),
             jax.ShapeDtypeStruct((tokens // 2, width), bf16),
-            jax.ShapeDtypeStruct((requests, inner + 16, STATE), bf16),
-            jax.ShapeDtypeStruct((requests // SIDE * 8, 2 * STATE), bf16),
+            jax.ShapeDtypeStruct((tokens, 128), jnp.float32),
+            jax.ShapeDtypeStruct((tokens, inner), jnp.float32),
+            jax.ShapeDtypeStruct((tokens, STATE), bf16),
+            jax.ShapeDtypeStruct((tokens, inner), bf16),
+            jax.ShapeDtypeStruct((tokens, 2 * STATE), bf16),
         ],
         in_specs=[pl.BlockSpec(memory_space=pltpu.HBM)] * 22,
-        out_specs=[whole] * 4,
+        out_specs=[whole] * 7,
         scratch_shapes=[
             *(pltpu.SMEM(a.shape, a.dtype) for a in scalars),
             *(pltpu.VMEM(a.shape, a.dtype) for a in small),
@@ -400,9 +509,10 @@
     )(
         *scalars, *small, w_query, w_kv, prompt_kv, w_x, w_bc, w_z, state, w_attn_out, w_mamba_out
     )
-
-
-def feed_kernel(first_ref, second_ref, both_ref, down_ref, _, first_out, second_out):
+    return far, near, *keeper(member, accepted, *series, *small[-2:], state)
+
+
+def feed_kernel(first_ref, second_ref, both_ref, down_ref, first_out, second_out):
     hidden = down_ref.shape[0]
     rows = first_ref.shape[0]
     joined = jnp.concatenate([first_ref[...], second_ref[...]], axis=0)
@@ -414,13 +524,13 @@
     second_out[...] = parts[rows:]
 
 
-def feed(first, second, w_both, w_down, token):
+def feed(first, second, w_both, w_down):
     rows, width = first.shape
     whole = pl.BlockSpec(memory_space=pltpu.VMEM)
     return pl.pallas_call(
         feed_kernel,
         out_shape=[jax.ShapeDtypeStruct((rows, width), jnp.bfloat16)] * 2,
-        in_specs=[whole] * 4 + [pl.BlockSpec(memory_space=pl.ANY)],
+        in_specs=[whole] * 4,
         out_specs=[whole] * 2,
         compiler_params=pltpu.CompilerParams(vmem_limit_bytes=16 << 20),
         cost_estimate=pl.CostEstimate(
@@ -429,7 +539,7 @@
             transcendentals=2 * rows * w_down.shape[0],
         ),
         name="feed",
-    )(first, second, w_both, w_down, token)
+    )(first, second, w_both, w_down)
 
 
 def head_kernel(targets_ref, owners_ref, *refs):
@@ -536,7 +646,6 @@
     own_tokens = own_reqs * draft_len
     flat_rows = hidden_in.reshape(row_tokens, width)
     local_inner = w_x.shape[1]
-    edge_len = CONV - 1
     far, near, kept, own_bc = mixer(
         flat_rows, mixer_gain, w_query, w_kv, w_attn_out, prompt_kv, prompt_lengths, member, accepted, w_z, w_x, w_bc,
         w_dt, conv_x, conv_bc, ssm_rate, dt_bias, skip_d, prompt_state, prompt_conv_x, prompt_conv_bc, w_mamba_out,
@@ -550,14 +659,6 @@
     )
     own_rows = lax.dynamic_slice_in_dim(flat_rows, mdl_rank * own_tokens, own_tokens, 0)
     after_mixer = (own_rows.astype(jnp.float32) + mixed).astype(jnp.bfloat16)
-    kept, token = lax.optimization_barrier((kept, after_mixer[:8, :128]))
-    kept_out = lax.all_to_all(
-        kept.reshape(mdl_count, own_reqs, local_inner + 16, STATE),
-        "mdl",
-        split_axis=0,
-        concat_axis=0,
-        tiled=True,
-    )
     prepared = rms_scale(after_mixer, mlp_gain).astype(jnp.bfloat16)
     w_both = jnp.concatenate([w_gate, w_up], axis=1)
     held, late = gather_rows(prepared)
@@ -576,32 +677,19 @@
     targets = targets.reshape(8, 8 * draft_len)
     owners = jnp.broadcast_to(owner[:, None], (64, draft_len)).reshape(8, 8 * draft_len)
 
-    early_parts = [feed(*rows, w_both, w_down, token) for rows in early]
-    later_token, kept_out = lax.optimization_barrier((token, kept_out))
-    late_parts = [
-        feed(*late[0], w_both, w_down, token),
-        feed(*late[1], w_both, w_down, later_token),
-    ]
-    summed = scatter_rows(early_parts, late_parts)
-    kept_state = (
-        kept_out[:, :, :local_inner, :]
-        .transpose(1, 0, 2, 3)
-        .astype(jnp.float32)
-        .reshape(own_reqs, mdl_count * local_inner // SSM_DIM, SSM_DIM, STATE)
-    )
-    edges = kept_out[:, :, local_inner:, :]
-    edges = jnp.concatenate(
-        [edges[:, :, :edge_len, :], edges[:, :, 8 : 8 + edge_len, : local_inner - STATE]], axis=3
-    )
-    kept_conv = jnp.concatenate(
-        [
-            edges.transpose(1, 2, 0, 3).reshape(own_reqs, edge_len, mdl_count * local_inner),
-            own_bc.reshape(own_reqs, 8, 2 * STATE)[:, :edge_len, :],
-        ],
-        axis=2,
-    )
-    final_gain, kept_state, kept_conv, targets, owners = lax.optimization_barrier(
-        (final_gain, kept_state, kept_conv, targets, owners)
+    early_parts = [feed(*rows, w_both, w_down) for rows in early]
+    late_parts = [feed(*rows, w_both, w_down) for rows in late]
+    summed, tip = scatter_rows(early_parts, late_parts)
+    kept, tip = lax.optimization_barrier((kept, tip))
+    kept_out = lax.all_to_all(
+        kept.reshape(mdl_count, own_reqs, local_inner + 16, STATE),
+        "mdl",
+        split_axis=0,
+        concat_axis=0,
+        tiled=True,
+    )
+    final_gain, kept_out, targets, owners = lax.optimization_barrier(
+        (final_gain, kept_out, targets, owners)
     )
     after_feed = (after_mixer.astype(jnp.float32) + summed).astype(jnp.bfloat16)
     final_rows = rms_scale(after_feed, final_gain).astype(jnp.bfloat16)
@@ -612,6 +700,8 @@
     sibling = [swap_core(part) for part in late]
     stats = [first_stats, head_stats(targets[4:6], owners[4:6], late, head_weight, req_count)]
     stats = head_stats(targets[6:], owners[6:], sibling, head_weight, req_count, stats)
+    kept_state, kept_conv = unpack(kept_out, own_bc, stats, tip)
+    kept_state = kept_state.reshape(own_reqs, -1, SSM_DIM, STATE)
     shared = lax.all_to_all(stats, "req", split_axis=0, concat_axis=0, tiled=True)
     shared = shared.reshape(req_count, 8, 128)[:, :, :own_tokens]
     tops, totals, hits = shared[:, 0], shared[:, 1], shared[:, 2]

time: 149 us -> 148 us (level)
  starting transfers between devices: 55.4 us -> 68.4 us
  blocking collectives: 12.6 us -> 0 us
  other arithmetic: 11.3 us -> 4.92 us
  waiting for transfers between devices: 32.3 us -> 37.5 us
  local copies, waits for them, and re-layouts: 7.64 us -> 5.93 us
    all_to_all x1 -> x0, blocking collectives: 12.6 us -> none  [shards(): lax.all_to_all(stats, 'req', split_axis=0, concat_axis=0, tiled=True)]
    ppermute x21, waiting for transfers between devices: 28.3 us -> 16.5 us  [hop(): return lax.ppermute(part, 'req', flip_pairs(ring, flip))]
    all_to_all x1, waiting for transfers between devices: 0.01 us -> 8.96 us  [shards(): lax.all_to_all(kept.reshape(mdl_count, own_reqs, local_inner + 16, STATE)...]
    ppermute x21, starting transfers between devices: 21.4 us -> 28.9 us  [hop(): return lax.ppermute(part, 'req', flip_pairs(ring, flip))]
    pallas_call x0 -> x2, Pallas kernels: none -> 5.67 us  [the longest x1 3.6 us: keeper(): pl.pallas_call(keeper_kernel, out_shape=[jax.ShapeDtypeStruct((requests,...]
    all_to_all x0 -> x1, waiting for transfers between devices: none -> 5.55 us  [shards(): lax.all_to_all(stats, 'req', split_axis=0, concat_axis=0, tiled=True)]
    all_to_all x0 -> x1, starting transfers between devices: none -> 4.38 us  [shards(): lax.all_to_all(stats, 'req', split_axis=0, concat_axis=0, tiled=True)]
    reshape x2 -> x0, local copies, waits for them, and re-layouts: 3.78 us -> none  [the longest x1 3.76 us: shards(): kept_state = kept_out[:, :, :local_inner, :].transpose(1, 0, 2, 3).astype...]
  transfers between devices with their start and end apart: 36 -> 37, of which waited for: 15 -> 19; matrix products, arithmetic and copies ran while one was open for 11% -> 4% of each run, Pallas kernels for 11% -> 12%
where the time goes in v3:
time: 148 us
  starting transfers between devices  68.4 us (46%)
  waiting for transfers between devices  37.5 us (25%)
  Pallas kernels  29.7 us (20%)
  local copies, waits for them, and re-layouts  5.93 us (4%)
  other arithmetic  4.92 us (3%)
    ppermute x21, starting transfers between devices, hop(): return lax.ppermute(part, 'req', flip_pairs(ring, flip))  28.9 us
    ppermute x12, starting transfers between devices, swap_core(): return lax.ppermute(part, 'req', CORE_PAIRS)  24.3 us
    ppermute x21, waiting for transfers between devices, hop(): return lax.ppermute(part, 'req', flip_pairs(ring, flip))  16.5 us
    pallas_call x3, Pallas kernels, head_stats(): pl.pallas_call(head_kernel, out_shape=jax.ShapeDtypeStruct((devices * 8,...  10.2 us
    all_to_all x1, waiting for transfers between devices, shards(): lax.all_to_all(kept.reshape(mdl_count, own_reqs, local_inner + 16, STATE)...  8.96 us
    pallas_call x1, Pallas kernels, mixer(): pl.pallas_call(mixer_kernel, out_shape=[jax.ShapeDtypeStruct((tokens // 2...  8.65 us
    all_to_all x1, waiting for transfers between devices, shards(): lax.all_to_all(stats, 'req', split_axis=0, concat_axis=0, tiled=True)  5.55 us
    pallas_call x4, Pallas kernels, feed(): pl.pallas_call(feed_kernel, out_shape=[jax.ShapeDtypeStruct((rows, width)...  5.17 us
  transfers between devices with their start and end apart: 37, of which 19 were waited for; matrix products, arithmetic and copies ran while one was open for 4% of the time, Pallas kernels for 12%

profile of v3, /device:TPU:1, one launch (start us, length us, event | category | flops | bytes accessed | tf_op | source)
XLA Modules:
  0.0 147.9 jit_solution(603494807322764407)
XLA Ops:
  0.7 8.6 %mixer.1 = (bf16[64,2048]{1,0:T(8,128)(2,1)}, bf16[64,2048]{1,0:T(8,128)(2,1)}, f32[128,128]{1,0:T(8,128)}, f32[128,384]{1,0:T(8,128)}, bf16[128,256]{1,0:T(8,12...) custom-call(s32[8]{0:T(128)} %refs_0_.3, s32[8]{0:T(128)} %refs_1_.3, s32[2]{0:T(128)} %refs_2_.3, f32[6]{0:T(128)} %refs_3_.1, ...), custom_call_target="tpu_custom_call" | custom-call | flops 3000000000 | bytes 20000000 | tf_op jit(solution)/shard_map/mixer/pallas_call | solution.py:476
  9.3 2.5 %collective-permute-start = (bf16[64,2048]{1,0:T(8,128)(2,1)}, bf16[64,2048]{1,0:T(8,128)(2,1)S(1)}, u32[]{:S(2)}, u32[]{:S(2)}) collective-permute-start(bf16[64,2048]{1,0:T(8,128)(2,1)} %get-tuple-element.33), channel_id=1, source_target_pairs={{0,3},{1,2},{2,1},{3,0},{4,5},{5,4},{6,7},{7,6},{8,11},{9,10},{10,... | collective-permute-start | bytes 786440 | tf_op jit(solution)/shard_map/ppermute | solution.py:653
  11.9 3.9 %collective-permute-done = bf16[64,2048]{1,0:T(8,128)(2,1)S(1)} collective-permute-done((bf16[64,2048]{1,0:T(8,128)(2,1)}, bf16[64,2048]{1,0:T(8,128)(2,1)S(1)}, u32[]{:S(2)}, u32[]{:S(2)}) %collective-permute-start) | collective-permute-done | bytes 262176 | tf_op jit(solution)/shard_map/ppermute | solution.py:653
  16.9 3.9 %collective-permute-start.1 = (bf16[32,2048]{1,0:T(8,128)(2,1)S(1)}, bf16[32,2048]{1,0:T(8,128)(2,1)S(1)}, u32[]{:S(2)}, u32[]{:S(2)}) collective-permute-start(bf16[32,2048]{1,0:T(8,128)(2,1)S(1)} %add_convert_fusion.9), channel_id=1, source_target_pairs={{0,1},{1,0},{2,3},{3,2},{4,7},{5,6},{6,5},{7,4},{8,9},{9,8},{10,11... | collective-permute-start | bytes 393224 | tf_op jit(solution)/shard_map/ppermute | solution.py:654
  25.9 1.9 %collective-permute-start.4 = (bf16[32,2048]{1,0:T(8,128)(2,1)S(1)}, bf16[32,2048]{1,0:T(8,128)(2,1)S(1)}, u32[]{:S(2)}, u32[]{:S(2)}) collective-permute-start(bf16[32,2048]{1,0:T(8,128)(2,1)S(1)} %fusion.5), channel_id=1, source_target_pairs={{0,24},{4,100},{8,16},{12,108},{16,8},{20,116},{24,0},{28,124},{32... | collective-permute-start | bytes 393224 | tf_op jit(solution)/shard_map/ppermute | solution.py:49
  31.1 2.0 %collective-permute-done.5 = bf16[32,2048]{1,0:T(8,128)(2,1)S(1)} collective-permute-done((bf16[32,2048]{1,0:T(8,128)(2,1)S(1)}, bf16[32,2048]{1,0:T(8,128)(2,1)S(1)}, u32[]{:S(2)}, u32[]{:S(2)}) %collective-permute-start.5) | collective-permute-done | bytes 131104 | tf_op jit(solution)/shard_map/ppermute | solution.py:49
  33.1 2.6 %collective-permute-start.6 = (bf16[64,2048]{1,0:T(8,128)(2,1)S(1)}, bf16[64,2048]{1,0:T(8,128)(2,1)S(1)}, u32[]{:S(2)}, u32[]{:S(2)}) collective-permute-start(bf16[64,2048]{1,0:T(8,128)(2,1)S(1)} %pad_maximum_fusion.3), channel_id=1, source_target_pairs={{0,96},{4,28},{8,104},{12,20},{16,112},{20,12},{24,120},{28,4},{32... | collective-permute-start | bytes 786440 | tf_op jit(solution)/shard_map/ppermute | solution.py:49
  35.8 2.4 %collective-permute-start.10 = (bf16[128,2048]{1,0:T(8,128)(2,1)S(1)}, bf16[128,2048]{1,0:T(8,128)(2,1)S(1)}, u32[]{:S(2)}, u32[]{:S(2)}) collective-permute-start(bf16[128,2048]{1,0:T(8,128)(2,1)S(1)} %pad_maximum_fusion.first_ref), channel_id=1, source_target_pairs={{0,96},{4,28},{8,104},{12,20},{16,112},{20,12},{24,120},{28,4},{32... | collective-permute-start | bytes 1572872 | tf_op jit(solution)/shard_map/ppermute | solution.py:49
  38.2 3.8 %collective-permute-start.7 = (bf16[128,2048]{1,0:T(8,128)(2,1)S(1)}, bf16[128,2048]{1,0:T(8,128)(2,1)S(1)}, u32[]{:S(2)}, u32[]{:S(2)}) collective-permute-start(bf16[128,2048]{1,0:T(8,128)(2,1)S(1)} %pad_maximum_fusion.first_ref), channel_id=1, source_target_pairs={{0,4},{4,0},{8,12},{12,8},{16,20},{20,16},{24,28},{28,24},{32,36},... | collective-permute-start | bytes 1572872 | tf_op jit(solution)/shard_map/ppermute | solution.py:53
  43.2 3.4 %collective-permute-start.8 = (bf16[128,2048]{1,0:T(8,128)(2,1)S(1)}, bf16[128,2048]{1,0:T(8,128)(2,1)S(1)}, u32[]{:S(2)}, u32[]{:S(2)}) collective-permute-start(bf16[128,2048]{1,0:T(8,128)(2,1)S(1)} %constant_dynamic-update-slice_fusion.second_ref), channel_id=1, source_target_pairs={{0,4},{4,0},{8,12},{12,8},{16,20},{20,16},{24,28},{28,24},{32,36},... | collective-permute-start | bytes 1572872 | tf_op jit(solution)/shard_map/ppermute | solution.py:53
  46.7 3.6 %keeper.1 = (bf16[8,400,256]{2,1,0:T(8,128)(2,1)}, bf16[16,512]{1,0:T(8,128)(2,1)S(1)}) custom-call(s32[8]{0:T(128)S(1)} %copy-done.3, s32[8]{0:T(128)S(1)} %copy-done.4, f32[128,128]{1,0:T(8,128)S(1)} %copy-done.11, f32[128,384]{1,0:T(8,128)S(1)} %copy-done.8, bf16[128,256]{1,0:T(8,128)(2,1)S(1)} %copy-done.12, bf16[128,384]{1,0:T(8,128)(2,1)S(1)} %copy-done.10, ...), custom_call_target="tpu_custom_call" | custom-call | flops 2000000000 | bytes 5000000 | tf_op jit(solution)/shard_map/keeper/pallas_call | solution.py:206
  50.6 1.5 %collective-permute-start.12 = (bf16[128,2048]{1,0:T(8,128)(2,1)S(1)}, bf16[128,2048]{1,0:T(8,128)(2,1)S(1)}, u32[]{:S(2)}, u32[]{:S(2)}) collective-permute-start(bf16[128,2048]{1,0:T(8,128)(2,1)S(1)} %collective-permute-done.10.first_ref), channel_id=1, source_target_pairs={{0,4},{4,0},{8,12},{12,8},{16,20},{20,16},{24,28},{28,24},{32,36},... | collective-permute-start | bytes 1572872 | tf_op jit(solution)/shard_map/ppermute | solution.py:53
  52.1 3.3 %collective-permute-start.13 = (bf16[128,2048]{1,0:T(8,128)(2,1)S(1)}, bf16[128,2048]{1,0:T(8,128)(2,1)S(1)}, u32[]{:S(2)}, u32[]{:S(2)}) collective-permute-start(bf16[128,2048]{1,0:T(8,128)(2,1)S(1)} %collective-permute-done.11.second_ref), channel_id=1, source_target_pairs={{0,4},{4,0},{8,12},{12,8},{16,20},{20,16},{24,28},{28,24},{32,36},... | collective-permute-start | bytes 1572872 | tf_op jit(solution)/shard_map/ppermute | solution.py:53
  63.1 6.1 %collective-permute-done.20 = bf16[128,2048]{1,0:T(8,128)(2,1)S(1)} collective-permute-done((bf16[128,2048]{1,0:T(8,128)(2,1)S(1)}, bf16[128,2048]{1,0:T(8,128)(2,1)S(1)}, u32[]{:S(2)}, u32[]{:S(2)}) %collective-permute-start.20) | collective-permute-done | bytes 524320 | tf_op jit(solution)/shard_map/ppermute | solution.py:49
  72.1 4.3 %all-to-all-start = ((bf16[4,2,400,256]{3,2,1,0:T(8,128)(2,1)}), bf16[4,2,400,256]{3,2,1,0:T(8,128)(2,1)S(1)}, u32[]{:S(2)}, u32[]{:S(2)}) async-start(bf16[4,2,400,256]{3,2,1,0:T(8,128)(2,1)} %bitcast.7), calls=%async_computation | async-start | bytes 3276800 | tf_op jit(solution)/shard_map/all_to_all | solution.py:684
  77.8 1.9 %collective-permute-start.23 = (bf16[32,2048]{1,0:T(8,128)(2,1)}, bf16[32,2048]{1,0:T(8,128)(2,1)S(1)}, u32[]{:S(2)}, u32[]{:S(2)}) collective-permute-start(bf16[32,2048]{1,0:T(8,128)(2,1)} %get-tuple-element.67), channel_id=1, source_target_pairs={{0,16},{4,68},{8,24},{12,76},{16,0},{20,84},{24,8},{28,92},{32,48}... | collective-permute-start | bytes 393224 | tf_op jit(solution)/shard_map/ppermute | solution.py:49
  81.9 1.4 collective-permute-done.23
  83.4 1.7 %collective-permute-done.22 = bf16[32,2048]{1,0:T(8,128)(2,1)S(1)} collective-permute-done((bf16[32,2048]{1,0:T(8,128)(2,1)S(1)}, bf16[32,2048]{1,0:T(8,128)(2,1)S(1)}, u32[]{:S(2)}, u32[]{:S(2)}) %collective-permute-start.22) | collective-permute-done | bytes 131104 | tf_op jit(solution)/shard_map/ppermute | solution.py:49
  85.7 9.0 %all-to-all-done.kept_hbm = bf16[4,2,400,256]{3,2,1,0:T(8,128)(2,1)S(1)} async-done(((bf16[4,2,400,256]{3,2,1,0:T(8,128)(2,1)}), bf16[4,2,400,256]{3,2,1,0:T(8,128)(2,1)S(1)}, u32[]{:S(2)}, u32[]{:S(2)}) %all-to-all-start) | async-done | bytes 1638432 | tf_op jit(solution)/shard_map/all_to_all | solution.py:684
  94.8 4.6 %collective-permute-start.27 = (bf16[32,2048]{1,0:T(8,128)(2,1)S(1)}, bf16[32,2048]{1,0:T(8,128)(2,1)S(1)}, u32[]{:S(2)}, u32[]{:S(2)}) collective-permute-start(bf16[32,2048]{1,0:T(8,128)(2,1)S(1)} %fusion.2), channel_id=1, source_target_pairs={{0,24},{4,100},{8,16},{12,108},{16,8},{20,116},{24,0},{28,124},{32... | collective-permute-start | bytes 393224 | tf_op jit(solution)/shard_map/ppermute | solution.py:49
  100.5 3.2 %collective-permute-start.25 = (bf16[64,2048]{1,0:T(8,128)(2,1)S(1)}, bf16[64,2048]{1,0:T(8,128)(2,1)S(1)}, u32[]{:S(2)}, u32[]{:S(2)}) collective-permute-start(bf16[64,2048]{1,0:T(8,128)(2,1)S(1)} %pad_maximum_fusion.4), channel_id=1, source_target_pairs={{0,32},{4,12},{8,40},{12,4},{16,48},{20,28},{24,56},{28,20},{32,0}... | collective-permute-start | bytes 786440 | tf_op jit(solution)/shard_map/ppermute | solution.py:49
  104.7 3.5 %collective-permute-start.29 = (bf16[64,2048]{1,0:T(8,128)(2,1)S(1)}, bf16[64,2048]{1,0:T(8,128)(2,1)S(1)}, u32[]{:S(2)}, u32[]{:S(2)}) collective-permute-start(bf16[64,2048]{1,0:T(8,128)(2,1)S(1)} %pad_maximum_fusion.5), channel_id=1, source_target_pairs={{0,96},{4,28},{8,104},{12,20},{16,112},{20,12},{24,120},{28,4},{32... | collective-permute-start | bytes 786440 | tf_op jit(solution)/shard_map/ppermute | solution.py:49
  109.2 4.0 %collective-permute-start.31 = (bf16[128,2048]{1,0:T(8,128)(2,1)S(1)}, bf16[128,2048]{1,0:T(8,128)(2,1)S(1)}, u32[]{:S(2)}, u32[]{:S(2)}) collective-permute-start(bf16[128,2048]{1,0:T(8,128)(2,1)S(1)} %pad_maximum_fusion.1.refs_0_), channel_id=1, source_target_pairs={{0,4},{4,0},{8,12},{12,8},{16,20},{20,16},{24,28},{28,24},{32,36},... | collective-permute-start | bytes 1572872 | tf_op jit(solution)/shard_map/ppermute | solution.py:53
  113.2 5.2 %collective-permute-start.32 = (bf16[128,2048]{1,0:T(8,128)(2,1)S(1)}, bf16[128,2048]{1,0:T(8,128)(2,1)S(1)}, u32[]{:S(2)}, u32[]{:S(2)}) collective-permute-start(bf16[128,2048]{1,0:T(8,128)(2,1)S(1)} %constant_dynamic-update-slice_fusion.5.refs_1_), channel_id=1, source_target_pairs={{0,4},{4,0},{8,12},{12,8},{16,20},{20,16},{24,28},{28,24},{32,36},... | collective-permute-start | bytes 1572872 | tf_op jit(solution)/shard_map/ppermute | solution.py:53
  119.9 2.2 %copy-done.5 = bf16[1024,2048]{1,0:T(8,128)(2,1)S(1)} copy-done((bf16[1024,2048]{1,0:T(8,128)(2,1)S(1)}, bf16[1024,2048]{1,0:T(8,128)(2,1)}, u32[]{:S(2)}) %copy-start.5) | copy-done | bytes 4194328
  122.1 5.6 %head_stats.3.refs_3_ = f32[256,128]{1,0:T(8,128)S(1)} custom-call(s32[4,128]{1,0:T(4,128)S(1)} %slice.109.targets_ref, s32[4,128]{1,0:T(4,128)S(1)} %slice.110.owners_ref, bf16[128,2048]{1,0:T(8,128)(2,1)S(1)} %pad_maximum_fusion.1.refs_0_, bf16[128,2048]{1,0:T(8,128)(2,1)S(1)} %constant_dynamic-update-slice_fusion.5.refs_1_, ...), custom_call_target="tpu_custom_call" | custom-call | flops 21474836480 | bytes 6291456 | tf_op jit(solution)/shard_map/head_stats/pallas_call | solution.py:585
  128.0 2.0 %collective-permute-start.33 = (bf16[128,2048]{1,0:T(8,128)(2,1)S(1)}, bf16[128,2048]{1,0:T(8,128)(2,1)S(1)}, u32[]{:S(2)}, u32[]{:S(2)}) collective-permute-start(bf16[128,2048]{1,0:T(8,128)(2,1)S(1)} %collective-permute-done.26.refs_0_), channel_id=1, source_target_pairs={{0,4},{4,0},{8,12},{12,8},{16,20},{20,16},{24,28},{28,24},{32,36},... | collective-permute-start | bytes 1572872 | tf_op jit(solution)/shard_map/ppermute | solution.py:53
  130.0 2.0 %head_stats.4.refs_4_ = f32[256,128]{1,0:T(8,128)S(1)} custom-call(s32[2,128]{1,0:T(2,128)S(1)} %get-tuple-element.76.targets_ref, s32[2,128]{1,0:T(2,128)S(1)} %get-tuple-element.71.owners_ref, bf16[128,2048]{1,0:T(8,128)(2,1)S(1)} %collective-permute-done.26.refs_0_, bf16[128,2048]{1,0:T(8,128)(2,1)S(1)} %collective-permute-done.30.refs_1_, ...), custom_call_target="tpu_custom_call" | custom-call | flops 10737418240 | bytes 5242880 | tf_op jit(solution)/shard_map/head_stats/pallas_call | solution.py:585
  132.3 2.6 %head_stats.5._stats = f32[256,128]{1,0:T(8,128)} custom-call(s32[2,128]{1,0:T(2,128)S(1)} %get-tuple-element.75.targets_ref, s32[2,128]{1,0:T(2,128)S(1)} %get-tuple-element.72.owners_ref, bf16[128,2048]{1,0:T(8,128)(2,1)S(1)} %collective-permute-done.33.refs_0_, bf16[128,2048]{1,0:T(8,128)(2,1)S(1)} %collective-permute-done.34.refs_1_, ...), custom_call_target="tpu_custom_call" | custom-call | flops 10737418240 | bytes 5242880 | tf_op jit(solution)/shard_map/head_stats/pallas_call | solution.py:585
  135.0 4.4 %all-to-all-start.1 = ((f32[32,8,128]{2,1,0:T(8,128)}), f32[32,8,128]{2,1,0:T(8,128)S(1)}, u32[]{:S(2)}, u32[]{:S(2)}) async-start(f32[32,8,128]{2,1,0:T(8,128)} %bitcast.9), calls=%async_computation.1 | async-start | bytes 262144 | tf_op jit(solution)/shard_map/all_to_all | solution.py:705
  139.3 2.1 %unpack.1 = (f32[2,1536,256]{2,1,0:T(8,128)}, bf16[3,2,2048]{2,1,0:T(2,128)(2,1)}) custom-call(bf16[4,2,400,256]{3,2,1,0:T(8,128)(2,1)S(1)} %all-to-all-done.kept_hbm, bf16[16,512]{1,0:T(8,128)(2,1)S(1)} %get-tuple-element.56.bc_ref, f32[256,128]{1,0:T(8,128)} %head_stats.5._stats, bf16[8,128]{1,0:T(8,128)(2,1)S(1)} %slice.126._tip), custom_call_target="tpu_custom_call" | custom-call | flops 1000000 | bytes 20000000 | tf_op jit(solution)/shard_map/unpack/pallas_call | solution.py:253
  141.4 5.5 %all-to-all-done.1 = f32[32,8,128]{2,1,0:T(8,128)S(1)} async-done(((f32[32,8,128]{2,1,0:T(8,128)}), f32[32,8,128]{2,1,0:T(8,128)S(1)}, u32[]{:S(2)}, u32[]{:S(2)}) %all-to-all-start.1) | async-done | bytes 131104 | tf_op jit(solution)/shard_map/all_to_all | solution.py:705
  (152 shorter events, 31.9 us)
Async XLA Ops:
  9.3 6.5 %collective-permute-start = (bf16[64,2048]{1,0:T(8,128)(2,1)}, bf16[64,2048]{1,0:T(8,128)(2,1)S(1)}, u32[]{:S(2)}, u32[]{:S(2)}) collective-permute-start(bf16[64,2048]{1,0:T(8,128)(2,1)} %get-tuple-element.33), channel_id=1, source_target_pairs={{0,3},{1,2},{2,1},{3,0},{4,5},{5,4},{6,7},{7,6},{8,11},{9,10},{10,... | collective-permute-start | bytes 786440 | tf_op jit(solution)/shard_map/ppermute | solution.py:653
  16.9 6.3 %collective-permute-start.1 = (bf16[32,2048]{1,0:T(8,128)(2,1)S(1)}, bf16[32,2048]{1,0:T(8,128)(2,1)S(1)}, u32[]{:S(2)}, u32[]{:S(2)}) collective-permute-start(bf16[32,2048]{1,0:T(8,128)(2,1)S(1)} %add_convert_fusion.9), channel_id=1, source_target_pairs={{0,1},{1,0},{2,3},{3,2},{4,7},{5,6},{6,5},{7,4},{8,9},{9,8},{10,11... | collective-permute-start | bytes 393224 | tf_op jit(solution)/shard_map/ppermute | solution.py:654
  25.9 5.2 %collective-permute-start.4 = (bf16[32,2048]{1,0:T(8,128)(2,1)S(1)}, bf16[32,2048]{1,0:T(8,128)(2,1)S(1)}, u32[]{:S(2)}, u32[]{:S(2)}) collective-permute-start(bf16[32,2048]{1,0:T(8,128)(2,1)S(1)} %fusion.5), channel_id=1, source_target_pairs={{0,24},{4,100},{8,16},{12,108},{16,8},{20,116},{24,0},{28,124},{32... | collective-permute-start | bytes 393224 | tf_op jit(solution)/shard_map/ppermute | solution.py:49
  27.8 5.3 %collective-permute-start.5 = (bf16[32,2048]{1,0:T(8,128)(2,1)S(1)}, bf16[32,2048]{1,0:T(8,128)(2,1)S(1)}, u32[]{:S(2)}, u32[]{:S(2)}) collective-permute-start(bf16[32,2048]{1,0:T(8,128)(2,1)S(1)} %fusion.5), channel_id=1, source_target_pairs={{0,16},{4,68},{8,24},{12,76},{16,0},{20,84},{24,8},{28,92},{32,48}... | collective-permute-start | bytes 393224 | tf_op jit(solution)/shard_map/ppermute | solution.py:49
  28.6 7.1 %collective-permute-start.3 = (bf16[64,2048]{1,0:T(8,128)(2,1)S(1)}, bf16[64,2048]{1,0:T(8,128)(2,1)S(1)}, u32[]{:S(2)}, u32[]{:S(2)}) collective-permute-start(bf16[64,2048]{1,0:T(8,128)(2,1)S(1)} %pad_maximum_fusion.2), channel_id=1, source_target_pairs={{0,32},{4,12},{8,40},{12,4},{16,48},{20,28},{24,56},{28,20},{32,0}... | collective-permute-start | bytes 786440 | tf_op jit(solution)/shard_map/ppermute | solution.py:49
  33.1 8.8 %collective-permute-start.6 = (bf16[64,2048]{1,0:T(8,128)(2,1)S(1)}, bf16[64,2048]{1,0:T(8,128)(2,1)S(1)}, u32[]{:S(2)}, u32[]{:S(2)}) collective-permute-start(bf16[64,2048]{1,0:T(8,128)(2,1)S(1)} %pad_maximum_fusion.3), channel_id=1, source_target_pairs={{0,96},{4,28},{8,104},{12,20},{16,112},{20,12},{24,120},{28,4},{32... | collective-permute-start | bytes 786440 | tf_op jit(solution)/shard_map/ppermute | solution.py:49
  35.8 14.8 %collective-permute-start.10 = (bf16[128,2048]{1,0:T(8,128)(2,1)S(1)}, bf16[128,2048]{1,0:T(8,128)(2,1)S(1)}, u32[]{:S(2)}, u32[]{:S(2)}) collective-permute-start(bf16[128,2048]{1,0:T(8,128)(2,1)S(1)} %pad_maximum_fusion.first_ref), channel_id=1, source_target_pairs={{0,96},{4,28},{8,104},{12,20},{16,112},{20,12},{24,120},{28,4},{32... | collective-permute-start | bytes 1572872 | tf_op jit(solution)/shard_map/ppermute | solution.py:49
  38.2 17.2 %collective-permute-start.7 = (bf16[128,2048]{1,0:T(8,128)(2,1)S(1)}, bf16[128,2048]{1,0:T(8,128)(2,1)S(1)}, u32[]{:S(2)}, u32[]{:S(2)}) collective-permute-start(bf16[128,2048]{1,0:T(8,128)(2,1)S(1)} %pad_maximum_fusion.first_ref), channel_id=1, source_target_pairs={{0,4},{4,0},{8,12},{12,8},{16,20},{20,16},{24,28},{28,24},{32,36},... | collective-permute-start | bytes 1572872 | tf_op jit(solution)/shard_map/ppermute | solution.py:53
  42.0 10.1 %collective-permute-start.11 = (bf16[128,2048]{1,0:T(8,128)(2,1)S(1)}, bf16[128,2048]{1,0:T(8,128)(2,1)S(1)}, u32[]{:S(2)}, u32[]{:S(2)}) collective-permute-start(bf16[128,2048]{1,0:T(8,128)(2,1)S(1)} %constant_dynamic-update-slice_fusion.second_ref), channel_id=1, source_target_pairs={{0,32},{4,12},{8,40},{12,4},{16,48},{20,28},{24,56},{28,20},{32,0}... | collective-permute-start | bytes 1572872 | tf_op jit(solution)/shard_map/ppermute | solution.py:49
  43.2 12.2 %collective-permute-start.8 = (bf16[128,2048]{1,0:T(8,128)(2,1)S(1)}, bf16[128,2048]{1,0:T(8,128)(2,1)S(1)}, u32[]{:S(2)}, u32[]{:S(2)}) collective-permute-start(bf16[128,2048]{1,0:T(8,128)(2,1)S(1)} %constant_dynamic-update-slice_fusion.second_ref), channel_id=1, source_target_pairs={{0,4},{4,0},{8,12},{12,8},{16,20},{20,16},{24,28},{28,24},{32,36},... | collective-permute-start | bytes 1572872 | tf_op jit(solution)/shard_map/ppermute | solution.py:53
  50.6 6.7 %collective-permute-start.12 = (bf16[128,2048]{1,0:T(8,128)(2,1)S(1)}, bf16[128,2048]{1,0:T(8,128)(2,1)S(1)}, u32[]{:S(2)}, u32[]{:S(2)}) collective-permute-start(bf16[128,2048]{1,0:T(8,128)(2,1)S(1)} %collective-permute-done.10.first_ref), channel_id=1, source_target_pairs={{0,4},{4,0},{8,12},{12,8},{16,20},{20,16},{24,28},{28,24},{32,36},... | collective-permute-start | bytes 1572872 | tf_op jit(solution)/shard_map/ppermute | solution.py:53
  52.1 5.2 %collective-permute-start.13 = (bf16[128,2048]{1,0:T(8,128)(2,1)S(1)}, bf16[128,2048]{1,0:T(8,128)(2,1)S(1)}, u32[]{:S(2)}, u32[]{:S(2)}) collective-permute-start(bf16[128,2048]{1,0:T(8,128)(2,1)S(1)} %collective-permute-done.11.second_ref), channel_id=1, source_target_pairs={{0,4},{4,0},{8,12},{12,8},{16,20},{20,16},{24,28},{28,24},{32,36},... | collective-permute-start | bytes 1572872 | tf_op jit(solution)/shard_map/ppermute | solution.py:53
  56.7 6.3 %collective-permute-start.18 = (bf16[128,2048]{1,0:T(8,128)(2,1)S(1)}, bf16[128,2048]{1,0:T(8,128)(2,1)S(1)}, u32[]{:S(2)}, u32[]{:S(2)}) collective-permute-start(bf16[128,2048]{1,0:T(8,128)(2,1)S(1)} %get-tuple-element.39), channel_id=1, source_target_pairs={{0,4},{4,0},{8,12},{12,8},{16,20},{20,16},{24,28},{28,24},{32,36},... | collective-permute-start | bytes 1572872 | tf_op jit(solution)/shard_map/ppermute | solution.py:53
  56.8 13.4 %collective-permute-start.9 = (bf16[128,2048]{1,0:T(8,128)(2,1)S(1)}, bf16[128,2048]{1,0:T(8,128)(2,1)S(1)}, u32[]{:S(2)}, u32[]{:S(2)}) collective-permute-start(bf16[128,2048]{1,0:T(8,128)(2,1)S(1)} %get-tuple-element.35), channel_id=1, source_target_pairs={{0,4},{4,0},{8,12},{12,8},{16,20},{20,16},{24,28},{28,24},{32,36},... | collective-permute-start | bytes 1572872 | tf_op jit(solution)/shard_map/ppermute | solution.py:53
  60.8 8.4 %collective-permute-start.20 = (bf16[128,2048]{1,0:T(8,128)(2,1)S(1)}, bf16[128,2048]{1,0:T(8,128)(2,1)S(1)}, u32[]{:S(2)}, u32[]{:S(2)}) collective-permute-start(bf16[128,2048]{1,0:T(8,128)(2,1)S(1)} %add_convert_fusion.1), channel_id=1, source_target_pairs={{0,32},{4,12},{8,40},{12,4},{16,48},{20,28},{24,56},{28,20},{32,0}... | collective-permute-start | bytes 1572872 | tf_op jit(solution)/shard_map/ppermute | solution.py:49
  61.5 9.6 %collective-permute-start.15 = (bf16[128,2048]{1,0:T(8,128)(2,1)S(1)}, bf16[128,2048]{1,0:T(8,128)(2,1)S(1)}, u32[]{:S(2)}, u32[]{:S(2)}) collective-permute-start(bf16[128,2048]{1,0:T(8,128)(2,1)S(1)} %add_convert_fusion.4), channel_id=1, source_target_pairs={{0,96},{4,28},{8,104},{12,20},{16,112},{20,12},{24,120},{28,4},{32... | collective-permute-start | bytes 1572872 | tf_op jit(solution)/shard_map/ppermute | solution.py:49
  70.1 6.9 %collective-permute-start.21 = (bf16[64,2048]{1,0:T(8,128)(2,1)}, bf16[64,2048]{1,0:T(8,128)(2,1)S(1)}, u32[]{:S(2)}, u32[]{:S(2)}) collective-permute-start(bf16[64,2048]{1,0:T(8,128)(2,1)} %slice.123), channel_id=1, source_target_pairs={{0,96},{4,28},{8,104},{12,20},{16,112},{20,12},{24,120},{28,4},{32... | collective-permute-start | bytes 786440 | tf_op jit(solution)/shard_map/ppermute | solution.py:49
  72.1 8.4 %collective-permute-start.16 = (bf16[64,2048]{1,0:T(8,128)(2,1)}, bf16[64,2048]{1,0:T(8,128)(2,1)S(1)}, u32[]{:S(2)}, u32[]{:S(2)}) collective-permute-start(bf16[64,2048]{1,0:T(8,128)(2,1)} %slice.119), channel_id=1, source_target_pairs={{0,32},{4,12},{8,40},{12,4},{16,48},{20,28},{24,56},{28,20},{32,0}... | collective-permute-start | bytes 786440 | tf_op jit(solution)/shard_map/ppermute | solution.py:49
  72.1 22.5 %all-to-all-start = ((bf16[4,2,400,256]{3,2,1,0:T(8,128)(2,1)}), bf16[4,2,400,256]{3,2,1,0:T(8,128)(2,1)S(1)}, u32[]{:S(2)}, u32[]{:S(2)}) async-start(bf16[4,2,400,256]{3,2,1,0:T(8,128)(2,1)} %bitcast.7), calls=%async_computation | async-start | bytes 3276800 | tf_op jit(solution)/shard_map/all_to_all | solution.py:684
  77.8 5.5 %collective-permute-start.23 = (bf16[32,2048]{1,0:T(8,128)(2,1)}, bf16[32,2048]{1,0:T(8,128)(2,1)S(1)}, u32[]{:S(2)}, u32[]{:S(2)}) collective-permute-start(bf16[32,2048]{1,0:T(8,128)(2,1)} %get-tuple-element.67), channel_id=1, source_target_pairs={{0,16},{4,68},{8,24},{12,76},{16,0},{20,84},{24,8},{28,92},{32,48}... | collective-permute-start | bytes 393224 | tf_op jit(solution)/shard_map/ppermute | solution.py:49
  79.7 5.4 %collective-permute-start.22 = (bf16[32,2048]{1,0:T(8,128)(2,1)S(1)}, bf16[32,2048]{1,0:T(8,128)(2,1)S(1)}, u32[]{:S(2)}, u32[]{:S(2)}) collective-permute-start(bf16[32,2048]{1,0:T(8,128)(2,1)S(1)} %get-tuple-element.66), channel_id=1, source_target_pairs={{0,24},{4,100},{8,16},{12,108},{16,8},{20,116},{24,0},{28,124},{32... | collective-permute-start | bytes 393224 | tf_op jit(solution)/shard_map/ppermute | solution.py:49
  80.6 4.8 %collective-permute-start.17 = (bf16[32,2048]{1,0:T(8,128)(2,1)S(1)}, bf16[32,2048]{1,0:T(8,128)(2,1)S(1)}, u32[]{:S(2)}, u32[]{:S(2)}) collective-permute-start(bf16[32,2048]{1,0:T(8,128)(2,1)S(1)} %slice.121), channel_id=1, source_target_pairs={{0,8},{4,36},{8,0},{12,44},{16,24},{20,52},{24,16},{28,60},{32,40}... | collective-permute-start | bytes 393224 | tf_op jit(solution)/shard_map/ppermute | solution.py:49
  94.7 5.8 %collective-permute-start.24 = (bf16[32,2048]{1,0:T(8,128)(2,1)S(1)}, bf16[32,2048]{1,0:T(8,128)(2,1)S(1)}, u32[]{:S(2)}, u32[]{:S(2)}) collective-permute-start(bf16[32,2048]{1,0:T(8,128)(2,1)S(1)} %fusion.2), channel_id=1, source_target_pairs={{0,8},{4,36},{8,0},{12,44},{16,24},{20,52},{24,16},{28,60},{32,40}... | collective-permute-start | bytes 393224 | tf_op jit(solution)/shard_map/ppermute | solution.py:49
  94.8 8.9 %collective-permute-start.27 = (bf16[32,2048]{1,0:T(8,128)(2,1)S(1)}, bf16[32,2048]{1,0:T(8,128)(2,1)S(1)}, u32[]{:S(2)}, u32[]{:S(2)}) collective-permute-start(bf16[32,2048]{1,0:T(8,128)(2,1)S(1)} %fusion.2), channel_id=1, source_target_pairs={{0,24},{4,100},{8,16},{12,108},{16,8},{20,116},{24,0},{28,124},{32... | collective-permute-start | bytes 393224 | tf_op jit(solution)/shard_map/ppermute | solution.py:49
  99.4 5.3 %collective-permute-start.28 = (bf16[32,2048]{1,0:T(8,128)(2,1)S(1)}, bf16[32,2048]{1,0:T(8,128)(2,1)S(1)}, u32[]{:S(2)}, u32[]{:S(2)}) collective-permute-start(bf16[32,2048]{1,0:T(8,128)(2,1)S(1)} %fusion.2), channel_id=1, source_target_pairs={{0,16},{4,68},{8,24},{12,76},{16,0},{20,84},{24,8},{28,92},{32,48}... | collective-permute-start | bytes 393224 | tf_op jit(solution)/shard_map/ppermute | solution.py:49
  100.5 8.7 %collective-permute-start.25 = (bf16[64,2048]{1,0:T(8,128)(2,1)S(1)}, bf16[64,2048]{1,0:T(8,128)(2,1)S(1)}, u32[]{:S(2)}, u32[]{:S(2)}) collective-permute-start(bf16[64,2048]{1,0:T(8,128)(2,1)S(1)} %pad_maximum_fusion.4), channel_id=1, source_target_pairs={{0,32},{4,12},{8,40},{12,4},{16,48},{20,28},{24,56},{28,20},{32,0}... | collective-permute-start | bytes 786440 | tf_op jit(solution)/shard_map/ppermute | solution.py:49
  104.7 8.5 %collective-permute-start.29 = (bf16[64,2048]{1,0:T(8,128)(2,1)S(1)}, bf16[64,2048]{1,0:T(8,128)(2,1)S(1)}, u32[]{:S(2)}, u32[]{:S(2)}) collective-permute-start(bf16[64,2048]{1,0:T(8,128)(2,1)S(1)} %pad_maximum_fusion.5), channel_id=1, source_target_pairs={{0,96},{4,28},{8,104},{12,20},{16,112},{20,12},{24,120},{28,4},{32... | collective-permute-start | bytes 786440 | tf_op jit(solution)/shard_map/ppermute | solution.py:49
  109.2 10.3 %collective-permute-start.31 = (bf16[128,2048]{1,0:T(8,128)(2,1)S(1)}, bf16[128,2048]{1,0:T(8,128)(2,1)S(1)}, u32[]{:S(2)}, u32[]{:S(2)}) collective-permute-start(bf16[128,2048]{1,0:T(8,128)(2,1)S(1)} %pad_maximum_fusion.1.refs_0_), channel_id=1, source_target_pairs={{0,4},{4,0},{8,12},{12,8},{16,20},{20,16},{24,28},{28,24},{32,36},... | collective-permute-start | bytes 1572872 | tf_op jit(solution)/shard_map/ppermute | solution.py:53
  113.2 6.7 %collective-permute-start.32 = (bf16[128,2048]{1,0:T(8,128)(2,1)S(1)}, bf16[128,2048]{1,0:T(8,128)(2,1)S(1)}, u32[]{:S(2)}, u32[]{:S(2)}) collective-permute-start(bf16[128,2048]{1,0:T(8,128)(2,1)S(1)} %constant_dynamic-update-slice_fusion.5.refs_1_), channel_id=1, source_target_pairs={{0,4},{4,0},{8,12},{12,8},{16,20},{20,16},{24,28},{28,24},{32,36},... | collective-permute-start | bytes 1572872 | tf_op jit(solution)/shard_map/ppermute | solution.py:53
  118.4 9.6 %collective-permute-start.26 = (bf16[128,2048]{1,0:T(8,128)(2,1)S(1)}, bf16[128,2048]{1,0:T(8,128)(2,1)S(1)}, u32[]{:S(2)}, u32[]{:S(2)}) collective-permute-start(bf16[128,2048]{1,0:T(8,128)(2,1)S(1)} %pad_maximum_fusion.1.refs_0_), channel_id=1, source_target_pairs={{0,96},{4,28},{8,104},{12,20},{16,112},{20,12},{24,120},{28,4},{32... | collective-permute-start | bytes 1572872 | tf_op jit(solution)/shard_map/ppermute | solution.py:49
  119.5 8.5 %collective-permute-start.30 = (bf16[128,2048]{1,0:T(8,128)(2,1)S(1)}, bf16[128,2048]{1,0:T(8,128)(2,1)S(1)}, u32[]{:S(2)}, u32[]{:S(2)}) collective-permute-start(bf16[128,2048]{1,0:T(8,128)(2,1)S(1)} %constant_dynamic-update-slice_fusion.5.refs_1_), channel_id=1, source_target_pairs={{0,32},{4,12},{8,40},{12,4},{16,48},{20,28},{24,56},{28,20},{32,0}... | collective-permute-start | bytes 1572872 | tf_op jit(solution)/shard_map/ppermute | solution.py:49
  135.0 12.0 %all-to-all-start.1 = ((f32[32,8,128]{2,1,0:T(8,128)}), f32[32,8,128]{2,1,0:T(8,128)S(1)}, u32[]{:S(2)}, u32[]{:S(2)}) async-start(f32[32,8,128]{2,1,0:T(8,128)} %bitcast.9), calls=%async_computation.1 | async-start | bytes 262144 | tf_op jit(solution)/shard_map/all_to_all | solution.py:705
  (27 other events, 442.3 us)

commit v4 on v3

--- a/solution.py
+++ b/solution.py
@@ -72,7 +72,6 @@
     came = [swap_core(part) for part in early[1]]
     held = [added(early[0][s], came[s]) for s in range(2)]
     held = [added(held[s], late[s]) for s in range(2)]
-    tip = held[1][:8, :128]
     half = held[0].shape[0] // 2
     came = [hop(held[s][half:], 1, EDGES[s][0]) for s in range(2)]
     held = [added(held[s][:half], came[s]) for s in range(2)]
@@ -80,7 +79,7 @@
     blocks = (held[0][half:], held[1][:half], held[1][half:])
     came = [hop(block, 0, flip) for block, flip in zip(blocks, DIRECT, strict=True)]
     total = held[0][:half].astype(jnp.float32)
-    return sum((part.astype(jnp.float32) for part in came), total), tip
+    return sum((part.astype(jnp.float32) for part in came), total)
 
 
 def block_table():
@@ -269,8 +268,9 @@
 
 def mixer_kernel(*refs):
     sources, refs = refs[:22], refs[22:]
-    far_ref, near_ref, decay_ref, scaled_ref, b_ref, in_x_ref, in_bc_ref = refs[:7]
-    held, (mixed_scr, lanes_scr, sems) = refs[7:-3], refs[-3:]
+    part_refs = refs[:SIDE]
+    decay_ref, scaled_ref, b_ref, in_x_ref, in_bc_ref = refs[SIDE : SIDE + 5]
+    held, (mixed_scr, lanes_scr, sems) = refs[SIDE + 5 : -3], refs[-3:]
     member_ref, accepted_ref, lengths_ref, rate_ref, bias_ref, skip_ref = held[:6]
     hidden_ref, gain_ref, w_dt_ref, conv_x_ref, conv_bc_ref, past_x_ref, past_bc_ref = held[6:13]
     w_query, w_kv, prompt, w_x, w_bc, w_z, state, w_out = held[13:]
@@ -280,7 +280,6 @@
     heads = inner // SSM_DIM
     query_width = w_query.shape[1]
     rank = lax.axis_index("mdl")
-    core = lax.axis_index("req") % CORES
     group = rank * (query_width // HEAD_DIM) // (Q_HEADS // KV_HEADS)
     query_hbm, kv_hbm, prompt_hbm, x_hbm, bc_hbm, z_hbm, state_hbm, attn_hbm, mamba_hbm = sources[13:]
     moves = [(source, target) for source, target in zip(sources[:13], held[:13], strict=True)]
@@ -440,17 +439,16 @@
     own_rows = tokens // SIDE
     copies[8].wait()
     copies[9].wait()
-    first_flip = jnp.where(core == 0, 3, 1)
-    for out_ref, flips in ((far_ref, (first_flip, 2)), (near_ref, (0, first_flip ^ 2))):
-        rows = jnp.concatenate(
-            [
-                mixed_scr[pl.ds(pl.multiple_of((rank ^ flip) * own_rows, own_rows), own_rows), :]
-                for flip in flips
-            ],
-            axis=0,
-        )
-        out_ref[...] = dot32(rows, w_out[...]).astype(jnp.bfloat16)
-
+    rows = jnp.concatenate(
+        [
+            mixed_scr[pl.ds(pl.multiple_of((rank ^ flip) * own_rows, own_rows), own_rows), :]
+            for flip in (0, *DIRECT)
+        ],
+        axis=0,
+    )
+    parts = dot32(rows, w_out[...]).astype(jnp.bfloat16)
+    for block, part_ref in enumerate(part_refs):
+        part_ref[...] = parts[block * own_rows : (block + 1) * own_rows]
     decay_ref[...] = log_decay
     scaled_ref[...] = scaled_x
     b_ref[...] = b_part
@@ -473,11 +471,10 @@
     ]
     scalars = [member, accepted, prompt_lengths, ssm_rate, dt_bias, skip_d]
     whole = pl.BlockSpec(memory_space=pltpu.VMEM)
-    far, near, *series = pl.pallas_call(
+    outs = pl.pallas_call(
         mixer_kernel,
         out_shape=[
-            jax.ShapeDtypeStruct((tokens // 2, width), bf16),
-            jax.ShapeDtypeStruct((tokens // 2, width), bf16),
+            *([jax.ShapeDtypeStruct((tokens // SIDE, width), bf16)] * SIDE),
             jax.ShapeDtypeStruct((tokens, 128), jnp.float32),
             jax.ShapeDtypeStruct((tokens, inner), jnp.float32),
             jax.ShapeDtypeStruct((tokens, STATE), bf16),
@@ -485,7 +482,7 @@
             jax.ShapeDtypeStruct((tokens, 2 * STATE), bf16),
         ],
         in_specs=[pl.BlockSpec(memory_space=pltpu.HBM)] * 22,
-        out_specs=[whole] * 7,
+        out_specs=[whole] * (SIDE + 5),
         scratch_shapes=[
             *(pltpu.SMEM(a.shape, a.dtype) for a in scalars),
             *(pltpu.VMEM(a.shape, a.dtype) for a in small),
@@ -509,7 +506,7 @@
     )(
         *scalars, *small, w_query, w_kv, prompt_kv, w_x, w_bc, w_z, state, w_attn_out, w_mamba_out
     )
-    return far, near, *keeper(member, accepted, *series, *small[-2:], state)
+    return outs[:SIDE], *keeper(member, accepted, *outs[SIDE:], *small[-2:], state)
 
 
 def feed_kernel(first_ref, second_ref, both_ref, down_ref, first_out, second_out):
@@ -595,14 +592,6 @@
         ),
         name="head_stats",
     )(targets, owners, *rows, head_weight, *others)
-
-
-def mdl_pairs(step):
-    pairs = []
-    for device in range(SIDE * SIDE * CORES):
-        flip = (3, 1)[(device + step) % 2]
-        pairs += [(device * SIDE + z, device * SIDE + (z ^ flip)) for z in range(SIDE)]
-    return pairs
 
 
 def shards(
@@ -646,17 +635,15 @@
     own_tokens = own_reqs * draft_len
     flat_rows = hidden_in.reshape(row_tokens, width)
     local_inner = w_x.shape[1]
-    far, near, kept, own_bc = mixer(
+    parts, kept, own_bc = mixer(
         flat_rows, mixer_gain, w_query, w_kv, w_attn_out, prompt_kv, prompt_lengths, member, accepted, w_z, w_x, w_bc,
         w_dt, conv_x, conv_bc, ssm_rate, dt_bias, skip_d, prompt_state, prompt_conv_x, prompt_conv_bc, w_mamba_out,
     )
-    came = lax.ppermute(far, ("req", "mdl"), mdl_pairs(0))
-    last = lax.ppermute(added(near[own_tokens:], came[own_tokens:]), ("req", "mdl"), mdl_pairs(1))
-    mixed = (
-        near[:own_tokens].astype(jnp.float32)
-        + came[:own_tokens].astype(jnp.float32)
-        + last.astype(jnp.float32)
-    )
+    came = [
+        lax.ppermute(part, "mdl", [(z, z ^ flip) for z in range(SIDE)])
+        for part, flip in zip(parts[1:], DIRECT, strict=True)
+    ]
+    mixed = sum((part.astype(jnp.float32) for part in came), parts[0].astype(jnp.float32))
     own_rows = lax.dynamic_slice_in_dim(flat_rows, mdl_rank * own_tokens, own_tokens, 0)
     after_mixer = (own_rows.astype(jnp.float32) + mixed).astype(jnp.bfloat16)
     prepared = rms_scale(after_mixer, mlp_gain).astype(jnp.bfloat16)
@@ -679,7 +666,8 @@
 
     early_parts = [feed(*rows, w_both, w_down) for rows in early]
     late_parts = [feed(*rows, w_both, w_down) for rows in late]
-    summed, tip = scatter_rows(early_parts, late_parts)
+    summed = scatter_rows(early_parts, late_parts)
+    tip = early_parts[0][0][:8, :128]
     kept, tip = lax.optimization_barrier((kept, tip))
     kept_out = lax.all_to_all(
         kept.reshape(mdl_count, own_reqs, local_inner + 16, STATE),

time: 148 us -> 137 us (0.926)
  starting transfers between devices: 68.4 us -> 61.3 us
  waiting for transfers between devices: 37.5 us -> 33.1 us
  local copies, waits for them, and re-layouts: 5.93 us -> 2.34 us
  other arithmetic: 4.92 us -> 8.07 us
    all_to_all x1, waiting for transfers between devices: 8.96 us -> 4.13 us  [shards(): lax.all_to_all(kept.reshape(mdl_count, own_reqs, local_inner + 16, STATE)...]
    ppermute x12, starting transfers between devices: 24.3 us -> 19.6 us  [swap_core(): return lax.ppermute(part, 'req', CORE_PAIRS)]
    convert_element_type x7 -> x6, other arithmetic: 1.81 us -> 4.83 us  [added(): (left.astype(jnp.float32) + right.astype(jnp.float32)).astype(jnp.bfloat16)]
    unnamed x47 -> x45, local copies, waits for them, and re-layouts: 2.43 us -> 0.24 us
    ppermute x21, starting transfers between devices: 28.9 us -> 27.3 us  [hop(): return lax.ppermute(part, 'req', flip_pairs(ring, flip))]
    ppermute x2 -> x3, starting transfers between devices: 6.5 us -> 5.24 us  [shards(): lax.ppermute(part, 'mdl', [(z, z ^ flip) for z in range(SIDE)])]
    ppermute x2 -> x3, waiting for transfers between devices: 5.13 us -> 4.81 us  [shards(): lax.ppermute(part, 'mdl', [(z, z ^ flip) for z in range(SIDE)])]
  transfers between devices with their start and end apart: 37 -> 38, of which waited for: 19 -> 16; matrix products, arithmetic and copies ran while one was open for 4% -> 6% of each run, Pallas kernels for 12% -> 14%
where the time goes in v4:
time: 137 us; the launch traced here: 136 us
  starting transfers between devices  61.3 us (45%)
  waiting for transfers between devices  33.1 us (24%)
  Pallas kernels  30.2 us (22%)
  other arithmetic  8.07 us (6%)
  local copies, waits for them, and re-layouts  2.34 us (2%)
    ppermute x21, starting transfers between devices, hop(): return lax.ppermute(part, 'req', flip_pairs(ring, flip))  27.3 us
    ppermute x12, starting transfers between devices, swap_core(): return lax.ppermute(part, 'req', CORE_PAIRS)  19.6 us
    ppermute x21, waiting for transfers between devices, hop(): return lax.ppermute(part, 'req', flip_pairs(ring, flip))  17.8 us
    pallas_call x3, Pallas kernels, head_stats(): pl.pallas_call(head_kernel, out_shape=jax.ShapeDtypeStruct((devices * 8,...  10.2 us
    pallas_call x1, Pallas kernels, mixer(): pl.pallas_call(mixer_kernel, out_shape=[*[jax.ShapeDtypeStruct((tokens //...  8.3 us
    pallas_call x4, Pallas kernels, feed(): pl.pallas_call(feed_kernel, out_shape=[jax.ShapeDtypeStruct((rows, width)...  5.98 us
    all_to_all x1, starting transfers between devices, shards(): lax.all_to_all(stats, 'req', split_axis=0, concat_axis=0, tiled=True)  5.57 us
    all_to_all x1, waiting for transfers between devices, shards(): lax.all_to_all(stats, 'req', split_axis=0, concat_axis=0, tiled=True)  5.55 us
  transfers between devices with their start and end apart: 38, of which 16 were waited for; matrix products, arithmetic and copies ran while one was open for 6% of the time, Pallas kernels for 14%

profile of v4, /device:TPU:1, one launch (start us, length us, event | category | flops | bytes accessed | tf_op | source)
XLA Modules:
  0.0 136.4 jit_solution(7201139581436076512)
XLA Ops:
  0.7 8.3 %mixer.1 = (bf16[32,2048]{1,0:T(8,128)(2,1)}, bf16[32,2048]{1,0:T(8,128)(2,1)}, bf16[32,2048]{1,0:T(8,128)(2,1)}, bf16[32,2048]{1,0:T(8,128)(2,1)}, f32[128,128]...) custom-call(s32[8]{0:T(128)} %refs_0_.3, ...), custom_call_target="tpu_custom_call" | custom-call | flops 3000000000 | bytes 20000000 | tf_op jit(solution)/shard_map/mixer/pallas_call | solution.py:474
  9.0 4.5 %collective-permute-start.2 = (bf16[32,2048]{1,0:T(8,128)(2,1)}, bf16[32,2048]{1,0:T(8,128)(2,1)S(1)}, u32[]{:S(2)}, u32[]{:S(2)}) collective-permute-start(bf16[32,2048]{1,0:T(8,128)(2,1)} %get-tuple-element.37), channel_id=1, source_target_pairs={{0,2},{1,3},{2,0},{3,1},{4,6},{5,7},{6,4},{7,5},{8,10},{9,11},{10,... | collective-permute-start | bytes 393224 | tf_op jit(solution)/shard_map/ppermute | solution.py:643
  15.4 1.5 %collective-permute-done.2 = bf16[32,2048]{1,0:T(8,128)(2,1)S(1)} collective-permute-done((bf16[32,2048]{1,0:T(8,128)(2,1)}, bf16[32,2048]{1,0:T(8,128)(2,1)S(1)}, u32[]{:S(2)}, u32[]{:S(2)}) %collective-permute-start.2) | collective-permute-done | bytes 131104 | tf_op jit(solution)/shard_map/ppermute | solution.py:643
  16.9 3.3 %collective-permute-done.1 = bf16[32,2048]{1,0:T(8,128)(2,1)S(1)} collective-permute-done((bf16[32,2048]{1,0:T(8,128)(2,1)}, bf16[32,2048]{1,0:T(8,128)(2,1)S(1)}, u32[]{:S(2)}, u32[]{:S(2)}) %collective-permute-start.1) | collective-permute-done | bytes 131104 | tf_op jit(solution)/shard_map/ppermute | solution.py:643
  23.1 1.9 %collective-permute-start.5 = (bf16[32,2048]{1,0:T(8,128)(2,1)S(1)}, bf16[32,2048]{1,0:T(8,128)(2,1)S(1)}, u32[]{:S(2)}, u32[]{:S(2)}) collective-permute-start(bf16[32,2048]{1,0:T(8,128)(2,1)S(1)} %fusion.5), channel_id=1, source_target_pairs={{0,24},{4,100},{8,16},{12,108},{16,8},{20,116},{24,0},{28,124},{32... | collective-permute-start | bytes 393224 | tf_op jit(solution)/shard_map/ppermute | solution.py:49
  28.3 2.0 %collective-permute-done.6 = bf16[32,2048]{1,0:T(8,128)(2,1)S(1)} collective-permute-done((bf16[32,2048]{1,0:T(8,128)(2,1)S(1)}, bf16[32,2048]{1,0:T(8,128)(2,1)S(1)}, u32[]{:S(2)}, u32[]{:S(2)}) %collective-permute-start.6) | collective-permute-done | bytes 131104 | tf_op jit(solution)/shard_map/ppermute | solution.py:49
  30.3 2.9 %collective-permute-start.7 = (bf16[64,2048]{1,0:T(8,128)(2,1)S(1)}, bf16[64,2048]{1,0:T(8,128)(2,1)S(1)}, u32[]{:S(2)}, u32[]{:S(2)}) collective-permute-start(bf16[64,2048]{1,0:T(8,128)(2,1)S(1)} %pad_maximum_fusion.3), channel_id=1, source_target_pairs={{0,96},{4,28},{8,104},{12,20},{16,112},{20,12},{24,120},{28,4},{32... | collective-permute-start | bytes 786440 | tf_op jit(solution)/shard_map/ppermute | solution.py:49
  33.3 2.1 %collective-permute-start.11 = (bf16[128,2048]{1,0:T(8,128)(2,1)S(1)}, bf16[128,2048]{1,0:T(8,128)(2,1)S(1)}, u32[]{:S(2)}, u32[]{:S(2)}) collective-permute-start(bf16[128,2048]{1,0:T(8,128)(2,1)S(1)} %pad_maximum_fusion.first_ref), channel_id=1, source_target_pairs={{0,96},{4,28},{8,104},{12,20},{16,112},{20,12},{24,120},{28,4},{32... | collective-permute-start | bytes 1572872 | tf_op jit(solution)/shard_map/ppermute | solution.py:49
  35.4 2.8 %collective-permute-start.8 = (bf16[128,2048]{1,0:T(8,128)(2,1)S(1)}, bf16[128,2048]{1,0:T(8,128)(2,1)S(1)}, u32[]{:S(2)}, u32[]{:S(2)}) collective-permute-start(bf16[128,2048]{1,0:T(8,128)(2,1)S(1)} %pad_maximum_fusion.first_ref), channel_id=1, source_target_pairs={{0,4},{4,0},{8,12},{12,8},{16,20},{20,16},{24,28},{28,24},{32,36},... | collective-permute-start | bytes 1572872 | tf_op jit(solution)/shard_map/ppermute | solution.py:53
  39.2 3.7 %collective-permute-start.9 = (bf16[128,2048]{1,0:T(8,128)(2,1)S(1)}, bf16[128,2048]{1,0:T(8,128)(2,1)S(1)}, u32[]{:S(2)}, u32[]{:S(2)}) collective-permute-start(bf16[128,2048]{1,0:T(8,128)(2,1)S(1)} %constant_dynamic-update-slice_fusion.second_ref), channel_id=1, source_target_pairs={{0,4},{4,0},{8,12},{12,8},{16,20},{20,16},{24,28},{28,24},{32,36},... | collective-permute-start | bytes 1572872 | tf_op jit(solution)/shard_map/ppermute | solution.py:53
  43.0 3.6 %keeper.1 = (bf16[8,400,256]{2,1,0:T(8,128)(2,1)}, bf16[16,512]{1,0:T(8,128)(2,1)S(1)}) custom-call(s32[8]{0:T(128)S(1)} %copy-done.3, s32[8]{0:T(128)S(1)} %copy-done.4, f32[128,128]{1,0:T(8,128)S(1)} %copy-done.10, f32[128,384]{1,0:T(8,128)S(1)} %copy-done.7, bf16[128,256]{1,0:T(8,128)(2,1)S(1)} %copy-done.11, bf16[128,384]{1,0:T(8,128)(2,1)S(1)} %copy-done.9, ...), custom_call_target="tpu_custom_call" | custom-call | flops 2000000000 | bytes 5000000 | tf_op jit(solution)/shard_map/keeper/pallas_call | solution.py:205
  46.9 1.5 %collective-permute-start.13 = (bf16[128,2048]{1,0:T(8,128)(2,1)S(1)}, bf16[128,2048]{1,0:T(8,128)(2,1)S(1)}, u32[]{:S(2)}, u32[]{:S(2)}) collective-permute-start(bf16[128,2048]{1,0:T(8,128)(2,1)S(1)} %collective-permute-done.11.first_ref), channel_id=1, source_target_pairs={{0,4},{4,0},{8,12},{12,8},{16,20},{20,16},{24,28},{28,24},{32,36},... | collective-permute-start | bytes 1572872 | tf_op jit(solution)/shard_map/ppermute | solution.py:53
  48.4 3.2 %collective-permute-start.14 = (bf16[128,2048]{1,0:T(8,128)(2,1)S(1)}, bf16[128,2048]{1,0:T(8,128)(2,1)S(1)}, u32[]{:S(2)}, u32[]{:S(2)}) collective-permute-start(bf16[128,2048]{1,0:T(8,128)(2,1)S(1)} %collective-permute-done.12.second_ref), channel_id=1, source_target_pairs={{0,4},{4,0},{8,12},{12,8},{16,20},{20,16},{24,28},{28,24},{32,36},... | collective-permute-start | bytes 1572872 | tf_op jit(solution)/shard_map/ppermute | solution.py:53
  51.7 2.1 %feed.5 = (bf16[128,2048]{1,0:T(8,128)(2,1)S(1)}, bf16[128,2048]{1,0:T(8,128)(2,1)}) custom-call(bf16[128,2048]{1,0:T(8,128)(2,1)S(1)} %collective-permute-done.8.first_ref, bf16[128,2048]{1,0:T(8,128)(2,1)S(1)} %collective-permute-done.9.second_ref, bf16[2048,256]{1,0:T(8,128)(2,1)S(1)} %constant_dynamic-update-slice_fusion.3.both_ref, ...), custom_call_target="tpu_custom_call" | custom-call | flops 8053063680 | bytes 3670016 | tf_op jit(solution)/shard_map/feed/pallas_call | solution.py:527
  61.7 3.6 %all-to-all-start = ((bf16[4,2,400,256]{3,2,1,0:T(8,128)(2,1)}), bf16[4,2,400,256]{3,2,1,0:T(8,128)(2,1)S(1)}, u32[]{:S(2)}, u32[]{:S(2)}) async-start(bf16[4,2,400,256]{3,2,1,0:T(8,128)(2,1)} %bitcast.7), calls=%async_computation | async-start | bytes 3276800 | tf_op jit(solution)/shard_map/all_to_all | solution.py:672
  65.3 1.9 %collective-permute-done.21 = bf16[128,2048]{1,0:T(8,128)(2,1)} collective-permute-done((bf16[128,2048]{1,0:T(8,128)(2,1)}, bf16[128,2048]{1,0:T(8,128)(2,1)}, u32[]{:S(2)}, u32[]{:S(2)}) %collective-permute-start.21) | collective-permute-done | bytes 524320 | tf_op jit(solution)/shard_map/ppermute | solution.py:49
  71.2 4.2 %collective-permute-done.22 = bf16[64,2048]{1,0:T(8,128)(2,1)S(1)} collective-permute-done((bf16[64,2048]{1,0:T(8,128)(2,1)S(1)}, bf16[64,2048]{1,0:T(8,128)(2,1)S(1)}, u32[]{:S(2)}, u32[]{:S(2)}) %collective-permute-start.22) | collective-permute-done | bytes 262176 | tf_op jit(solution)/shard_map/ppermute | solution.py:49
  76.2 2.2 %collective-permute-start.24 = (bf16[32,2048]{1,0:T(8,128)(2,1)}, bf16[32,2048]{1,0:T(8,128)(2,1)S(1)}, u32[]{:S(2)}, u32[]{:S(2)}) collective-permute-start(bf16[32,2048]{1,0:T(8,128)(2,1)} %get-tuple-element.71), channel_id=1, source_target_pairs={{0,16},{4,68},{8,24},{12,76},{16,0},{20,84},{24,8},{28,92},{32,48}... | collective-permute-start | bytes 393224 | tf_op jit(solution)/shard_map/ppermute | solution.py:49
  80.4 4.1 %all-to-all-done.kept_hbm = bf16[4,2,400,256]{3,2,1,0:T(8,128)(2,1)S(1)} async-done(((bf16[4,2,400,256]{3,2,1,0:T(8,128)(2,1)}), bf16[4,2,400,256]{3,2,1,0:T(8,128)(2,1)S(1)}, u32[]{:S(2)}, u32[]{:S(2)}) %all-to-all-start) | async-done | bytes 1638432 | tf_op jit(solution)/shard_map/all_to_all | solution.py:672
  84.9 5.3 %collective-permute-start.28 = (bf16[32,2048]{1,0:T(8,128)(2,1)S(1)}, bf16[32,2048]{1,0:T(8,128)(2,1)S(1)}, u32[]{:S(2)}, u32[]{:S(2)}) collective-permute-start(bf16[32,2048]{1,0:T(8,128)(2,1)S(1)} %fusion.2), channel_id=1, source_target_pairs={{0,24},{4,100},{8,16},{12,108},{16,8},{20,116},{24,0},{28,124},{32... | collective-permute-start | bytes 393224 | tf_op jit(solution)/shard_map/ppermute | solution.py:49
  93.6 2.0 %collective-permute-done.29 = bf16[32,2048]{1,0:T(8,128)(2,1)S(1)} collective-permute-done((bf16[32,2048]{1,0:T(8,128)(2,1)S(1)}, bf16[32,2048]{1,0:T(8,128)(2,1)S(1)}, u32[]{:S(2)}, u32[]{:S(2)}) %collective-permute-start.29) | collective-permute-done | bytes 131104 | tf_op jit(solution)/shard_map/ppermute | solution.py:49
  95.6 1.8 %collective-permute-start.30 = (bf16[64,2048]{1,0:T(8,128)(2,1)S(1)}, bf16[64,2048]{1,0:T(8,128)(2,1)S(1)}, u32[]{:S(2)}, u32[]{:S(2)}) collective-permute-start(bf16[64,2048]{1,0:T(8,128)(2,1)S(1)} %pad_maximum_fusion.5), channel_id=1, source_target_pairs={{0,96},{4,28},{8,104},{12,20},{16,112},{20,12},{24,120},{28,4},{32... | collective-permute-start | bytes 786440 | tf_op jit(solution)/shard_map/ppermute | solution.py:49
  98.4 1.7 %collective-permute-start.32 = (bf16[128,2048]{1,0:T(8,128)(2,1)S(1)}, bf16[128,2048]{1,0:T(8,128)(2,1)S(1)}, u32[]{:S(2)}, u32[]{:S(2)}) collective-permute-start(bf16[128,2048]{1,0:T(8,128)(2,1)S(1)} %pad_maximum_fusion.1.refs_0_), channel_id=1, source_target_pairs={{0,4},{4,0},{8,12},{12,8},{16,20},{20,16},{24,28},{28,24},{32,36},... | collective-permute-start | bytes 1572872 | tf_op jit(solution)/shard_map/ppermute | solution.py:53
  100.1 2.0 %collective-permute-done.30 = bf16[64,2048]{1,0:T(8,128)(2,1)S(1)} collective-permute-done((bf16[64,2048]{1,0:T(8,128)(2,1)S(1)}, bf16[64,2048]{1,0:T(8,128)(2,1)S(1)}, u32[]{:S(2)}, u32[]{:S(2)}) %collective-permute-start.30) | collective-permute-done | bytes 262176 | tf_op jit(solution)/shard_map/ppermute | solution.py:49
  102.1 4.7 %collective-permute-start.33 = (bf16[128,2048]{1,0:T(8,128)(2,1)S(1)}, bf16[128,2048]{1,0:T(8,128)(2,1)S(1)}, u32[]{:S(2)}, u32[]{:S(2)}) collective-permute-start(bf16[128,2048]{1,0:T(8,128)(2,1)S(1)} %constant_dynamic-update-slice_fusion.5.refs_1_), channel_id=1, source_target_pairs={{0,4},{4,0},{8,12},{12,8},{16,20},{20,16},{24,28},{28,24},{32,36},... | collective-permute-start | bytes 1572872 | tf_op jit(solution)/shard_map/ppermute | solution.py:53
  108.4 5.6 %head_stats.3.refs_3_ = f32[256,128]{1,0:T(8,128)S(1)} custom-call(s32[4,128]{1,0:T(4,128)S(1)} %slice.93.targets_ref, s32[4,128]{1,0:T(4,128)S(1)} %slice.94.owners_ref, bf16[128,2048]{1,0:T(8,128)(2,1)S(1)} %pad_maximum_fusion.1.refs_0_, bf16[128,2048]{1,0:T(8,128)(2,1)S(1)} %constant_dynamic-update-slice_fusion.5.refs_1_, ...), custom_call_target="tpu_custom_call" | custom-call | flops 21474836480 | bytes 6291456 | tf_op jit(solution)/shard_map/head_stats/pallas_call | solution.py:582
  114.0 2.4 %collective-permute-done.27.refs_0_ = bf16[128,2048]{1,0:T(8,128)(2,1)S(1)} collective-permute-done((bf16[128,2048]{1,0:T(8,128)(2,1)S(1)}, bf16[128,2048]{1,0:T(8,128)(2,1)S(1)}, u32[]{:S(2)}, u32[]{:S(2)}) %collective-permute-start.27) | collective-permute-done | bytes 524320 | tf_op jit(solution)/shard_map/ppermute | solution.py:49
  117.4 2.0 %head_stats.4.refs_4_ = f32[256,128]{1,0:T(8,128)S(1)} custom-call(s32[2,128]{1,0:T(2,128)S(1)} %get-tuple-element.80.targets_ref, s32[2,128]{1,0:T(2,128)S(1)} %get-tuple-element.75.owners_ref, bf16[128,2048]{1,0:T(8,128)(2,1)S(1)} %collective-permute-done.27.refs_0_, bf16[128,2048]{1,0:T(8,128)(2,1)S(1)} %collective-permute-done.31.refs_1_, ...), custom_call_target="tpu_custom_call" | custom-call | flops 10737418240 | bytes 5242880 | tf_op jit(solution)/shard_map/head_stats/pallas_call | solution.py:582
  119.6 2.6 %head_stats.5._stats = f32[256,128]{1,0:T(8,128)} custom-call(s32[2,128]{1,0:T(2,128)S(1)} %get-tuple-element.79.targets_ref, s32[2,128]{1,0:T(2,128)S(1)} %get-tuple-element.76.owners_ref, bf16[128,2048]{1,0:T(8,128)(2,1)S(1)} %collective-permute-done.34.refs_0_, bf16[128,2048]{1,0:T(8,128)(2,1)S(1)} %collective-permute-done.35.refs_1_, ...), custom_call_target="tpu_custom_call" | custom-call | flops 10737418240 | bytes 5242880 | tf_op jit(solution)/shard_map/head_stats/pallas_call | solution.py:582
  122.3 5.6 %all-to-all-start.1 = ((f32[32,8,128]{2,1,0:T(8,128)}), f32[32,8,128]{2,1,0:T(8,128)S(1)}, u32[]{:S(2)}, u32[]{:S(2)}) async-start(f32[32,8,128]{2,1,0:T(8,128)} %bitcast.9), calls=%async_computation.1 | async-start | bytes 262144 | tf_op jit(solution)/shard_map/all_to_all | solution.py:693
  127.8 2.1 %unpack.1 = (f32[2,1536,256]{2,1,0:T(8,128)}, bf16[3,2,2048]{2,1,0:T(2,128)(2,1)}) custom-call(bf16[4,2,400,256]{3,2,1,0:T(8,128)(2,1)S(1)} %all-to-all-done.kept_hbm, bf16[16,512]{1,0:T(8,128)(2,1)S(1)} %get-tuple-element.60.bc_ref, f32[256,128]{1,0:T(8,128)} %head_stats.5._stats, bf16[8,128]{1,0:T(8,128)(2,1)S(1)} %slice.84._tip), custom_call_target="tpu_custom_call" | custom-call | flops 1000000 | bytes 20000000 | tf_op jit(solution)/shard_map/unpack/pallas_call | solution.py:252
  129.9 5.5 %all-to-all-done.1 = f32[32,8,128]{2,1,0:T(8,128)S(1)} async-done(((f32[32,8,128]{2,1,0:T(8,128)}), f32[32,8,128]{2,1,0:T(8,128)S(1)}, u32[]{:S(2)}, u32[]{:S(2)}) %all-to-all-start.1) | async-done | bytes 131104 | tf_op jit(solution)/shard_map/all_to_all | solution.py:693
  (151 shorter events, 32.3 us)
Async XLA Ops:
  9.0 7.9 %collective-permute-start.2 = (bf16[32,2048]{1,0:T(8,128)(2,1)}, bf16[32,2048]{1,0:T(8,128)(2,1)S(1)}, u32[]{:S(2)}, u32[]{:S(2)}) collective-permute-start(bf16[32,2048]{1,0:T(8,128)(2,1)} %get-tuple-element.37), channel_id=1, source_target_pairs={{0,2},{1,3},{2,0},{3,1},{4,6},{5,7},{6,4},{7,5},{8,10},{9,11},{10,... | collective-permute-start | bytes 393224 | tf_op jit(solution)/shard_map/ppermute | solution.py:643
  13.5 6.8 %collective-permute-start.1 = (bf16[32,2048]{1,0:T(8,128)(2,1)}, bf16[32,2048]{1,0:T(8,128)(2,1)S(1)}, u32[]{:S(2)}, u32[]{:S(2)}) collective-permute-start(bf16[32,2048]{1,0:T(8,128)(2,1)} %get-tuple-element.36), channel_id=1, source_target_pairs={{0,3},{1,2},{2,1},{3,0},{4,7},{5,6},{6,5},{7,4},{8,11},{9,10},{10,... | collective-permute-start | bytes 393224 | tf_op jit(solution)/shard_map/ppermute | solution.py:643
  13.9 6.3 %collective-permute-start = (bf16[32,2048]{1,0:T(8,128)(2,1)}, bf16[32,2048]{1,0:T(8,128)(2,1)S(1)}, u32[]{:S(2)}, u32[]{:S(2)}) collective-permute-start(bf16[32,2048]{1,0:T(8,128)(2,1)} %get-tuple-element.35), channel_id=1, source_target_pairs={{0,1},{1,0},{2,3},{3,2},{4,5},{5,4},{6,7},{7,6},{8,9},{9,8},{10,11... | collective-permute-start | bytes 393224 | tf_op jit(solution)/shard_map/ppermute | solution.py:643
  25.0 5.3 %collective-permute-start.6 = (bf16[32,2048]{1,0:T(8,128)(2,1)S(1)}, bf16[32,2048]{1,0:T(8,128)(2,1)S(1)}, u32[]{:S(2)}, u32[]{:S(2)}) collective-permute-start(bf16[32,2048]{1,0:T(8,128)(2,1)S(1)} %fusion.5), channel_id=1, source_target_pairs={{0,16},{4,68},{8,24},{12,76},{16,0},{20,84},{24,8},{28,92},{32,48}... | collective-permute-start | bytes 393224 | tf_op jit(solution)/shard_map/ppermute | solution.py:49
  25.8 7.4 %collective-permute-start.4 = (bf16[64,2048]{1,0:T(8,128)(2,1)S(1)}, bf16[64,2048]{1,0:T(8,128)(2,1)S(1)}, u32[]{:S(2)}, u32[]{:S(2)}) collective-permute-start(bf16[64,2048]{1,0:T(8,128)(2,1)S(1)} %pad_maximum_fusion.2), channel_id=1, source_target_pairs={{0,32},{4,12},{8,40},{12,4},{16,48},{20,28},{24,56},{28,20},{32,0}... | collective-permute-start | bytes 786440 | tf_op jit(solution)/shard_map/ppermute | solution.py:49
  30.3 7.9 %collective-permute-start.7 = (bf16[64,2048]{1,0:T(8,128)(2,1)S(1)}, bf16[64,2048]{1,0:T(8,128)(2,1)S(1)}, u32[]{:S(2)}, u32[]{:S(2)}) collective-permute-start(bf16[64,2048]{1,0:T(8,128)(2,1)S(1)} %pad_maximum_fusion.3), channel_id=1, source_target_pairs={{0,96},{4,28},{8,104},{12,20},{16,112},{20,12},{24,120},{28,4},{32... | collective-permute-start | bytes 786440 | tf_op jit(solution)/shard_map/ppermute | solution.py:49
  33.3 13.6 %collective-permute-start.11 = (bf16[128,2048]{1,0:T(8,128)(2,1)S(1)}, bf16[128,2048]{1,0:T(8,128)(2,1)S(1)}, u32[]{:S(2)}, u32[]{:S(2)}) collective-permute-start(bf16[128,2048]{1,0:T(8,128)(2,1)S(1)} %pad_maximum_fusion.first_ref), channel_id=1, source_target_pairs={{0,96},{4,28},{8,104},{12,20},{16,112},{20,12},{24,120},{28,4},{32... | collective-permute-start | bytes 1572872 | tf_op jit(solution)/shard_map/ppermute | solution.py:49
  35.4 16.2 %collective-permute-start.8 = (bf16[128,2048]{1,0:T(8,128)(2,1)S(1)}, bf16[128,2048]{1,0:T(8,128)(2,1)S(1)}, u32[]{:S(2)}, u32[]{:S(2)}) collective-permute-start(bf16[128,2048]{1,0:T(8,128)(2,1)S(1)} %pad_maximum_fusion.first_ref), channel_id=1, source_target_pairs={{0,4},{4,0},{8,12},{12,8},{16,20},{20,16},{24,28},{28,24},{32,36},... | collective-permute-start | bytes 1572872 | tf_op jit(solution)/shard_map/ppermute | solution.py:53
  38.2 10.2 %collective-permute-start.12 = (bf16[128,2048]{1,0:T(8,128)(2,1)S(1)}, bf16[128,2048]{1,0:T(8,128)(2,1)S(1)}, u32[]{:S(2)}, u32[]{:S(2)}) collective-permute-start(bf16[128,2048]{1,0:T(8,128)(2,1)S(1)} %constant_dynamic-update-slice_fusion.second_ref), channel_id=1, source_target_pairs={{0,32},{4,12},{8,40},{12,4},{16,48},{20,28},{24,56},{28,20},{32,0}... | collective-permute-start | bytes 1572872 | tf_op jit(solution)/shard_map/ppermute | solution.py:49
  39.2 12.5 %collective-permute-start.9 = (bf16[128,2048]{1,0:T(8,128)(2,1)S(1)}, bf16[128,2048]{1,0:T(8,128)(2,1)S(1)}, u32[]{:S(2)}, u32[]{:S(2)}) collective-permute-start(bf16[128,2048]{1,0:T(8,128)(2,1)S(1)} %constant_dynamic-update-slice_fusion.second_ref), channel_id=1, source_target_pairs={{0,4},{4,0},{8,12},{12,8},{16,20},{20,16},{24,28},{28,24},{32,36},... | collective-permute-start | bytes 1572872 | tf_op jit(solution)/shard_map/ppermute | solution.py:53
  46.9 7.4 %collective-permute-start.13 = (bf16[128,2048]{1,0:T(8,128)(2,1)S(1)}, bf16[128,2048]{1,0:T(8,128)(2,1)S(1)}, u32[]{:S(2)}, u32[]{:S(2)}) collective-permute-start(bf16[128,2048]{1,0:T(8,128)(2,1)S(1)} %collective-permute-done.11.first_ref), channel_id=1, source_target_pairs={{0,4},{4,0},{8,12},{12,8},{16,20},{20,16},{24,28},{28,24},{32,36},... | collective-permute-start | bytes 1572872 | tf_op jit(solution)/shard_map/ppermute | solution.py:53
  48.4 5.9 %collective-permute-start.14 = (bf16[128,2048]{1,0:T(8,128)(2,1)S(1)}, bf16[128,2048]{1,0:T(8,128)(2,1)S(1)}, u32[]{:S(2)}, u32[]{:S(2)}) collective-permute-start(bf16[128,2048]{1,0:T(8,128)(2,1)S(1)} %collective-permute-done.12.second_ref), channel_id=1, source_target_pairs={{0,4},{4,0},{8,12},{12,8},{16,20},{20,16},{24,28},{28,24},{32,36},... | collective-permute-start | bytes 1572872 | tf_op jit(solution)/shard_map/ppermute | solution.py:53
  53.8 11.5 %collective-permute-start.19 = (bf16[128,2048]{1,0:T(8,128)(2,1)}, bf16[128,2048]{1,0:T(8,128)(2,1)}, u32[]{:S(2)}, u32[]{:S(2)}) collective-permute-start(bf16[128,2048]{1,0:T(8,128)(2,1)} %get-tuple-element.43), channel_id=1, source_target_pairs={{0,4},{4,0},{8,12},{12,8},{16,20},{20,16},{24,28},{28,24},{32,36},... | collective-permute-start | bytes 1572872 | tf_op jit(solution)/shard_map/ppermute | solution.py:53
  53.8 15.8 %collective-permute-start.10 = (bf16[128,2048]{1,0:T(8,128)(2,1)S(1)}, bf16[128,2048]{1,0:T(8,128)(2,1)}, u32[]{:S(2)}, u32[]{:S(2)}) collective-permute-start(bf16[128,2048]{1,0:T(8,128)(2,1)S(1)} %get-tuple-element.39), channel_id=1, source_target_pairs={{0,4},{4,0},{8,12},{12,8},{16,20},{20,16},{24,28},{28,24},{32,36},... | collective-permute-start | bytes 1572872 | tf_op jit(solution)/shard_map/ppermute | solution.py:53
  58.5 8.6 %collective-permute-start.21 = (bf16[128,2048]{1,0:T(8,128)(2,1)}, bf16[128,2048]{1,0:T(8,128)(2,1)}, u32[]{:S(2)}, u32[]{:S(2)}) collective-permute-start(bf16[128,2048]{1,0:T(8,128)(2,1)} %add_convert_fusion.1), channel_id=1, source_target_pairs={{0,32},{4,12},{8,40},{12,4},{16,48},{20,28},{24,56},{28,20},{32,0}... | collective-permute-start | bytes 1572872 | tf_op jit(solution)/shard_map/ppermute | solution.py:49
  59.8 9.9 %collective-permute-start.16 = (bf16[128,2048]{1,0:T(8,128)(2,1)}, bf16[128,2048]{1,0:T(8,128)(2,1)}, u32[]{:S(2)}, u32[]{:S(2)}) collective-permute-start(bf16[128,2048]{1,0:T(8,128)(2,1)} %add_convert_fusion.4), channel_id=1, source_target_pairs={{0,96},{4,28},{8,104},{12,20},{16,112},{20,12},{24,120},{28,4},{32... | collective-permute-start | bytes 1572872 | tf_op jit(solution)/shard_map/ppermute | solution.py:49
  61.7 22.8 %all-to-all-start = ((bf16[4,2,400,256]{3,2,1,0:T(8,128)(2,1)}), bf16[4,2,400,256]{3,2,1,0:T(8,128)(2,1)S(1)}, u32[]{:S(2)}, u32[]{:S(2)}) async-start(bf16[4,2,400,256]{3,2,1,0:T(8,128)(2,1)} %bitcast.7), calls=%async_computation | async-start | bytes 3276800 | tf_op jit(solution)/shard_map/all_to_all | solution.py:672
  68.7 6.8 %collective-permute-start.22 = (bf16[64,2048]{1,0:T(8,128)(2,1)S(1)}, bf16[64,2048]{1,0:T(8,128)(2,1)S(1)}, u32[]{:S(2)}, u32[]{:S(2)}) collective-permute-start(bf16[64,2048]{1,0:T(8,128)(2,1)S(1)} %slice.105), channel_id=1, source_target_pairs={{0,96},{4,28},{8,104},{12,20},{16,112},{20,12},{24,120},{28,4},{32... | collective-permute-start | bytes 786440 | tf_op jit(solution)/shard_map/ppermute | solution.py:49
  71.1 7.9 %collective-permute-start.17 = (bf16[64,2048]{1,0:T(8,128)(2,1)S(1)}, bf16[64,2048]{1,0:T(8,128)(2,1)S(1)}, u32[]{:S(2)}, u32[]{:S(2)}) collective-permute-start(bf16[64,2048]{1,0:T(8,128)(2,1)S(1)} %slice.101), channel_id=1, source_target_pairs={{0,32},{4,12},{8,40},{12,4},{16,48},{20,28},{24,56},{28,20},{32,0}... | collective-permute-start | bytes 786440 | tf_op jit(solution)/shard_map/ppermute | solution.py:49
  76.2 8.3 %collective-permute-start.24 = (bf16[32,2048]{1,0:T(8,128)(2,1)}, bf16[32,2048]{1,0:T(8,128)(2,1)S(1)}, u32[]{:S(2)}, u32[]{:S(2)}) collective-permute-start(bf16[32,2048]{1,0:T(8,128)(2,1)} %get-tuple-element.71), channel_id=1, source_target_pairs={{0,16},{4,68},{8,24},{12,76},{16,0},{20,84},{24,8},{28,92},{32,48}... | collective-permute-start | bytes 393224 | tf_op jit(solution)/shard_map/ppermute | solution.py:49
  78.4 6.1 %collective-permute-start.23 = (bf16[32,2048]{1,0:T(8,128)(2,1)S(1)}, bf16[32,2048]{1,0:T(8,128)(2,1)S(1)}, u32[]{:S(2)}, u32[]{:S(2)}) collective-permute-start(bf16[32,2048]{1,0:T(8,128)(2,1)S(1)} %get-tuple-element.70), channel_id=1, source_target_pairs={{0,24},{4,100},{8,16},{12,108},{16,8},{20,116},{24,0},{28,124},{32... | collective-permute-start | bytes 393224 | tf_op jit(solution)/shard_map/ppermute | solution.py:49
  79.1 5.4 %collective-permute-start.18 = (bf16[32,2048]{1,0:T(8,128)(2,1)S(1)}, bf16[32,2048]{1,0:T(8,128)(2,1)S(1)}, u32[]{:S(2)}, u32[]{:S(2)}) collective-permute-start(bf16[32,2048]{1,0:T(8,128)(2,1)S(1)} %slice.103), channel_id=1, source_target_pairs={{0,8},{4,36},{8,0},{12,44},{16,24},{20,52},{24,16},{28,60},{32,40}... | collective-permute-start | bytes 393224 | tf_op jit(solution)/shard_map/ppermute | solution.py:49
  84.9 6.5 %collective-permute-start.25 = (bf16[32,2048]{1,0:T(8,128)(2,1)S(1)}, bf16[32,2048]{1,0:T(8,128)(2,1)S(1)}, u32[]{:S(2)}, u32[]{:S(2)}) collective-permute-start(bf16[32,2048]{1,0:T(8,128)(2,1)S(1)} %fusion.2), channel_id=1, source_target_pairs={{0,8},{4,36},{8,0},{12,44},{16,24},{20,52},{24,16},{28,60},{32,40}... | collective-permute-start | bytes 393224 | tf_op jit(solution)/shard_map/ppermute | solution.py:49
  84.9 8.6 %collective-permute-start.28 = (bf16[32,2048]{1,0:T(8,128)(2,1)S(1)}, bf16[32,2048]{1,0:T(8,128)(2,1)S(1)}, u32[]{:S(2)}, u32[]{:S(2)}) collective-permute-start(bf16[32,2048]{1,0:T(8,128)(2,1)S(1)} %fusion.2), channel_id=1, source_target_pairs={{0,24},{4,100},{8,16},{12,108},{16,8},{20,116},{24,0},{28,124},{32... | collective-permute-start | bytes 393224 | tf_op jit(solution)/shard_map/ppermute | solution.py:49
  90.3 5.3 %collective-permute-start.29 = (bf16[32,2048]{1,0:T(8,128)(2,1)S(1)}, bf16[32,2048]{1,0:T(8,128)(2,1)S(1)}, u32[]{:S(2)}, u32[]{:S(2)}) collective-permute-start(bf16[32,2048]{1,0:T(8,128)(2,1)S(1)} %fusion.2), channel_id=1, source_target_pairs={{0,16},{4,68},{8,24},{12,76},{16,0},{20,84},{24,8},{28,92},{32,48}... | collective-permute-start | bytes 393224 | tf_op jit(solution)/shard_map/ppermute | solution.py:49
  91.4 7.0 %collective-permute-start.26 = (bf16[64,2048]{1,0:T(8,128)(2,1)S(1)}, bf16[64,2048]{1,0:T(8,128)(2,1)S(1)}, u32[]{:S(2)}, u32[]{:S(2)}) collective-permute-start(bf16[64,2048]{1,0:T(8,128)(2,1)S(1)} %pad_maximum_fusion.4), channel_id=1, source_target_pairs={{0,32},{4,12},{8,40},{12,4},{16,48},{20,28},{24,56},{28,20},{32,0}... | collective-permute-start | bytes 786440 | tf_op jit(solution)/shard_map/ppermute | solution.py:49
  95.6 6.5 %collective-permute-start.30 = (bf16[64,2048]{1,0:T(8,128)(2,1)S(1)}, bf16[64,2048]{1,0:T(8,128)(2,1)S(1)}, u32[]{:S(2)}, u32[]{:S(2)}) collective-permute-start(bf16[64,2048]{1,0:T(8,128)(2,1)S(1)} %pad_maximum_fusion.5), channel_id=1, source_target_pairs={{0,96},{4,28},{8,104},{12,20},{16,112},{20,12},{24,120},{28,4},{32... | collective-permute-start | bytes 786440 | tf_op jit(solution)/shard_map/ppermute | solution.py:49
  98.4 9.5 %collective-permute-start.32 = (bf16[128,2048]{1,0:T(8,128)(2,1)S(1)}, bf16[128,2048]{1,0:T(8,128)(2,1)S(1)}, u32[]{:S(2)}, u32[]{:S(2)}) collective-permute-start(bf16[128,2048]{1,0:T(8,128)(2,1)S(1)} %pad_maximum_fusion.1.refs_0_), channel_id=1, source_target_pairs={{0,4},{4,0},{8,12},{12,8},{16,20},{20,16},{24,28},{28,24},{32,36},... | collective-permute-start | bytes 1572872 | tf_op jit(solution)/shard_map/ppermute | solution.py:53
  102.1 6.2 %collective-permute-start.33 = (bf16[128,2048]{1,0:T(8,128)(2,1)S(1)}, bf16[128,2048]{1,0:T(8,128)(2,1)S(1)}, u32[]{:S(2)}, u32[]{:S(2)}) collective-permute-start(bf16[128,2048]{1,0:T(8,128)(2,1)S(1)} %constant_dynamic-update-slice_fusion.5.refs_1_), channel_id=1, source_target_pairs={{0,4},{4,0},{8,12},{12,8},{16,20},{20,16},{24,28},{28,24},{32,36},... | collective-permute-start | bytes 1572872 | tf_op jit(solution)/shard_map/ppermute | solution.py:53
  106.8 9.6 %collective-permute-start.27 = (bf16[128,2048]{1,0:T(8,128)(2,1)S(1)}, bf16[128,2048]{1,0:T(8,128)(2,1)S(1)}, u32[]{:S(2)}, u32[]{:S(2)}) collective-permute-start(bf16[128,2048]{1,0:T(8,128)(2,1)S(1)} %pad_maximum_fusion.1.refs_0_), channel_id=1, source_target_pairs={{0,96},{4,28},{8,104},{12,20},{16,112},{20,12},{24,120},{28,4},{32... | collective-permute-start | bytes 1572872 | tf_op jit(solution)/shard_map/ppermute | solution.py:49
  107.9 8.5 %collective-permute-start.31 = (bf16[128,2048]{1,0:T(8,128)(2,1)S(1)}, bf16[128,2048]{1,0:T(8,128)(2,1)S(1)}, u32[]{:S(2)}, u32[]{:S(2)}) collective-permute-start(bf16[128,2048]{1,0:T(8,128)(2,1)S(1)} %constant_dynamic-update-slice_fusion.5.refs_1_), channel_id=1, source_target_pairs={{0,32},{4,12},{8,40},{12,4},{16,48},{20,28},{24,56},{28,20},{32,0}... | collective-permute-start | bytes 1572872 | tf_op jit(solution)/shard_map/ppermute | solution.py:49
  122.3 13.2 %all-to-all-start.1 = ((f32[32,8,128]{2,1,0:T(8,128)}), f32[32,8,128]{2,1,0:T(8,128)S(1)}, u32[]{:S(2)}, u32[]{:S(2)}) async-start(f32[32,8,128]{2,1,0:T(8,128)} %bitcast.9), calls=%async_computation.1 | async-start | bytes 262144 | tf_op jit(solution)/shard_map/all_to_all | solution.py:693
  (27 other events, 383.2 us)

commit v5 on v4

--- a/solution.py
+++ b/solution.py
@@ -56,39 +56,50 @@
 def gather_rows(rows):
     came = [hop(rows, 0, flip) for flip in DIRECT]
     held = [jnp.concatenate([rows, came[0]], axis=0), jnp.concatenate(came[1:], axis=0)]
-    came = [hop(held[s], 1, EDGES[s][0]) for s in range(2)]
-    held = [jnp.concatenate([held[s], came[s]], axis=0) for s in range(2)]
-    late = [hop(held[s], 1, EDGES[s][1]) for s in range(2)]
-    return held, late
-
-
-def added(left, right):
-    return (left.astype(jnp.float32) + right.astype(jnp.float32)).astype(jnp.bfloat16)
+    near = [hop(held[s], 1, EDGES[s][0]) for s in range(2)]
+    far = [hop(held[s], 1, EDGES[s][1]) for s in range(2)]
+    last = [hop(near[s], 1, EDGES[s][1]) for s in range(2)]
+    return held + near + far, last
+
+
+def added(*parts):
+    return sum(part.astype(jnp.float32) for part in parts).astype(jnp.bfloat16)
 
 
 def scatter_rows(early, late):
-    came = [swap_core(part) for part in late[1]]
-    late = [hop(added(late[0][s], came[s]), 1, EDGES[s][1]) for s in range(2)]
-    came = [swap_core(part) for part in early[1]]
-    held = [added(early[0][s], came[s]) for s in range(2)]
-    held = [added(held[s], late[s]) for s in range(2)]
+    rows = late[0][0].shape[0]
+
+    def stream(joined, s):
+        return joined[s * rows : (s + 1) * rows]
+
+    came = swap_core(late[1][0])
+    last = [hop(added(late[0][s], stream(came, s)), 1, EDGES[s][1]) for s in range(2)]
+    kept, near, far = (swap_core(part) for part in early[1])
+    own = early[0]
+    far = [hop(added(own[4 + s], stream(far, s)), 1, EDGES[s][1]) for s in range(2)]
+    near = [hop(added(own[2 + s], stream(near, s), last[s]), 1, EDGES[s][0]) for s in range(2)]
+    held = [added(own[s], stream(kept, s), far[s], near[s]) for s in range(2)]
     half = held[0].shape[0] // 2
-    came = [hop(held[s][half:], 1, EDGES[s][0]) for s in range(2)]
-    held = [added(held[s][:half], came[s]) for s in range(2)]
-    half = half // 2
     blocks = (held[0][half:], held[1][:half], held[1][half:])
     came = [hop(block, 0, flip) for block, flip in zip(blocks, DIRECT, strict=True)]
     total = held[0][:half].astype(jnp.float32)
     return sum((part.astype(jnp.float32) for part in came), total)
 
 
+def swap_early(arrays):
+    kept = [swap_core(part) for part in arrays[:2]]
+    return kept + [swap_core(jnp.concatenate(arrays[k : k + 2], axis=0)) for k in (2, 4)]
+
+
 def block_table():
-    table = np.zeros((CORES, 2, 2, 2, 2, 2, 2, 4), np.int32)
-    for core, late, half, stream, second, block, request in np.ndindex(table.shape[:-1]):
+    arrays = [(half, kind) for half in range(2) for kind in range(3)] + [(0, 3), (1, 3)]
+    table = np.zeros((CORES, len(arrays), 2, 2, 2, 4), np.int32)
+    for core, array, stream, block, request in np.ndindex(table.shape[:-1]):
+        half, kind = arrays[array]
         first = ((0, 1), (3, 2))[stream][block]
-        other = (EDGES[stream][1] if late else 0) ^ (EDGES[stream][0] if second else 0)
+        other = (0, *EDGES[stream], 2)[kind]
         y, x = (other, first) if core == half else (first, other)
-        table[core, late, half, stream, second, block, request] = (y, x, half, request)
+        table[core, array, stream, block, request] = (y, x, half, request)
     return table.reshape(CORES, 64, 4)
 
 
@@ -215,7 +226,7 @@
             *(pltpu.VMEM(a.shape, a.dtype) for a in operands[2:]),
             pltpu.SemaphoreType.DMA((len(operands),)),
         ],
-        compiler_params=pltpu.CompilerParams(vmem_limit_bytes=32 << 20),
+        compiler_params=pltpu.CompilerParams(vmem_limit_bytes=12 << 20),
         cost_estimate=pl.CostEstimate(
             flops=2_000_000_000, bytes_accessed=5_000_000, transcendentals=200_000
         ),
@@ -259,7 +270,7 @@
         + [pl.BlockSpec(memory_space=pl.ANY)] * len(tokens),
         out_specs=[whole] * 2,
         scratch_shapes=[pltpu.VMEM(kept_out.shape, kept_out.dtype), pltpu.SemaphoreType.DMA],
-        compiler_params=pltpu.CompilerParams(vmem_limit_bytes=48 << 20),
+        compiler_params=pltpu.CompilerParams(vmem_limit_bytes=10 << 20),
         cost_estimate=pl.CostEstimate(flops=1_000_000, bytes_accessed=20_000_000, transcendentals=0),
         name="unpack",
     )(kept_out, own_bc, *tokens)
@@ -509,86 +520,87 @@
     return outs[:SIDE], *keeper(member, accepted, *outs[SIDE:], *small[-2:], state)
 
 
-def feed_kernel(first_ref, second_ref, both_ref, down_ref, first_out, second_out):
+def feed_kernel(count, both_ref, down_ref, _token, *refs):
     hidden = down_ref.shape[0]
-    rows = first_ref.shape[0]
-    joined = jnp.concatenate([first_ref[...], second_ref[...]], axis=0)
+    rows_refs, out_refs = refs[:count], refs[count:]
+    joined = jnp.concatenate([ref[...] for ref in rows_refs], axis=0)
     pair = dot32(joined, both_ref[...])
     gate, up = pair[:, :hidden], pair[:, hidden:]
     active = (gate * jax.nn.sigmoid(gate) * up).astype(jnp.bfloat16)
     parts = dot32(active, down_ref[...]).astype(jnp.bfloat16)
-    first_out[...] = parts[:rows]
-    second_out[...] = parts[rows:]
-
-
-def feed(first, second, w_both, w_down):
-    rows, width = first.shape
+    first = 0
+    for out_ref in out_refs:
+        out_ref[...] = parts[first : first + out_ref.shape[0]]
+        first += out_ref.shape[0]
+
+
+def feed(arrays, out_rows, w_both, w_down, token):
+    rows, width = sum(a.shape[0] for a in arrays), arrays[0].shape[1]
     whole = pl.BlockSpec(memory_space=pltpu.VMEM)
     return pl.pallas_call(
-        feed_kernel,
-        out_shape=[jax.ShapeDtypeStruct((rows, width), jnp.bfloat16)] * 2,
-        in_specs=[whole] * 4,
-        out_specs=[whole] * 2,
-        compiler_params=pltpu.CompilerParams(vmem_limit_bytes=16 << 20),
+        functools.partial(feed_kernel, len(arrays)),
+        out_shape=[jax.ShapeDtypeStruct((r, width), jnp.bfloat16) for r in out_rows],
+        in_specs=[whole] * 2
+        + [pl.BlockSpec(memory_space=pl.ANY)]
+        + [whole] * len(arrays),
+        out_specs=[whole] * len(out_rows),
+        compiler_params=pltpu.CompilerParams(vmem_limit_bytes=12 << 20),
         cost_estimate=pl.CostEstimate(
-            flops=20 * 2 * rows * width * 2 * 3 * w_down.shape[0],
-            bytes_accessed=4 * rows * width * 2 + 3 * w_down.size * 2,
-            transcendentals=2 * rows * w_down.shape[0],
+            flops=4 * rows * width * 2 * 3 * w_down.shape[0],
+            bytes_accessed=2 * rows * width * 2 + 3 * w_down.size * 2,
+            transcendentals=rows * w_down.shape[0],
         ),
         name="feed",
-    )(first, second, w_both, w_down)
-
-
-def head_kernel(targets_ref, owners_ref, *refs):
-    count = targets_ref.shape[0]
+    )(w_both, w_down, token, *arrays)
+
+
+def head_kernel(count, targets_ref, owners_ref, *refs):
+    groups, lanes = targets_ref.shape
     rows_refs, head_ref, others, out_ref = refs[:count], refs[count], refs[count + 1 : -1], refs[-1]
     vocab = head_ref.shape[0]
-    lanes = 2 * rows_refs[0].shape[0]
-    slots = out_ref.shape[0]
+    devices = out_ref.shape[0]
     base = lax.axis_index("req") * vocab
-    lane = lax.broadcasted_iota(jnp.int32, (lanes, 128), 0)
-    column = lax.broadcasted_iota(jnp.int32, (lanes, 128), 1)
-    place = (column == lane % (2 * DRAFT)).astype(jnp.bfloat16)
     ids = lax.broadcasted_iota(jnp.int32, (vocab, lanes), 0) + base
-    slot = lax.broadcasted_iota(jnp.int32, (slots, lanes), 0)
-    packed = jnp.zeros(out_ref.shape, jnp.float32)
+    device = lax.broadcasted_iota(jnp.int32, (devices, lanes), 0)
+    source = lax.broadcasted_iota(jnp.int32, (3 * lanes, 128), 0)
+    column = lax.broadcasted_iota(jnp.int32, (3 * lanes, 128), 1)
+    place = (column == source // lanes * (2 * DRAFT) + source % (2 * DRAFT)).astype(jnp.bfloat16)
+    packed = jnp.zeros((devices, 128), jnp.float32)
     for other in others:
-        packed = packed + other[...]
-    for pair in range(count // 2):
-        joined = jnp.concatenate([rows_refs[2 * pair][...], rows_refs[2 * pair + 1][...]], axis=0)
-        wanted = jnp.concatenate(
-            [targets_ref[2 * pair : 2 * pair + 1, :], targets_ref[2 * pair + 1 : 2 * pair + 2, :]],
-            axis=1,
-        )
-        owner = jnp.concatenate(
-            [owners_ref[2 * pair : 2 * pair + 1, :], owners_ref[2 * pair + 1 : 2 * pair + 2, :]],
-            axis=1,
-        )
+        packed = packed + other[:, 0, :]
+    for group in range(groups):
+        members, first = [], 0
+        for ref in rows_refs:
+            if group * lanes <= first < (group + 1) * lanes:
+                members.append(ref[...])
+            first += ref.shape[0]
+        joined = jnp.concatenate(members, axis=0)
         logits = dot32(head_ref[...], joined, NEXT_TO)
+        wanted = targets_ref[group : group + 1, :]
         target = jnp.sum(jnp.where(ids == wanted, logits, 0.0), axis=0, keepdims=True)
         top = jnp.max(logits, axis=0, keepdims=True)
         total = jnp.sum(jnp.exp(logits - top), axis=0, keepdims=True)
-        stats = jnp.where(slot % 8 == 0, top, jnp.where(slot % 8 == 1, total, target))
-        rest = jnp.where((slot // 8 == owner) & (slot % 8 < 3), stats, 0.0)
+        here = device == owners_ref[group : group + 1, :]
+        rest = jnp.concatenate([jnp.where(here, stat, 0.0) for stat in (top, total, target)], axis=1)
         for _ in range(3):
             part = rest.astype(jnp.bfloat16)
             packed = packed + dot32(part, place)
             rest = rest - part.astype(jnp.float32)
-    out_ref[...] = packed
+    out_ref[:, 0, :] = packed
 
 
 def head_stats(targets, owners, rows, head_weight, devices, others=()):
     whole = pl.BlockSpec(memory_space=pltpu.VMEM)
     return pl.pallas_call(
-        head_kernel,
-        out_shape=jax.ShapeDtypeStruct((devices * 8, 128), jnp.float32),
+        functools.partial(head_kernel, len(rows)),
+        out_shape=jax.ShapeDtypeStruct((devices, 1, 128), jnp.float32),
         in_specs=[whole] * (3 + len(rows) + len(others)),
         out_specs=whole,
-        compiler_params=pltpu.CompilerParams(vmem_limit_bytes=32 << 20),
+        compiler_params=pltpu.CompilerParams(vmem_limit_bytes=20 << 20),
         cost_estimate=pl.CostEstimate(
-            flops=10 * 2 * len(rows) * rows[0].size * head_weight.shape[0],
-            bytes_accessed=2 * len(rows) * rows[0].size + 2 * head_weight.size,
-            transcendentals=len(rows) * rows[0].shape[0] * head_weight.shape[0],
+            flops=1 * 2 * targets.size * head_weight.size,
+            bytes_accessed=2 * targets.size * head_weight.shape[1] + 2 * head_weight.size,
+            transcendentals=targets.size * head_weight.shape[0],
         ),
         name="head_stats",
     )(targets, owners, *rows, head_weight, *others)
@@ -648,8 +660,8 @@
     after_mixer = (own_rows.astype(jnp.float32) + mixed).astype(jnp.bfloat16)
     prepared = rms_scale(after_mixer, mlp_gain).astype(jnp.bfloat16)
     w_both = jnp.concatenate([w_gate, w_up], axis=1)
-    held, late = gather_rows(prepared)
-    early = (held, [swap_core(part) for part in held])
+    early, late = gather_rows(prepared)
+    early = (early, swap_early(early))
     late = (late, [swap_core(part) for part in late])
 
     core = req_rank % CORES
@@ -661,11 +673,18 @@
     next_ids = jnp.concatenate([draft_ids[:, 1:], draft_ids[:, :1]], axis=1)
     picked = (request[:, None] == jnp.arange(draft_ids.shape[0])[None, :]).astype(jnp.float32)
     targets = jnp.dot(picked, next_ids.astype(jnp.float32), precision=HIGHEST).astype(jnp.int32)
-    targets = targets.reshape(8, 8 * draft_len)
-    owners = jnp.broadcast_to(owner[:, None], (64, draft_len)).reshape(8, 8 * draft_len)
-
-    early_parts = [feed(*rows, w_both, w_down) for rows in early]
-    late_parts = [feed(*rows, w_both, w_down) for rows in late]
+    targets = targets.reshape(4, 16 * draft_len)
+    owners = jnp.broadcast_to(owner[:, None], (64, draft_len)).reshape(4, 16 * draft_len)
+
+    half = 2 * own_tokens
+    early_parts = [
+        feed(rows, out_rows, w_both, w_down, mlp_gain)
+        for rows, out_rows in zip(early, ([half] * 6, [2 * half] * 3), strict=True)
+    ]
+    late_parts = [
+        feed(rows, out_rows, w_both, w_down, own_bc)
+        for rows, out_rows in zip(late, ([half] * 2, [2 * half]), strict=True)
+    ]
     summed = scatter_rows(early_parts, late_parts)
     tip = early_parts[0][0][:8, :128]
     kept, tip = lax.optimization_barrier((kept, tip))
@@ -681,18 +700,18 @@
     )
     after_feed = (after_mixer.astype(jnp.float32) + summed).astype(jnp.bfloat16)
     final_rows = rms_scale(after_feed, final_gain).astype(jnp.bfloat16)
-    held, late = gather_rows(final_rows)
-    early = held + [swap_core(part) for part in held]
-    first_stats = head_stats(targets[:4], owners[:4], early, head_weight, req_count)
+    early, late = gather_rows(final_rows)
+    early = early + swap_early(early)
+    first_stats = head_stats(targets[:3], owners[:3], early, head_weight, req_count)
     late, first_stats = lax.optimization_barrier((late, first_stats))
-    sibling = [swap_core(part) for part in late]
-    stats = [first_stats, head_stats(targets[4:6], owners[4:6], late, head_weight, req_count)]
-    stats = head_stats(targets[6:], owners[6:], sibling, head_weight, req_count, stats)
+    late = late + [swap_core(part) for part in late]
+    stats = head_stats(targets[3:], owners[3:], late, head_weight, req_count, [first_stats])
     kept_state, kept_conv = unpack(kept_out, own_bc, stats, tip)
     kept_state = kept_state.reshape(own_reqs, -1, SSM_DIM, STATE)
     shared = lax.all_to_all(stats, "req", split_axis=0, concat_axis=0, tiled=True)
-    shared = shared.reshape(req_count, 8, 128)[:, :, :own_tokens]
-    tops, totals, hits = shared[:, 0], shared[:, 1], shared[:, 2]
+    tops, totals, hits = (
+        shared[:, 0, kind * own_tokens : (kind + 1) * own_tokens] for kind in range(3)
+    )
     top = jnp.max(tops, axis=0)
     total = jnp.sum(totals * jnp.exp(tops - top[None, :]), axis=0)
     log_total = top + jnp.log(total)

time: 137 us -> 144 us (1.051)
  waiting for transfers between devices: 33.1 us -> 45.1 us
  starting transfers between devices: 61.3 us -> 58.6 us
    all_to_all x1, waiting for transfers between devices: 4.13 us -> 13 us  [shards(): lax.all_to_all(kept.reshape(mdl_count, own_reqs, local_inner + 16, STATE)...]
    ppermute x12 -> x16, waiting for transfers between devices: 0.83 us -> 2.98 us  [swap_core(): return lax.ppermute(part, 'req', CORE_PAIRS)]
    ppermute x12 -> x16, starting transfers between devices: 19.6 us -> 18.3 us  [swap_core(): return lax.ppermute(part, 'req', CORE_PAIRS)]
    convert_element_type x6 -> x4, other arithmetic: 4.83 us -> 3.76 us  [added(): sum((part.astype(jnp.float32) for part in parts)).astype(jnp.bfloat16)]
    pallas_call x7 -> x6, Pallas kernels: 16.2 us -> 15.4 us  [the longest x2 9.26 us: head_stats(): pl.pallas_call(functools.partial(head_kernel, len(rows)), out_shape=jax.S...]
    ppermute x21 -> x27, starting transfers between devices: 27.3 us -> 26.6 us  [hop(): return lax.ppermute(part, 'req', flip_pairs(ring, flip))]
    ppermute x21 -> x27, waiting for transfers between devices: 17.8 us -> 18.1 us  [hop(): return lax.ppermute(part, 'req', flip_pairs(ring, flip))]
  transfers between devices with their start and end apart: 38 -> 48, of which waited for: 16 -> 18; matrix products, arithmetic and copies ran while one was open for 6% -> 4% of each run, Pallas kernels for 14% -> 13%
where the time goes in v5:
time: 144 us; the launch traced here: 143 us
  starting transfers between devices  58.6 us (41%)
  waiting for transfers between devices  45.1 us (31%)
  Pallas kernels  29.4 us (20%)
  other arithmetic  7.12 us (5%)
  local copies, waits for them, and re-layouts  1.65 us (1%)
    ppermute x27, starting transfers between devices, hop(): return lax.ppermute(part, 'req', flip_pairs(ring, flip))  26.6 us
    ppermute x16, starting transfers between devices, swap_core(): return lax.ppermute(part, 'req', CORE_PAIRS)  18.3 us
    ppermute x27, waiting for transfers between devices, hop(): return lax.ppermute(part, 'req', flip_pairs(ring, flip))  18.1 us
    all_to_all x1, waiting for transfers between devices, shards(): lax.all_to_all(kept.reshape(mdl_count, own_reqs, local_inner + 16, STATE)...  13 us
    pallas_call x2, Pallas kernels, head_stats(): pl.pallas_call(functools.partial(head_kernel, len(rows)), out_shape=jax.S...  9.26 us
    pallas_call x1, Pallas kernels, mixer(): pl.pallas_call(mixer_kernel, out_shape=[*[jax.ShapeDtypeStruct((tokens //...  8.3 us
    ppermute x3, waiting for transfers between devices, shards(): lax.ppermute(part, 'mdl', [(z, z ^ flip) for z in range(SIDE)])  6.13 us
    pallas_call x4, Pallas kernels, feed(): pl.pallas_call(functools.partial(feed_kernel, len(arrays)), out_shape=[ja...  6.12 us
  transfers between devices with their start and end apart: 48, of which 18 were waited for; matrix products, arithmetic and copies ran while one was open for 4% of the time, Pallas kernels for 13%

profile of v5, /device:TPU:1, one launch (start us, length us, event | category | flops | bytes accessed | tf_op | source)
XLA Modules:
  0.0 143.4 jit_solution(5179276498174496746)
XLA Ops:
  0.6 8.3 %mixer.1 = (bf16[32,2048]{1,0:T(8,128)(2,1)}, bf16[32,2048]{1,0:T(8,128)(2,1)}, bf16[32,2048]{1,0:T(8,128)(2,1)}, bf16[32,2048]{1,0:T(8,128)(2,1)}, f32[128,128]...) custom-call(s32[8]{0:T(128)} %refs_0_.3, ...), custom_call_target="tpu_custom_call" | custom-call | flops 3000000000 | bytes 20000000 | tf_op jit(solution)/shard_map/mixer/pallas_call | solution.py:485
  9.0 2.5 %collective-permute-start = (bf16[32,2048]{1,0:T(8,128)(2,1)}, bf16[32,2048]{1,0:T(8,128)(2,1)S(1)}, u32[]{:S(2)}, u32[]{:S(2)}) collective-permute-start(bf16[32,2048]{1,0:T(8,128)(2,1)} %get-tuple-element.38), channel_id=1, source_target_pairs={{0,1},{1,0},{2,3},{3,2},{4,5},{5,4},{6,7},{7,6},{8,9},{9,8},{10,11... | collective-permute-start | bytes 393224 | tf_op jit(solution)/shard_map/ppermute | solution.py:655
  11.5 2.2 %collective-permute-start.1 = (bf16[32,2048]{1,0:T(8,128)(2,1)}, bf16[32,2048]{1,0:T(8,128)(2,1)S(1)}, u32[]{:S(2)}, u32[]{:S(2)}) collective-permute-start(bf16[32,2048]{1,0:T(8,128)(2,1)} %get-tuple-element.39), channel_id=1, source_target_pairs={{0,3},{1,2},{2,1},{3,0},{4,7},{5,6},{6,5},{7,4},{8,11},{9,10},{10,... | collective-permute-start | bytes 393224 | tf_op jit(solution)/shard_map/ppermute | solution.py:655
  14.9 4.3 %collective-permute-done.1 = bf16[32,2048]{1,0:T(8,128)(2,1)S(1)} collective-permute-done((bf16[32,2048]{1,0:T(8,128)(2,1)}, bf16[32,2048]{1,0:T(8,128)(2,1)S(1)}, u32[]{:S(2)}, u32[]{:S(2)}) %collective-permute-start.1) | collective-permute-done | bytes 131104 | tf_op jit(solution)/shard_map/ppermute | solution.py:655
  19.2 1.8 %collective-permute-done.2 = bf16[32,2048]{1,0:T(8,128)(2,1)S(1)} collective-permute-done((bf16[32,2048]{1,0:T(8,128)(2,1)}, bf16[32,2048]{1,0:T(8,128)(2,1)S(1)}, u32[]{:S(2)}, u32[]{:S(2)}) %collective-permute-start.2) | collective-permute-done | bytes 131104 | tf_op jit(solution)/shard_map/ppermute | solution.py:655
  22.5 2.8 %collective-permute-start.4 = (bf16[32,2048]{1,0:T(8,128)(2,1)S(1)}, bf16[32,2048]{1,0:T(8,128)(2,1)S(1)}, u32[]{:S(2)}, u32[]{:S(2)}) collective-permute-start(bf16[32,2048]{1,0:T(8,128)(2,1)S(1)} %fusion.5), channel_id=1, source_target_pairs={{0,24},{4,100},{8,16},{12,108},{16,8},{20,116},{24,0},{28,124},{32... | collective-permute-start | bytes 393224 | tf_op jit(solution)/shard_map/ppermute | solution.py:49
  25.9 2.6 %collective-permute-done.4 = bf16[32,2048]{1,0:T(8,128)(2,1)S(1)} collective-permute-done((bf16[32,2048]{1,0:T(8,128)(2,1)S(1)}, bf16[32,2048]{1,0:T(8,128)(2,1)S(1)}, u32[]{:S(2)}, u32[]{:S(2)}) %collective-permute-start.4) | collective-permute-done | bytes 131104 | tf_op jit(solution)/shard_map/ppermute | solution.py:49
  28.6 2.0 %collective-permute-done.5 = bf16[32,2048]{1,0:T(8,128)(2,1)S(1)} collective-permute-done((bf16[32,2048]{1,0:T(8,128)(2,1)S(1)}, bf16[32,2048]{1,0:T(8,128)(2,1)S(1)}, u32[]{:S(2)}, u32[]{:S(2)}) %collective-permute-start.5) | collective-permute-done | bytes 131104 | tf_op jit(solution)/shard_map/ppermute | solution.py:49
  30.6 2.6 %collective-permute-start.7 = (bf16[64,2048]{1,0:T(8,128)(2,1)S(1)}, bf16[64,2048]{1,0:T(8,128)(2,1)S(1)}, u32[]{:S(2)}, u32[]{:S(2)}) collective-permute-start(bf16[64,2048]{1,0:T(8,128)(2,1)S(1)} %constant_dynamic-update-slice_fusion.2.refs_1_), channel_id=1, source_target_pairs={{0,96},{4,28},{8,104},{12,20},{16,112},{20,12},{24,120},{28,4},{32... | collective-permute-start | bytes 786440 | tf_op jit(solution)/shard_map/ppermute | solution.py:49
  35.2 1.9 %collective-permute-done.7.refs_3_ = bf16[64,2048]{1,0:T(8,128)(2,1)S(1)} collective-permute-done((bf16[64,2048]{1,0:T(8,128)(2,1)S(1)}, bf16[64,2048]{1,0:T(8,128)(2,1)S(1)}, u32[]{:S(2)}, u32[]{:S(2)}) %collective-permute-start.7) | collective-permute-done | bytes 262176 | tf_op jit(solution)/shard_map/ppermute | solution.py:49
  40.0 3.6 %keeper.1 = (bf16[8,400,256]{2,1,0:T(8,128)(2,1)}, bf16[16,512]{1,0:T(8,128)(2,1)S(1)}) custom-call(s32[8]{0:T(128)S(1)} %copy-done.5, s32[8]{0:T(128)S(1)} %copy-done.6, f32[128,128]{1,0:T(8,128)S(1)} %copy-done.12, f32[128,384]{1,0:T(8,128)S(1)} %copy-done.9, bf16[128,256]{1,0:T(8,128)(2,1)S(1)} %copy-done.13, bf16[128,384]{1,0:T(8,128)(2,1)S(1)} %copy-done.11, ...), custom_call_target="tpu_custom_call" | custom-call | flops 2000000000 | bytes 5000000 | tf_op jit(solution)/shard_map/keeper/pallas_call | solution.py:216
  43.7 4.0 %collective-permute-start.13 = (bf16[128,2048]{1,0:T(8,128)(2,1)S(1)}, bf16[128,2048]{1,0:T(8,128)(2,1)S(1)}, u32[]{:S(2)}, u32[]{:S(2)}) collective-permute-start(bf16[128,2048]{1,0:T(8,128)(2,1)S(1)} %pad_maximum_fusion.1), channel_id=1, source_target_pairs={{0,4},{4,0},{8,12},{12,8},{16,20},{20,16},{24,28},{28,24},{32,36},... | collective-permute-start | bytes 1572872 | tf_op jit(solution)/shard_map/ppermute | solution.py:53
  48.3 2.1 %collective-permute-start.20 = (bf16[64,2048]{1,0:T(8,128)(2,1)}, bf16[64,2048]{1,0:T(8,128)(2,1)S(1)}, u32[]{:S(2)}, u32[]{:S(2)}) collective-permute-start(bf16[64,2048]{1,0:T(8,128)(2,1)} %collective-permute-done.18.refs_0_), channel_id=1, source_target_pairs={{0,4},{4,0},{8,12},{12,8},{16,20},{20,16},{24,28},{28,24},{32,36},... | collective-permute-start | bytes 786440 | tf_op jit(solution)/shard_map/ppermute | solution.py:53
  53.0 1.8 %feed.4 = (bf16[64,2048]{1,0:T(8,128)(2,1)S(1)}, bf16[64,2048]{1,0:T(8,128)(2,1)S(1)}, bf16[64,2048]{1,0:T(8,128)(2,1)S(1)}, bf16[64,2048]{1,0:T(8,128)(2,1)S(1)...) custom-call(bf16[2048,256]{1,0:T(8,128)(2,1)S(1)} %constant_dynamic-update-slice_fusion.both_ref, ...), custom_call_target="tpu_custom_call" | custom-call | flops 2415919104 | bytes 4718592 | tf_op jit(solution)/shard_map/feed/pallas_call | solution.py:540
  54.8 1.8 %feed.5 = (bf16[128,2048]{1,0:T(8,128)(2,1)S(1)}, bf16[128,2048]{1,0:T(8,128)(2,1)S(1)}, bf16[128,2048]{1,0:T(8,128)(2,1)S(1)}) custom-call(bf16[2048,256]{1,0:T(8,128)(2,1)S(1)} %constant_dynamic-update-slice_fusion.both_ref, bf16[128,2048]{1,0:T(8,128)(2,1)S(1)} %copy-done.8, bf16[2048]{0:T(1024)(128)(2,1)S(1)} %copy-done.4, ...), custom_call_target="tpu_custom_call" | custom-call | flops 2415919104 | bytes 4718592 | tf_op jit(solution)/shard_map/feed/pallas_call | solution.py:540
  56.9 1.7 %feed.6 = (bf16[64,2048]{1,0:T(8,128)(2,1)S(1)}, bf16[64,2048]{1,0:T(8,128)(2,1)S(1)}) custom-call(bf16[2048,256]{1,0:T(8,128)(2,1)S(1)} %constant_dynamic-update-slice_fusion.both_ref, bf16[128,2048]{1,0:T(8,128)(2,1)S(1)} %copy-done.8, bf16[16,512]{1,0:T(8,128)(2,1)S(1)} %get-tuple-element.52._token.bc_ref, ...), custom_call_target="tpu_custom_call" | custom-call | flops 805306368 | bytes 2621440 | tf_op jit(solution)/shard_map/feed/pallas_call | solution.py:540
  61.2 1.8 %collective-permute-start.16 = (bf16[64,2048]{1,0:T(8,128)(2,1)}, bf16[64,2048]{1,0:T(8,128)(2,1)S(1)}, u32[]{:S(2)}, u32[]{:S(2)}) collective-permute-start(bf16[64,2048]{1,0:T(8,128)(2,1)} %get-tuple-element.78), channel_id=1, source_target_pairs={{0,96},{4,28},{8,104},{12,20},{16,112},{20,12},{24,120},{28,4},{32... | collective-permute-start | bytes 786440 | tf_op jit(solution)/shard_map/ppermute | solution.py:49
  63.9 2.3 %collective-permute-done.23 = bf16[64,2048]{1,0:T(8,128)(2,1)S(1)} collective-permute-done((bf16[64,2048]{1,0:T(8,128)(2,1)S(1)}, bf16[64,2048]{1,0:T(8,128)(2,1)S(1)}, u32[]{:S(2)}, u32[]{:S(2)}) %collective-permute-start.23) | collective-permute-done | bytes 262176 | tf_op jit(solution)/shard_map/ppermute | solution.py:49
  69.9 3.6 %all-to-all-start = ((bf16[4,2,400,256]{3,2,1,0:T(8,128)(2,1)}), bf16[4,2,400,256]{3,2,1,0:T(8,128)(2,1)S(1)}, u32[]{:S(2)}, u32[]{:S(2)}) async-start(bf16[4,2,400,256]{3,2,1,0:T(8,128)(2,1)} %bitcast.7), calls=%async_computation | async-start | bytes 3276800 | tf_op jit(solution)/shard_map/all_to_all | solution.py:691
  77.6 1.8 %collective-permute-start.25 = (bf16[32,2048]{1,0:T(8,128)(2,1)S(1)}, bf16[32,2048]{1,0:T(8,128)(2,1)S(1)}, u32[]{:S(2)}, u32[]{:S(2)}) collective-permute-start(bf16[32,2048]{1,0:T(8,128)(2,1)S(1)} %slice.109), channel_id=1, source_target_pairs={{0,8},{4,36},{8,0},{12,44},{16,24},{20,52},{24,16},{28,60},{32,40}... | collective-permute-start | bytes 393224 | tf_op jit(solution)/shard_map/ppermute | solution.py:49
  80.0 13.0 %all-to-all-done.kept_hbm = bf16[4,2,400,256]{3,2,1,0:T(8,128)(2,1)S(1)} async-done(((bf16[4,2,400,256]{3,2,1,0:T(8,128)(2,1)}), bf16[4,2,400,256]{3,2,1,0:T(8,128)(2,1)S(1)}, u32[]{:S(2)}, u32[]{:S(2)}) %all-to-all-start) | async-done | bytes 1638432 | tf_op jit(solution)/shard_map/all_to_all | solution.py:691
  94.1 2.6 %collective-permute-start.31 = (bf16[32,2048]{1,0:T(8,128)(2,1)S(1)}, bf16[32,2048]{1,0:T(8,128)(2,1)S(1)}, u32[]{:S(2)}, u32[]{:S(2)}) collective-permute-start(bf16[32,2048]{1,0:T(8,128)(2,1)S(1)} %fusion.2), channel_id=1, source_target_pairs={{0,8},{4,36},{8,0},{12,44},{16,24},{20,52},{24,16},{28,60},{32,40}... | collective-permute-start | bytes 393224 | tf_op jit(solution)/shard_map/ppermute | solution.py:49
  96.8 3.2 %collective-permute-done.34 = bf16[32,2048]{1,0:T(8,128)(2,1)S(1)} collective-permute-done((bf16[32,2048]{1,0:T(8,128)(2,1)S(1)}, bf16[32,2048]{1,0:T(8,128)(2,1)S(1)}, u32[]{:S(2)}, u32[]{:S(2)}) %collective-permute-start.34) | collective-permute-done | bytes 131104 | tf_op jit(solution)/shard_map/ppermute | solution.py:49
  100.0 1.9 %collective-permute-start.39 = (bf16[64,2048]{1,0:T(8,128)(2,1)S(1)}, bf16[64,2048]{1,0:T(8,128)(2,1)S(1)}, u32[]{:S(2)}, u32[]{:S(2)}) collective-permute-start(bf16[64,2048]{1,0:T(8,128)(2,1)S(1)} %constant_dynamic-update-slice_fusion.4.refs_1_), channel_id=1, source_target_pairs={{0,32},{4,12},{8,40},{12,4},{16,48},{20,28},{24,56},{28,20},{32,0}... | collective-permute-start | bytes 786440 | tf_op jit(solution)/shard_map/ppermute | solution.py:49
  104.6 2.1 %collective-permute-done.39.refs_5_ = bf16[64,2048]{1,0:T(8,128)(2,1)S(1)} collective-permute-done((bf16[64,2048]{1,0:T(8,128)(2,1)S(1)}, bf16[64,2048]{1,0:T(8,128)(2,1)S(1)}, u32[]{:S(2)}, u32[]{:S(2)}) %collective-permute-start.39) | collective-permute-done | bytes 262176 | tf_op jit(solution)/shard_map/ppermute | solution.py:49
  108.4 5.1 %collective-permute-start.43 = (bf16[128,2048]{1,0:T(8,128)(2,1)S(1)}, bf16[128,2048]{1,0:T(8,128)(2,1)S(1)}, u32[]{:S(2)}, u32[]{:S(2)}) collective-permute-start(bf16[128,2048]{1,0:T(8,128)(2,1)S(1)} %pad_maximum_fusion.3), channel_id=1, source_target_pairs={{0,4},{4,0},{8,12},{12,8},{16,20},{20,16},{24,28},{28,24},{32,36},... | collective-permute-start | bytes 1572872 | tf_op jit(solution)/shard_map/ppermute | solution.py:53
  113.6 2.8 %collective-permute-start.42 = (bf16[128,2048]{1,0:T(8,128)(2,1)S(1)}, bf16[128,2048]{1,0:T(8,128)(2,1)S(1)}, u32[]{:S(2)}, u32[]{:S(2)}) collective-permute-start(bf16[128,2048]{1,0:T(8,128)(2,1)S(1)} %pad_maximum_fusion.2), channel_id=1, source_target_pairs={{0,4},{4,0},{8,12},{12,8},{16,20},{20,16},{24,28},{28,24},{32,36},... | collective-permute-start | bytes 1572872 | tf_op jit(solution)/shard_map/ppermute | solution.py:53
  119.2 6.8 %head_stats.2.refs_5_ = f32[32,1,128]{2,1,0:T(1,128)S(1)} custom-call(s32[3,256]{1,0:T(4,128)S(1)} %bitcast.27, s32[3,256]{1,0:T(4,128)S(1)} %bitcast.28, bf16[64,2048]{1,0:T(8,128)(2,1)S(1)} %pad_maximum_fusion.5.refs_0_, bf16[64,2048]{1,0:T(8,128)(2,1)S(1)} %constant_dynamic-update-slice_fusion.4.refs_1_, ...), custom_call_target="tpu_custom_call" | custom-call | flops 3221225472 | bytes 7340032 | tf_op jit(solution)/shard_map/head_stats/pallas_call | solution.py:594
  128.6 2.5 %head_stats.3._stats = f32[32,1,128]{2,1,0:T(1,128)} custom-call(s32[1,256]{1,0:T(1,128)S(1)} %slice.97.targets_ref, s32[1,256]{1,0:T(1,128)S(1)} %slice.98.owners_ref, bf16[64,2048]{1,0:T(8,128)(2,1)S(1)} %collective-permute-done.33.refs_0_, bf16[64,2048]{1,0:T(8,128)(2,1)S(1)} %collective-permute-done.37.refs_1_, ...), custom_call_target="tpu_custom_call" | custom-call | flops 1073741824 | bytes 5242880 | tf_op jit(solution)/shard_map/head_stats/pallas_call | solution.py:594
  131.1 4.4 %all-to-all-start.1 = ((f32[32,1,128]{2,1,0:T(1,128)}), f32[32,1,128]{2,1,0:T(1,128)S(1)}, u32[]{:S(2)}, u32[]{:S(2)}) async-start(f32[32,1,128]{2,1,0:T(1,128)} %head_stats.3._stats), calls=%async_computation.1 | async-start | bytes 32768 | tf_op jit(solution)/shard_map/all_to_all | solution.py:711
  135.4 2.1 %unpack.1 = (f32[2,1536,256]{2,1,0:T(8,128)}, bf16[3,2,2048]{2,1,0:T(2,128)(2,1)}) custom-call(bf16[4,2,400,256]{3,2,1,0:T(8,128)(2,1)S(1)} %all-to-all-done.kept_hbm, bf16[16,512]{1,0:T(8,128)(2,1)S(1)} %get-tuple-element.52._token.bc_ref, f32[32,1,128]{2,1,0:T(1,128)} %head_stats.3._stats, bf16[8,128]{1,0:T(8,128)(2,1)S(1)} %slice.90._tip), custom_call_target="tpu_custom_call" | custom-call | flops 1000000 | bytes 20000000 | tf_op jit(solution)/shard_map/unpack/pallas_call | solution.py:263
  137.5 4.9 %all-to-all-done.1 = f32[32,1,128]{2,1,0:T(1,128)S(1)} async-done(((f32[32,1,128]{2,1,0:T(1,128)}), f32[32,1,128]{2,1,0:T(1,128)S(1)}, u32[]{:S(2)}, u32[]{:S(2)}) %all-to-all-start.1) | async-done | bytes 16416 | tf_op jit(solution)/shard_map/all_to_all | solution.py:711
  (171 shorter events, 35.3 us)
Async XLA Ops:
  9.0 6.0 %collective-permute-start = (bf16[32,2048]{1,0:T(8,128)(2,1)}, bf16[32,2048]{1,0:T(8,128)(2,1)S(1)}, u32[]{:S(2)}, u32[]{:S(2)}) collective-permute-start(bf16[32,2048]{1,0:T(8,128)(2,1)} %get-tuple-element.38), channel_id=1, source_target_pairs={{0,1},{1,0},{2,3},{3,2},{4,5},{5,4},{6,7},{7,6},{8,9},{9,8},{10,11... | collective-permute-start | bytes 393224 | tf_op jit(solution)/shard_map/ppermute | solution.py:655
  11.5 7.7 %collective-permute-start.1 = (bf16[32,2048]{1,0:T(8,128)(2,1)}, bf16[32,2048]{1,0:T(8,128)(2,1)S(1)}, u32[]{:S(2)}, u32[]{:S(2)}) collective-permute-start(bf16[32,2048]{1,0:T(8,128)(2,1)} %get-tuple-element.39), channel_id=1, source_target_pairs={{0,3},{1,2},{2,1},{3,0},{4,7},{5,6},{6,5},{7,4},{8,11},{9,10},{10,... | collective-permute-start | bytes 393224 | tf_op jit(solution)/shard_map/ppermute | solution.py:655
  13.8 7.2 %collective-permute-start.2 = (bf16[32,2048]{1,0:T(8,128)(2,1)}, bf16[32,2048]{1,0:T(8,128)(2,1)S(1)}, u32[]{:S(2)}, u32[]{:S(2)}) collective-permute-start(bf16[32,2048]{1,0:T(8,128)(2,1)} %get-tuple-element.40), channel_id=1, source_target_pairs={{0,2},{1,3},{2,0},{3,1},{4,6},{5,7},{6,4},{7,5},{8,10},{9,11},{10,... | collective-permute-start | bytes 393224 | tf_op jit(solution)/shard_map/ppermute | solution.py:655
  22.5 6.1 %collective-permute-start.4 = (bf16[32,2048]{1,0:T(8,128)(2,1)S(1)}, bf16[32,2048]{1,0:T(8,128)(2,1)S(1)}, u32[]{:S(2)}, u32[]{:S(2)}) collective-permute-start(bf16[32,2048]{1,0:T(8,128)(2,1)S(1)} %fusion.5), channel_id=1, source_target_pairs={{0,24},{4,100},{8,16},{12,108},{16,8},{20,116},{24,0},{28,124},{32... | collective-permute-start | bytes 393224 | tf_op jit(solution)/shard_map/ppermute | solution.py:49
  25.6 7.5 %collective-permute-start.3 = (bf16[32,2048]{1,0:T(8,128)(2,1)S(1)}, bf16[32,2048]{1,0:T(8,128)(2,1)S(1)}, u32[]{:S(2)}, u32[]{:S(2)}) collective-permute-start(bf16[32,2048]{1,0:T(8,128)(2,1)S(1)} %fusion.5), channel_id=1, source_target_pairs={{0,8},{4,36},{8,0},{12,44},{16,24},{20,52},{24,16},{28,60},{32,40}... | collective-permute-start | bytes 393224 | tf_op jit(solution)/shard_map/ppermute | solution.py:49
  30.6 6.5 %collective-permute-start.7 = (bf16[64,2048]{1,0:T(8,128)(2,1)S(1)}, bf16[64,2048]{1,0:T(8,128)(2,1)S(1)}, u32[]{:S(2)}, u32[]{:S(2)}) collective-permute-start(bf16[64,2048]{1,0:T(8,128)(2,1)S(1)} %constant_dynamic-update-slice_fusion.2.refs_1_), channel_id=1, source_target_pairs={{0,96},{4,28},{8,104},{12,20},{16,112},{20,12},{24,120},{28,4},{32... | collective-permute-start | bytes 786440 | tf_op jit(solution)/shard_map/ppermute | solution.py:49
  33.4 10.3 %collective-permute-start.9 = (bf16[64,2048]{1,0:T(8,128)(2,1)S(1)}, bf16[64,2048]{1,0:T(8,128)(2,1)S(1)}, u32[]{:S(2)}, u32[]{:S(2)}) collective-permute-start(bf16[64,2048]{1,0:T(8,128)(2,1)S(1)} %constant_dynamic-update-slice_fusion.2.refs_1_), channel_id=1, source_target_pairs={{0,32},{4,12},{8,40},{12,4},{16,48},{20,28},{24,56},{28,20},{32,0}... | collective-permute-start | bytes 786440 | tf_op jit(solution)/shard_map/ppermute | solution.py:49
  34.9 8.8 %collective-permute-start.8 = (bf16[64,2048]{1,0:T(8,128)(2,1)S(1)}, bf16[64,2048]{1,0:T(8,128)(2,1)S(1)}, u32[]{:S(2)}, u32[]{:S(2)}) collective-permute-start(bf16[64,2048]{1,0:T(8,128)(2,1)S(1)} %pad_maximum_fusion.4.refs_0_), channel_id=1, source_target_pairs={{0,96},{4,28},{8,104},{12,20},{16,112},{20,12},{24,120},{28,4},{32... | collective-permute-start | bytes 786440 | tf_op jit(solution)/shard_map/ppermute | solution.py:49
  37.1 10.6 %collective-permute-start.19 = (bf16[64,2048]{1,0:T(8,128)(2,1)S(1)}, bf16[64,2048]{1,0:T(8,128)(2,1)S(1)}, u32[]{:S(2)}, u32[]{:S(2)}) collective-permute-start(bf16[64,2048]{1,0:T(8,128)(2,1)S(1)} %collective-permute-done.7.refs_3_), channel_id=1, source_target_pairs={{0,32},{4,12},{8,40},{12,4},{16,48},{20,28},{24,56},{28,20},{32,0}... | collective-permute-start | bytes 786440 | tf_op jit(solution)/shard_map/ppermute | solution.py:49
  38.8 9.5 %collective-permute-start.18 = (bf16[64,2048]{1,0:T(8,128)(2,1)S(1)}, bf16[64,2048]{1,0:T(8,128)(2,1)}, u32[]{:S(2)}, u32[]{:S(2)}) collective-permute-start(bf16[64,2048]{1,0:T(8,128)(2,1)S(1)} %collective-permute-done.6.refs_2_), channel_id=1, source_target_pairs={{0,96},{4,28},{8,104},{12,20},{16,112},{20,12},{24,120},{28,4},{32... | collective-permute-start | bytes 786440 | tf_op jit(solution)/shard_map/ppermute | solution.py:49
  43.7 11.1 %collective-permute-start.13 = (bf16[128,2048]{1,0:T(8,128)(2,1)S(1)}, bf16[128,2048]{1,0:T(8,128)(2,1)S(1)}, u32[]{:S(2)}, u32[]{:S(2)}) collective-permute-start(bf16[128,2048]{1,0:T(8,128)(2,1)S(1)} %pad_maximum_fusion.1), channel_id=1, source_target_pairs={{0,4},{4,0},{8,12},{12,8},{16,20},{20,16},{24,28},{28,24},{32,36},... | collective-permute-start | bytes 1572872 | tf_op jit(solution)/shard_map/ppermute | solution.py:53
  52.5 6.7 %collective-permute-start.22 = (bf16[128,2048]{1,0:T(8,128)(2,1)S(1)}, bf16[128,2048]{1,0:T(8,128)(2,1)S(1)}, u32[]{:S(2)}, u32[]{:S(2)}) collective-permute-start(bf16[128,2048]{1,0:T(8,128)(2,1)S(1)} %feed.7), channel_id=1, source_target_pairs={{0,4},{4,0},{8,12},{12,8},{16,20},{20,16},{24,28},{28,24},{32,36},... | collective-permute-start | bytes 1572872 | tf_op jit(solution)/shard_map/ppermute | solution.py:53
  59.1 14.4 %collective-permute-start.14 = (bf16[128,2048]{1,0:T(8,128)(2,1)S(1)}, bf16[128,2048]{1,0:T(8,128)(2,1)}, u32[]{:S(2)}, u32[]{:S(2)}) collective-permute-start(bf16[128,2048]{1,0:T(8,128)(2,1)S(1)} %get-tuple-element.42), channel_id=1, source_target_pairs={{0,4},{4,0},{8,12},{12,8},{16,20},{20,16},{24,28},{28,24},{32,36},... | collective-permute-start | bytes 1572872 | tf_op jit(solution)/shard_map/ppermute | solution.py:53
  59.3 6.8 %collective-permute-start.23 = (bf16[64,2048]{1,0:T(8,128)(2,1)S(1)}, bf16[64,2048]{1,0:T(8,128)(2,1)S(1)}, u32[]{:S(2)}, u32[]{:S(2)}) collective-permute-start(bf16[64,2048]{1,0:T(8,128)(2,1)S(1)} %get-tuple-element.82), channel_id=1, source_target_pairs={{0,96},{4,28},{8,104},{12,20},{16,112},{20,12},{24,120},{28,4},{32... | collective-permute-start | bytes 786440 | tf_op jit(solution)/shard_map/ppermute | solution.py:49
  61.2 12.3 %collective-permute-start.16 = (bf16[64,2048]{1,0:T(8,128)(2,1)}, bf16[64,2048]{1,0:T(8,128)(2,1)S(1)}, u32[]{:S(2)}, u32[]{:S(2)}) collective-permute-start(bf16[64,2048]{1,0:T(8,128)(2,1)} %get-tuple-element.78), channel_id=1, source_target_pairs={{0,96},{4,28},{8,104},{12,20},{16,112},{20,12},{24,120},{28,4},{32... | collective-permute-start | bytes 786440 | tf_op jit(solution)/shard_map/ppermute | solution.py:49
  63.0 10.5 %collective-permute-start.26 = (bf16[64,2048]{1,0:T(8,128)(2,1)}, bf16[64,2048]{1,0:T(8,128)(2,1)}, u32[]{:S(2)}, u32[]{:S(2)}) collective-permute-start(bf16[64,2048]{1,0:T(8,128)(2,1)} %get-tuple-element.79), channel_id=1, source_target_pairs={{0,32},{4,12},{8,40},{12,4},{16,48},{20,28},{24,56},{28,20},{32,0}... | collective-permute-start | bytes 786440 | tf_op jit(solution)/shard_map/ppermute | solution.py:49
  67.2 6.4 %collective-permute-start.24 = (bf16[64,2048]{1,0:T(8,128)(2,1)}, bf16[64,2048]{1,0:T(8,128)(2,1)}, u32[]{:S(2)}, u32[]{:S(2)}) collective-permute-start(bf16[64,2048]{1,0:T(8,128)(2,1)} %get-tuple-element.80), channel_id=1, source_target_pairs={{0,32},{4,12},{8,40},{12,4},{16,48},{20,28},{24,56},{28,20},{32,0}... | collective-permute-start | bytes 786440 | tf_op jit(solution)/shard_map/ppermute | solution.py:49
  67.2 7.0 %collective-permute-start.28 = (bf16[64,2048]{1,0:T(8,128)(2,1)}, bf16[64,2048]{1,0:T(8,128)(2,1)}, u32[]{:S(2)}, u32[]{:S(2)}) collective-permute-start(bf16[64,2048]{1,0:T(8,128)(2,1)} %get-tuple-element.81), channel_id=1, source_target_pairs={{0,96},{4,28},{8,104},{12,20},{16,112},{20,12},{24,120},{28,4},{32... | collective-permute-start | bytes 786440 | tf_op jit(solution)/shard_map/ppermute | solution.py:49
  69.9 23.2 %all-to-all-start = ((bf16[4,2,400,256]{3,2,1,0:T(8,128)(2,1)}), bf16[4,2,400,256]{3,2,1,0:T(8,128)(2,1)S(1)}, u32[]{:S(2)}, u32[]{:S(2)}) async-start(bf16[4,2,400,256]{3,2,1,0:T(8,128)(2,1)} %bitcast.7), calls=%async_computation | async-start | bytes 3276800 | tf_op jit(solution)/shard_map/all_to_all | solution.py:691
  76.0 17.1 %collective-permute-start.29 = (bf16[32,2048]{1,0:T(8,128)(2,1)S(1)}, bf16[32,2048]{1,0:T(8,128)(2,1)S(1)}, u32[]{:S(2)}, u32[]{:S(2)}) collective-permute-start(bf16[32,2048]{1,0:T(8,128)(2,1)S(1)} %get-tuple-element.84), channel_id=1, source_target_pairs={{0,24},{4,100},{8,16},{12,108},{16,8},{20,116},{24,0},{28,124},{32... | collective-permute-start | bytes 393224 | tf_op jit(solution)/shard_map/ppermute | solution.py:49
  76.9 16.2 %collective-permute-start.30 = (bf16[32,2048]{1,0:T(8,128)(2,1)S(1)}, bf16[32,2048]{1,0:T(8,128)(2,1)S(1)}, u32[]{:S(2)}, u32[]{:S(2)}) collective-permute-start(bf16[32,2048]{1,0:T(8,128)(2,1)S(1)} %get-tuple-element.85), channel_id=1, source_target_pairs={{0,16},{4,68},{8,24},{12,76},{16,0},{20,84},{24,8},{28,92},{32,48}... | collective-permute-start | bytes 393224 | tf_op jit(solution)/shard_map/ppermute | solution.py:49
  77.6 15.5 %collective-permute-start.25 = (bf16[32,2048]{1,0:T(8,128)(2,1)S(1)}, bf16[32,2048]{1,0:T(8,128)(2,1)S(1)}, u32[]{:S(2)}, u32[]{:S(2)}) collective-permute-start(bf16[32,2048]{1,0:T(8,128)(2,1)S(1)} %slice.109), channel_id=1, source_target_pairs={{0,8},{4,36},{8,0},{12,44},{16,24},{20,52},{24,16},{28,60},{32,40}... | collective-permute-start | bytes 393224 | tf_op jit(solution)/shard_map/ppermute | solution.py:49
  93.4 6.5 %collective-permute-start.34 = (bf16[32,2048]{1,0:T(8,128)(2,1)S(1)}, bf16[32,2048]{1,0:T(8,128)(2,1)S(1)}, u32[]{:S(2)}, u32[]{:S(2)}) collective-permute-start(bf16[32,2048]{1,0:T(8,128)(2,1)S(1)} %fusion.2), channel_id=1, source_target_pairs={{0,24},{4,100},{8,16},{12,108},{16,8},{20,116},{24,0},{28,124},{32... | collective-permute-start | bytes 393224 | tf_op jit(solution)/shard_map/ppermute | solution.py:49
  94.1 7.7 %collective-permute-start.31 = (bf16[32,2048]{1,0:T(8,128)(2,1)S(1)}, bf16[32,2048]{1,0:T(8,128)(2,1)S(1)}, u32[]{:S(2)}, u32[]{:S(2)}) collective-permute-start(bf16[32,2048]{1,0:T(8,128)(2,1)S(1)} %fusion.2), channel_id=1, source_target_pairs={{0,8},{4,36},{8,0},{12,44},{16,24},{20,52},{24,16},{28,60},{32,40}... | collective-permute-start | bytes 393224 | tf_op jit(solution)/shard_map/ppermute | solution.py:49
  100.0 6.8 %collective-permute-start.39 = (bf16[64,2048]{1,0:T(8,128)(2,1)S(1)}, bf16[64,2048]{1,0:T(8,128)(2,1)S(1)}, u32[]{:S(2)}, u32[]{:S(2)}) collective-permute-start(bf16[64,2048]{1,0:T(8,128)(2,1)S(1)} %constant_dynamic-update-slice_fusion.4.refs_1_), channel_id=1, source_target_pairs={{0,32},{4,12},{8,40},{12,4},{16,48},{20,28},{24,56},{28,20},{32,0}... | collective-permute-start | bytes 786440 | tf_op jit(solution)/shard_map/ppermute | solution.py:49
  101.9 6.5 %collective-permute-start.38 = (bf16[64,2048]{1,0:T(8,128)(2,1)S(1)}, bf16[64,2048]{1,0:T(8,128)(2,1)S(1)}, u32[]{:S(2)}, u32[]{:S(2)}) collective-permute-start(bf16[64,2048]{1,0:T(8,128)(2,1)S(1)} %pad_maximum_fusion.5.refs_0_), channel_id=1, source_target_pairs={{0,96},{4,28},{8,104},{12,20},{16,112},{20,12},{24,120},{28,4},{32... | collective-permute-start | bytes 786440 | tf_op jit(solution)/shard_map/ppermute | solution.py:49
  103.5 10.1 %collective-permute-start.36 = (bf16[64,2048]{1,0:T(8,128)(2,1)S(1)}, bf16[64,2048]{1,0:T(8,128)(2,1)S(1)}, u32[]{:S(2)}, u32[]{:S(2)}) collective-permute-start(bf16[64,2048]{1,0:T(8,128)(2,1)S(1)} %constant_dynamic-update-slice_fusion.4.refs_1_), channel_id=1, source_target_pairs={{0,96},{4,28},{8,104},{12,20},{16,112},{20,12},{24,120},{28,4},{32... | collective-permute-start | bytes 786440 | tf_op jit(solution)/shard_map/ppermute | solution.py:49
  104.6 8.9 %collective-permute-start.32 = (bf16[64,2048]{1,0:T(8,128)(2,1)S(1)}, bf16[64,2048]{1,0:T(8,128)(2,1)S(1)}, u32[]{:S(2)}, u32[]{:S(2)}) collective-permute-start(bf16[64,2048]{1,0:T(8,128)(2,1)S(1)} %pad_maximum_fusion.5.refs_0_), channel_id=1, source_target_pairs={{0,32},{4,12},{8,40},{12,4},{16,48},{20,28},{24,56},{28,20},{32,0}... | collective-permute-start | bytes 786440 | tf_op jit(solution)/shard_map/ppermute | solution.py:49
  108.4 10.8 %collective-permute-start.43 = (bf16[128,2048]{1,0:T(8,128)(2,1)S(1)}, bf16[128,2048]{1,0:T(8,128)(2,1)S(1)}, u32[]{:S(2)}, u32[]{:S(2)}) collective-permute-start(bf16[128,2048]{1,0:T(8,128)(2,1)S(1)} %pad_maximum_fusion.3), channel_id=1, source_target_pairs={{0,4},{4,0},{8,12},{12,8},{16,20},{20,16},{24,28},{28,24},{32,36},... | collective-permute-start | bytes 1572872 | tf_op jit(solution)/shard_map/ppermute | solution.py:53
  116.9 9.1 %collective-permute-start.37 = (bf16[64,2048]{1,0:T(8,128)(2,1)S(1)}, bf16[64,2048]{1,0:T(8,128)(2,1)S(1)}, u32[]{:S(2)}, u32[]{:S(2)}) collective-permute-start(bf16[64,2048]{1,0:T(8,128)(2,1)S(1)} %collective-permute-done.36.refs_3_), channel_id=1, source_target_pairs={{0,32},{4,12},{8,40},{12,4},{16,48},{20,28},{24,56},{28,20},{32,0}... | collective-permute-start | bytes 786440 | tf_op jit(solution)/shard_map/ppermute | solution.py:49
  118.3 7.7 %collective-permute-start.33 = (bf16[64,2048]{1,0:T(8,128)(2,1)S(1)}, bf16[64,2048]{1,0:T(8,128)(2,1)S(1)}, u32[]{:S(2)}, u32[]{:S(2)}) collective-permute-start(bf16[64,2048]{1,0:T(8,128)(2,1)S(1)} %collective-permute-done.32.refs_2_), channel_id=1, source_target_pairs={{0,96},{4,28},{8,104},{12,20},{16,112},{20,12},{24,120},{28,4},{32... | collective-permute-start | bytes 786440 | tf_op jit(solution)/shard_map/ppermute | solution.py:49
  131.1 11.3 %all-to-all-start.1 = ((f32[32,1,128]{2,1,0:T(1,128)}), f32[32,1,128]{2,1,0:T(1,128)S(1)}, u32[]{:S(2)}, u32[]{:S(2)}) async-start(f32[32,1,128]{2,1,0:T(1,128)} %head_stats.3._stats), calls=%async_computation.1 | async-start | bytes 32768 | tf_op jit(solution)/shard_map/all_to_all | solution.py:711
  (41 other events, 477.8 us)

commit v6 on v5

--- a/solution.py
+++ b/solution.py
@@ -66,14 +66,18 @@
     return sum(part.astype(jnp.float32) for part in parts).astype(jnp.bfloat16)
 
 
+def stream(joined, s):
+    rows = joined.shape[0] // 2
+    return joined[s * rows : (s + 1) * rows]
+
+
+def late_sum(late):
+    came = swap_core(late[1][0])
+    return [added(late[0][s], stream(came, s)) for s in range(2)]
+
+
 def scatter_rows(early, late):
-    rows = late[0][0].shape[0]
-
-    def stream(joined, s):
-        return joined[s * rows : (s + 1) * rows]
-
-    came = swap_core(late[1][0])
-    last = [hop(added(late[0][s], stream(came, s)), 1, EDGES[s][1]) for s in range(2)]
+    last = [hop(late[s], 1, EDGES[s][1]) for s in range(2)]
     kept, near, far = (swap_core(part) for part in early[1])
     own = early[0]
     far = [hop(added(own[4 + s], stream(far, s)), 1, EDGES[s][1]) for s in range(2)]
@@ -677,13 +681,14 @@
     owners = jnp.broadcast_to(owner[:, None], (64, draft_len)).reshape(4, 16 * draft_len)
 
     half = 2 * own_tokens
-    early_parts = [
-        feed(rows, out_rows, w_both, w_down, mlp_gain)
-        for rows, out_rows in zip(early, ([half] * 6, [2 * half] * 3), strict=True)
-    ]
     late_parts = [
         feed(rows, out_rows, w_both, w_down, own_bc)
         for rows, out_rows in zip(late, ([half] * 2, [2 * half]), strict=True)
+    ]
+    late_parts = late_sum(late_parts)
+    early_parts = [
+        feed(rows, out_rows, w_both, w_down, late_parts[0])
+        for rows, out_rows in zip(early, ([half] * 6, [2 * half] * 3), strict=True)
     ]
     summed = scatter_rows(early_parts, late_parts)
     tip = early_parts[0][0][:8, :128]
@@ -695,9 +700,7 @@
         concat_axis=0,
         tiled=True,
     )
-    final_gain, kept_out, targets, owners = lax.optimization_barrier(
-        (final_gain, kept_out, targets, owners)
-    )
+    final_gain, targets, owners = lax.optimization_barrier((final_gain, targets, owners))
     after_feed = (after_mixer.astype(jnp.float32) + summed).astype(jnp.bfloat16)
     final_rows = rms_scale(after_feed, final_gain).astype(jnp.bfloat16)
     early, late = gather_rows(final_rows)

time: 144 us -> 145 us (level)
  waiting for transfers between devices: 45.1 us -> 37.1 us
  starting transfers between devices: 58.6 us -> 64.8 us
  local copies, waits for them, and re-layouts: 1.65 us -> 4.85 us
    all_to_all x1, waiting for transfers between devices: 13 us -> 0.01 us  [shards(): lax.all_to_all(kept.reshape(mdl_count, own_reqs, local_inner + 16, STATE)...]
    ppermute x27, waiting for transfers between devices: 18.1 us -> 24 us  [hop(): return lax.ppermute(part, 'req', flip_pairs(ring, flip))]
    ppermute x16, starting transfers between devices: 18.3 us -> 22.9 us  [swap_core(): return lax.ppermute(part, 'req', CORE_PAIRS)]
    unnamed x51 -> x49, local copies, waits for them, and re-layouts: 0.23 us -> 3.43 us
    all_to_all x1, starting transfers between devices: 4.36 us -> 5.84 us  [shards(): lax.all_to_all(stats, 'req', split_axis=0, concat_axis=0, tiled=True)]
  transfers between devices with their start and end apart: 48 -> 48, of which waited for: 18 -> 23; matrix products, arithmetic and copies ran while one was open for 4% -> 4% of each run, Pallas kernels for 13% -> 13%
where the time goes in v6:
time: 145 us
  starting transfers between devices  64.8 us (45%)
  waiting for transfers between devices  37.1 us (26%)
  Pallas kernels  29.5 us (20%)
  other arithmetic  7.48 us (5%)
  local copies, waits for them, and re-layouts  4.85 us (3%)
    ppermute x27, starting transfers between devices, hop(): return lax.ppermute(part, 'req', flip_pairs(ring, flip))  26.7 us
    ppermute x27, waiting for transfers between devices, hop(): return lax.ppermute(part, 'req', flip_pairs(ring, flip))  24 us
    ppermute x16, starting transfers between devices, swap_core(): return lax.ppermute(part, 'req', CORE_PAIRS)  22.9 us
    pallas_call x2, Pallas kernels, head_stats(): pl.pallas_call(functools.partial(head_kernel, len(rows)), out_shape=jax.S...  9.26 us
    pallas_call x1, Pallas kernels, mixer(): pl.pallas_call(mixer_kernel, out_shape=[*[jax.ShapeDtypeStruct((tokens //...  8.31 us
    pallas_call x4, Pallas kernels, feed(): pl.pallas_call(functools.partial(feed_kernel, len(arrays)), out_shape=[ja...  6.28 us
    ppermute x3, waiting for transfers between devices, shards(): lax.ppermute(part, 'mdl', [(z, z ^ flip) for z in range(SIDE)])  6.13 us
    ppermute x3, starting transfers between devices, shards(): lax.ppermute(part, 'mdl', [(z, z ^ flip) for z in range(SIDE)])  5.85 us
  transfers between devices with their start and end apart: 48, of which 23 were waited for; matrix products, arithmetic and copies ran while one was open for 4% of the time, Pallas kernels for 13%

profile of v6, /device:TPU:1, one launch (start us, length us, event | category | flops | bytes accessed | tf_op | source)
XLA Modules:
  0.0 145.0 jit_solution(14491819826169851340)
XLA Ops:
  0.6 8.3 %mixer.1 = (bf16[32,2048]{1,0:T(8,128)(2,1)}, bf16[32,2048]{1,0:T(8,128)(2,1)}, bf16[32,2048]{1,0:T(8,128)(2,1)}, bf16[32,2048]{1,0:T(8,128)(2,1)}, f32[128,128]...) custom-call(s32[8]{0:T(128)} %refs_0_.3, ...), custom_call_target="tpu_custom_call" | custom-call | flops 3000000000 | bytes 20000000 | tf_op jit(solution)/shard_map/mixer/pallas_call | solution.py:489
  9.0 2.5 %collective-permute-start = (bf16[32,2048]{1,0:T(8,128)(2,1)}, bf16[32,2048]{1,0:T(8,128)(2,1)S(1)}, u32[]{:S(2)}, u32[]{:S(2)}) collective-permute-start(bf16[32,2048]{1,0:T(8,128)(2,1)} %get-tuple-element.37), channel_id=1, source_target_pairs={{0,1},{1,0},{2,3},{3,2},{4,5},{5,4},{6,7},{7,6},{8,9},{9,8},{10,11... | collective-permute-start | bytes 393224 | tf_op jit(solution)/shard_map/ppermute | solution.py:659
  11.5 2.2 %collective-permute-start.1 = (bf16[32,2048]{1,0:T(8,128)(2,1)}, bf16[32,2048]{1,0:T(8,128)(2,1)S(1)}, u32[]{:S(2)}, u32[]{:S(2)}) collective-permute-start(bf16[32,2048]{1,0:T(8,128)(2,1)} %get-tuple-element.38), channel_id=1, source_target_pairs={{0,3},{1,2},{2,1},{3,0},{4,7},{5,6},{6,5},{7,4},{8,11},{9,10},{10,... | collective-permute-start | bytes 393224 | tf_op jit(solution)/shard_map/ppermute | solution.py:659
  14.9 4.3 %collective-permute-done.1 = bf16[32,2048]{1,0:T(8,128)(2,1)S(1)} collective-permute-done((bf16[32,2048]{1,0:T(8,128)(2,1)}, bf16[32,2048]{1,0:T(8,128)(2,1)S(1)}, u32[]{:S(2)}, u32[]{:S(2)}) %collective-permute-start.1) | collective-permute-done | bytes 131104 | tf_op jit(solution)/shard_map/ppermute | solution.py:659
  19.2 1.8 %collective-permute-done.2 = bf16[32,2048]{1,0:T(8,128)(2,1)S(1)} collective-permute-done((bf16[32,2048]{1,0:T(8,128)(2,1)}, bf16[32,2048]{1,0:T(8,128)(2,1)S(1)}, u32[]{:S(2)}, u32[]{:S(2)}) %collective-permute-start.2) | collective-permute-done | bytes 131104 | tf_op jit(solution)/shard_map/ppermute | solution.py:659
  22.4 2.8 %collective-permute-start.6 = (bf16[32,2048]{1,0:T(8,128)(2,1)S(1)}, bf16[32,2048]{1,0:T(8,128)(2,1)S(1)}, u32[]{:S(2)}, u32[]{:S(2)}) collective-permute-start(bf16[32,2048]{1,0:T(8,128)(2,1)S(1)} %fusion.5), channel_id=1, source_target_pairs={{0,24},{4,100},{8,16},{12,108},{16,8},{20,116},{24,0},{28,124},{32... | collective-permute-start | bytes 393224 | tf_op jit(solution)/shard_map/ppermute | solution.py:49
  25.9 2.6 %collective-permute-done.6 = bf16[32,2048]{1,0:T(8,128)(2,1)S(1)} collective-permute-done((bf16[32,2048]{1,0:T(8,128)(2,1)S(1)}, bf16[32,2048]{1,0:T(8,128)(2,1)S(1)}, u32[]{:S(2)}, u32[]{:S(2)}) %collective-permute-start.6) | collective-permute-done | bytes 131104 | tf_op jit(solution)/shard_map/ppermute | solution.py:49
  28.6 2.0 %collective-permute-done.7 = bf16[32,2048]{1,0:T(8,128)(2,1)S(1)} collective-permute-done((bf16[32,2048]{1,0:T(8,128)(2,1)S(1)}, bf16[32,2048]{1,0:T(8,128)(2,1)S(1)}, u32[]{:S(2)}, u32[]{:S(2)}) %collective-permute-start.7) | collective-permute-done | bytes 131104 | tf_op jit(solution)/shard_map/ppermute | solution.py:49
  30.6 2.6 %collective-permute-start.8 = (bf16[64,2048]{1,0:T(8,128)(2,1)S(1)}, bf16[64,2048]{1,0:T(8,128)(2,1)S(1)}, u32[]{:S(2)}, u32[]{:S(2)}) collective-permute-start(bf16[64,2048]{1,0:T(8,128)(2,1)S(1)} %constant_dynamic-update-slice_fusion.2.refs_1_), channel_id=1, source_target_pairs={{0,96},{4,28},{8,104},{12,20},{16,112},{20,12},{24,120},{28,4},{32... | collective-permute-start | bytes 786440 | tf_op jit(solution)/shard_map/ppermute | solution.py:49
  33.3 3.8 %collective-permute-done.8.refs_3_ = bf16[64,2048]{1,0:T(8,128)(2,1)S(1)} collective-permute-done((bf16[64,2048]{1,0:T(8,128)(2,1)S(1)}, bf16[64,2048]{1,0:T(8,128)(2,1)S(1)}, u32[]{:S(2)}, u32[]{:S(2)}) %collective-permute-start.8) | collective-permute-done | bytes 262176 | tf_op jit(solution)/shard_map/ppermute | solution.py:49
  37.1 1.7 %collective-permute-done.4.refs_2_ = bf16[64,2048]{1,0:T(8,128)(2,1)S(1)} collective-permute-done((bf16[64,2048]{1,0:T(8,128)(2,1)S(1)}, bf16[64,2048]{1,0:T(8,128)(2,1)S(1)}, u32[]{:S(2)}, u32[]{:S(2)}) %collective-permute-start.4) | collective-permute-done | bytes 262176 | tf_op jit(solution)/shard_map/ppermute | solution.py:49
  40.0 2.3 %collective-permute-done.9.refs_1_ = bf16[64,2048]{1,0:T(8,128)(2,1)S(1)} collective-permute-done((bf16[64,2048]{1,0:T(8,128)(2,1)S(1)}, bf16[64,2048]{1,0:T(8,128)(2,1)S(1)}, u32[]{:S(2)}, u32[]{:S(2)}) %collective-permute-start.9) | collective-permute-done | bytes 262176 | tf_op jit(solution)/shard_map/ppermute | solution.py:49
  42.3 4.8 %collective-permute-start.11 = (bf16[64,2048]{1,0:T(8,128)(2,1)S(1)}, bf16[64,2048]{1,0:T(8,128)(2,1)S(1)}, u32[]{:S(2)}, u32[]{:S(2)}) collective-permute-start(bf16[64,2048]{1,0:T(8,128)(2,1)S(1)} %collective-permute-done.9.refs_1_), channel_id=1, source_target_pairs={{0,4},{4,0},{8,12},{12,8},{16,20},{20,16},{24,28},{28,24},{32,36},... | collective-permute-start | bytes 786440 | tf_op jit(solution)/shard_map/ppermute | solution.py:53
  47.1 3.1 %collective-permute-start.10 = (bf16[64,2048]{1,0:T(8,128)(2,1)S(1)}, bf16[64,2048]{1,0:T(8,128)(2,1)S(1)}, u32[]{:S(2)}, u32[]{:S(2)}) collective-permute-start(bf16[64,2048]{1,0:T(8,128)(2,1)S(1)} %collective-permute-done.5.refs_0_), channel_id=1, source_target_pairs={{0,4},{4,0},{8,12},{12,8},{16,20},{20,16},{24,28},{28,24},{32,36},... | collective-permute-start | bytes 786440 | tf_op jit(solution)/shard_map/ppermute | solution.py:53
  51.5 3.6 %keeper.1 = (bf16[8,400,256]{2,1,0:T(8,128)(2,1)}, bf16[16,512]{1,0:T(8,128)(2,1)S(1)}) custom-call(s32[8]{0:T(128)S(1)} %copy-done.5, s32[8]{0:T(128)S(1)} %copy-done.6, f32[128,128]{1,0:T(8,128)S(1)} %copy-done.12, f32[128,384]{1,0:T(8,128)S(1)} %copy-done.9, bf16[128,256]{1,0:T(8,128)(2,1)S(1)} %copy-done.13, bf16[128,384]{1,0:T(8,128)(2,1)S(1)} %copy-done.11, ...), custom_call_target="tpu_custom_call" | custom-call | flops 2000000000 | bytes 5000000 | tf_op jit(solution)/shard_map/keeper/pallas_call | solution.py:220
  60.8 2.9 %feed.7 = (bf16[128,2048]{1,0:T(8,128)(2,1)}, bf16[128,2048]{1,0:T(8,128)(2,1)}, bf16[128,2048]{1,0:T(8,128)(2,1)}) custom-call(bf16[2048,256]{1,0:T(8,128)(2,1)S(1)} %constant_dynamic-update-slice_fusion.both_ref, bf16[128,2048]{1,0:T(8,128)(2,1)S(1)} %copy-done.7, bf16[64,2048]{1,0:T(8,128)(2,1)S(1)} %get-tuple-element.80._token, ...), custom_call_target="tpu_custom_call" | custom-call | flops 2415919104 | bytes 4718592 | tf_op jit(solution)/shard_map/feed/pallas_call | solution.py:544
  68.0 1.8 %feed.6 = (bf16[64,2048]{1,0:T(8,128)(2,1)S(1)}, bf16[64,2048]{1,0:T(8,128)(2,1)S(1)}, bf16[64,2048]{1,0:T(8,128)(2,1)S(1)}, bf16[64,2048]{1,0:T(8,128)(2,1)S(1)...) custom-call(bf16[2048,256]{1,0:T(8,128)(2,1)S(1)} %constant_dynamic-update-slice_fusion.both_ref, ...), custom_call_target="tpu_custom_call" | custom-call | flops 2415919104 | bytes 4718592 | tf_op jit(solution)/shard_map/feed/pallas_call | solution.py:544
  78.1 2.8 %collective-permute-done.24 = bf16[64,2048]{1,0:T(8,128)(2,1)S(1)} collective-permute-done((bf16[64,2048]{1,0:T(8,128)(2,1)S(1)}, bf16[64,2048]{1,0:T(8,128)(2,1)S(1)}, u32[]{:S(2)}, u32[]{:S(2)}) %collective-permute-start.24) | collective-permute-done | bytes 262176 | tf_op jit(solution)/shard_map/ppermute | solution.py:49
  82.5 1.9 %collective-permute-start.29 = (bf16[32,2048]{1,0:T(8,128)(2,1)S(1)}, bf16[32,2048]{1,0:T(8,128)(2,1)S(1)}, u32[]{:S(2)}, u32[]{:S(2)}) collective-permute-start(bf16[32,2048]{1,0:T(8,128)(2,1)S(1)} %get-tuple-element.82), channel_id=1, source_target_pairs={{0,24},{4,100},{8,16},{12,108},{16,8},{20,116},{24,0},{28,124},{32... | collective-permute-start | bytes 393224 | tf_op jit(solution)/shard_map/ppermute | solution.py:49
  87.6 2.1 %collective-permute-done.30 = bf16[32,2048]{1,0:T(8,128)(2,1)S(1)} collective-permute-done((bf16[32,2048]{1,0:T(8,128)(2,1)S(1)}, bf16[32,2048]{1,0:T(8,128)(2,1)S(1)}, u32[]{:S(2)}, u32[]{:S(2)}) %collective-permute-start.30) | collective-permute-done | bytes 131104 | tf_op jit(solution)/shard_map/ppermute | solution.py:49
  93.6 1.8 %collective-permute-done.34 = bf16[32,2048]{1,0:T(8,128)(2,1)S(1)} collective-permute-done((bf16[32,2048]{1,0:T(8,128)(2,1)S(1)}, bf16[32,2048]{1,0:T(8,128)(2,1)S(1)}, u32[]{:S(2)}, u32[]{:S(2)}) %collective-permute-start.34) | collective-permute-done | bytes 131104 | tf_op jit(solution)/shard_map/ppermute | solution.py:49
  95.4 1.8 %collective-permute-done.35 = bf16[32,2048]{1,0:T(8,128)(2,1)S(1)} collective-permute-done((bf16[32,2048]{1,0:T(8,128)(2,1)S(1)}, bf16[32,2048]{1,0:T(8,128)(2,1)S(1)}, u32[]{:S(2)}, u32[]{:S(2)}) %collective-permute-start.35) | collective-permute-done | bytes 131104 | tf_op jit(solution)/shard_map/ppermute | solution.py:49
  100.3 3.6 %all-to-all-start.1 = ((bf16[4,2,400,256]{3,2,1,0:T(8,128)(2,1)}), bf16[4,2,400,256]{3,2,1,0:T(8,128)(2,1)S(1)}, u32[]{:S(2)}, u32[]{:S(2)}) async-start(bf16[4,2,400,256]{3,2,1,0:T(8,128)(2,1)} %bitcast.11), calls=%async_computation.1 | async-start | bytes 3276800 | tf_op jit(solution)/shard_map/all_to_all | solution.py:696
  104.1 6.9 %collective-permute-start.43 = (bf16[128,2048]{1,0:T(8,128)(2,1)S(1)}, bf16[128,2048]{1,0:T(8,128)(2,1)S(1)}, u32[]{:S(2)}, u32[]{:S(2)}) collective-permute-start(bf16[128,2048]{1,0:T(8,128)(2,1)S(1)} %pad_maximum_fusion.3), channel_id=1, source_target_pairs={{0,4},{4,0},{8,12},{12,8},{16,20},{20,16},{24,28},{28,24},{32,36},... | collective-permute-start | bytes 1572872 | tf_op jit(solution)/shard_map/ppermute | solution.py:53
  111.1 2.8 %collective-permute-start.42 = (bf16[128,2048]{1,0:T(8,128)(2,1)S(1)}, bf16[128,2048]{1,0:T(8,128)(2,1)S(1)}, u32[]{:S(2)}, u32[]{:S(2)}) collective-permute-start(bf16[128,2048]{1,0:T(8,128)(2,1)S(1)} %pad_maximum_fusion.2), channel_id=1, source_target_pairs={{0,4},{4,0},{8,12},{12,8},{16,20},{20,16},{24,28},{28,24},{32,36},... | collective-permute-start | bytes 1572872 | tf_op jit(solution)/shard_map/ppermute | solution.py:53
  114.3 2.2 %collective-permute-start.37 = (bf16[64,2048]{1,0:T(8,128)(2,1)S(1)}, bf16[64,2048]{1,0:T(8,128)(2,1)S(1)}, u32[]{:S(2)}, u32[]{:S(2)}) collective-permute-start(bf16[64,2048]{1,0:T(8,128)(2,1)S(1)} %collective-permute-done.36.refs_3_), channel_id=1, source_target_pairs={{0,32},{4,12},{8,40},{12,4},{16,48},{20,28},{24,56},{28,20},{32,0}... | collective-permute-start | bytes 786440 | tf_op jit(solution)/shard_map/ppermute | solution.py:49
  117.7 2.2 %copy-done = bf16[1024,2048]{1,0:T(8,128)(2,1)S(1)} copy-done((bf16[1024,2048]{1,0:T(8,128)(2,1)S(1)}, bf16[1024,2048]{1,0:T(8,128)(2,1)}, u32[]{:S(2)}) %copy-start) | copy-done | bytes 4194328
  119.9 6.8 %head_stats.2.refs_5_ = f32[32,1,128]{2,1,0:T(1,128)S(1)} custom-call(s32[3,256]{1,0:T(4,128)S(1)} %bitcast.27, s32[3,256]{1,0:T(4,128)S(1)} %bitcast.28, bf16[64,2048]{1,0:T(8,128)(2,1)S(1)} %pad_maximum_fusion.5.refs_0_, bf16[64,2048]{1,0:T(8,128)(2,1)S(1)} %constant_dynamic-update-slice_fusion.4.refs_1_, ...), custom_call_target="tpu_custom_call" | custom-call | flops 3221225472 | bytes 7340032 | tf_op jit(solution)/shard_map/head_stats/pallas_call | solution.py:598
  128.7 2.5 %head_stats.3._stats = f32[32,1,128]{2,1,0:T(1,128)} custom-call(s32[1,256]{1,0:T(1,128)S(1)} %slice.96.targets_ref, s32[1,256]{1,0:T(1,128)S(1)} %slice.97.owners_ref, bf16[64,2048]{1,0:T(8,128)(2,1)S(1)} %collective-permute-done.33.refs_0_, bf16[64,2048]{1,0:T(8,128)(2,1)S(1)} %collective-permute-done.37.refs_1_, ...), custom_call_target="tpu_custom_call" | custom-call | flops 1073741824 | bytes 5242880 | tf_op jit(solution)/shard_map/head_stats/pallas_call | solution.py:598
  131.2 5.8 %all-to-all-start = ((f32[32,1,128]{2,1,0:T(1,128)}), f32[32,1,128]{2,1,0:T(1,128)S(1)}, u32[]{:S(2)}, u32[]{:S(2)}) async-start(f32[32,1,128]{2,1,0:T(1,128)} %head_stats.3._stats), calls=%async_computation | async-start | bytes 32768 | tf_op jit(solution)/shard_map/all_to_all | solution.py:714
  137.1 2.1 %unpack.1 = (f32[2,1536,256]{2,1,0:T(8,128)}, bf16[3,2,2048]{2,1,0:T(2,128)(2,1)}) custom-call(bf16[4,2,400,256]{3,2,1,0:T(8,128)(2,1)S(1)} %all-to-all-done.1.kept_hbm, bf16[16,512]{1,0:T(8,128)(2,1)S(1)} %get-tuple-element.45._token.bc_ref, f32[32,1,128]{2,1,0:T(1,128)} %head_stats.3._stats, bf16[8,128]{1,0:T(8,128)(2,1)S(1)} %slice.103._tip), custom_call_target="tpu_custom_call" | custom-call | flops 1000000 | bytes 20000000 | tf_op jit(solution)/shard_map/unpack/pallas_call | solution.py:267
  139.1 4.9 %all-to-all-done = f32[32,1,128]{2,1,0:T(1,128)S(1)} async-done(((f32[32,1,128]{2,1,0:T(1,128)}), f32[32,1,128]{2,1,0:T(1,128)S(1)}, u32[]{:S(2)}, u32[]{:S(2)}) %all-to-all-start) | async-done | bytes 16416 | tf_op jit(solution)/shard_map/all_to_all | solution.py:714
  (169 shorter events, 40.6 us)
Async XLA Ops:
  9.0 6.0 %collective-permute-start = (bf16[32,2048]{1,0:T(8,128)(2,1)}, bf16[32,2048]{1,0:T(8,128)(2,1)S(1)}, u32[]{:S(2)}, u32[]{:S(2)}) collective-permute-start(bf16[32,2048]{1,0:T(8,128)(2,1)} %get-tuple-element.37), channel_id=1, source_target_pairs={{0,1},{1,0},{2,3},{3,2},{4,5},{5,4},{6,7},{7,6},{8,9},{9,8},{10,11... | collective-permute-start | bytes 393224 | tf_op jit(solution)/shard_map/ppermute | solution.py:659
  11.5 7.7 %collective-permute-start.1 = (bf16[32,2048]{1,0:T(8,128)(2,1)}, bf16[32,2048]{1,0:T(8,128)(2,1)S(1)}, u32[]{:S(2)}, u32[]{:S(2)}) collective-permute-start(bf16[32,2048]{1,0:T(8,128)(2,1)} %get-tuple-element.38), channel_id=1, source_target_pairs={{0,3},{1,2},{2,1},{3,0},{4,7},{5,6},{6,5},{7,4},{8,11},{9,10},{10,... | collective-permute-start | bytes 393224 | tf_op jit(solution)/shard_map/ppermute | solution.py:659
  13.8 7.2 %collective-permute-start.2 = (bf16[32,2048]{1,0:T(8,128)(2,1)}, bf16[32,2048]{1,0:T(8,128)(2,1)S(1)}, u32[]{:S(2)}, u32[]{:S(2)}) collective-permute-start(bf16[32,2048]{1,0:T(8,128)(2,1)} %get-tuple-element.39), channel_id=1, source_target_pairs={{0,2},{1,3},{2,0},{3,1},{4,6},{5,7},{6,4},{7,5},{8,10},{9,11},{10,... | collective-permute-start | bytes 393224 | tf_op jit(solution)/shard_map/ppermute | solution.py:659
  22.4 6.1 %collective-permute-start.6 = (bf16[32,2048]{1,0:T(8,128)(2,1)S(1)}, bf16[32,2048]{1,0:T(8,128)(2,1)S(1)}, u32[]{:S(2)}, u32[]{:S(2)}) collective-permute-start(bf16[32,2048]{1,0:T(8,128)(2,1)S(1)} %fusion.5), channel_id=1, source_target_pairs={{0,24},{4,100},{8,16},{12,108},{16,8},{20,116},{24,0},{28,124},{32... | collective-permute-start | bytes 393224 | tf_op jit(solution)/shard_map/ppermute | solution.py:49
  25.3 5.3 %collective-permute-start.7 = (bf16[32,2048]{1,0:T(8,128)(2,1)S(1)}, bf16[32,2048]{1,0:T(8,128)(2,1)S(1)}, u32[]{:S(2)}, u32[]{:S(2)}) collective-permute-start(bf16[32,2048]{1,0:T(8,128)(2,1)S(1)} %fusion.5), channel_id=1, source_target_pairs={{0,16},{4,68},{8,24},{12,76},{16,0},{20,84},{24,8},{28,92},{32,48}... | collective-permute-start | bytes 393224 | tf_op jit(solution)/shard_map/ppermute | solution.py:49
  25.6 7.5 %collective-permute-start.3 = (bf16[32,2048]{1,0:T(8,128)(2,1)S(1)}, bf16[32,2048]{1,0:T(8,128)(2,1)S(1)}, u32[]{:S(2)}, u32[]{:S(2)}) collective-permute-start(bf16[32,2048]{1,0:T(8,128)(2,1)S(1)} %fusion.5), channel_id=1, source_target_pairs={{0,8},{4,36},{8,0},{12,44},{16,24},{20,52},{24,16},{28,60},{32,40}... | collective-permute-start | bytes 393224 | tf_op jit(solution)/shard_map/ppermute | solution.py:49
  30.6 6.5 %collective-permute-start.8 = (bf16[64,2048]{1,0:T(8,128)(2,1)S(1)}, bf16[64,2048]{1,0:T(8,128)(2,1)S(1)}, u32[]{:S(2)}, u32[]{:S(2)}) collective-permute-start(bf16[64,2048]{1,0:T(8,128)(2,1)S(1)} %constant_dynamic-update-slice_fusion.2.refs_1_), channel_id=1, source_target_pairs={{0,96},{4,28},{8,104},{12,20},{16,112},{20,12},{24,120},{28,4},{32... | collective-permute-start | bytes 786440 | tf_op jit(solution)/shard_map/ppermute | solution.py:49
  33.2 5.6 %collective-permute-start.4 = (bf16[64,2048]{1,0:T(8,128)(2,1)S(1)}, bf16[64,2048]{1,0:T(8,128)(2,1)S(1)}, u32[]{:S(2)}, u32[]{:S(2)}) collective-permute-start(bf16[64,2048]{1,0:T(8,128)(2,1)S(1)} %pad_maximum_fusion.4.refs_0_), channel_id=1, source_target_pairs={{0,32},{4,12},{8,40},{12,4},{16,48},{20,28},{24,56},{28,20},{32,0}... | collective-permute-start | bytes 786440 | tf_op jit(solution)/shard_map/ppermute | solution.py:49
  38.8 8.4 %collective-permute-start.5 = (bf16[64,2048]{1,0:T(8,128)(2,1)S(1)}, bf16[64,2048]{1,0:T(8,128)(2,1)S(1)}, u32[]{:S(2)}, u32[]{:S(2)}) collective-permute-start(bf16[64,2048]{1,0:T(8,128)(2,1)S(1)} %collective-permute-done.4.refs_2_), channel_id=1, source_target_pairs={{0,96},{4,28},{8,104},{12,20},{16,112},{20,12},{24,120},{28,4},{32... | collective-permute-start | bytes 786440 | tf_op jit(solution)/shard_map/ppermute | solution.py:49
  42.3 13.8 %collective-permute-start.11 = (bf16[64,2048]{1,0:T(8,128)(2,1)S(1)}, bf16[64,2048]{1,0:T(8,128)(2,1)S(1)}, u32[]{:S(2)}, u32[]{:S(2)}) collective-permute-start(bf16[64,2048]{1,0:T(8,128)(2,1)S(1)} %collective-permute-done.9.refs_1_), channel_id=1, source_target_pairs={{0,4},{4,0},{8,12},{12,8},{16,20},{20,16},{24,28},{28,24},{32,36},... | collective-permute-start | bytes 786440 | tf_op jit(solution)/shard_map/ppermute | solution.py:53
  47.1 9.1 %collective-permute-start.10 = (bf16[64,2048]{1,0:T(8,128)(2,1)S(1)}, bf16[64,2048]{1,0:T(8,128)(2,1)S(1)}, u32[]{:S(2)}, u32[]{:S(2)}) collective-permute-start(bf16[64,2048]{1,0:T(8,128)(2,1)S(1)} %collective-permute-done.5.refs_0_), channel_id=1, source_target_pairs={{0,4},{4,0},{8,12},{12,8},{16,20},{20,16},{24,28},{28,24},{32,36},... | collective-permute-start | bytes 786440 | tf_op jit(solution)/shard_map/ppermute | solution.py:53
  50.4 7.4 %collective-permute-start.14 = (bf16[64,2048]{1,0:T(8,128)(2,1)S(1)}, bf16[64,2048]{1,0:T(8,128)(2,1)S(1)}, u32[]{:S(2)}, u32[]{:S(2)}) collective-permute-start(bf16[64,2048]{1,0:T(8,128)(2,1)S(1)} %constant_dynamic-update-slice_fusion.2.refs_1_), channel_id=1, source_target_pairs={{0,32},{4,12},{8,40},{12,4},{16,48},{20,28},{24,56},{28,20},{32,0}... | collective-permute-start | bytes 786440 | tf_op jit(solution)/shard_map/ppermute | solution.py:49
  50.5 7.3 %collective-permute-start.13 = (bf16[64,2048]{1,0:T(8,128)(2,1)S(1)}, bf16[64,2048]{1,0:T(8,128)(2,1)S(1)}, u32[]{:S(2)}, u32[]{:S(2)}) collective-permute-start(bf16[64,2048]{1,0:T(8,128)(2,1)S(1)} %pad_maximum_fusion.4.refs_0_), channel_id=1, source_target_pairs={{0,96},{4,28},{8,104},{12,20},{16,112},{20,12},{24,120},{28,4},{32... | collective-permute-start | bytes 786440 | tf_op jit(solution)/shard_map/ppermute | solution.py:49
  63.7 6.1 %collective-permute-start.20 = (bf16[128,2048]{1,0:T(8,128)(2,1)}, bf16[128,2048]{1,0:T(8,128)(2,1)}, u32[]{:S(2)}, u32[]{:S(2)}) collective-permute-start(bf16[128,2048]{1,0:T(8,128)(2,1)} %get-tuple-element.50), channel_id=1, source_target_pairs={{0,4},{4,0},{8,12},{12,8},{16,20},{20,16},{24,28},{28,24},{32,36},... | collective-permute-start | bytes 1572872 | tf_op jit(solution)/shard_map/ppermute | solution.py:53
  64.7 7.9 %collective-permute-start.23 = (bf16[64,2048]{1,0:T(8,128)(2,1)S(1)}, bf16[64,2048]{1,0:T(8,128)(2,1)S(1)}, u32[]{:S(2)}, u32[]{:S(2)}) collective-permute-start(bf16[64,2048]{1,0:T(8,128)(2,1)S(1)} %get-tuple-element.80._token), channel_id=1, source_target_pairs={{0,96},{4,28},{8,104},{12,20},{16,112},{20,12},{24,120},{28,4},{32... | collective-permute-start | bytes 786440 | tf_op jit(solution)/shard_map/ppermute | solution.py:49
  65.6 7.0 %collective-permute-start.22 = (bf16[128,2048]{1,0:T(8,128)(2,1)}, bf16[128,2048]{1,0:T(8,128)(2,1)S(1)}, u32[]{:S(2)}, u32[]{:S(2)}) collective-permute-start(bf16[128,2048]{1,0:T(8,128)(2,1)} %get-tuple-element.52), channel_id=1, source_target_pairs={{0,4},{4,0},{8,12},{12,8},{16,20},{20,16},{24,28},{28,24},{32,36},... | collective-permute-start | bytes 1572872 | tf_op jit(solution)/shard_map/ppermute | solution.py:53
  66.4 6.2 %collective-permute-start.27 = (bf16[64,2048]{1,0:T(8,128)(2,1)}, bf16[64,2048]{1,0:T(8,128)(2,1)S(1)}, u32[]{:S(2)}, u32[]{:S(2)}) collective-permute-start(bf16[64,2048]{1,0:T(8,128)(2,1)} %get-tuple-element.81), channel_id=1, source_target_pairs={{0,32},{4,12},{8,40},{12,4},{16,48},{20,28},{24,56},{28,20},{32,0}... | collective-permute-start | bytes 786440 | tf_op jit(solution)/shard_map/ppermute | solution.py:49
  66.4 10.4 %collective-permute-start.19 = (bf16[128,2048]{1,0:T(8,128)(2,1)}, bf16[128,2048]{1,0:T(8,128)(2,1)}, u32[]{:S(2)}, u32[]{:S(2)}) collective-permute-start(bf16[128,2048]{1,0:T(8,128)(2,1)} %get-tuple-element.48), channel_id=1, source_target_pairs={{0,4},{4,0},{8,12},{12,8},{16,20},{20,16},{24,28},{28,24},{32,36},... | collective-permute-start | bytes 1572872 | tf_op jit(solution)/shard_map/ppermute | solution.py:53
  71.0 6.8 %collective-permute-start.21 = (bf16[64,2048]{1,0:T(8,128)(2,1)S(1)}, bf16[64,2048]{1,0:T(8,128)(2,1)S(1)}, u32[]{:S(2)}, u32[]{:S(2)}) collective-permute-start(bf16[64,2048]{1,0:T(8,128)(2,1)S(1)} %get-tuple-element.76), channel_id=1, source_target_pairs={{0,96},{4,28},{8,104},{12,20},{16,112},{20,12},{24,120},{28,4},{32... | collective-permute-start | bytes 786440 | tf_op jit(solution)/shard_map/ppermute | solution.py:49
  72.6 5.5 %collective-permute-start.26 = (bf16[64,2048]{1,0:T(8,128)(2,1)S(1)}, bf16[64,2048]{1,0:T(8,128)(2,1)S(1)}, u32[]{:S(2)}, u32[]{:S(2)}) collective-permute-start(bf16[64,2048]{1,0:T(8,128)(2,1)S(1)} %get-tuple-element.77), channel_id=1, source_target_pairs={{0,32},{4,12},{8,40},{12,4},{16,48},{20,28},{24,56},{28,20},{32,0}... | collective-permute-start | bytes 786440 | tf_op jit(solution)/shard_map/ppermute | solution.py:49
  72.9 8.0 %collective-permute-start.24 = (bf16[64,2048]{1,0:T(8,128)(2,1)S(1)}, bf16[64,2048]{1,0:T(8,128)(2,1)S(1)}, u32[]{:S(2)}, u32[]{:S(2)}) collective-permute-start(bf16[64,2048]{1,0:T(8,128)(2,1)S(1)} %get-tuple-element.78), channel_id=1, source_target_pairs={{0,32},{4,12},{8,40},{12,4},{16,48},{20,28},{24,56},{28,20},{32,0}... | collective-permute-start | bytes 786440 | tf_op jit(solution)/shard_map/ppermute | solution.py:49
  74.4 6.7 %collective-permute-start.28 = (bf16[64,2048]{1,0:T(8,128)(2,1)S(1)}, bf16[64,2048]{1,0:T(8,128)(2,1)S(1)}, u32[]{:S(2)}, u32[]{:S(2)}) collective-permute-start(bf16[64,2048]{1,0:T(8,128)(2,1)S(1)} %get-tuple-element.79), channel_id=1, source_target_pairs={{0,96},{4,28},{8,104},{12,20},{16,112},{20,12},{24,120},{28,4},{32... | collective-permute-start | bytes 786440 | tf_op jit(solution)/shard_map/ppermute | solution.py:49
  97.2 6.7 %collective-permute-start.39 = (bf16[64,2048]{1,0:T(8,128)(2,1)S(1)}, bf16[64,2048]{1,0:T(8,128)(2,1)S(1)}, u32[]{:S(2)}, u32[]{:S(2)}) collective-permute-start(bf16[64,2048]{1,0:T(8,128)(2,1)S(1)} %constant_dynamic-update-slice_fusion.4.refs_1_), channel_id=1, source_target_pairs={{0,32},{4,12},{8,40},{12,4},{16,48},{20,28},{24,56},{28,20},{32,0}... | collective-permute-start | bytes 786440 | tf_op jit(solution)/shard_map/ppermute | solution.py:49
  97.4 6.7 %collective-permute-start.38 = (bf16[64,2048]{1,0:T(8,128)(2,1)S(1)}, bf16[64,2048]{1,0:T(8,128)(2,1)S(1)}, u32[]{:S(2)}, u32[]{:S(2)}) collective-permute-start(bf16[64,2048]{1,0:T(8,128)(2,1)S(1)} %pad_maximum_fusion.5.refs_0_), channel_id=1, source_target_pairs={{0,96},{4,28},{8,104},{12,20},{16,112},{20,12},{24,120},{28,4},{32... | collective-permute-start | bytes 786440 | tf_op jit(solution)/shard_map/ppermute | solution.py:49
  98.7 12.3 %collective-permute-start.36 = (bf16[64,2048]{1,0:T(8,128)(2,1)S(1)}, bf16[64,2048]{1,0:T(8,128)(2,1)S(1)}, u32[]{:S(2)}, u32[]{:S(2)}) collective-permute-start(bf16[64,2048]{1,0:T(8,128)(2,1)S(1)} %constant_dynamic-update-slice_fusion.4.refs_1_), channel_id=1, source_target_pairs={{0,96},{4,28},{8,104},{12,20},{16,112},{20,12},{24,120},{28,4},{32... | collective-permute-start | bytes 786440 | tf_op jit(solution)/shard_map/ppermute | solution.py:49
  100.2 10.9 %collective-permute-start.32 = (bf16[64,2048]{1,0:T(8,128)(2,1)S(1)}, bf16[64,2048]{1,0:T(8,128)(2,1)S(1)}, u32[]{:S(2)}, u32[]{:S(2)}) collective-permute-start(bf16[64,2048]{1,0:T(8,128)(2,1)S(1)} %pad_maximum_fusion.5.refs_0_), channel_id=1, source_target_pairs={{0,32},{4,12},{8,40},{12,4},{16,48},{20,28},{24,56},{28,20},{32,0}... | collective-permute-start | bytes 786440 | tf_op jit(solution)/shard_map/ppermute | solution.py:49
  100.3 30.9 %all-to-all-start.1 = ((bf16[4,2,400,256]{3,2,1,0:T(8,128)(2,1)}), bf16[4,2,400,256]{3,2,1,0:T(8,128)(2,1)S(1)}, u32[]{:S(2)}, u32[]{:S(2)}) async-start(bf16[4,2,400,256]{3,2,1,0:T(8,128)(2,1)} %bitcast.11), calls=%async_computation.1 | async-start | bytes 3276800 | tf_op jit(solution)/shard_map/all_to_all | solution.py:696
  104.1 13.6 %collective-permute-start.43 = (bf16[128,2048]{1,0:T(8,128)(2,1)S(1)}, bf16[128,2048]{1,0:T(8,128)(2,1)S(1)}, u32[]{:S(2)}, u32[]{:S(2)}) collective-permute-start(bf16[128,2048]{1,0:T(8,128)(2,1)S(1)} %pad_maximum_fusion.3), channel_id=1, source_target_pairs={{0,4},{4,0},{8,12},{12,8},{16,20},{20,16},{24,28},{28,24},{32,36},... | collective-permute-start | bytes 1572872 | tf_op jit(solution)/shard_map/ppermute | solution.py:53
  111.1 6.7 %collective-permute-start.42 = (bf16[128,2048]{1,0:T(8,128)(2,1)S(1)}, bf16[128,2048]{1,0:T(8,128)(2,1)S(1)}, u32[]{:S(2)}, u32[]{:S(2)}) collective-permute-start(bf16[128,2048]{1,0:T(8,128)(2,1)S(1)} %pad_maximum_fusion.2), channel_id=1, source_target_pairs={{0,4},{4,0},{8,12},{12,8},{16,20},{20,16},{24,28},{28,24},{32,36},... | collective-permute-start | bytes 1572872 | tf_op jit(solution)/shard_map/ppermute | solution.py:53
  114.3 12.4 %collective-permute-start.37 = (bf16[64,2048]{1,0:T(8,128)(2,1)S(1)}, bf16[64,2048]{1,0:T(8,128)(2,1)S(1)}, u32[]{:S(2)}, u32[]{:S(2)}) collective-permute-start(bf16[64,2048]{1,0:T(8,128)(2,1)S(1)} %collective-permute-done.36.refs_3_), channel_id=1, source_target_pairs={{0,32},{4,12},{8,40},{12,4},{16,48},{20,28},{24,56},{28,20},{32,0}... | collective-permute-start | bytes 786440 | tf_op jit(solution)/shard_map/ppermute | solution.py:49
  116.5 10.2 %collective-permute-start.33 = (bf16[64,2048]{1,0:T(8,128)(2,1)S(1)}, bf16[64,2048]{1,0:T(8,128)(2,1)S(1)}, u32[]{:S(2)}, u32[]{:S(2)}) collective-permute-start(bf16[64,2048]{1,0:T(8,128)(2,1)S(1)} %collective-permute-done.32.refs_2_), channel_id=1, source_target_pairs={{0,96},{4,28},{8,104},{12,20},{16,112},{20,12},{24,120},{28,4},{32... | collective-permute-start | bytes 786440 | tf_op jit(solution)/shard_map/ppermute | solution.py:49
  131.2 12.8 %all-to-all-start = ((f32[32,1,128]{2,1,0:T(1,128)}), f32[32,1,128]{2,1,0:T(1,128)S(1)}, u32[]{:S(2)}, u32[]{:S(2)}) async-start(f32[32,1,128]{2,1,0:T(1,128)} %head_stats.3._stats), calls=%async_computation | async-start | bytes 32768 | tf_op jit(solution)/shard_map/all_to_all | solution.py:714
  (40 other events, 525.4 us)

commit v7 on v6

--- a/solution.py
+++ b/solution.py
@@ -666,6 +666,7 @@
     w_both = jnp.concatenate([w_gate, w_up], axis=1)
     early, late = gather_rows(prepared)
     early = (early, swap_early(early))
+    late, own_bc = lax.optimization_barrier((late, own_bc))
     late = (late, [swap_core(part) for part in late])
 
     core = req_rank % CORES
@@ -677,8 +678,8 @@
     next_ids = jnp.concatenate([draft_ids[:, 1:], draft_ids[:, :1]], axis=1)
     picked = (request[:, None] == jnp.arange(draft_ids.shape[0])[None, :]).astype(jnp.float32)
     targets = jnp.dot(picked, next_ids.astype(jnp.float32), precision=HIGHEST).astype(jnp.int32)
-    targets = targets.reshape(4, 16 * draft_len)
-    owners = jnp.broadcast_to(owner[:, None], (64, draft_len)).reshape(4, 16 * draft_len)
+    targets = targets.reshape(1, 64 * draft_len)
+    owners = jnp.broadcast_to(owner[:, None], (64, draft_len)).reshape(1, 64 * draft_len)
 
     half = 2 * own_tokens
     late_parts = [
@@ -704,11 +705,17 @@
     after_feed = (after_mixer.astype(jnp.float32) + summed).astype(jnp.bfloat16)
     final_rows = rms_scale(after_feed, final_gain).astype(jnp.bfloat16)
     early, late = gather_rows(final_rows)
-    early = early + swap_early(early)
-    first_stats = head_stats(targets[:3], owners[:3], early, head_weight, req_count)
-    late, first_stats = lax.optimization_barrier((late, first_stats))
+    sibling = swap_early(early)
+    most = 6 * half
+    first = head_stats(targets[:, :most], owners[:, :most], early, head_weight, req_count)
+    second = head_stats(
+        targets[:, most : 2 * most], owners[:, most : 2 * most], sibling, head_weight, req_count
+    )
+    late, first, second = lax.optimization_barrier((late, first, second))
     late = late + [swap_core(part) for part in late]
-    stats = head_stats(targets[3:], owners[3:], late, head_weight, req_count, [first_stats])
+    stats = head_stats(
+        targets[:, 2 * most :], owners[:, 2 * most :], late, head_weight, req_count, [first, second]
+    )
     kept_state, kept_conv = unpack(kept_out, own_bc, stats, tip)
     kept_state = kept_state.reshape(own_reqs, -1, SSM_DIM, STATE)
     shared = lax.all_to_all(stats, "req", split_axis=0, concat_axis=0, tiled=True)

time: 145 us -> 144 us (level)
  waiting for transfers between devices: 37.1 us -> 38.7 us
    ppermute x27, waiting for transfers between devices: 24 us -> 26.2 us  [hop(): return lax.ppermute(part, 'req', flip_pairs(ring, flip))]
    pallas_call x2 -> x3, Pallas kernels: 9.26 us -> 8.49 us  [head_stats(): pl.pallas_call(functools.partial(head_kernel, len(rows)), out_shape=jax.S...]
    unnamed x49 -> x47, local copies, waits for them, and re-layouts: 3.43 us -> 3.45 us
  transfers between devices with their start and end apart: 48 -> 48, of which waited for: 23 -> 22; matrix products, arithmetic and copies ran while one was open for 4% -> 2% of each run, Pallas kernels for 13% -> 12%
where the time goes in v7:
time: 144 us; the launch traced here: 143 us
  starting transfers between devices  63.8 us (44%)
  waiting for transfers between devices  38.7 us (27%)
  Pallas kernels  28.7 us (20%)
  other arithmetic  6.17 us (4%)
  local copies, waits for them, and re-layouts  4.26 us (3%)
    ppermute x27, waiting for transfers between devices, hop(): return lax.ppermute(part, 'req', flip_pairs(ring, flip))  26.2 us
    ppermute x27, starting transfers between devices, hop(): return lax.ppermute(part, 'req', flip_pairs(ring, flip))  25.6 us
    ppermute x16, starting transfers between devices, swap_core(): return lax.ppermute(part, 'req', CORE_PAIRS)  23.5 us
    pallas_call x3, Pallas kernels, head_stats(): pl.pallas_call(functools.partial(head_kernel, len(rows)), out_shape=jax.S...  8.49 us
    pallas_call x1, Pallas kernels, mixer(): pl.pallas_call(mixer_kernel, out_shape=[*[jax.ShapeDtypeStruct((tokens //...  8.29 us
    pallas_call x4, Pallas kernels, feed(): pl.pallas_call(functools.partial(feed_kernel, len(arrays)), out_shape=[ja...  6.26 us
    ppermute x3, waiting for transfers between devices, shards(): lax.ppermute(part, 'mdl', [(z, z ^ flip) for z in range(SIDE)])  6.13 us
    ppermute x3, starting transfers between devices, shards(): lax.ppermute(part, 'mdl', [(z, z ^ flip) for z in range(SIDE)])  5.85 us
  transfers between devices with their start and end apart: 48, of which 22 were waited for; matrix products, arithmetic and copies ran while one was open for 2% of the time, Pallas kernels for 12%

profile of v7, /device:TPU:1, one launch (start us, length us, event | category | flops | bytes accessed | tf_op | source)
XLA Modules:
  0.0 143.2 jit_solution(18259240048330456207)
XLA Ops:
  0.6 8.3 %mixer.1 = (bf16[32,2048]{1,0:T(8,128)(2,1)}, bf16[32,2048]{1,0:T(8,128)(2,1)}, bf16[32,2048]{1,0:T(8,128)(2,1)}, bf16[32,2048]{1,0:T(8,128)(2,1)}, f32[128,128]...) custom-call(s32[8]{0:T(128)} %refs_0_.3, ...), custom_call_target="tpu_custom_call" | custom-call | flops 3000000000 | bytes 20000000 | tf_op jit(solution)/shard_map/mixer/pallas_call | solution.py:489
  9.1 2.5 %collective-permute-start = (bf16[32,2048]{1,0:T(8,128)(2,1)}, bf16[32,2048]{1,0:T(8,128)(2,1)S(1)}, u32[]{:S(2)}, u32[]{:S(2)}) collective-permute-start(bf16[32,2048]{1,0:T(8,128)(2,1)} %get-tuple-element.41), channel_id=1, source_target_pairs={{0,1},{1,0},{2,3},{3,2},{4,5},{5,4},{6,7},{7,6},{8,9},{9,8},{10,11... | collective-permute-start | bytes 393224 | tf_op jit(solution)/shard_map/ppermute | solution.py:659
  11.6 2.2 %collective-permute-start.1 = (bf16[32,2048]{1,0:T(8,128)(2,1)}, bf16[32,2048]{1,0:T(8,128)(2,1)S(1)}, u32[]{:S(2)}, u32[]{:S(2)}) collective-permute-start(bf16[32,2048]{1,0:T(8,128)(2,1)} %get-tuple-element.42), channel_id=1, source_target_pairs={{0,3},{1,2},{2,1},{3,0},{4,7},{5,6},{6,5},{7,4},{8,11},{9,10},{10,... | collective-permute-start | bytes 393224 | tf_op jit(solution)/shard_map/ppermute | solution.py:659
  15.0 4.3 %collective-permute-done.1 = bf16[32,2048]{1,0:T(8,128)(2,1)S(1)} collective-permute-done((bf16[32,2048]{1,0:T(8,128)(2,1)}, bf16[32,2048]{1,0:T(8,128)(2,1)S(1)}, u32[]{:S(2)}, u32[]{:S(2)}) %collective-permute-start.1) | collective-permute-done | bytes 131104 | tf_op jit(solution)/shard_map/ppermute | solution.py:659
  19.3 1.8 %collective-permute-done.2 = bf16[32,2048]{1,0:T(8,128)(2,1)S(1)} collective-permute-done((bf16[32,2048]{1,0:T(8,128)(2,1)}, bf16[32,2048]{1,0:T(8,128)(2,1)S(1)}, u32[]{:S(2)}, u32[]{:S(2)}) %collective-permute-start.2) | collective-permute-done | bytes 131104 | tf_op jit(solution)/shard_map/ppermute | solution.py:659
  22.3 2.8 %collective-permute-start.6 = (bf16[32,2048]{1,0:T(8,128)(2,1)S(1)}, bf16[32,2048]{1,0:T(8,128)(2,1)S(1)}, u32[]{:S(2)}, u32[]{:S(2)}) collective-permute-start(bf16[32,2048]{1,0:T(8,128)(2,1)S(1)} %fusion.5), channel_id=1, source_target_pairs={{0,24},{4,100},{8,16},{12,108},{16,8},{20,116},{24,0},{28,124},{32... | collective-permute-start | bytes 393224 | tf_op jit(solution)/shard_map/ppermute | solution.py:49
  25.8 2.6 %collective-permute-done.6 = bf16[32,2048]{1,0:T(8,128)(2,1)S(1)} collective-permute-done((bf16[32,2048]{1,0:T(8,128)(2,1)S(1)}, bf16[32,2048]{1,0:T(8,128)(2,1)S(1)}, u32[]{:S(2)}, u32[]{:S(2)}) %collective-permute-start.6) | collective-permute-done | bytes 131104 | tf_op jit(solution)/shard_map/ppermute | solution.py:49
  28.5 2.0 %collective-permute-done.7 = bf16[32,2048]{1,0:T(8,128)(2,1)S(1)} collective-permute-done((bf16[32,2048]{1,0:T(8,128)(2,1)S(1)}, bf16[32,2048]{1,0:T(8,128)(2,1)S(1)}, u32[]{:S(2)}, u32[]{:S(2)}) %collective-permute-start.7) | collective-permute-done | bytes 131104 | tf_op jit(solution)/shard_map/ppermute | solution.py:49
  30.5 2.6 %collective-permute-start.8 = (bf16[64,2048]{1,0:T(8,128)(2,1)S(1)}, bf16[64,2048]{1,0:T(8,128)(2,1)S(1)}, u32[]{:S(2)}, u32[]{:S(2)}) collective-permute-start(bf16[64,2048]{1,0:T(8,128)(2,1)S(1)} %constant_dynamic-update-slice_fusion.2.refs_1_), channel_id=1, source_target_pairs={{0,96},{4,28},{8,104},{12,20},{16,112},{20,12},{24,120},{28,4},{32... | collective-permute-start | bytes 786440 | tf_op jit(solution)/shard_map/ppermute | solution.py:49
  33.2 3.8 %collective-permute-done.8.refs_3_ = bf16[64,2048]{1,0:T(8,128)(2,1)S(1)} collective-permute-done((bf16[64,2048]{1,0:T(8,128)(2,1)S(1)}, bf16[64,2048]{1,0:T(8,128)(2,1)S(1)}, u32[]{:S(2)}, u32[]{:S(2)}) %collective-permute-start.8) | collective-permute-done | bytes 262176 | tf_op jit(solution)/shard_map/ppermute | solution.py:49
  37.0 1.7 %collective-permute-done.4.refs_2_ = bf16[64,2048]{1,0:T(8,128)(2,1)S(1)} collective-permute-done((bf16[64,2048]{1,0:T(8,128)(2,1)S(1)}, bf16[64,2048]{1,0:T(8,128)(2,1)S(1)}, u32[]{:S(2)}, u32[]{:S(2)}) %collective-permute-start.4) | collective-permute-done | bytes 262176 | tf_op jit(solution)/shard_map/ppermute | solution.py:49
  39.9 3.6 %keeper.1 = (bf16[8,400,256]{2,1,0:T(8,128)(2,1)}, bf16[16,512]{1,0:T(8,128)(2,1)S(1)}) custom-call(s32[8]{0:T(128)S(1)} %copy-done.5, s32[8]{0:T(128)S(1)} %copy-done.6, f32[128,128]{1,0:T(8,128)S(1)} %copy-done.12, f32[128,384]{1,0:T(8,128)S(1)} %copy-done.9, bf16[128,256]{1,0:T(8,128)(2,1)S(1)} %copy-done.13, bf16[128,384]{1,0:T(8,128)(2,1)S(1)} %copy-done.11, ...), custom_call_target="tpu_custom_call" | custom-call | flops 2000000000 | bytes 5000000 | tf_op jit(solution)/shard_map/keeper/pallas_call | solution.py:220
  45.1 5.0 %collective-permute-start.10 = (bf16[64,2048]{1,0:T(8,128)(2,1)S(1)}, bf16[64,2048]{1,0:T(8,128)(2,1)S(1)}, u32[]{:S(2)}, u32[]{:S(2)}) collective-permute-start(bf16[64,2048]{1,0:T(8,128)(2,1)S(1)} %collective-permute-done.5.refs_0_), channel_id=1, source_target_pairs={{0,4},{4,0},{8,12},{12,8},{16,20},{20,16},{24,28},{28,24},{32,36},... | collective-permute-start | bytes 786440 | tf_op jit(solution)/shard_map/ppermute | solution.py:53
  60.4 2.9 %feed.7 = (bf16[128,2048]{1,0:T(8,128)(2,1)}, bf16[128,2048]{1,0:T(8,128)(2,1)}, bf16[128,2048]{1,0:T(8,128)(2,1)}) custom-call(bf16[2048,256]{1,0:T(8,128)(2,1)S(1)} %constant_dynamic-update-slice_fusion.both_ref, bf16[128,2048]{1,0:T(8,128)(2,1)S(1)} %copy-done.7, bf16[64,2048]{1,0:T(8,128)(2,1)S(1)} %get-tuple-element.88._token, ...), custom_call_target="tpu_custom_call" | custom-call | flops 2415919104 | bytes 4718592 | tf_op jit(solution)/shard_map/feed/pallas_call | solution.py:544
  66.7 1.8 %feed.6 = (bf16[64,2048]{1,0:T(8,128)(2,1)S(1)}, bf16[64,2048]{1,0:T(8,128)(2,1)S(1)}, bf16[64,2048]{1,0:T(8,128)(2,1)S(1)}, bf16[64,2048]{1,0:T(8,128)(2,1)S(1)...) custom-call(bf16[2048,256]{1,0:T(8,128)(2,1)S(1)} %constant_dynamic-update-slice_fusion.both_ref, ...), custom_call_target="tpu_custom_call" | custom-call | flops 2415919104 | bytes 4718592 | tf_op jit(solution)/shard_map/feed/pallas_call | solution.py:544
  69.7 1.9 %collective-permute-start.21 = (bf16[64,2048]{1,0:T(8,128)(2,1)S(1)}, bf16[64,2048]{1,0:T(8,128)(2,1)S(1)}, u32[]{:S(2)}, u32[]{:S(2)}) collective-permute-start(bf16[64,2048]{1,0:T(8,128)(2,1)S(1)} %get-tuple-element.84), channel_id=1, source_target_pairs={{0,96},{4,28},{8,104},{12,20},{16,112},{20,12},{24,120},{28,4},{32... | collective-permute-start | bytes 786440 | tf_op jit(solution)/shard_map/ppermute | solution.py:49
  74.4 2.1 %collective-permute-done.21 = bf16[64,2048]{1,0:T(8,128)(2,1)S(1)} collective-permute-done((bf16[64,2048]{1,0:T(8,128)(2,1)S(1)}, bf16[64,2048]{1,0:T(8,128)(2,1)S(1)}, u32[]{:S(2)}, u32[]{:S(2)}) %collective-permute-start.21) | collective-permute-done | bytes 262176 | tf_op jit(solution)/shard_map/ppermute | solution.py:49
  77.2 2.8 %collective-permute-done.24 = bf16[64,2048]{1,0:T(8,128)(2,1)S(1)} collective-permute-done((bf16[64,2048]{1,0:T(8,128)(2,1)S(1)}, bf16[64,2048]{1,0:T(8,128)(2,1)S(1)}, u32[]{:S(2)}, u32[]{:S(2)}) %collective-permute-start.24) | collective-permute-done | bytes 262176 | tf_op jit(solution)/shard_map/ppermute | solution.py:49
  82.5 1.8 %collective-permute-start.30 = (bf16[32,2048]{1,0:T(8,128)(2,1)S(1)}, bf16[32,2048]{1,0:T(8,128)(2,1)S(1)}, u32[]{:S(2)}, u32[]{:S(2)}) collective-permute-start(bf16[32,2048]{1,0:T(8,128)(2,1)S(1)} %get-tuple-element.91), channel_id=1, source_target_pairs={{0,16},{4,68},{8,24},{12,76},{16,0},{20,84},{24,8},{28,92},{32,48}... | collective-permute-start | bytes 393224 | tf_op jit(solution)/shard_map/ppermute | solution.py:49
  85.6 2.8 %collective-permute-done.29 = bf16[32,2048]{1,0:T(8,128)(2,1)S(1)} collective-permute-done((bf16[32,2048]{1,0:T(8,128)(2,1)S(1)}, bf16[32,2048]{1,0:T(8,128)(2,1)S(1)}, u32[]{:S(2)}, u32[]{:S(2)}) %collective-permute-start.29) | collective-permute-done | bytes 131104 | tf_op jit(solution)/shard_map/ppermute | solution.py:49
  92.6 1.8 %collective-permute-done.34 = bf16[32,2048]{1,0:T(8,128)(2,1)S(1)} collective-permute-done((bf16[32,2048]{1,0:T(8,128)(2,1)S(1)}, bf16[32,2048]{1,0:T(8,128)(2,1)S(1)}, u32[]{:S(2)}, u32[]{:S(2)}) %collective-permute-start.34) | collective-permute-done | bytes 131104 | tf_op jit(solution)/shard_map/ppermute | solution.py:49
  99.2 3.6 %all-to-all-start.1 = ((bf16[4,2,400,256]{3,2,1,0:T(8,128)(2,1)}), bf16[4,2,400,256]{3,2,1,0:T(8,128)(2,1)S(1)}, u32[]{:S(2)}, u32[]{:S(2)}) async-start(bf16[4,2,400,256]{3,2,1,0:T(8,128)(2,1)} %bitcast.12), calls=%async_computation.1 | async-start | bytes 3276800 | tf_op jit(solution)/shard_map/all_to_all | solution.py:697
  103.1 7.6 %collective-permute-start.43 = (bf16[128,2048]{1,0:T(8,128)(2,1)S(1)}, bf16[128,2048]{1,0:T(8,128)(2,1)S(1)}, u32[]{:S(2)}, u32[]{:S(2)}) collective-permute-start(bf16[128,2048]{1,0:T(8,128)(2,1)S(1)} %pad_maximum_fusion.3), channel_id=1, source_target_pairs={{0,4},{4,0},{8,12},{12,8},{16,20},{20,16},{24,28},{28,24},{32,36},... | collective-permute-start | bytes 1572872 | tf_op jit(solution)/shard_map/ppermute | solution.py:53
  110.7 2.8 %collective-permute-start.42 = (bf16[128,2048]{1,0:T(8,128)(2,1)S(1)}, bf16[128,2048]{1,0:T(8,128)(2,1)S(1)}, u32[]{:S(2)}, u32[]{:S(2)}) collective-permute-start(bf16[128,2048]{1,0:T(8,128)(2,1)S(1)} %pad_maximum_fusion.2), channel_id=1, source_target_pairs={{0,4},{4,0},{8,12},{12,8},{16,20},{20,16},{24,28},{28,24},{32,36},... | collective-permute-start | bytes 1572872 | tf_op jit(solution)/shard_map/ppermute | solution.py:53
  113.9 1.9 %collective-permute-start.37 = (bf16[64,2048]{1,0:T(8,128)(2,1)S(1)}, bf16[64,2048]{1,0:T(8,128)(2,1)S(1)}, u32[]{:S(2)}, u32[]{:S(2)}) collective-permute-start(bf16[64,2048]{1,0:T(8,128)(2,1)S(1)} %collective-permute-done.36.refs_3_), channel_id=1, source_target_pairs={{0,32},{4,12},{8,40},{12,4},{16,48},{20,28},{24,56},{28,20},{32,0}... | collective-permute-start | bytes 786440 | tf_op jit(solution)/shard_map/ppermute | solution.py:49
  116.6 2.2 %copy-done = bf16[1024,2048]{1,0:T(8,128)(2,1)S(1)} copy-done((bf16[1024,2048]{1,0:T(8,128)(2,1)S(1)}, bf16[1024,2048]{1,0:T(8,128)(2,1)}, u32[]{:S(2)}) %copy-start) | copy-done | bytes 4194328
  118.8 3.0 %head_stats.3.refs_5_ = f32[32,1,128]{2,1,0:T(1,128)S(1)} custom-call(s32[1,384]{1,0:T(1,128)S(1)} %get-tuple-element.98.targets_ref, s32[1,384]{1,0:T(1,128)S(1)} %get-tuple-element.95.owners_ref, bf16[64,2048]{1,0:T(8,128)(2,1)S(1)} %pad_maximum_fusion.5.refs_0_, bf16[64,2048]{1,0:T(8,128)(2,1)S(1)} %constant_dynamic-update-slice_fusion.4.refs_1_, ...), custom_call_target="tpu_custom_call" | custom-call | flops 1610612736 | bytes 5767168 | tf_op jit(solution)/shard_map/head_stats/pallas_call | solution.py:598
  121.8 3.0 %head_stats.4.refs_6_ = f32[32,1,128]{2,1,0:T(1,128)S(1)} custom-call(s32[1,384]{1,0:T(1,128)S(1)} %get-tuple-element.99.targets_ref, s32[1,384]{1,0:T(1,128)S(1)} %get-tuple-element.94.owners_ref, bf16[64,2048]{1,0:T(8,128)(2,1)S(1)} %collective-permute-done.40.refs_0_, bf16[64,2048]{1,0:T(8,128)(2,1)S(1)} %collective-permute-done.41.refs_1_, ...), custom_call_target="tpu_custom_call" | custom-call | flops 1610612736 | bytes 5767168 | tf_op jit(solution)/shard_map/head_stats/pallas_call | solution.py:598
  127.4 2.5 %head_stats.5._stats = f32[32,1,128]{2,1,0:T(1,128)} custom-call(s32[1,256]{1,0:T(1,128)S(1)} %slice.102.targets_ref, s32[1,256]{1,0:T(1,128)S(1)} %slice.103.owners_ref, bf16[64,2048]{1,0:T(8,128)(2,1)S(1)} %collective-permute-done.33.refs_0_, bf16[64,2048]{1,0:T(8,128)(2,1)S(1)} %collective-permute-done.37.refs_1_, ...), custom_call_target="tpu_custom_call" | custom-call | flops 1073741824 | bytes 5242880 | tf_op jit(solution)/shard_map/head_stats/pallas_call | solution.py:598
  129.9 5.3 %all-to-all-start = ((f32[32,1,128]{2,1,0:T(1,128)}), f32[32,1,128]{2,1,0:T(1,128)S(1)}, u32[]{:S(2)}, u32[]{:S(2)}) async-start(f32[32,1,128]{2,1,0:T(1,128)} %head_stats.5._stats), calls=%async_computation | async-start | bytes 32768 | tf_op jit(solution)/shard_map/all_to_all | solution.py:721
  135.2 2.1 %unpack.1 = (f32[2,1536,256]{2,1,0:T(8,128)}, bf16[3,2,2048]{2,1,0:T(2,128)(2,1)}) custom-call(bf16[4,2,400,256]{3,2,1,0:T(8,128)(2,1)S(1)} %all-to-all-done.1.kept_hbm, bf16[16,512]{1,0:T(8,128)(2,1)S(1)} %get-tuple-element.50._token.bc_ref, f32[32,1,128]{2,1,0:T(1,128)} %head_stats.5._stats, bf16[8,128]{1,0:T(8,128)(2,1)S(1)} %slice.111._tip), custom_call_target="tpu_custom_call" | custom-call | flops 1000000 | bytes 20000000 | tf_op jit(solution)/shard_map/unpack/pallas_call | solution.py:267
  137.3 4.9 %all-to-all-done = f32[32,1,128]{2,1,0:T(1,128)S(1)} async-done(((f32[32,1,128]{2,1,0:T(1,128)}), f32[32,1,128]{2,1,0:T(1,128)S(1)}, u32[]{:S(2)}, u32[]{:S(2)}) %all-to-all-start) | async-done | bytes 16416 | tf_op jit(solution)/shard_map/all_to_all | solution.py:721
  (166 shorter events, 42.0 us)
Async XLA Ops:
  9.1 6.0 %collective-permute-start = (bf16[32,2048]{1,0:T(8,128)(2,1)}, bf16[32,2048]{1,0:T(8,128)(2,1)S(1)}, u32[]{:S(2)}, u32[]{:S(2)}) collective-permute-start(bf16[32,2048]{1,0:T(8,128)(2,1)} %get-tuple-element.41), channel_id=1, source_target_pairs={{0,1},{1,0},{2,3},{3,2},{4,5},{5,4},{6,7},{7,6},{8,9},{9,8},{10,11... | collective-permute-start | bytes 393224 | tf_op jit(solution)/shard_map/ppermute | solution.py:659
  11.6 7.7 %collective-permute-start.1 = (bf16[32,2048]{1,0:T(8,128)(2,1)}, bf16[32,2048]{1,0:T(8,128)(2,1)S(1)}, u32[]{:S(2)}, u32[]{:S(2)}) collective-permute-start(bf16[32,2048]{1,0:T(8,128)(2,1)} %get-tuple-element.42), channel_id=1, source_target_pairs={{0,3},{1,2},{2,1},{3,0},{4,7},{5,6},{6,5},{7,4},{8,11},{9,10},{10,... | collective-permute-start | bytes 393224 | tf_op jit(solution)/shard_map/ppermute | solution.py:659
  13.8 7.2 %collective-permute-start.2 = (bf16[32,2048]{1,0:T(8,128)(2,1)}, bf16[32,2048]{1,0:T(8,128)(2,1)S(1)}, u32[]{:S(2)}, u32[]{:S(2)}) collective-permute-start(bf16[32,2048]{1,0:T(8,128)(2,1)} %get-tuple-element.43), channel_id=1, source_target_pairs={{0,2},{1,3},{2,0},{3,1},{4,6},{5,7},{6,4},{7,5},{8,10},{9,11},{10,... | collective-permute-start | bytes 393224 | tf_op jit(solution)/shard_map/ppermute | solution.py:659
  22.3 6.1 %collective-permute-start.6 = (bf16[32,2048]{1,0:T(8,128)(2,1)S(1)}, bf16[32,2048]{1,0:T(8,128)(2,1)S(1)}, u32[]{:S(2)}, u32[]{:S(2)}) collective-permute-start(bf16[32,2048]{1,0:T(8,128)(2,1)S(1)} %fusion.5), channel_id=1, source_target_pairs={{0,24},{4,100},{8,16},{12,108},{16,8},{20,116},{24,0},{28,124},{32... | collective-permute-start | bytes 393224 | tf_op jit(solution)/shard_map/ppermute | solution.py:49
  25.5 7.5 %collective-permute-start.3 = (bf16[32,2048]{1,0:T(8,128)(2,1)S(1)}, bf16[32,2048]{1,0:T(8,128)(2,1)S(1)}, u32[]{:S(2)}, u32[]{:S(2)}) collective-permute-start(bf16[32,2048]{1,0:T(8,128)(2,1)S(1)} %fusion.5), channel_id=1, source_target_pairs={{0,8},{4,36},{8,0},{12,44},{16,24},{20,52},{24,16},{28,60},{32,40}... | collective-permute-start | bytes 393224 | tf_op jit(solution)/shard_map/ppermute | solution.py:49
  30.5 6.5 %collective-permute-start.8 = (bf16[64,2048]{1,0:T(8,128)(2,1)S(1)}, bf16[64,2048]{1,0:T(8,128)(2,1)S(1)}, u32[]{:S(2)}, u32[]{:S(2)}) collective-permute-start(bf16[64,2048]{1,0:T(8,128)(2,1)S(1)} %constant_dynamic-update-slice_fusion.2.refs_1_), channel_id=1, source_target_pairs={{0,96},{4,28},{8,104},{12,20},{16,112},{20,12},{24,120},{28,4},{32... | collective-permute-start | bytes 786440 | tf_op jit(solution)/shard_map/ppermute | solution.py:49
  37.0 6.5 %collective-permute-start.9 = (bf16[64,2048]{1,0:T(8,128)(2,1)S(1)}, bf16[64,2048]{1,0:T(8,128)(2,1)S(1)}, u32[]{:S(2)}, u32[]{:S(2)}) collective-permute-start(bf16[64,2048]{1,0:T(8,128)(2,1)S(1)} %collective-permute-done.8.refs_3_), channel_id=1, source_target_pairs={{0,32},{4,12},{8,40},{12,4},{16,48},{20,28},{24,56},{28,20},{32,0}... | collective-permute-start | bytes 786440 | tf_op jit(solution)/shard_map/ppermute | solution.py:49
  38.7 6.4 %collective-permute-start.5 = (bf16[64,2048]{1,0:T(8,128)(2,1)S(1)}, bf16[64,2048]{1,0:T(8,128)(2,1)S(1)}, u32[]{:S(2)}, u32[]{:S(2)}) collective-permute-start(bf16[64,2048]{1,0:T(8,128)(2,1)S(1)} %collective-permute-done.4.refs_2_), channel_id=1, source_target_pairs={{0,96},{4,28},{8,104},{12,20},{16,112},{20,12},{24,120},{28,4},{32... | collective-permute-start | bytes 786440 | tf_op jit(solution)/shard_map/ppermute | solution.py:49
  45.1 7.8 %collective-permute-start.10 = (bf16[64,2048]{1,0:T(8,128)(2,1)S(1)}, bf16[64,2048]{1,0:T(8,128)(2,1)S(1)}, u32[]{:S(2)}, u32[]{:S(2)}) collective-permute-start(bf16[64,2048]{1,0:T(8,128)(2,1)S(1)} %collective-permute-done.5.refs_0_), channel_id=1, source_target_pairs={{0,4},{4,0},{8,12},{12,8},{16,20},{20,16},{24,28},{28,24},{32,36},... | collective-permute-start | bytes 786440 | tf_op jit(solution)/shard_map/ppermute | solution.py:53
  50.5 6.9 %collective-permute-start.13 = (bf16[64,2048]{1,0:T(8,128)(2,1)S(1)}, bf16[64,2048]{1,0:T(8,128)(2,1)S(1)}, u32[]{:S(2)}, u32[]{:S(2)}) collective-permute-start(bf16[64,2048]{1,0:T(8,128)(2,1)S(1)} %pad_maximum_fusion.4.refs_0_), channel_id=1, source_target_pairs={{0,96},{4,28},{8,104},{12,20},{16,112},{20,12},{24,120},{28,4},{32... | collective-permute-start | bytes 786440 | tf_op jit(solution)/shard_map/ppermute | solution.py:49
  51.4 9.0 %collective-permute-start.16 = (bf16[64,2048]{1,0:T(8,128)(2,1)S(1)}, bf16[64,2048]{1,0:T(8,128)(2,1)S(1)}, u32[]{:S(2)}, u32[]{:S(2)}) collective-permute-start(bf16[64,2048]{1,0:T(8,128)(2,1)S(1)} %constant_dynamic-update-slice_fusion.2.refs_1_), channel_id=1, source_target_pairs={{0,4},{4,0},{8,12},{12,8},{16,20},{20,16},{24,28},{28,24},{32,36},... | collective-permute-start | bytes 786440 | tf_op jit(solution)/shard_map/ppermute | solution.py:53
  52.9 7.5 %collective-permute-start.15 = (bf16[64,2048]{1,0:T(8,128)(2,1)S(1)}, bf16[64,2048]{1,0:T(8,128)(2,1)S(1)}, u32[]{:S(2)}, u32[]{:S(2)}) collective-permute-start(bf16[64,2048]{1,0:T(8,128)(2,1)S(1)} %pad_maximum_fusion.4.refs_0_), channel_id=1, source_target_pairs={{0,4},{4,0},{8,12},{12,8},{16,20},{20,16},{24,28},{28,24},{32,36},... | collective-permute-start | bytes 786440 | tf_op jit(solution)/shard_map/ppermute | solution.py:53
  63.6 8.1 %collective-permute-start.23 = (bf16[64,2048]{1,0:T(8,128)(2,1)S(1)}, bf16[64,2048]{1,0:T(8,128)(2,1)S(1)}, u32[]{:S(2)}, u32[]{:S(2)}) collective-permute-start(bf16[64,2048]{1,0:T(8,128)(2,1)S(1)} %get-tuple-element.88._token), channel_id=1, source_target_pairs={{0,96},{4,28},{8,104},{12,20},{16,112},{20,12},{24,120},{28,4},{32... | collective-permute-start | bytes 786440 | tf_op jit(solution)/shard_map/ppermute | solution.py:49
  64.4 7.2 %collective-permute-start.22 = (bf16[128,2048]{1,0:T(8,128)(2,1)}, bf16[128,2048]{1,0:T(8,128)(2,1)S(1)}, u32[]{:S(2)}, u32[]{:S(2)}) collective-permute-start(bf16[128,2048]{1,0:T(8,128)(2,1)} %get-tuple-element.59), channel_id=1, source_target_pairs={{0,4},{4,0},{8,12},{12,8},{16,20},{20,16},{24,28},{28,24},{32,36},... | collective-permute-start | bytes 1572872 | tf_op jit(solution)/shard_map/ppermute | solution.py:53
  65.7 6.0 %collective-permute-start.27 = (bf16[64,2048]{1,0:T(8,128)(2,1)}, bf16[64,2048]{1,0:T(8,128)(2,1)S(1)}, u32[]{:S(2)}, u32[]{:S(2)}) collective-permute-start(bf16[64,2048]{1,0:T(8,128)(2,1)} %get-tuple-element.89), channel_id=1, source_target_pairs={{0,32},{4,12},{8,40},{12,4},{16,48},{20,28},{24,56},{28,20},{32,0}... | collective-permute-start | bytes 786440 | tf_op jit(solution)/shard_map/ppermute | solution.py:49
  65.7 8.8 %collective-permute-start.19 = (bf16[128,2048]{1,0:T(8,128)(2,1)}, bf16[128,2048]{1,0:T(8,128)(2,1)}, u32[]{:S(2)}, u32[]{:S(2)}) collective-permute-start(bf16[128,2048]{1,0:T(8,128)(2,1)} %get-tuple-element.55), channel_id=1, source_target_pairs={{0,4},{4,0},{8,12},{12,8},{16,20},{20,16},{24,28},{28,24},{32,36},... | collective-permute-start | bytes 1572872 | tf_op jit(solution)/shard_map/ppermute | solution.py:53
  69.7 6.8 %collective-permute-start.21 = (bf16[64,2048]{1,0:T(8,128)(2,1)S(1)}, bf16[64,2048]{1,0:T(8,128)(2,1)S(1)}, u32[]{:S(2)}, u32[]{:S(2)}) collective-permute-start(bf16[64,2048]{1,0:T(8,128)(2,1)S(1)} %get-tuple-element.84), channel_id=1, source_target_pairs={{0,96},{4,28},{8,104},{12,20},{16,112},{20,12},{24,120},{28,4},{32... | collective-permute-start | bytes 786440 | tf_op jit(solution)/shard_map/ppermute | solution.py:49
  71.9 8.0 %collective-permute-start.24 = (bf16[64,2048]{1,0:T(8,128)(2,1)S(1)}, bf16[64,2048]{1,0:T(8,128)(2,1)S(1)}, u32[]{:S(2)}, u32[]{:S(2)}) collective-permute-start(bf16[64,2048]{1,0:T(8,128)(2,1)S(1)} %get-tuple-element.86), channel_id=1, source_target_pairs={{0,32},{4,12},{8,40},{12,4},{16,48},{20,28},{24,56},{28,20},{32,0}... | collective-permute-start | bytes 786440 | tf_op jit(solution)/shard_map/ppermute | solution.py:49
  73.5 6.7 %collective-permute-start.28 = (bf16[64,2048]{1,0:T(8,128)(2,1)S(1)}, bf16[64,2048]{1,0:T(8,128)(2,1)S(1)}, u32[]{:S(2)}, u32[]{:S(2)}) collective-permute-start(bf16[64,2048]{1,0:T(8,128)(2,1)S(1)} %get-tuple-element.87), channel_id=1, source_target_pairs={{0,96},{4,28},{8,104},{12,20},{16,112},{20,12},{24,120},{28,4},{32... | collective-permute-start | bytes 786440 | tf_op jit(solution)/shard_map/ppermute | solution.py:49
  81.6 6.8 %collective-permute-start.29 = (bf16[32,2048]{1,0:T(8,128)(2,1)S(1)}, bf16[32,2048]{1,0:T(8,128)(2,1)S(1)}, u32[]{:S(2)}, u32[]{:S(2)}) collective-permute-start(bf16[32,2048]{1,0:T(8,128)(2,1)S(1)} %get-tuple-element.90), channel_id=1, source_target_pairs={{0,24},{4,100},{8,16},{12,108},{16,8},{20,116},{24,0},{28,124},{32... | collective-permute-start | bytes 393224 | tf_op jit(solution)/shard_map/ppermute | solution.py:49
  82.5 5.9 %collective-permute-start.30 = (bf16[32,2048]{1,0:T(8,128)(2,1)S(1)}, bf16[32,2048]{1,0:T(8,128)(2,1)S(1)}, u32[]{:S(2)}, u32[]{:S(2)}) collective-permute-start(bf16[32,2048]{1,0:T(8,128)(2,1)S(1)} %get-tuple-element.91), channel_id=1, source_target_pairs={{0,16},{4,68},{8,24},{12,76},{16,0},{20,84},{24,8},{28,92},{32,48}... | collective-permute-start | bytes 393224 | tf_op jit(solution)/shard_map/ppermute | solution.py:49
  95.8 7.2 %collective-permute-start.39 = (bf16[64,2048]{1,0:T(8,128)(2,1)S(1)}, bf16[64,2048]{1,0:T(8,128)(2,1)S(1)}, u32[]{:S(2)}, u32[]{:S(2)}) collective-permute-start(bf16[64,2048]{1,0:T(8,128)(2,1)S(1)} %constant_dynamic-update-slice_fusion.4.refs_1_), channel_id=1, source_target_pairs={{0,32},{4,12},{8,40},{12,4},{16,48},{20,28},{24,56},{28,20},{32,0}... | collective-permute-start | bytes 786440 | tf_op jit(solution)/shard_map/ppermute | solution.py:49
  96.4 6.6 %collective-permute-start.38 = (bf16[64,2048]{1,0:T(8,128)(2,1)S(1)}, bf16[64,2048]{1,0:T(8,128)(2,1)S(1)}, u32[]{:S(2)}, u32[]{:S(2)}) collective-permute-start(bf16[64,2048]{1,0:T(8,128)(2,1)S(1)} %pad_maximum_fusion.5.refs_0_), channel_id=1, source_target_pairs={{0,96},{4,28},{8,104},{12,20},{16,112},{20,12},{24,120},{28,4},{32... | collective-permute-start | bytes 786440 | tf_op jit(solution)/shard_map/ppermute | solution.py:49
  97.5 13.1 %collective-permute-start.36 = (bf16[64,2048]{1,0:T(8,128)(2,1)S(1)}, bf16[64,2048]{1,0:T(8,128)(2,1)S(1)}, u32[]{:S(2)}, u32[]{:S(2)}) collective-permute-start(bf16[64,2048]{1,0:T(8,128)(2,1)S(1)} %constant_dynamic-update-slice_fusion.4.refs_1_), channel_id=1, source_target_pairs={{0,96},{4,28},{8,104},{12,20},{16,112},{20,12},{24,120},{28,4},{32... | collective-permute-start | bytes 786440 | tf_op jit(solution)/shard_map/ppermute | solution.py:49
  99.2 11.5 %collective-permute-start.32 = (bf16[64,2048]{1,0:T(8,128)(2,1)S(1)}, bf16[64,2048]{1,0:T(8,128)(2,1)S(1)}, u32[]{:S(2)}, u32[]{:S(2)}) collective-permute-start(bf16[64,2048]{1,0:T(8,128)(2,1)S(1)} %pad_maximum_fusion.5.refs_0_), channel_id=1, source_target_pairs={{0,32},{4,12},{8,40},{12,4},{16,48},{20,28},{24,56},{28,20},{32,0}... | collective-permute-start | bytes 786440 | tf_op jit(solution)/shard_map/ppermute | solution.py:49
  99.2 30.7 %all-to-all-start.1 = ((bf16[4,2,400,256]{3,2,1,0:T(8,128)(2,1)}), bf16[4,2,400,256]{3,2,1,0:T(8,128)(2,1)S(1)}, u32[]{:S(2)}, u32[]{:S(2)}) async-start(bf16[4,2,400,256]{3,2,1,0:T(8,128)(2,1)} %bitcast.12), calls=%async_computation.1 | async-start | bytes 3276800 | tf_op jit(solution)/shard_map/all_to_all | solution.py:697
  103.1 18.7 %collective-permute-start.43 = (bf16[128,2048]{1,0:T(8,128)(2,1)S(1)}, bf16[128,2048]{1,0:T(8,128)(2,1)S(1)}, u32[]{:S(2)}, u32[]{:S(2)}) collective-permute-start(bf16[128,2048]{1,0:T(8,128)(2,1)S(1)} %pad_maximum_fusion.3), channel_id=1, source_target_pairs={{0,4},{4,0},{8,12},{12,8},{16,20},{20,16},{24,28},{28,24},{32,36},... | collective-permute-start | bytes 1572872 | tf_op jit(solution)/shard_map/ppermute | solution.py:53
  110.7 11.1 %collective-permute-start.42 = (bf16[128,2048]{1,0:T(8,128)(2,1)S(1)}, bf16[128,2048]{1,0:T(8,128)(2,1)S(1)}, u32[]{:S(2)}, u32[]{:S(2)}) collective-permute-start(bf16[128,2048]{1,0:T(8,128)(2,1)S(1)} %pad_maximum_fusion.2), channel_id=1, source_target_pairs={{0,4},{4,0},{8,12},{12,8},{16,20},{20,16},{24,28},{28,24},{32,36},... | collective-permute-start | bytes 1572872 | tf_op jit(solution)/shard_map/ppermute | solution.py:53
  113.5 8.3 %collective-permute-start.40 = (bf16[64,2048]{1,0:T(8,128)(2,1)S(1)}, bf16[64,2048]{1,0:T(8,128)(2,1)S(1)}, u32[]{:S(2)}, u32[]{:S(2)}) collective-permute-start(bf16[64,2048]{1,0:T(8,128)(2,1)S(1)} %pad_maximum_fusion.5.refs_0_), channel_id=1, source_target_pairs={{0,4},{4,0},{8,12},{12,8},{16,20},{20,16},{24,28},{28,24},{32,36},... | collective-permute-start | bytes 786440 | tf_op jit(solution)/shard_map/ppermute | solution.py:53
  113.9 10.9 %collective-permute-start.37 = (bf16[64,2048]{1,0:T(8,128)(2,1)S(1)}, bf16[64,2048]{1,0:T(8,128)(2,1)S(1)}, u32[]{:S(2)}, u32[]{:S(2)}) collective-permute-start(bf16[64,2048]{1,0:T(8,128)(2,1)S(1)} %collective-permute-done.36.refs_3_), channel_id=1, source_target_pairs={{0,32},{4,12},{8,40},{12,4},{16,48},{20,28},{24,56},{28,20},{32,0}... | collective-permute-start | bytes 786440 | tf_op jit(solution)/shard_map/ppermute | solution.py:49
  115.9 9.0 %collective-permute-start.33 = (bf16[64,2048]{1,0:T(8,128)(2,1)S(1)}, bf16[64,2048]{1,0:T(8,128)(2,1)S(1)}, u32[]{:S(2)}, u32[]{:S(2)}) collective-permute-start(bf16[64,2048]{1,0:T(8,128)(2,1)S(1)} %collective-permute-done.32.refs_2_), channel_id=1, source_target_pairs={{0,96},{4,28},{8,104},{12,20},{16,112},{20,12},{24,120},{28,4},{32... | collective-permute-start | bytes 786440 | tf_op jit(solution)/shard_map/ppermute | solution.py:49
  129.9 12.2 %all-to-all-start = ((f32[32,1,128]{2,1,0:T(1,128)}), f32[32,1,128]{2,1,0:T(1,128)S(1)}, u32[]{:S(2)}, u32[]{:S(2)}) async-start(f32[32,1,128]{2,1,0:T(1,128)} %head_stats.5._stats), calls=%async_computation | async-start | bytes 32768 | tf_op jit(solution)/shard_map/all_to_all | solution.py:721
  (39 other events, 482.0 us)

commit v8 on v7

--- a/solution.py
+++ b/solution.py
@@ -66,18 +66,14 @@
     return sum(part.astype(jnp.float32) for part in parts).astype(jnp.bfloat16)
 
 
-def stream(joined, s):
-    rows = joined.shape[0] // 2
-    return joined[s * rows : (s + 1) * rows]
-
-
-def late_sum(late):
+def scatter_rows(early, late):
+    rows = late[0][0].shape[0]
+
+    def stream(joined, s):
+        return joined[s * rows : (s + 1) * rows]
+
     came = swap_core(late[1][0])
-    return [added(late[0][s], stream(came, s)) for s in range(2)]
-
-
-def scatter_rows(early, late):
-    last = [hop(late[s], 1, EDGES[s][1]) for s in range(2)]
+    last = [hop(added(late[0][s], stream(came, s)), 1, EDGES[s][1]) for s in range(2)]
     kept, near, far = (swap_core(part) for part in early[1])
     own = early[0]
     far = [hop(added(own[4 + s], stream(far, s)), 1, EDGES[s][1]) for s in range(2)]
@@ -666,7 +662,6 @@
     w_both = jnp.concatenate([w_gate, w_up], axis=1)
     early, late = gather_rows(prepared)
     early = (early, swap_early(early))
-    late, own_bc = lax.optimization_barrier((late, own_bc))
     late = (late, [swap_core(part) for part in late])
 
     core = req_rank % CORES
@@ -682,14 +677,13 @@
     owners = jnp.broadcast_to(owner[:, None], (64, draft_len)).reshape(1, 64 * draft_len)
 
     half = 2 * own_tokens
+    early_parts = [
+        feed(rows, out_rows, w_both, w_down, mlp_gain)
+        for rows, out_rows in zip(early, ([half] * 6, [2 * half] * 3), strict=True)
+    ]
     late_parts = [
         feed(rows, out_rows, w_both, w_down, own_bc)
         for rows, out_rows in zip(late, ([half] * 2, [2 * half]), strict=True)
-    ]
-    late_parts = late_sum(late_parts)
-    early_parts = [
-        feed(rows, out_rows, w_both, w_down, late_parts[0])
-        for rows, out_rows in zip(early, ([half] * 6, [2 * half] * 3), strict=True)
     ]
     summed = scatter_rows(early_parts, late_parts)
     tip = early_parts[0][0][:8, :128]

time: 144 us -> 136 us (0.944)
  starting transfers between devices: 63.8 us -> 60.7 us
  waiting for transfers between devices: 38.7 us -> 36.3 us
  other arithmetic: 6.17 us -> 4.22 us
    ppermute x27, waiting for transfers between devices: 26.2 us -> 23 us  [hop(): return lax.ppermute(part, 'req', flip_pairs(ring, flip))]
    ppermute x16, starting transfers between devices: 23.5 us -> 21.5 us  [swap_core(): return lax.ppermute(part, 'req', CORE_PAIRS)]
    convert_element_type x4, other arithmetic: 3.59 us -> 1.66 us  [added(): sum((part.astype(jnp.float32) for part in parts)).astype(jnp.bfloat16)]
    unnamed x47 -> x49, local copies, waits for them, and re-layouts: 3.45 us -> 3.45 us
  transfers between devices with their start and end apart: 48 -> 48, of which waited for: 22 -> 20; matrix products, arithmetic and copies ran while one was open for 2% -> 3% of each run, Pallas kernels for 12% -> 15%
where the time goes in v8:
time: 136 us
  starting transfers between devices  60.7 us (45%)
  waiting for transfers between devices  36.3 us (27%)
  Pallas kernels  28.6 us (21%)
  local copies, waits for them, and re-layouts  4.26 us (3%)
  other arithmetic  4.22 us (3%)
    ppermute x27, starting transfers between devices, hop(): return lax.ppermute(part, 'req', flip_pairs(ring, flip))  25.7 us
    ppermute x27, waiting for transfers between devices, hop(): return lax.ppermute(part, 'req', flip_pairs(ring, flip))  23 us
    ppermute x16, starting transfers between devices, swap_core(): return lax.ppermute(part, 'req', CORE_PAIRS)  21.5 us
    pallas_call x3, Pallas kernels, head_stats(): pl.pallas_call(functools.partial(head_kernel, len(rows)), out_shape=jax.S...  8.48 us
    pallas_call x1, Pallas kernels, mixer(): pl.pallas_call(mixer_kernel, out_shape=[*[jax.ShapeDtypeStruct((tokens //...  8.31 us
    pallas_call x4, Pallas kernels, feed(): pl.pallas_call(functools.partial(feed_kernel, len(arrays)), out_shape=[ja...  6.19 us
    ppermute x3, waiting for transfers between devices, shards(): lax.ppermute(part, 'mdl', [(z, z ^ flip) for z in range(SIDE)])  6.1 us
    ppermute x3, starting transfers between devices, shards(): lax.ppermute(part, 'mdl', [(z, z ^ flip) for z in range(SIDE)])  5.85 us
  transfers between devices with their start and end apart: 48, of which 20 were waited for; matrix products, arithmetic and copies ran while one was open for 3% of the time, Pallas kernels for 15%

profile of v8, /device:TPU:1, one launch (start us, length us, event | category | flops | bytes accessed | tf_op | source)
XLA Modules:
  0.0 135.6 jit_solution(14499703263613243199)
XLA Ops:
  0.6 8.3 %mixer.1 = (bf16[32,2048]{1,0:T(8,128)(2,1)}, bf16[32,2048]{1,0:T(8,128)(2,1)}, bf16[32,2048]{1,0:T(8,128)(2,1)}, bf16[32,2048]{1,0:T(8,128)(2,1)}, f32[128,128]...) custom-call(s32[8]{0:T(128)} %refs_0_.3, ...), custom_call_target="tpu_custom_call" | custom-call | flops 3000000000 | bytes 20000000 | tf_op jit(solution)/shard_map/mixer/pallas_call | solution.py:485
  9.0 2.5 %collective-permute-start = (bf16[32,2048]{1,0:T(8,128)(2,1)}, bf16[32,2048]{1,0:T(8,128)(2,1)S(1)}, u32[]{:S(2)}, u32[]{:S(2)}) collective-permute-start(bf16[32,2048]{1,0:T(8,128)(2,1)} %get-tuple-element.38), channel_id=1, source_target_pairs={{0,1},{1,0},{2,3},{3,2},{4,5},{5,4},{6,7},{7,6},{8,9},{9,8},{10,11... | collective-permute-start | bytes 393224 | tf_op jit(solution)/shard_map/ppermute | solution.py:655
  11.6 2.2 %collective-permute-start.1 = (bf16[32,2048]{1,0:T(8,128)(2,1)}, bf16[32,2048]{1,0:T(8,128)(2,1)S(1)}, u32[]{:S(2)}, u32[]{:S(2)}) collective-permute-start(bf16[32,2048]{1,0:T(8,128)(2,1)} %get-tuple-element.39), channel_id=1, source_target_pairs={{0,3},{1,2},{2,1},{3,0},{4,7},{5,6},{6,5},{7,4},{8,11},{9,10},{10,... | collective-permute-start | bytes 393224 | tf_op jit(solution)/shard_map/ppermute | solution.py:655
  15.0 4.3 %collective-permute-done.1 = bf16[32,2048]{1,0:T(8,128)(2,1)S(1)} collective-permute-done((bf16[32,2048]{1,0:T(8,128)(2,1)}, bf16[32,2048]{1,0:T(8,128)(2,1)S(1)}, u32[]{:S(2)}, u32[]{:S(2)}) %collective-permute-start.1) | collective-permute-done | bytes 131104 | tf_op jit(solution)/shard_map/ppermute | solution.py:655
  19.2 1.8 %collective-permute-done.2 = bf16[32,2048]{1,0:T(8,128)(2,1)S(1)} collective-permute-done((bf16[32,2048]{1,0:T(8,128)(2,1)}, bf16[32,2048]{1,0:T(8,128)(2,1)S(1)}, u32[]{:S(2)}, u32[]{:S(2)}) %collective-permute-start.2) | collective-permute-done | bytes 131104 | tf_op jit(solution)/shard_map/ppermute | solution.py:655
  22.3 2.8 %collective-permute-start.4 = (bf16[32,2048]{1,0:T(8,128)(2,1)S(1)}, bf16[32,2048]{1,0:T(8,128)(2,1)S(1)}, u32[]{:S(2)}, u32[]{:S(2)}) collective-permute-start(bf16[32,2048]{1,0:T(8,128)(2,1)S(1)} %fusion.5), channel_id=1, source_target_pairs={{0,24},{4,100},{8,16},{12,108},{16,8},{20,116},{24,0},{28,124},{32... | collective-permute-start | bytes 393224 | tf_op jit(solution)/shard_map/ppermute | solution.py:49
  25.8 2.6 %collective-permute-done.4 = bf16[32,2048]{1,0:T(8,128)(2,1)S(1)} collective-permute-done((bf16[32,2048]{1,0:T(8,128)(2,1)S(1)}, bf16[32,2048]{1,0:T(8,128)(2,1)S(1)}, u32[]{:S(2)}, u32[]{:S(2)}) %collective-permute-start.4) | collective-permute-done | bytes 131104 | tf_op jit(solution)/shard_map/ppermute | solution.py:49
  28.5 2.0 %collective-permute-done.5 = bf16[32,2048]{1,0:T(8,128)(2,1)S(1)} collective-permute-done((bf16[32,2048]{1,0:T(8,128)(2,1)S(1)}, bf16[32,2048]{1,0:T(8,128)(2,1)S(1)}, u32[]{:S(2)}, u32[]{:S(2)}) %collective-permute-start.5) | collective-permute-done | bytes 131104 | tf_op jit(solution)/shard_map/ppermute | solution.py:49
  30.5 2.6 %collective-permute-start.7 = (bf16[64,2048]{1,0:T(8,128)(2,1)S(1)}, bf16[64,2048]{1,0:T(8,128)(2,1)S(1)}, u32[]{:S(2)}, u32[]{:S(2)}) collective-permute-start(bf16[64,2048]{1,0:T(8,128)(2,1)S(1)} %constant_dynamic-update-slice_fusion.2.refs_1_), channel_id=1, source_target_pairs={{0,96},{4,28},{8,104},{12,20},{16,112},{20,12},{24,120},{28,4},{32... | collective-permute-start | bytes 786440 | tf_op jit(solution)/shard_map/ppermute | solution.py:49
  39.8 3.6 %keeper.1 = (bf16[8,400,256]{2,1,0:T(8,128)(2,1)}, bf16[16,512]{1,0:T(8,128)(2,1)S(1)}) custom-call(s32[8]{0:T(128)S(1)} %copy-done.6, s32[8]{0:T(128)S(1)} %copy-done.7, f32[128,128]{1,0:T(8,128)S(1)} %copy-done.13, f32[128,384]{1,0:T(8,128)S(1)} %copy-done.10, bf16[128,256]{1,0:T(8,128)(2,1)S(1)} %copy-done.14, bf16[128,384]{1,0:T(8,128)(2,1)S(1)} %copy-done.12, ...), custom_call_target="tpu_custom_call" | custom-call | flops 2000000000 | bytes 5000000 | tf_op jit(solution)/shard_map/keeper/pallas_call | solution.py:216
  43.6 4.0 %collective-permute-start.13 = (bf16[128,2048]{1,0:T(8,128)(2,1)S(1)}, bf16[128,2048]{1,0:T(8,128)(2,1)S(1)}, u32[]{:S(2)}, u32[]{:S(2)}) collective-permute-start(bf16[128,2048]{1,0:T(8,128)(2,1)S(1)} %pad_maximum_fusion.1), channel_id=1, source_target_pairs={{0,4},{4,0},{8,12},{12,8},{16,20},{20,16},{24,28},{28,24},{32,36},... | collective-permute-start | bytes 1572872 | tf_op jit(solution)/shard_map/ppermute | solution.py:53
  48.3 2.0 %collective-permute-start.20 = (bf16[64,2048]{1,0:T(8,128)(2,1)}, bf16[64,2048]{1,0:T(8,128)(2,1)S(1)}, u32[]{:S(2)}, u32[]{:S(2)}) collective-permute-start(bf16[64,2048]{1,0:T(8,128)(2,1)} %collective-permute-done.18.refs_0_), channel_id=1, source_target_pairs={{0,4},{4,0},{8,12},{12,8},{16,20},{20,16},{24,28},{28,24},{32,36},... | collective-permute-start | bytes 786440 | tf_op jit(solution)/shard_map/ppermute | solution.py:53
  52.9 1.8 %feed.4 = (bf16[64,2048]{1,0:T(8,128)(2,1)S(1)}, bf16[64,2048]{1,0:T(8,128)(2,1)S(1)}, bf16[64,2048]{1,0:T(8,128)(2,1)S(1)}, bf16[64,2048]{1,0:T(8,128)(2,1)S(1)...) custom-call(bf16[2048,256]{1,0:T(8,128)(2,1)S(1)} %constant_dynamic-update-slice_fusion.both_ref, ...), custom_call_target="tpu_custom_call" | custom-call | flops 2415919104 | bytes 4718592 | tf_op jit(solution)/shard_map/feed/pallas_call | solution.py:540
  54.7 1.8 %feed.5 = (bf16[128,2048]{1,0:T(8,128)(2,1)S(1)}, bf16[128,2048]{1,0:T(8,128)(2,1)S(1)}, bf16[128,2048]{1,0:T(8,128)(2,1)S(1)}) custom-call(bf16[2048,256]{1,0:T(8,128)(2,1)S(1)} %constant_dynamic-update-slice_fusion.both_ref, bf16[128,2048]{1,0:T(8,128)(2,1)S(1)} %copy-done.9, bf16[2048]{0:T(1024)(128)(2,1)S(1)} %copy-done.5, ...), custom_call_target="tpu_custom_call" | custom-call | flops 2415919104 | bytes 4718592 | tf_op jit(solution)/shard_map/feed/pallas_call | solution.py:540
  56.7 1.8 %feed.6 = (bf16[64,2048]{1,0:T(8,128)(2,1)S(1)}, bf16[64,2048]{1,0:T(8,128)(2,1)S(1)}) custom-call(bf16[2048,256]{1,0:T(8,128)(2,1)S(1)} %constant_dynamic-update-slice_fusion.both_ref, bf16[128,2048]{1,0:T(8,128)(2,1)S(1)} %copy-done.9, bf16[16,512]{1,0:T(8,128)(2,1)S(1)} %get-tuple-element.52._token.bc_ref, ...), custom_call_target="tpu_custom_call" | custom-call | flops 805306368 | bytes 2621440 | tf_op jit(solution)/shard_map/feed/pallas_call | solution.py:540
  60.4 1.9 %collective-permute-start.16 = (bf16[64,2048]{1,0:T(8,128)(2,1)S(1)}, bf16[64,2048]{1,0:T(8,128)(2,1)S(1)}, u32[]{:S(2)}, u32[]{:S(2)}) collective-permute-start(bf16[64,2048]{1,0:T(8,128)(2,1)S(1)} %get-tuple-element.78), channel_id=1, source_target_pairs={{0,96},{4,28},{8,104},{12,20},{16,112},{20,12},{24,120},{28,4},{32... | collective-permute-start | bytes 786440 | tf_op jit(solution)/shard_map/ppermute | solution.py:49
  63.2 3.0 %collective-permute-done.23 = bf16[64,2048]{1,0:T(8,128)(2,1)S(1)} collective-permute-done((bf16[64,2048]{1,0:T(8,128)(2,1)S(1)}, bf16[64,2048]{1,0:T(8,128)(2,1)S(1)}, u32[]{:S(2)}, u32[]{:S(2)}) %collective-permute-start.23) | collective-permute-done | bytes 262176 | tf_op jit(solution)/shard_map/ppermute | solution.py:49
  68.9 4.0 %collective-permute-done.24 = bf16[64,2048]{1,0:T(8,128)(2,1)S(1)} collective-permute-done((bf16[64,2048]{1,0:T(8,128)(2,1)}, bf16[64,2048]{1,0:T(8,128)(2,1)S(1)}, u32[]{:S(2)}, u32[]{:S(2)}) %collective-permute-start.24) | collective-permute-done | bytes 262176 | tf_op jit(solution)/shard_map/ppermute | solution.py:49
  76.2 1.8 %collective-permute-start.25 = (bf16[32,2048]{1,0:T(8,128)(2,1)S(1)}, bf16[32,2048]{1,0:T(8,128)(2,1)S(1)}, u32[]{:S(2)}, u32[]{:S(2)}) collective-permute-start(bf16[32,2048]{1,0:T(8,128)(2,1)S(1)} %slice.117), channel_id=1, source_target_pairs={{0,8},{4,36},{8,0},{12,44},{16,24},{20,52},{24,16},{28,60},{32,40}... | collective-permute-start | bytes 393224 | tf_op jit(solution)/shard_map/ppermute | solution.py:49
  78.6 2.8 %collective-permute-done.29 = bf16[32,2048]{1,0:T(8,128)(2,1)S(1)} collective-permute-done((bf16[32,2048]{1,0:T(8,128)(2,1)S(1)}, bf16[32,2048]{1,0:T(8,128)(2,1)S(1)}, u32[]{:S(2)}, u32[]{:S(2)}) %collective-permute-start.29) | collective-permute-done | bytes 131104 | tf_op jit(solution)/shard_map/ppermute | solution.py:49
  85.7 3.2 %collective-permute-done.34 = bf16[32,2048]{1,0:T(8,128)(2,1)S(1)} collective-permute-done((bf16[32,2048]{1,0:T(8,128)(2,1)S(1)}, bf16[32,2048]{1,0:T(8,128)(2,1)S(1)}, u32[]{:S(2)}, u32[]{:S(2)}) %collective-permute-start.34) | collective-permute-done | bytes 131104 | tf_op jit(solution)/shard_map/ppermute | solution.py:49
  89.5 1.8 %collective-permute-start.38 = (bf16[64,2048]{1,0:T(8,128)(2,1)S(1)}, bf16[64,2048]{1,0:T(8,128)(2,1)S(1)}, u32[]{:S(2)}, u32[]{:S(2)}) collective-permute-start(bf16[64,2048]{1,0:T(8,128)(2,1)S(1)} %pad_maximum_fusion.5.refs_0_), channel_id=1, source_target_pairs={{0,96},{4,28},{8,104},{12,20},{16,112},{20,12},{24,120},{28,4},{32... | collective-permute-start | bytes 786440 | tf_op jit(solution)/shard_map/ppermute | solution.py:49
  92.2 3.6 %all-to-all-start.1 = ((bf16[4,2,400,256]{3,2,1,0:T(8,128)(2,1)}), bf16[4,2,400,256]{3,2,1,0:T(8,128)(2,1)S(1)}, u32[]{:S(2)}, u32[]{:S(2)}) async-start(bf16[4,2,400,256]{3,2,1,0:T(8,128)(2,1)} %bitcast.12), calls=%async_computation.1 | async-start | bytes 3276800 | tf_op jit(solution)/shard_map/all_to_all | solution.py:691
  96.3 7.7 %collective-permute-start.43 = (bf16[128,2048]{1,0:T(8,128)(2,1)S(1)}, bf16[128,2048]{1,0:T(8,128)(2,1)S(1)}, u32[]{:S(2)}, u32[]{:S(2)}) collective-permute-start(bf16[128,2048]{1,0:T(8,128)(2,1)S(1)} %pad_maximum_fusion.3), channel_id=1, source_target_pairs={{0,4},{4,0},{8,12},{12,8},{16,20},{20,16},{24,28},{28,24},{32,36},... | collective-permute-start | bytes 1572872 | tf_op jit(solution)/shard_map/ppermute | solution.py:53
  104.0 2.8 %collective-permute-start.42 = (bf16[128,2048]{1,0:T(8,128)(2,1)S(1)}, bf16[128,2048]{1,0:T(8,128)(2,1)S(1)}, u32[]{:S(2)}, u32[]{:S(2)}) collective-permute-start(bf16[128,2048]{1,0:T(8,128)(2,1)S(1)} %pad_maximum_fusion.2), channel_id=1, source_target_pairs={{0,4},{4,0},{8,12},{12,8},{16,20},{20,16},{24,28},{28,24},{32,36},... | collective-permute-start | bytes 1572872 | tf_op jit(solution)/shard_map/ppermute | solution.py:53
  109.7 2.2 %copy-done = bf16[1024,2048]{1,0:T(8,128)(2,1)S(1)} copy-done((bf16[1024,2048]{1,0:T(8,128)(2,1)S(1)}, bf16[1024,2048]{1,0:T(8,128)(2,1)}, u32[]{:S(2)}) %copy-start) | copy-done | bytes 4194328
  111.9 3.0 %head_stats.3.refs_5_ = f32[32,1,128]{2,1,0:T(1,128)S(1)} custom-call(s32[1,384]{1,0:T(1,128)S(1)} %get-tuple-element.92.targets_ref, s32[1,384]{1,0:T(1,128)S(1)} %get-tuple-element.89.owners_ref, bf16[64,2048]{1,0:T(8,128)(2,1)S(1)} %pad_maximum_fusion.5.refs_0_, bf16[64,2048]{1,0:T(8,128)(2,1)S(1)} %constant_dynamic-update-slice_fusion.4.refs_1_, ...), custom_call_target="tpu_custom_call" | custom-call | flops 1610612736 | bytes 5767168 | tf_op jit(solution)/shard_map/head_stats/pallas_call | solution.py:594
  115.0 3.0 %head_stats.4.refs_6_ = f32[32,1,128]{2,1,0:T(1,128)S(1)} custom-call(s32[1,384]{1,0:T(1,128)S(1)} %get-tuple-element.93.targets_ref, s32[1,384]{1,0:T(1,128)S(1)} %get-tuple-element.88.owners_ref, bf16[64,2048]{1,0:T(8,128)(2,1)S(1)} %collective-permute-done.40.refs_0_, bf16[64,2048]{1,0:T(8,128)(2,1)S(1)} %collective-permute-done.41.refs_1_, ...), custom_call_target="tpu_custom_call" | custom-call | flops 1610612736 | bytes 5767168 | tf_op jit(solution)/shard_map/head_stats/pallas_call | solution.py:594
  121.1 2.5 %head_stats.5._stats = f32[32,1,128]{2,1,0:T(1,128)} custom-call(s32[1,256]{1,0:T(1,128)S(1)} %slice.102.targets_ref, s32[1,256]{1,0:T(1,128)S(1)} %slice.103.owners_ref, bf16[64,2048]{1,0:T(8,128)(2,1)S(1)} %collective-permute-done.33.refs_0_, bf16[64,2048]{1,0:T(8,128)(2,1)S(1)} %collective-permute-done.37.refs_1_, ...), custom_call_target="tpu_custom_call" | custom-call | flops 1073741824 | bytes 5242880 | tf_op jit(solution)/shard_map/head_stats/pallas_call | solution.py:594
  123.6 4.0 %all-to-all-start = ((f32[32,1,128]{2,1,0:T(1,128)}), f32[32,1,128]{2,1,0:T(1,128)S(1)}, u32[]{:S(2)}, u32[]{:S(2)}) async-start(f32[32,1,128]{2,1,0:T(1,128)} %head_stats.5._stats), calls=%async_computation | async-start | bytes 32768 | tf_op jit(solution)/shard_map/all_to_all | solution.py:715
  127.6 2.1 %unpack.1 = (f32[2,1536,256]{2,1,0:T(8,128)}, bf16[3,2,2048]{2,1,0:T(2,128)(2,1)}) custom-call(bf16[4,2,400,256]{3,2,1,0:T(8,128)(2,1)S(1)} %all-to-all-done.1.kept_hbm, bf16[16,512]{1,0:T(8,128)(2,1)S(1)} %get-tuple-element.52._token.bc_ref, f32[32,1,128]{2,1,0:T(1,128)} %head_stats.5._stats, bf16[8,128]{1,0:T(8,128)(2,1)S(1)} %slice.111._tip), custom_call_target="tpu_custom_call" | custom-call | flops 1000000 | bytes 20000000 | tf_op jit(solution)/shard_map/unpack/pallas_call | solution.py:263
  129.7 4.9 %all-to-all-done = f32[32,1,128]{2,1,0:T(1,128)S(1)} async-done(((f32[32,1,128]{2,1,0:T(1,128)}), f32[32,1,128]{2,1,0:T(1,128)S(1)}, u32[]{:S(2)}, u32[]{:S(2)}) %all-to-all-start) | async-done | bytes 16416 | tf_op jit(solution)/shard_map/all_to_all | solution.py:715
  (168 shorter events, 36.1 us)
Async XLA Ops:
  9.0 6.0 %collective-permute-start = (bf16[32,2048]{1,0:T(8,128)(2,1)}, bf16[32,2048]{1,0:T(8,128)(2,1)S(1)}, u32[]{:S(2)}, u32[]{:S(2)}) collective-permute-start(bf16[32,2048]{1,0:T(8,128)(2,1)} %get-tuple-element.38), channel_id=1, source_target_pairs={{0,1},{1,0},{2,3},{3,2},{4,5},{5,4},{6,7},{7,6},{8,9},{9,8},{10,11... | collective-permute-start | bytes 393224 | tf_op jit(solution)/shard_map/ppermute | solution.py:655
  11.6 7.7 %collective-permute-start.1 = (bf16[32,2048]{1,0:T(8,128)(2,1)}, bf16[32,2048]{1,0:T(8,128)(2,1)S(1)}, u32[]{:S(2)}, u32[]{:S(2)}) collective-permute-start(bf16[32,2048]{1,0:T(8,128)(2,1)} %get-tuple-element.39), channel_id=1, source_target_pairs={{0,3},{1,2},{2,1},{3,0},{4,7},{5,6},{6,5},{7,4},{8,11},{9,10},{10,... | collective-permute-start | bytes 393224 | tf_op jit(solution)/shard_map/ppermute | solution.py:655
  13.8 7.2 %collective-permute-start.2 = (bf16[32,2048]{1,0:T(8,128)(2,1)}, bf16[32,2048]{1,0:T(8,128)(2,1)S(1)}, u32[]{:S(2)}, u32[]{:S(2)}) collective-permute-start(bf16[32,2048]{1,0:T(8,128)(2,1)} %get-tuple-element.40), channel_id=1, source_target_pairs={{0,2},{1,3},{2,0},{3,1},{4,6},{5,7},{6,4},{7,5},{8,10},{9,11},{10,... | collective-permute-start | bytes 393224 | tf_op jit(solution)/shard_map/ppermute | solution.py:655
  22.3 6.1 %collective-permute-start.4 = (bf16[32,2048]{1,0:T(8,128)(2,1)S(1)}, bf16[32,2048]{1,0:T(8,128)(2,1)S(1)}, u32[]{:S(2)}, u32[]{:S(2)}) collective-permute-start(bf16[32,2048]{1,0:T(8,128)(2,1)S(1)} %fusion.5), channel_id=1, source_target_pairs={{0,24},{4,100},{8,16},{12,108},{16,8},{20,116},{24,0},{28,124},{32... | collective-permute-start | bytes 393224 | tf_op jit(solution)/shard_map/ppermute | solution.py:49
  25.5 7.5 %collective-permute-start.3 = (bf16[32,2048]{1,0:T(8,128)(2,1)S(1)}, bf16[32,2048]{1,0:T(8,128)(2,1)S(1)}, u32[]{:S(2)}, u32[]{:S(2)}) collective-permute-start(bf16[32,2048]{1,0:T(8,128)(2,1)S(1)} %fusion.5), channel_id=1, source_target_pairs={{0,8},{4,36},{8,0},{12,44},{16,24},{20,52},{24,16},{28,60},{32,40}... | collective-permute-start | bytes 393224 | tf_op jit(solution)/shard_map/ppermute | solution.py:49
  30.5 6.5 %collective-permute-start.7 = (bf16[64,2048]{1,0:T(8,128)(2,1)S(1)}, bf16[64,2048]{1,0:T(8,128)(2,1)S(1)}, u32[]{:S(2)}, u32[]{:S(2)}) collective-permute-start(bf16[64,2048]{1,0:T(8,128)(2,1)S(1)} %constant_dynamic-update-slice_fusion.2.refs_1_), channel_id=1, source_target_pairs={{0,96},{4,28},{8,104},{12,20},{16,112},{20,12},{24,120},{28,4},{32... | collective-permute-start | bytes 786440 | tf_op jit(solution)/shard_map/ppermute | solution.py:49
  33.1 10.3 %collective-permute-start.9 = (bf16[64,2048]{1,0:T(8,128)(2,1)S(1)}, bf16[64,2048]{1,0:T(8,128)(2,1)S(1)}, u32[]{:S(2)}, u32[]{:S(2)}) collective-permute-start(bf16[64,2048]{1,0:T(8,128)(2,1)S(1)} %constant_dynamic-update-slice_fusion.2.refs_1_), channel_id=1, source_target_pairs={{0,32},{4,12},{8,40},{12,4},{16,48},{20,28},{24,56},{28,20},{32,0}... | collective-permute-start | bytes 786440 | tf_op jit(solution)/shard_map/ppermute | solution.py:49
  34.6 8.9 %collective-permute-start.8 = (bf16[64,2048]{1,0:T(8,128)(2,1)S(1)}, bf16[64,2048]{1,0:T(8,128)(2,1)S(1)}, u32[]{:S(2)}, u32[]{:S(2)}) collective-permute-start(bf16[64,2048]{1,0:T(8,128)(2,1)S(1)} %pad_maximum_fusion.4.refs_0_), channel_id=1, source_target_pairs={{0,96},{4,28},{8,104},{12,20},{16,112},{20,12},{24,120},{28,4},{32... | collective-permute-start | bytes 786440 | tf_op jit(solution)/shard_map/ppermute | solution.py:49
  37.0 10.6 %collective-permute-start.19 = (bf16[64,2048]{1,0:T(8,128)(2,1)S(1)}, bf16[64,2048]{1,0:T(8,128)(2,1)}, u32[]{:S(2)}, u32[]{:S(2)}) collective-permute-start(bf16[64,2048]{1,0:T(8,128)(2,1)S(1)} %collective-permute-done.7.refs_3_), channel_id=1, source_target_pairs={{0,32},{4,12},{8,40},{12,4},{16,48},{20,28},{24,56},{28,20},{32,0}... | collective-permute-start | bytes 786440 | tf_op jit(solution)/shard_map/ppermute | solution.py:49
  38.7 9.6 %collective-permute-start.18 = (bf16[64,2048]{1,0:T(8,128)(2,1)S(1)}, bf16[64,2048]{1,0:T(8,128)(2,1)}, u32[]{:S(2)}, u32[]{:S(2)}) collective-permute-start(bf16[64,2048]{1,0:T(8,128)(2,1)S(1)} %collective-permute-done.6.refs_2_), channel_id=1, source_target_pairs={{0,96},{4,28},{8,104},{12,20},{16,112},{20,12},{24,120},{28,4},{32... | collective-permute-start | bytes 786440 | tf_op jit(solution)/shard_map/ppermute | solution.py:49
  43.6 11.1 %collective-permute-start.13 = (bf16[128,2048]{1,0:T(8,128)(2,1)S(1)}, bf16[128,2048]{1,0:T(8,128)(2,1)S(1)}, u32[]{:S(2)}, u32[]{:S(2)}) collective-permute-start(bf16[128,2048]{1,0:T(8,128)(2,1)S(1)} %pad_maximum_fusion.1), channel_id=1, source_target_pairs={{0,4},{4,0},{8,12},{12,8},{16,20},{20,16},{24,28},{28,24},{32,36},... | collective-permute-start | bytes 1572872 | tf_op jit(solution)/shard_map/ppermute | solution.py:53
  52.4 6.7 %collective-permute-start.22 = (bf16[128,2048]{1,0:T(8,128)(2,1)S(1)}, bf16[128,2048]{1,0:T(8,128)(2,1)S(1)}, u32[]{:S(2)}, u32[]{:S(2)}) collective-permute-start(bf16[128,2048]{1,0:T(8,128)(2,1)S(1)} %feed.7), channel_id=1, source_target_pairs={{0,4},{4,0},{8,12},{12,8},{16,20},{20,16},{24,28},{28,24},{32,36},... | collective-permute-start | bytes 1572872 | tf_op jit(solution)/shard_map/ppermute | solution.py:53
  59.0 9.9 %collective-permute-start.14 = (bf16[128,2048]{1,0:T(8,128)(2,1)S(1)}, bf16[128,2048]{1,0:T(8,128)(2,1)S(1)}, u32[]{:S(2)}, u32[]{:S(2)}) collective-permute-start(bf16[128,2048]{1,0:T(8,128)(2,1)S(1)} %get-tuple-element.42), channel_id=1, source_target_pairs={{0,4},{4,0},{8,12},{12,8},{16,20},{20,16},{24,28},{28,24},{32,36},... | collective-permute-start | bytes 1572872 | tf_op jit(solution)/shard_map/ppermute | solution.py:53
  59.3 6.8 %collective-permute-start.23 = (bf16[64,2048]{1,0:T(8,128)(2,1)S(1)}, bf16[64,2048]{1,0:T(8,128)(2,1)S(1)}, u32[]{:S(2)}, u32[]{:S(2)}) collective-permute-start(bf16[64,2048]{1,0:T(8,128)(2,1)S(1)} %get-tuple-element.82), channel_id=1, source_target_pairs={{0,96},{4,28},{8,104},{12,20},{16,112},{20,12},{24,120},{28,4},{32... | collective-permute-start | bytes 786440 | tf_op jit(solution)/shard_map/ppermute | solution.py:49
  60.3 5.9 %collective-permute-start.27 = (bf16[64,2048]{1,0:T(8,128)(2,1)S(1)}, bf16[64,2048]{1,0:T(8,128)(2,1)S(1)}, u32[]{:S(2)}, u32[]{:S(2)}) collective-permute-start(bf16[64,2048]{1,0:T(8,128)(2,1)S(1)} %get-tuple-element.83), channel_id=1, source_target_pairs={{0,32},{4,12},{8,40},{12,4},{16,48},{20,28},{24,56},{28,20},{32,0}... | collective-permute-start | bytes 786440 | tf_op jit(solution)/shard_map/ppermute | solution.py:49
  60.4 8.5 %collective-permute-start.16 = (bf16[64,2048]{1,0:T(8,128)(2,1)S(1)}, bf16[64,2048]{1,0:T(8,128)(2,1)S(1)}, u32[]{:S(2)}, u32[]{:S(2)}) collective-permute-start(bf16[64,2048]{1,0:T(8,128)(2,1)S(1)} %get-tuple-element.78), channel_id=1, source_target_pairs={{0,96},{4,28},{8,104},{12,20},{16,112},{20,12},{24,120},{28,4},{32... | collective-permute-start | bytes 786440 | tf_op jit(solution)/shard_map/ppermute | solution.py:49
  62.3 6.6 %collective-permute-start.26 = (bf16[64,2048]{1,0:T(8,128)(2,1)S(1)}, bf16[64,2048]{1,0:T(8,128)(2,1)S(1)}, u32[]{:S(2)}, u32[]{:S(2)}) collective-permute-start(bf16[64,2048]{1,0:T(8,128)(2,1)S(1)} %get-tuple-element.79), channel_id=1, source_target_pairs={{0,32},{4,12},{8,40},{12,4},{16,48},{20,28},{24,56},{28,20},{32,0}... | collective-permute-start | bytes 786440 | tf_op jit(solution)/shard_map/ppermute | solution.py:49
  67.2 7.0 %collective-permute-start.28 = (bf16[64,2048]{1,0:T(8,128)(2,1)}, bf16[64,2048]{1,0:T(8,128)(2,1)S(1)}, u32[]{:S(2)}, u32[]{:S(2)}) collective-permute-start(bf16[64,2048]{1,0:T(8,128)(2,1)} %get-tuple-element.81), channel_id=1, source_target_pairs={{0,96},{4,28},{8,104},{12,20},{16,112},{20,12},{24,120},{28,4},{32... | collective-permute-start | bytes 786440 | tf_op jit(solution)/shard_map/ppermute | solution.py:49
  74.6 6.8 %collective-permute-start.29 = (bf16[32,2048]{1,0:T(8,128)(2,1)S(1)}, bf16[32,2048]{1,0:T(8,128)(2,1)S(1)}, u32[]{:S(2)}, u32[]{:S(2)}) collective-permute-start(bf16[32,2048]{1,0:T(8,128)(2,1)S(1)} %get-tuple-element.84), channel_id=1, source_target_pairs={{0,24},{4,100},{8,16},{12,108},{16,8},{20,116},{24,0},{28,124},{32... | collective-permute-start | bytes 393224 | tf_op jit(solution)/shard_map/ppermute | solution.py:49
  75.5 5.9 %collective-permute-start.30 = (bf16[32,2048]{1,0:T(8,128)(2,1)S(1)}, bf16[32,2048]{1,0:T(8,128)(2,1)S(1)}, u32[]{:S(2)}, u32[]{:S(2)}) collective-permute-start(bf16[32,2048]{1,0:T(8,128)(2,1)S(1)} %get-tuple-element.85), channel_id=1, source_target_pairs={{0,16},{4,68},{8,24},{12,76},{16,0},{20,84},{24,8},{28,92},{32,48}... | collective-permute-start | bytes 393224 | tf_op jit(solution)/shard_map/ppermute | solution.py:49
  82.3 6.5 %collective-permute-start.34 = (bf16[32,2048]{1,0:T(8,128)(2,1)S(1)}, bf16[32,2048]{1,0:T(8,128)(2,1)S(1)}, u32[]{:S(2)}, u32[]{:S(2)}) collective-permute-start(bf16[32,2048]{1,0:T(8,128)(2,1)S(1)} %fusion.2), channel_id=1, source_target_pairs={{0,24},{4,100},{8,16},{12,108},{16,8},{20,116},{24,0},{28,124},{32... | collective-permute-start | bytes 393224 | tf_op jit(solution)/shard_map/ppermute | solution.py:49
  88.9 7.3 %collective-permute-start.39 = (bf16[64,2048]{1,0:T(8,128)(2,1)S(1)}, bf16[64,2048]{1,0:T(8,128)(2,1)S(1)}, u32[]{:S(2)}, u32[]{:S(2)}) collective-permute-start(bf16[64,2048]{1,0:T(8,128)(2,1)S(1)} %constant_dynamic-update-slice_fusion.4.refs_1_), channel_id=1, source_target_pairs={{0,32},{4,12},{8,40},{12,4},{16,48},{20,28},{24,56},{28,20},{32,0}... | collective-permute-start | bytes 786440 | tf_op jit(solution)/shard_map/ppermute | solution.py:49
  89.5 6.8 %collective-permute-start.38 = (bf16[64,2048]{1,0:T(8,128)(2,1)S(1)}, bf16[64,2048]{1,0:T(8,128)(2,1)S(1)}, u32[]{:S(2)}, u32[]{:S(2)}) collective-permute-start(bf16[64,2048]{1,0:T(8,128)(2,1)S(1)} %pad_maximum_fusion.5.refs_0_), channel_id=1, source_target_pairs={{0,96},{4,28},{8,104},{12,20},{16,112},{20,12},{24,120},{28,4},{32... | collective-permute-start | bytes 786440 | tf_op jit(solution)/shard_map/ppermute | solution.py:49
  91.3 12.7 %collective-permute-start.36 = (bf16[64,2048]{1,0:T(8,128)(2,1)S(1)}, bf16[64,2048]{1,0:T(8,128)(2,1)S(1)}, u32[]{:S(2)}, u32[]{:S(2)}) collective-permute-start(bf16[64,2048]{1,0:T(8,128)(2,1)S(1)} %constant_dynamic-update-slice_fusion.4.refs_1_), channel_id=1, source_target_pairs={{0,96},{4,28},{8,104},{12,20},{16,112},{20,12},{24,120},{28,4},{32... | collective-permute-start | bytes 786440 | tf_op jit(solution)/shard_map/ppermute | solution.py:49
  92.2 11.7 %collective-permute-start.32 = (bf16[64,2048]{1,0:T(8,128)(2,1)S(1)}, bf16[64,2048]{1,0:T(8,128)(2,1)S(1)}, u32[]{:S(2)}, u32[]{:S(2)}) collective-permute-start(bf16[64,2048]{1,0:T(8,128)(2,1)S(1)} %pad_maximum_fusion.5.refs_0_), channel_id=1, source_target_pairs={{0,32},{4,12},{8,40},{12,4},{16,48},{20,28},{24,56},{28,20},{32,0}... | collective-permute-start | bytes 786440 | tf_op jit(solution)/shard_map/ppermute | solution.py:49
  92.2 31.4 %all-to-all-start.1 = ((bf16[4,2,400,256]{3,2,1,0:T(8,128)(2,1)}), bf16[4,2,400,256]{3,2,1,0:T(8,128)(2,1)S(1)}, u32[]{:S(2)}, u32[]{:S(2)}) async-start(bf16[4,2,400,256]{3,2,1,0:T(8,128)(2,1)} %bitcast.12), calls=%async_computation.1 | async-start | bytes 3276800 | tf_op jit(solution)/shard_map/all_to_all | solution.py:691
  96.3 18.7 %collective-permute-start.43 = (bf16[128,2048]{1,0:T(8,128)(2,1)S(1)}, bf16[128,2048]{1,0:T(8,128)(2,1)S(1)}, u32[]{:S(2)}, u32[]{:S(2)}) collective-permute-start(bf16[128,2048]{1,0:T(8,128)(2,1)S(1)} %pad_maximum_fusion.3), channel_id=1, source_target_pairs={{0,4},{4,0},{8,12},{12,8},{16,20},{20,16},{24,28},{28,24},{32,36},... | collective-permute-start | bytes 1572872 | tf_op jit(solution)/shard_map/ppermute | solution.py:53
  104.0 11.0 %collective-permute-start.42 = (bf16[128,2048]{1,0:T(8,128)(2,1)S(1)}, bf16[128,2048]{1,0:T(8,128)(2,1)S(1)}, u32[]{:S(2)}, u32[]{:S(2)}) collective-permute-start(bf16[128,2048]{1,0:T(8,128)(2,1)S(1)} %pad_maximum_fusion.2), channel_id=1, source_target_pairs={{0,4},{4,0},{8,12},{12,8},{16,20},{20,16},{24,28},{28,24},{32,36},... | collective-permute-start | bytes 1572872 | tf_op jit(solution)/shard_map/ppermute | solution.py:53
  106.8 8.1 %collective-permute-start.40 = (bf16[64,2048]{1,0:T(8,128)(2,1)S(1)}, bf16[64,2048]{1,0:T(8,128)(2,1)S(1)}, u32[]{:S(2)}, u32[]{:S(2)}) collective-permute-start(bf16[64,2048]{1,0:T(8,128)(2,1)S(1)} %pad_maximum_fusion.5.refs_0_), channel_id=1, source_target_pairs={{0,4},{4,0},{8,12},{12,8},{16,20},{20,16},{24,28},{28,24},{32,36},... | collective-permute-start | bytes 786440 | tf_op jit(solution)/shard_map/ppermute | solution.py:53
  107.3 10.7 %collective-permute-start.37 = (bf16[64,2048]{1,0:T(8,128)(2,1)S(1)}, bf16[64,2048]{1,0:T(8,128)(2,1)S(1)}, u32[]{:S(2)}, u32[]{:S(2)}) collective-permute-start(bf16[64,2048]{1,0:T(8,128)(2,1)S(1)} %collective-permute-done.36.refs_3_), channel_id=1, source_target_pairs={{0,32},{4,12},{8,40},{12,4},{16,48},{20,28},{24,56},{28,20},{32,0}... | collective-permute-start | bytes 786440 | tf_op jit(solution)/shard_map/ppermute | solution.py:49
  108.7 9.3 %collective-permute-start.33 = (bf16[64,2048]{1,0:T(8,128)(2,1)S(1)}, bf16[64,2048]{1,0:T(8,128)(2,1)S(1)}, u32[]{:S(2)}, u32[]{:S(2)}) collective-permute-start(bf16[64,2048]{1,0:T(8,128)(2,1)S(1)} %collective-permute-done.32.refs_2_), channel_id=1, source_target_pairs={{0,96},{4,28},{8,104},{12,20},{16,112},{20,12},{24,120},{28,4},{32... | collective-permute-start | bytes 786440 | tf_op jit(solution)/shard_map/ppermute | solution.py:49
  123.6 10.9 %all-to-all-start = ((f32[32,1,128]{2,1,0:T(1,128)}), f32[32,1,128]{2,1,0:T(1,128)S(1)}, u32[]{:S(2)}, u32[]{:S(2)}) async-start(f32[32,1,128]{2,1,0:T(1,128)} %head_stats.5._stats), calls=%async_computation | async-start | bytes 32768 | tf_op jit(solution)/shard_map/all_to_all | solution.py:715
  (40 other events, 480.7 us)

commit v9 on v7

--- a/solution.py
+++ b/solution.py
@@ -682,15 +682,13 @@
     owners = jnp.broadcast_to(owner[:, None], (64, draft_len)).reshape(1, 64 * draft_len)
 
     half = 2 * own_tokens
+    sibling_parts = feed(early[1], [2 * half] * 3, w_both, w_down, mlp_gain)
     late_parts = [
         feed(rows, out_rows, w_both, w_down, own_bc)
         for rows, out_rows in zip(late, ([half] * 2, [2 * half]), strict=True)
     ]
     late_parts = late_sum(late_parts)
-    early_parts = [
-        feed(rows, out_rows, w_both, w_down, late_parts[0])
-        for rows, out_rows in zip(early, ([half] * 6, [2 * half] * 3), strict=True)
-    ]
+    early_parts = [feed(early[0], [half] * 6, w_both, w_down, late_parts[0]), sibling_parts]
     summed = scatter_rows(early_parts, late_parts)
     tip = early_parts[0][0][:8, :128]
     kept, tip = lax.optimization_barrier((kept, tip))

time: 144 us -> 140 us (0.972)
  starting transfers between devices: 63.8 us -> 60 us
  waiting for transfers between devices: 38.7 us -> 35 us
  Pallas kernels: 28.7 us -> 30.6 us
    ppermute x27, waiting for transfers between devices: 26.2 us -> 21.8 us  [hop(): return lax.ppermute(part, 'req', flip_pairs(ring, flip))]
    ppermute x16, starting transfers between devices: 23.5 us -> 20.7 us  [swap_core(): return lax.ppermute(part, 'req', CORE_PAIRS)]
    pallas_call x4, Pallas kernels: 6.26 us -> 8.13 us  [feed(): pl.pallas_call(functools.partial(feed_kernel, len(arrays)), out_shape=[ja...]
    concatenate x4, other arithmetic: 0.14 us -> 1.75 us  [swap_early(): jnp.concatenate(arrays[k:k + 2], axis=0)]
    unnamed x47 -> x59, local copies, waits for them, and re-layouts: 3.45 us -> 4.33 us
  transfers between devices with their start and end apart: 48 -> 48, of which waited for: 22 -> 21; matrix products, arithmetic and copies ran while one was open for 2% -> 3% of each run, Pallas kernels for 12% -> 16%
where the time goes in v9:
time: 140 us; the launch traced here: 139 us
  starting transfers between devices  60 us (43%)
  waiting for transfers between devices  35 us (25%)
  Pallas kernels  30.6 us (22%)
  other arithmetic  7.06 us (5%)
  local copies, waits for them, and re-layouts  5.14 us (4%)
    ppermute x27, starting transfers between devices, hop(): return lax.ppermute(part, 'req', flip_pairs(ring, flip))  25.9 us
    ppermute x27, waiting for transfers between devices, hop(): return lax.ppermute(part, 'req', flip_pairs(ring, flip))  21.8 us
    ppermute x16, starting transfers between devices, swap_core(): return lax.ppermute(part, 'req', CORE_PAIRS)  20.7 us
    pallas_call x3, Pallas kernels, head_stats(): pl.pallas_call(functools.partial(head_kernel, len(rows)), out_shape=jax.S...  8.49 us
    pallas_call x1, Pallas kernels, mixer(): pl.pallas_call(mixer_kernel, out_shape=[*[jax.ShapeDtypeStruct((tokens //...  8.3 us
    pallas_call x4, Pallas kernels, feed(): pl.pallas_call(functools.partial(feed_kernel, len(arrays)), out_shape=[ja...  8.13 us
    ppermute x3, waiting for transfers between devices, shards(): lax.ppermute(part, 'mdl', [(z, z ^ flip) for z in range(SIDE)])  6.1 us
    ppermute x3, starting transfers between devices, shards(): lax.ppermute(part, 'mdl', [(z, z ^ flip) for z in range(SIDE)])  5.85 us
  transfers between devices with their start and end apart: 48, of which 21 were waited for; matrix products, arithmetic and copies ran while one was open for 3% of the time, Pallas kernels for 16%

profile of v9, /device:TPU:1, one launch (start us, length us, event | category | flops | bytes accessed | tf_op | source)
XLA Modules:
  0.0 139.3 jit_solution(6475164982155595673)
XLA Ops:
  0.6 8.3 %mixer.1 = (bf16[32,2048]{1,0:T(8,128)(2,1)}, bf16[32,2048]{1,0:T(8,128)(2,1)}, bf16[32,2048]{1,0:T(8,128)(2,1)}, bf16[32,2048]{1,0:T(8,128)(2,1)}, f32[128,128]...) custom-call(s32[8]{0:T(128)} %refs_0_.3, ...), custom_call_target="tpu_custom_call" | custom-call | flops 3000000000 | bytes 20000000 | tf_op jit(solution)/shard_map/mixer/pallas_call | solution.py:489
  9.0 2.5 %collective-permute-start = (bf16[32,2048]{1,0:T(8,128)(2,1)}, bf16[32,2048]{1,0:T(8,128)(2,1)S(1)}, u32[]{:S(2)}, u32[]{:S(2)}) collective-permute-start(bf16[32,2048]{1,0:T(8,128)(2,1)} %get-tuple-element.41), channel_id=1, source_target_pairs={{0,1},{1,0},{2,3},{3,2},{4,5},{5,4},{6,7},{7,6},{8,9},{9,8},{10,11... | collective-permute-start | bytes 393224 | tf_op jit(solution)/shard_map/ppermute | solution.py:659
  11.6 2.2 %collective-permute-start.1 = (bf16[32,2048]{1,0:T(8,128)(2,1)}, bf16[32,2048]{1,0:T(8,128)(2,1)S(1)}, u32[]{:S(2)}, u32[]{:S(2)}) collective-permute-start(bf16[32,2048]{1,0:T(8,128)(2,1)} %get-tuple-element.42), channel_id=1, source_target_pairs={{0,3},{1,2},{2,1},{3,0},{4,7},{5,6},{6,5},{7,4},{8,11},{9,10},{10,... | collective-permute-start | bytes 393224 | tf_op jit(solution)/shard_map/ppermute | solution.py:659
  15.0 4.3 %collective-permute-done.1 = bf16[32,2048]{1,0:T(8,128)(2,1)S(1)} collective-permute-done((bf16[32,2048]{1,0:T(8,128)(2,1)}, bf16[32,2048]{1,0:T(8,128)(2,1)S(1)}, u32[]{:S(2)}, u32[]{:S(2)}) %collective-permute-start.1) | collective-permute-done | bytes 131104 | tf_op jit(solution)/shard_map/ppermute | solution.py:659
  19.2 1.8 %collective-permute-done.2 = bf16[32,2048]{1,0:T(8,128)(2,1)S(1)} collective-permute-done((bf16[32,2048]{1,0:T(8,128)(2,1)}, bf16[32,2048]{1,0:T(8,128)(2,1)S(1)}, u32[]{:S(2)}, u32[]{:S(2)}) %collective-permute-start.2) | collective-permute-done | bytes 131104 | tf_op jit(solution)/shard_map/ppermute | solution.py:659
  22.3 2.8 %collective-permute-start.6 = (bf16[32,2048]{1,0:T(8,128)(2,1)S(1)}, bf16[32,2048]{1,0:T(8,128)(2,1)S(1)}, u32[]{:S(2)}, u32[]{:S(2)}) collective-permute-start(bf16[32,2048]{1,0:T(8,128)(2,1)S(1)} %fusion.5), channel_id=1, source_target_pairs={{0,24},{4,100},{8,16},{12,108},{16,8},{20,116},{24,0},{28,124},{32... | collective-permute-start | bytes 393224 | tf_op jit(solution)/shard_map/ppermute | solution.py:49
  25.8 2.6 %collective-permute-done.6 = bf16[32,2048]{1,0:T(8,128)(2,1)S(1)} collective-permute-done((bf16[32,2048]{1,0:T(8,128)(2,1)S(1)}, bf16[32,2048]{1,0:T(8,128)(2,1)S(1)}, u32[]{:S(2)}, u32[]{:S(2)}) %collective-permute-start.6) | collective-permute-done | bytes 131104 | tf_op jit(solution)/shard_map/ppermute | solution.py:49
  28.5 2.0 %collective-permute-done.7 = bf16[32,2048]{1,0:T(8,128)(2,1)S(1)} collective-permute-done((bf16[32,2048]{1,0:T(8,128)(2,1)S(1)}, bf16[32,2048]{1,0:T(8,128)(2,1)S(1)}, u32[]{:S(2)}, u32[]{:S(2)}) %collective-permute-start.7) | collective-permute-done | bytes 131104 | tf_op jit(solution)/shard_map/ppermute | solution.py:49
  30.5 2.6 %collective-permute-start.8 = (bf16[64,2048]{1,0:T(8,128)(2,1)S(1)}, bf16[64,2048]{1,0:T(8,128)(2,1)S(1)}, u32[]{:S(2)}, u32[]{:S(2)}) collective-permute-start(bf16[64,2048]{1,0:T(8,128)(2,1)S(1)} %constant_dynamic-update-slice_fusion.2.refs_1_), channel_id=1, source_target_pairs={{0,96},{4,28},{8,104},{12,20},{16,112},{20,12},{24,120},{28,4},{32... | collective-permute-start | bytes 786440 | tf_op jit(solution)/shard_map/ppermute | solution.py:49
  35.0 2.0 %collective-permute-done.8.refs_3_ = bf16[64,2048]{1,0:T(8,128)(2,1)S(1)} collective-permute-done((bf16[64,2048]{1,0:T(8,128)(2,1)S(1)}, bf16[64,2048]{1,0:T(8,128)(2,1)S(1)}, u32[]{:S(2)}, u32[]{:S(2)}) %collective-permute-start.8) | collective-permute-done | bytes 262176 | tf_op jit(solution)/shard_map/ppermute | solution.py:49
  37.0 1.7 %collective-permute-done.4.refs_2_ = bf16[64,2048]{1,0:T(8,128)(2,1)S(1)} collective-permute-done((bf16[64,2048]{1,0:T(8,128)(2,1)S(1)}, bf16[64,2048]{1,0:T(8,128)(2,1)S(1)}, u32[]{:S(2)}, u32[]{:S(2)}) %collective-permute-start.4) | collective-permute-done | bytes 262176 | tf_op jit(solution)/shard_map/ppermute | solution.py:49
  39.8 3.6 %keeper.1 = (bf16[8,400,256]{2,1,0:T(8,128)(2,1)}, bf16[16,512]{1,0:T(8,128)(2,1)S(1)}) custom-call(s32[8]{0:T(128)S(1)} %copy-done.6, s32[8]{0:T(128)S(1)} %copy-done.7, f32[128,128]{1,0:T(8,128)S(1)} %copy-done.17, f32[128,384]{1,0:T(8,128)S(1)} %copy-done.14, bf16[128,256]{1,0:T(8,128)(2,1)S(1)} %copy-done.18, bf16[128,384]{1,0:T(8,128)(2,1)S(1)} %copy-done.16, ...), custom_call_target="tpu_custom_call" | custom-call | flops 2000000000 | bytes 5000000 | tf_op jit(solution)/shard_map/keeper/pallas_call | solution.py:220
  44.3 3.9 %collective-permute-start.17 = (bf16[128,2048]{1,0:T(8,128)(2,1)}, bf16[128,2048]{1,0:T(8,128)(2,1)}, u32[]{:S(2)}, u32[]{:S(2)}) collective-permute-start(bf16[128,2048]{1,0:T(8,128)(2,1)} %pad_maximum_fusion), channel_id=1, source_target_pairs={{0,4},{4,0},{8,12},{12,8},{16,20},{20,16},{24,28},{28,24},{32,36},... | collective-permute-start | bytes 1572872 | tf_op jit(solution)/shard_map/ppermute | solution.py:53
  48.2 1.9 %collective-permute-start.10 = (bf16[64,2048]{1,0:T(8,128)(2,1)S(1)}, bf16[64,2048]{1,0:T(8,128)(2,1)S(1)}, u32[]{:S(2)}, u32[]{:S(2)}) collective-permute-start(bf16[64,2048]{1,0:T(8,128)(2,1)S(1)} %collective-permute-done.5.refs_0_), channel_id=1, source_target_pairs={{0,4},{4,0},{8,12},{12,8},{16,20},{20,16},{24,28},{28,24},{32,36},... | collective-permute-start | bytes 786440 | tf_op jit(solution)/shard_map/ppermute | solution.py:53
  56.9 3.9 %feed.7 = (bf16[128,2048]{1,0:T(8,128)(2,1)}, bf16[128,2048]{1,0:T(8,128)(2,1)S(1)}, bf16[128,2048]{1,0:T(8,128)(2,1)S(1)}) custom-call(bf16[2048,256]{1,0:T(8,128)(2,1)S(1)} %constant_dynamic-update-slice_fusion.both_ref, bf16[128,2048]{1,0:T(8,128)(2,1)S(1)} %copy-done.8, bf16[2048]{0:T(1024)(128)(2,1)S(1)} %copy-done.5, ...), custom_call_target="tpu_custom_call" | custom-call | flops 2415919104 | bytes 4718592 | tf_op jit(solution)/shard_map/feed/pallas_call | solution.py:544
  63.6 1.8 %feed.6 = (bf16[64,2048]{1,0:T(8,128)(2,1)S(1)}, bf16[64,2048]{1,0:T(8,128)(2,1)S(1)}, bf16[64,2048]{1,0:T(8,128)(2,1)S(1)}, bf16[64,2048]{1,0:T(8,128)(2,1)S(1)...) custom-call(bf16[2048,256]{1,0:T(8,128)(2,1)S(1)} %constant_dynamic-update-slice_fusion.both_ref, ...), custom_call_target="tpu_custom_call" | custom-call | flops 2415919104 | bytes 4718592 | tf_op jit(solution)/shard_map/feed/pallas_call | solution.py:544
  65.6 1.9 %collective-permute-start.21 = (bf16[64,2048]{1,0:T(8,128)(2,1)S(1)}, bf16[64,2048]{1,0:T(8,128)(2,1)S(1)}, u32[]{:S(2)}, u32[]{:S(2)}) collective-permute-start(bf16[64,2048]{1,0:T(8,128)(2,1)S(1)} %get-tuple-element.84), channel_id=1, source_target_pairs={{0,96},{4,28},{8,104},{12,20},{16,112},{20,12},{24,120},{28,4},{32... | collective-permute-start | bytes 786440 | tf_op jit(solution)/shard_map/ppermute | solution.py:49
  73.0 2.8 %collective-permute-done.24 = bf16[64,2048]{1,0:T(8,128)(2,1)S(1)} collective-permute-done((bf16[64,2048]{1,0:T(8,128)(2,1)S(1)}, bf16[64,2048]{1,0:T(8,128)(2,1)S(1)}, u32[]{:S(2)}, u32[]{:S(2)}) %collective-permute-start.24) | collective-permute-done | bytes 262176 | tf_op jit(solution)/shard_map/ppermute | solution.py:49
  79.3 2.2 %collective-permute-start.25 = (bf16[32,2048]{1,0:T(8,128)(2,1)S(1)}, bf16[32,2048]{1,0:T(8,128)(2,1)S(1)}, u32[]{:S(2)}, u32[]{:S(2)}) collective-permute-start(bf16[32,2048]{1,0:T(8,128)(2,1)S(1)} %slice.117), channel_id=1, source_target_pairs={{0,8},{4,36},{8,0},{12,44},{16,24},{20,52},{24,16},{28,60},{32,40}... | collective-permute-start | bytes 393224 | tf_op jit(solution)/shard_map/ppermute | solution.py:49
  82.1 2.8 %collective-permute-done.29 = bf16[32,2048]{1,0:T(8,128)(2,1)S(1)} collective-permute-done((bf16[32,2048]{1,0:T(8,128)(2,1)S(1)}, bf16[32,2048]{1,0:T(8,128)(2,1)S(1)}, u32[]{:S(2)}, u32[]{:S(2)}) %collective-permute-start.29) | collective-permute-done | bytes 131104 | tf_op jit(solution)/shard_map/ppermute | solution.py:49
  89.1 3.2 %collective-permute-done.34 = bf16[32,2048]{1,0:T(8,128)(2,1)S(1)} collective-permute-done((bf16[32,2048]{1,0:T(8,128)(2,1)S(1)}, bf16[32,2048]{1,0:T(8,128)(2,1)S(1)}, u32[]{:S(2)}, u32[]{:S(2)}) %collective-permute-start.34) | collective-permute-done | bytes 131104 | tf_op jit(solution)/shard_map/ppermute | solution.py:49
  92.9 1.8 %collective-permute-start.38 = (bf16[64,2048]{1,0:T(8,128)(2,1)S(1)}, bf16[64,2048]{1,0:T(8,128)(2,1)S(1)}, u32[]{:S(2)}, u32[]{:S(2)}) collective-permute-start(bf16[64,2048]{1,0:T(8,128)(2,1)S(1)} %pad_maximum_fusion.5.refs_0_), channel_id=1, source_target_pairs={{0,96},{4,28},{8,104},{12,20},{16,112},{20,12},{24,120},{28,4},{32... | collective-permute-start | bytes 786440 | tf_op jit(solution)/shard_map/ppermute | solution.py:49
  95.7 3.6 %all-to-all-start.1 = ((bf16[4,2,400,256]{3,2,1,0:T(8,128)(2,1)}), bf16[4,2,400,256]{3,2,1,0:T(8,128)(2,1)S(1)}, u32[]{:S(2)}, u32[]{:S(2)}) async-start(bf16[4,2,400,256]{3,2,1,0:T(8,128)(2,1)} %bitcast.12), calls=%async_computation.1 | async-start | bytes 3276800 | tf_op jit(solution)/shard_map/all_to_all | solution.py:695
  99.7 7.7 %collective-permute-start.43 = (bf16[128,2048]{1,0:T(8,128)(2,1)S(1)}, bf16[128,2048]{1,0:T(8,128)(2,1)S(1)}, u32[]{:S(2)}, u32[]{:S(2)}) collective-permute-start(bf16[128,2048]{1,0:T(8,128)(2,1)S(1)} %pad_maximum_fusion.3), channel_id=1, source_target_pairs={{0,4},{4,0},{8,12},{12,8},{16,20},{20,16},{24,28},{28,24},{32,36},... | collective-permute-start | bytes 1572872 | tf_op jit(solution)/shard_map/ppermute | solution.py:53
  107.4 3.0 %collective-permute-start.42 = (bf16[128,2048]{1,0:T(8,128)(2,1)S(1)}, bf16[128,2048]{1,0:T(8,128)(2,1)S(1)}, u32[]{:S(2)}, u32[]{:S(2)}) collective-permute-start(bf16[128,2048]{1,0:T(8,128)(2,1)S(1)} %pad_maximum_fusion.2), channel_id=1, source_target_pairs={{0,4},{4,0},{8,12},{12,8},{16,20},{20,16},{24,28},{28,24},{32,36},... | collective-permute-start | bytes 1572872 | tf_op jit(solution)/shard_map/ppermute | solution.py:53
  113.4 2.2 %copy-done = bf16[1024,2048]{1,0:T(8,128)(2,1)S(1)} copy-done((bf16[1024,2048]{1,0:T(8,128)(2,1)S(1)}, bf16[1024,2048]{1,0:T(8,128)(2,1)}, u32[]{:S(2)}) %copy-start) | copy-done | bytes 4194328
  115.6 3.0 %head_stats.3.refs_5_ = f32[32,1,128]{2,1,0:T(1,128)S(1)} custom-call(s32[1,384]{1,0:T(1,128)S(1)} %get-tuple-element.98.targets_ref, s32[1,384]{1,0:T(1,128)S(1)} %get-tuple-element.95.owners_ref, bf16[64,2048]{1,0:T(8,128)(2,1)S(1)} %pad_maximum_fusion.5.refs_0_, bf16[64,2048]{1,0:T(8,128)(2,1)S(1)} %constant_dynamic-update-slice_fusion.4.refs_1_, ...), custom_call_target="tpu_custom_call" | custom-call | flops 1610612736 | bytes 5767168 | tf_op jit(solution)/shard_map/head_stats/pallas_call | solution.py:598
  118.6 3.0 %head_stats.4.refs_6_ = f32[32,1,128]{2,1,0:T(1,128)S(1)} custom-call(s32[1,384]{1,0:T(1,128)S(1)} %get-tuple-element.99.targets_ref, s32[1,384]{1,0:T(1,128)S(1)} %get-tuple-element.94.owners_ref, bf16[64,2048]{1,0:T(8,128)(2,1)S(1)} %collective-permute-done.40.refs_0_, bf16[64,2048]{1,0:T(8,128)(2,1)S(1)} %collective-permute-done.41.refs_1_, ...), custom_call_target="tpu_custom_call" | custom-call | flops 1610612736 | bytes 5767168 | tf_op jit(solution)/shard_map/head_stats/pallas_call | solution.py:598
  124.8 2.5 %head_stats.5._stats = f32[32,1,128]{2,1,0:T(1,128)} custom-call(s32[1,256]{1,0:T(1,128)S(1)} %slice.102.targets_ref, s32[1,256]{1,0:T(1,128)S(1)} %slice.103.owners_ref, bf16[64,2048]{1,0:T(8,128)(2,1)S(1)} %collective-permute-done.33.refs_0_, bf16[64,2048]{1,0:T(8,128)(2,1)S(1)} %collective-permute-done.37.refs_1_, ...), custom_call_target="tpu_custom_call" | custom-call | flops 1073741824 | bytes 5242880 | tf_op jit(solution)/shard_map/head_stats/pallas_call | solution.py:598
  127.3 4.0 %all-to-all-start = ((f32[32,1,128]{2,1,0:T(1,128)}), f32[32,1,128]{2,1,0:T(1,128)S(1)}, u32[]{:S(2)}, u32[]{:S(2)}) async-start(f32[32,1,128]{2,1,0:T(1,128)} %head_stats.5._stats), calls=%async_computation | async-start | bytes 32768 | tf_op jit(solution)/shard_map/all_to_all | solution.py:719
  131.3 2.1 %unpack.1 = (f32[2,1536,256]{2,1,0:T(8,128)}, bf16[3,2,2048]{2,1,0:T(2,128)(2,1)}) custom-call(bf16[4,2,400,256]{3,2,1,0:T(8,128)(2,1)S(1)} %all-to-all-done.1.kept_hbm, bf16[16,512]{1,0:T(8,128)(2,1)S(1)} %get-tuple-element.50._token.bc_ref, f32[32,1,128]{2,1,0:T(1,128)} %head_stats.5._stats, bf16[8,128]{1,0:T(8,128)(2,1)S(1)} %slice.111._tip), custom_call_target="tpu_custom_call" | custom-call | flops 1000000 | bytes 20000000 | tf_op jit(solution)/shard_map/unpack/pallas_call | solution.py:267
  133.4 4.9 %all-to-all-done = f32[32,1,128]{2,1,0:T(1,128)S(1)} async-done(((f32[32,1,128]{2,1,0:T(1,128)}), f32[32,1,128]{2,1,0:T(1,128)S(1)}, u32[]{:S(2)}, u32[]{:S(2)}) %all-to-all-start) | async-done | bytes 16416 | tf_op jit(solution)/shard_map/all_to_all | solution.py:719
  (178 shorter events, 39.5 us)
Async XLA Ops:
  9.0 6.0 %collective-permute-start = (bf16[32,2048]{1,0:T(8,128)(2,1)}, bf16[32,2048]{1,0:T(8,128)(2,1)S(1)}, u32[]{:S(2)}, u32[]{:S(2)}) collective-permute-start(bf16[32,2048]{1,0:T(8,128)(2,1)} %get-tuple-element.41), channel_id=1, source_target_pairs={{0,1},{1,0},{2,3},{3,2},{4,5},{5,4},{6,7},{7,6},{8,9},{9,8},{10,11... | collective-permute-start | bytes 393224 | tf_op jit(solution)/shard_map/ppermute | solution.py:659
  11.6 7.7 %collective-permute-start.1 = (bf16[32,2048]{1,0:T(8,128)(2,1)}, bf16[32,2048]{1,0:T(8,128)(2,1)S(1)}, u32[]{:S(2)}, u32[]{:S(2)}) collective-permute-start(bf16[32,2048]{1,0:T(8,128)(2,1)} %get-tuple-element.42), channel_id=1, source_target_pairs={{0,3},{1,2},{2,1},{3,0},{4,7},{5,6},{6,5},{7,4},{8,11},{9,10},{10,... | collective-permute-start | bytes 393224 | tf_op jit(solution)/shard_map/ppermute | solution.py:659
  13.8 7.2 %collective-permute-start.2 = (bf16[32,2048]{1,0:T(8,128)(2,1)}, bf16[32,2048]{1,0:T(8,128)(2,1)S(1)}, u32[]{:S(2)}, u32[]{:S(2)}) collective-permute-start(bf16[32,2048]{1,0:T(8,128)(2,1)} %get-tuple-element.43), channel_id=1, source_target_pairs={{0,2},{1,3},{2,0},{3,1},{4,6},{5,7},{6,4},{7,5},{8,10},{9,11},{10,... | collective-permute-start | bytes 393224 | tf_op jit(solution)/shard_map/ppermute | solution.py:659
  22.3 6.1 %collective-permute-start.6 = (bf16[32,2048]{1,0:T(8,128)(2,1)S(1)}, bf16[32,2048]{1,0:T(8,128)(2,1)S(1)}, u32[]{:S(2)}, u32[]{:S(2)}) collective-permute-start(bf16[32,2048]{1,0:T(8,128)(2,1)S(1)} %fusion.5), channel_id=1, source_target_pairs={{0,24},{4,100},{8,16},{12,108},{16,8},{20,116},{24,0},{28,124},{32... | collective-permute-start | bytes 393224 | tf_op jit(solution)/shard_map/ppermute | solution.py:49
  25.5 7.5 %collective-permute-start.3 = (bf16[32,2048]{1,0:T(8,128)(2,1)S(1)}, bf16[32,2048]{1,0:T(8,128)(2,1)S(1)}, u32[]{:S(2)}, u32[]{:S(2)}) collective-permute-start(bf16[32,2048]{1,0:T(8,128)(2,1)S(1)} %fusion.5), channel_id=1, source_target_pairs={{0,8},{4,36},{8,0},{12,44},{16,24},{20,52},{24,16},{28,60},{32,40}... | collective-permute-start | bytes 393224 | tf_op jit(solution)/shard_map/ppermute | solution.py:49
  30.5 6.5 %collective-permute-start.8 = (bf16[64,2048]{1,0:T(8,128)(2,1)S(1)}, bf16[64,2048]{1,0:T(8,128)(2,1)S(1)}, u32[]{:S(2)}, u32[]{:S(2)}) collective-permute-start(bf16[64,2048]{1,0:T(8,128)(2,1)S(1)} %constant_dynamic-update-slice_fusion.2.refs_1_), channel_id=1, source_target_pairs={{0,96},{4,28},{8,104},{12,20},{16,112},{20,12},{24,120},{28,4},{32... | collective-permute-start | bytes 786440 | tf_op jit(solution)/shard_map/ppermute | solution.py:49
  33.3 16.9 %collective-permute-start.14 = (bf16[64,2048]{1,0:T(8,128)(2,1)S(1)}, bf16[64,2048]{1,0:T(8,128)(2,1)S(1)}, u32[]{:S(2)}, u32[]{:S(2)}) collective-permute-start(bf16[64,2048]{1,0:T(8,128)(2,1)S(1)} %constant_dynamic-update-slice_fusion.2.refs_1_), channel_id=1, source_target_pairs={{0,32},{4,12},{8,40},{12,4},{16,48},{20,28},{24,56},{28,20},{32,0}... | collective-permute-start | bytes 786440 | tf_op jit(solution)/shard_map/ppermute | solution.py:49
  34.8 15.4 %collective-permute-start.13 = (bf16[64,2048]{1,0:T(8,128)(2,1)S(1)}, bf16[64,2048]{1,0:T(8,128)(2,1)S(1)}, u32[]{:S(2)}, u32[]{:S(2)}) collective-permute-start(bf16[64,2048]{1,0:T(8,128)(2,1)S(1)} %pad_maximum_fusion.4.refs_0_), channel_id=1, source_target_pairs={{0,96},{4,28},{8,104},{12,20},{16,112},{20,12},{24,120},{28,4},{32... | collective-permute-start | bytes 786440 | tf_op jit(solution)/shard_map/ppermute | solution.py:49
  37.0 11.2 %collective-permute-start.9 = (bf16[64,2048]{1,0:T(8,128)(2,1)S(1)}, bf16[64,2048]{1,0:T(8,128)(2,1)S(1)}, u32[]{:S(2)}, u32[]{:S(2)}) collective-permute-start(bf16[64,2048]{1,0:T(8,128)(2,1)S(1)} %collective-permute-done.8.refs_3_), channel_id=1, source_target_pairs={{0,32},{4,12},{8,40},{12,4},{16,48},{20,28},{24,56},{28,20},{32,0}... | collective-permute-start | bytes 786440 | tf_op jit(solution)/shard_map/ppermute | solution.py:49
  38.6 9.6 %collective-permute-start.5 = (bf16[64,2048]{1,0:T(8,128)(2,1)S(1)}, bf16[64,2048]{1,0:T(8,128)(2,1)S(1)}, u32[]{:S(2)}, u32[]{:S(2)}) collective-permute-start(bf16[64,2048]{1,0:T(8,128)(2,1)S(1)} %collective-permute-done.4.refs_2_), channel_id=1, source_target_pairs={{0,96},{4,28},{8,104},{12,20},{16,112},{20,12},{24,120},{28,4},{32... | collective-permute-start | bytes 786440 | tf_op jit(solution)/shard_map/ppermute | solution.py:49
  44.3 12.6 %collective-permute-start.17 = (bf16[128,2048]{1,0:T(8,128)(2,1)}, bf16[128,2048]{1,0:T(8,128)(2,1)}, u32[]{:S(2)}, u32[]{:S(2)}) collective-permute-start(bf16[128,2048]{1,0:T(8,128)(2,1)} %pad_maximum_fusion), channel_id=1, source_target_pairs={{0,4},{4,0},{8,12},{12,8},{16,20},{20,16},{24,28},{28,24},{32,36},... | collective-permute-start | bytes 1572872 | tf_op jit(solution)/shard_map/ppermute | solution.py:53
  53.3 8.2 %collective-permute-start.12 = (bf16[128,2048]{1,0:T(8,128)(2,1)}, bf16[128,2048]{1,0:T(8,128)(2,1)}, u32[]{:S(2)}, u32[]{:S(2)}) collective-permute-start(bf16[128,2048]{1,0:T(8,128)(2,1)} %feed.5), channel_id=1, source_target_pairs={{0,4},{4,0},{8,12},{12,8},{16,20},{20,16},{24,28},{28,24},{32,36},... | collective-permute-start | bytes 1572872 | tf_op jit(solution)/shard_map/ppermute | solution.py:53
  61.0 6.5 %collective-permute-start.22 = (bf16[128,2048]{1,0:T(8,128)(2,1)S(1)}, bf16[128,2048]{1,0:T(8,128)(2,1)S(1)}, u32[]{:S(2)}, u32[]{:S(2)}) collective-permute-start(bf16[128,2048]{1,0:T(8,128)(2,1)S(1)} %get-tuple-element.59), channel_id=1, source_target_pairs={{0,4},{4,0},{8,12},{12,8},{16,20},{20,16},{24,28},{28,24},{32,36},... | collective-permute-start | bytes 1572872 | tf_op jit(solution)/shard_map/ppermute | solution.py:53
  61.4 10.1 %collective-permute-start.19 = (bf16[128,2048]{1,0:T(8,128)(2,1)}, bf16[128,2048]{1,0:T(8,128)(2,1)}, u32[]{:S(2)}, u32[]{:S(2)}) collective-permute-start(bf16[128,2048]{1,0:T(8,128)(2,1)} %get-tuple-element.55), channel_id=1, source_target_pairs={{0,4},{4,0},{8,12},{12,8},{16,20},{20,16},{24,28},{28,24},{32,36},... | collective-permute-start | bytes 1572872 | tf_op jit(solution)/shard_map/ppermute | solution.py:53
  62.7 6.8 %collective-permute-start.23 = (bf16[64,2048]{1,0:T(8,128)(2,1)S(1)}, bf16[64,2048]{1,0:T(8,128)(2,1)S(1)}, u32[]{:S(2)}, u32[]{:S(2)}) collective-permute-start(bf16[64,2048]{1,0:T(8,128)(2,1)S(1)} %get-tuple-element.88._token), channel_id=1, source_target_pairs={{0,96},{4,28},{8,104},{12,20},{16,112},{20,12},{24,120},{28,4},{32... | collective-permute-start | bytes 786440 | tf_op jit(solution)/shard_map/ppermute | solution.py:49
  65.6 6.8 %collective-permute-start.21 = (bf16[64,2048]{1,0:T(8,128)(2,1)S(1)}, bf16[64,2048]{1,0:T(8,128)(2,1)S(1)}, u32[]{:S(2)}, u32[]{:S(2)}) collective-permute-start(bf16[64,2048]{1,0:T(8,128)(2,1)S(1)} %get-tuple-element.84), channel_id=1, source_target_pairs={{0,96},{4,28},{8,104},{12,20},{16,112},{20,12},{24,120},{28,4},{32... | collective-permute-start | bytes 786440 | tf_op jit(solution)/shard_map/ppermute | solution.py:49
  69.8 6.1 %collective-permute-start.24 = (bf16[64,2048]{1,0:T(8,128)(2,1)S(1)}, bf16[64,2048]{1,0:T(8,128)(2,1)S(1)}, u32[]{:S(2)}, u32[]{:S(2)}) collective-permute-start(bf16[64,2048]{1,0:T(8,128)(2,1)S(1)} %get-tuple-element.86), channel_id=1, source_target_pairs={{0,32},{4,12},{8,40},{12,4},{16,48},{20,28},{24,56},{28,20},{32,0}... | collective-permute-start | bytes 786440 | tf_op jit(solution)/shard_map/ppermute | solution.py:49
  69.9 6.8 %collective-permute-start.28 = (bf16[64,2048]{1,0:T(8,128)(2,1)S(1)}, bf16[64,2048]{1,0:T(8,128)(2,1)S(1)}, u32[]{:S(2)}, u32[]{:S(2)}) collective-permute-start(bf16[64,2048]{1,0:T(8,128)(2,1)S(1)} %get-tuple-element.87), channel_id=1, source_target_pairs={{0,96},{4,28},{8,104},{12,20},{16,112},{20,12},{24,120},{28,4},{32... | collective-permute-start | bytes 786440 | tf_op jit(solution)/shard_map/ppermute | solution.py:49
  78.1 6.8 %collective-permute-start.29 = (bf16[32,2048]{1,0:T(8,128)(2,1)S(1)}, bf16[32,2048]{1,0:T(8,128)(2,1)S(1)}, u32[]{:S(2)}, u32[]{:S(2)}) collective-permute-start(bf16[32,2048]{1,0:T(8,128)(2,1)S(1)} %get-tuple-element.90), channel_id=1, source_target_pairs={{0,24},{4,100},{8,16},{12,108},{16,8},{20,116},{24,0},{28,124},{32... | collective-permute-start | bytes 393224 | tf_op jit(solution)/shard_map/ppermute | solution.py:49
  79.3 6.1 %collective-permute-start.25 = (bf16[32,2048]{1,0:T(8,128)(2,1)S(1)}, bf16[32,2048]{1,0:T(8,128)(2,1)S(1)}, u32[]{:S(2)}, u32[]{:S(2)}) collective-permute-start(bf16[32,2048]{1,0:T(8,128)(2,1)S(1)} %slice.117), channel_id=1, source_target_pairs={{0,8},{4,36},{8,0},{12,44},{16,24},{20,52},{24,16},{28,60},{32,40}... | collective-permute-start | bytes 393224 | tf_op jit(solution)/shard_map/ppermute | solution.py:49
  85.8 6.5 %collective-permute-start.34 = (bf16[32,2048]{1,0:T(8,128)(2,1)S(1)}, bf16[32,2048]{1,0:T(8,128)(2,1)S(1)}, u32[]{:S(2)}, u32[]{:S(2)}) collective-permute-start(bf16[32,2048]{1,0:T(8,128)(2,1)S(1)} %fusion.2), channel_id=1, source_target_pairs={{0,24},{4,100},{8,16},{12,108},{16,8},{20,116},{24,0},{28,124},{32... | collective-permute-start | bytes 393224 | tf_op jit(solution)/shard_map/ppermute | solution.py:49
  92.3 7.3 %collective-permute-start.39 = (bf16[64,2048]{1,0:T(8,128)(2,1)S(1)}, bf16[64,2048]{1,0:T(8,128)(2,1)S(1)}, u32[]{:S(2)}, u32[]{:S(2)}) collective-permute-start(bf16[64,2048]{1,0:T(8,128)(2,1)S(1)} %constant_dynamic-update-slice_fusion.4.refs_1_), channel_id=1, source_target_pairs={{0,32},{4,12},{8,40},{12,4},{16,48},{20,28},{24,56},{28,20},{32,0}... | collective-permute-start | bytes 786440 | tf_op jit(solution)/shard_map/ppermute | solution.py:49
  92.9 6.8 %collective-permute-start.38 = (bf16[64,2048]{1,0:T(8,128)(2,1)S(1)}, bf16[64,2048]{1,0:T(8,128)(2,1)S(1)}, u32[]{:S(2)}, u32[]{:S(2)}) collective-permute-start(bf16[64,2048]{1,0:T(8,128)(2,1)S(1)} %pad_maximum_fusion.5.refs_0_), channel_id=1, source_target_pairs={{0,96},{4,28},{8,104},{12,20},{16,112},{20,12},{24,120},{28,4},{32... | collective-permute-start | bytes 786440 | tf_op jit(solution)/shard_map/ppermute | solution.py:49
  94.7 12.7 %collective-permute-start.36 = (bf16[64,2048]{1,0:T(8,128)(2,1)S(1)}, bf16[64,2048]{1,0:T(8,128)(2,1)S(1)}, u32[]{:S(2)}, u32[]{:S(2)}) collective-permute-start(bf16[64,2048]{1,0:T(8,128)(2,1)S(1)} %constant_dynamic-update-slice_fusion.4.refs_1_), channel_id=1, source_target_pairs={{0,96},{4,28},{8,104},{12,20},{16,112},{20,12},{24,120},{28,4},{32... | collective-permute-start | bytes 786440 | tf_op jit(solution)/shard_map/ppermute | solution.py:49
  95.6 11.7 %collective-permute-start.32 = (bf16[64,2048]{1,0:T(8,128)(2,1)S(1)}, bf16[64,2048]{1,0:T(8,128)(2,1)S(1)}, u32[]{:S(2)}, u32[]{:S(2)}) collective-permute-start(bf16[64,2048]{1,0:T(8,128)(2,1)S(1)} %pad_maximum_fusion.5.refs_0_), channel_id=1, source_target_pairs={{0,32},{4,12},{8,40},{12,4},{16,48},{20,28},{24,56},{28,20},{32,0}... | collective-permute-start | bytes 786440 | tf_op jit(solution)/shard_map/ppermute | solution.py:49
  95.7 31.6 %all-to-all-start.1 = ((bf16[4,2,400,256]{3,2,1,0:T(8,128)(2,1)}), bf16[4,2,400,256]{3,2,1,0:T(8,128)(2,1)S(1)}, u32[]{:S(2)}, u32[]{:S(2)}) async-start(bf16[4,2,400,256]{3,2,1,0:T(8,128)(2,1)} %bitcast.12), calls=%async_computation.1 | async-start | bytes 3276800 | tf_op jit(solution)/shard_map/all_to_all | solution.py:695
  99.7 18.9 %collective-permute-start.43 = (bf16[128,2048]{1,0:T(8,128)(2,1)S(1)}, bf16[128,2048]{1,0:T(8,128)(2,1)S(1)}, u32[]{:S(2)}, u32[]{:S(2)}) collective-permute-start(bf16[128,2048]{1,0:T(8,128)(2,1)S(1)} %pad_maximum_fusion.3), channel_id=1, source_target_pairs={{0,4},{4,0},{8,12},{12,8},{16,20},{20,16},{24,28},{28,24},{32,36},... | collective-permute-start | bytes 1572872 | tf_op jit(solution)/shard_map/ppermute | solution.py:53
  107.4 11.2 %collective-permute-start.42 = (bf16[128,2048]{1,0:T(8,128)(2,1)S(1)}, bf16[128,2048]{1,0:T(8,128)(2,1)S(1)}, u32[]{:S(2)}, u32[]{:S(2)}) collective-permute-start(bf16[128,2048]{1,0:T(8,128)(2,1)S(1)} %pad_maximum_fusion.2), channel_id=1, source_target_pairs={{0,4},{4,0},{8,12},{12,8},{16,20},{20,16},{24,28},{28,24},{32,36},... | collective-permute-start | bytes 1572872 | tf_op jit(solution)/shard_map/ppermute | solution.py:53
  110.5 8.1 %collective-permute-start.40 = (bf16[64,2048]{1,0:T(8,128)(2,1)S(1)}, bf16[64,2048]{1,0:T(8,128)(2,1)S(1)}, u32[]{:S(2)}, u32[]{:S(2)}) collective-permute-start(bf16[64,2048]{1,0:T(8,128)(2,1)S(1)} %pad_maximum_fusion.5.refs_0_), channel_id=1, source_target_pairs={{0,4},{4,0},{8,12},{12,8},{16,20},{20,16},{24,28},{28,24},{32,36},... | collective-permute-start | bytes 786440 | tf_op jit(solution)/shard_map/ppermute | solution.py:53
  110.9 10.7 %collective-permute-start.37 = (bf16[64,2048]{1,0:T(8,128)(2,1)S(1)}, bf16[64,2048]{1,0:T(8,128)(2,1)S(1)}, u32[]{:S(2)}, u32[]{:S(2)}) collective-permute-start(bf16[64,2048]{1,0:T(8,128)(2,1)S(1)} %collective-permute-done.36.refs_3_), channel_id=1, source_target_pairs={{0,32},{4,12},{8,40},{12,4},{16,48},{20,28},{24,56},{28,20},{32,0}... | collective-permute-start | bytes 786440 | tf_op jit(solution)/shard_map/ppermute | solution.py:49
  112.3 9.3 %collective-permute-start.33 = (bf16[64,2048]{1,0:T(8,128)(2,1)S(1)}, bf16[64,2048]{1,0:T(8,128)(2,1)S(1)}, u32[]{:S(2)}, u32[]{:S(2)}) collective-permute-start(bf16[64,2048]{1,0:T(8,128)(2,1)S(1)} %collective-permute-done.32.refs_2_), channel_id=1, source_target_pairs={{0,96},{4,28},{8,104},{12,20},{16,112},{20,12},{24,120},{28,4},{32... | collective-permute-start | bytes 786440 | tf_op jit(solution)/shard_map/ppermute | solution.py:49
  127.3 10.9 %all-to-all-start = ((f32[32,1,128]{2,1,0:T(1,128)}), f32[32,1,128]{2,1,0:T(1,128)S(1)}, u32[]{:S(2)}, u32[]{:S(2)}) async-start(f32[32,1,128]{2,1,0:T(1,128)} %head_stats.5._stats), calls=%async_computation | async-start | bytes 32768 | tf_op jit(solution)/shard_map/all_to_all | solution.py:719
  (45 other events, 515.4 us)
